TPU v7x, 128 devices: a whole 4x4x4 slice. The times are simulated.
128 devices in a mesh: gx: 8 (over y, core), gy: 4 (over z), gz: 4 (over x).
Axes of the slice: x: 4, y: 4, z: 4, core: 2. Of those that a mesh axis runs over, the one named last changes fastest.
Arguments:
- displacement: float32 [3, 64, 512, 512], P(None, 'gx', 'gy', 'gz'), may hold values from -0.9 to 0.9
- density: float32 [64, 512, 512], P('gx', 'gy', 'gz'), may hold values from 0.05 to 1
- element_stiffness: float32 [24, 24], replicated, may hold values from -0.3 to 8.3, as said below
Outputs:
- design_sensitivity: float32 [64, 512, 512], P('gx', 'gy', 'gz')
Inputs may be any that keep to these rules, and one draw needn't show every extreme that they name: `element_stiffness`: symmetric.
All inputs are finite; a program needn't handle non-finite values.
Results may differ from a plain program's by a relative error of at most 0.00027.
Values sent between devices are 32-bit elements; how exact they have to be, the bound alone decides.
No kernel may reach another device: no remote copies, remote signals or barrier semaphores. Data moves between devices by JAX's collectives and lax.ppermute only.
A program may use at most 128 MiB of HBM per device.

v0:
```python
import jax
import jax.numpy as jnp
from jax import lax
from jax.sharding import PartitionSpec as P

LEVELS = 3
CYCLES = 2
PRE_SWEEPS = 2
POST_SWEEPS = 2
COARSE_SWEEPS = 8
FILTER_COEF = 36


DAMPING = 0.95


def with_halo(array, sides, width):
    for axis, dim in sides:
        size, length = (lax.axis_size(axis), array.shape[dim])
        up = [(i, (i + 1) % size) for i in range(size - 1)]
        down = [(j, i) for i, j in up]
        last = lax.slice_in_dim(array, length - width, length, axis=dim)
        first = lax.slice_in_dim(array, 0, width, axis=dim)
        before = lax.ppermute(last, axis, up)
        after = lax.ppermute(first, axis, down)
        array = jnp.concatenate([before, array, after], axis=dim)
    return array


def passed_along(value, axis, steps):
    count = lax.axis_size(axis)
    first, last = (max(0, -steps), min(count, count - steps))
    return lax.ppermute(value, axis, [(source, source + steps) for source in range(first, last)])


def beside_sum(padded):
    total = padded[2:, 1:-1, 1:-1] + padded[:-2, 1:-1, 1:-1]
    total = total + padded[1:-1, 2:, 1:-1] + padded[1:-1, :-2, 1:-1]
    total = total + padded[1:-1, 1:-1, 2:] + padded[1:-1, 1:-1, :-2]
    return total


def local_geometry(local_shape, starts, totals, margin, coefficient):
    full_shape = tuple((length + 2 * margin for length in local_shape))
    counts = jnp.zeros(full_shape, jnp.float32)
    inside = jnp.ones(full_shape, jnp.bool_)
    for axis_pos in range(3):
        places = starts[axis_pos] - margin + lax.iota(jnp.int32, full_shape[axis_pos])
        view_shape = [1, 1, 1]
        view_shape[axis_pos] = full_shape[axis_pos]
        places = places.reshape(view_shape)
        counts = (
            counts
            + (places > 0).astype(jnp.float32)
            + (places < totals[axis_pos] - 1).astype(jnp.float32)
        )
        inside = inside & (places >= 0) & (places < totals[axis_pos])
    return (1.0 + coefficient * counts, inside)


def relax_padded(iterate, source, padded, diagonal, coefficient):
    applied = diagonal * iterate - coefficient * beside_sum(padded)
    return iterate + DAMPING * (source - applied) / diagonal


def restrict_mean(residual):
    size_x, size_y, size_z = residual.shape
    return residual.reshape(size_x // 2, 2, size_y // 2, 2, size_z // 2, 2).mean(axis=(1, 3, 5))


def prolong(coarse):
    size_x, size_y, size_z = coarse.shape
    spread = jnp.broadcast_to(coarse[:, None, :, None, :, None], (size_x, 2, size_y, 2, size_z, 2))
    return spread.reshape(2 * size_x, 2 * size_y, 2 * size_z)


def face_halo(iterate):
    return with_halo(iterate, (("gx", 0), ("gy", 1), ("gz", 2)), 1)


def smooth(iterate, source, level, sweeps, zero_start):
    diagonal = level[4]
    coefficient = level[3]
    remaining = sweeps
    if zero_start:
        iterate = DAMPING * source / diagonal
        remaining = sweeps - 1
    for sweep_index in range(remaining):
        iterate = relax_padded(iterate, source, face_halo(iterate), diagonal, coefficient)
    return iterate


def coarse_solve(source, level):
    local_shape, starts, totals, coefficient, diagonal = level
    iterate = DAMPING * source / diagonal
    for sweep_index in range(COARSE_SWEEPS - 1):
        padded = with_halo(iterate, (("gx", 0), ("gy", 1), ("gz", 2)), 1)
        iterate = relax_padded(iterate, source, padded, diagonal, coefficient)
    return iterate


def vee_cycle(source, iterate, levels, level_index, zero_start):
    level = levels[level_index]
    if level_index == LEVELS - 1:
        return coarse_solve(source, level)
    coefficient = level[3]
    diagonal = level[4]
    iterate = smooth(iterate, source, level, PRE_SWEEPS, zero_start)
    applied = diagonal * iterate - coefficient * beside_sum(face_halo(iterate))
    residual = source - applied
    correction = vee_cycle(restrict_mean(residual), None, levels, level_index + 1, True)
    iterate = iterate + prolong(correction)
    return smooth(iterate, source, level, POST_SWEEPS, False)


def element_energy(extended, element_stiffness, cells_y, cells_z, block_index):
    window = lax.dynamic_slice_in_dim(extended, block_index * 4, 5, 1)
    corners = [
        window[:, shift_x : shift_x + 4, shift_y : shift_y + cells_y, shift_z : shift_z + cells_z]
        for shift_z in (0, 1)
        for shift_y in (0, 1)
        for shift_x in (0, 1)
    ]
    stacked = jnp.concatenate(corners, axis=0).reshape(24, -1)
    pushed = jnp.dot(element_stiffness, stacked, precision=lax.Precision.HIGHEST)
    return jnp.sum(stacked * pushed, axis=0).reshape(4, cells_y, cells_z)


def per_device(displacement, density, element_stiffness):
    extents = (lax.axis_size("gx"), lax.axis_size("gy"), lax.axis_size("gz"))
    positions = (lax.axis_index("gx"), lax.axis_index("gy"), lax.axis_index("gz"))
    upper_rim = passed_along(displacement[:, 0:1], "gx", -1)
    extended = jnp.concatenate((displacement, upper_rim), axis=1)
    upper_rim = passed_along(extended[:, :, 0:1], "gy", -1)
    extended = jnp.concatenate((extended, upper_rim), axis=2)
    upper_rim = passed_along(extended[:, :, :, 0:1], "gz", -1)
    extended = jnp.concatenate((extended, upper_rim), axis=3)
    cells_x, cells_y, cells_z = density.shape
    energy = lax.map(
        lambda block_index: element_energy(
            extended, element_stiffness, cells_y, cells_z, block_index
        ),
        jnp.arange(cells_x // 4, dtype=jnp.int32),
    )
    energy = energy.reshape(density.shape)
    physical_sens = -3.0 * density * density * energy
    levels = []
    for level_index in range(LEVELS):
        local_shape = (cells_x >> level_index, cells_y >> level_index, cells_z >> level_index)
        starts = tuple((positions[axis_pos] * local_shape[axis_pos] for axis_pos in range(3)))
        totals = tuple((extents[axis_pos] * local_shape[axis_pos] for axis_pos in range(3)))
        coefficient = FILTER_COEF / 4.0**level_index
        diagonal, inside = local_geometry(local_shape, starts, totals, 0, coefficient)
        levels.append((local_shape, starts, totals, coefficient, diagonal))
    iterate = jnp.zeros(density.shape, jnp.float32)
    for cycle_index in range(CYCLES):
        iterate = vee_cycle(physical_sens, iterate, levels, 0, cycle_index == 0)
    return iterate


def solution(mesh):
    return jax.shard_map(
        per_device,
        mesh=mesh,
        in_specs=(P(None, "gx", "gy", "gz"), P("gx", "gy", "gz"), P()),
        out_specs=P("gx", "gy", "gz"),
        check_vma=False,
    )
```

profile of v0, /device:TPU:1, one launch (start us, length us, event | category | flops | bytes accessed | tf_op | source)
XLA Modules:
  0.0 1026.9 jit_solution(12506260910748740151)
XLA Ops:
  27.7 51.1 %while.10 = (s32[]{:T(128)}, f32[2,4,128,128]{3,2,1,0:T(8,128)S(1)}, s32[2]{0:T(128)S(1)}, f32[3,9,129,129]{3,2,1,0:T(8,128)}, f32[24,24]{1,0:T(8,128)S(1)}, /*i...) while((s32[]{:T(128)}, f32[2,4,128,128]{3,2,1,0:T(8,128)S(1)}, s32[2]{0:T(128)S(1)}, ...), condition=%wide.region_2.3_spmd, body=%wide.region_0.2_spmd.sunk | while | flops 456065024 | bytes 26852296 | solution.py:139
  35.3 17.9 %fusion.411 = f32[65536]{0:T(1024)S(1)} fusion(f32[24,24]{1,0:T(8,128)S(1)} %get-tuple-element.303, f32[3,8,512,128]{3,2,1,0:T(8,128)S(1)} %bitcast.39), kind=kOutput, calls=%fused_computation.4.clone.1 | convolution fusion | flops 456065024 | bytes 6555904 | tf_op jit(solution)/shard_map/while/body/eval_jaxpr/dot_general | solution.py:125
  60.9 17.9 %fusion.411 = f32[65536]{0:T(1024)S(1)} fusion(f32[24,24]{1,0:T(8,128)S(1)} %get-tuple-element.303, f32[3,8,512,128]{3,2,1,0:T(8,128)S(1)} %bitcast.39), kind=kOutput, calls=%fused_computation.4.clone.1 | convolution fusion | flops 456065024 | bytes 6555904 | tf_op jit(solution)/shard_map/while/body/eval_jaxpr/dot_general | solution.py:125
  133.5 34.9 %reshape.174 = f32[4,2,64,2,64,2]{5,4,3,2,1,0:T(8,128)} reshape(f32[8,128,128]{2,1,0:T(8,128)S(1)} %fusion.84) | data formatting | bytes 1048576 | tf_op jit(solution)/shard_map/reshape | solution.py:68
  168.4 12.2 %reduce_sum.45 = f32[4,64,64]{2,1,0:T(8,128)S(1)} reduce(f32[4,2,64,2,64,2]{5,4,3,2,1,0:T(8,128)} %reshape.174, f32[]{:T(128)} %constant.40.clone.1), dimensions={1,3,5}, to_apply=%region_3.4 | reduce | flops 114688 | bytes 589828 | tf_op jit(solution)/shard_map/reduce_sum | solution.py:68
  180.8 4.7 collective-permute-start.16
  224.1 4.7 collective-permute-start.26
  234.1 5.7 reshape.175
  258.8 4.7 collective-permute-start.32
  281.9 4.6 collective-permute-start.38
  304.8 4.6 collective-permute-start.44
  327.7 4.6 collective-permute-start.50
  350.6 4.6 collective-permute-start.56
  373.5 4.6 collective-permute-start.62
  396.4 4.6 collective-permute-start.68
  406.0 4.9 reshape.176
  427.0 4.6 collective-permute-start.74
  451.9 4.7 collective-permute-start.80
  461.9 11.5 %broadcast_in_dim.16 = f32[4,2,64,2,64,2]{5,4,3,2,1,0:T(8,128)} broadcast(f32[4,64,64]{2,1,0:T(8,128)S(1)} %fusion.148), dimensions={0,2,4} | broadcast | bytes 589824 | tf_op jit(solution)/shard_map/broadcast_in_dim | solution.py:73
  473.4 24.0 %reshape.177 = f32[8,128,128]{2,1,0:T(8,128)S(1)} reshape(f32[4,2,64,2,64,2]{5,4,3,2,1,0:T(8,128)} %broadcast_in_dim.16) | data formatting | bytes 1048576 | tf_op jit(solution)/shard_map/reshape | solution.py:74
  513.7 4.7 collective-permute-start.86
  618.3 34.9 %reshape.178 = f32[4,2,64,2,64,2]{5,4,3,2,1,0:T(8,128)} reshape(f32[8,128,128]{2,1,0:T(8,128)S(1)} %fusion.32) | data formatting | bytes 1048576 | tf_op jit(solution)/shard_map/reshape | solution.py:68
  653.2 12.2 %reduce_sum.47 = f32[4,64,64]{2,1,0:T(8,128)S(1)} reduce(f32[4,2,64,2,64,2]{5,4,3,2,1,0:T(8,128)} %reshape.178, f32[]{:T(128)} %constant.40.clone.1), dimensions={1,3,5}, to_apply=%region_5.6 | reduce | flops 114688 | bytes 589828 | tf_op jit(solution)/shard_map/reduce_sum | solution.py:68
  707.0 4.7 collective-permute-start.122
  717.0 5.7 reshape.179
  739.8 4.7 collective-permute-start.128
  887.2 4.9 reshape.180
  908.3 4.6 collective-permute-start.170
  932.9 4.7 collective-permute-start.176
  942.9 11.5 %broadcast_in_dim.18 = f32[4,2,64,2,64,2]{5,4,3,2,1,0:T(8,128)} broadcast(f32[4,64,64]{2,1,0:T(8,128)S(1)} %fusion.107), dimensions={0,2,4} | broadcast | bytes 589824 | tf_op jit(solution)/shard_map/broadcast_in_dim | solution.py:73
  954.5 24.0 %reshape.181 = f32[8,128,128]{2,1,0:T(8,128)S(1)} reshape(f32[4,2,64,2,64,2]{5,4,3,2,1,0:T(8,128)} %broadcast_in_dim.18) | data formatting | bytes 1048576 | tf_op jit(solution)/shard_map/reshape | solution.py:74
  994.6 4.7 collective-permute-start.182
  (612 shorter events, 719.7 us)
Async XLA Ops:
  0.9 7.9 collective-permute-start
  123.9 8.7 collective-permute-start.14
  196.9 8.9 collective-permute-start.19
  198.2 9.2 collective-permute-start.20
  222.8 9.3 collective-permute-start.25
  224.1 9.7 collective-permute-start.26
  258.8 7.0 collective-permute-start.32
  281.9 6.9 collective-permute-start.38
  304.8 6.9 collective-permute-start.44
  327.7 6.9 collective-permute-start.50
  350.6 6.9 collective-permute-start.56
  373.5 6.9 collective-permute-start.62
  396.4 6.9 collective-permute-start.68
  425.7 9.2 collective-permute-start.73
  427.0 9.6 collective-permute-start.74
  450.6 9.3 collective-permute-start.79
  451.9 9.7 collective-permute-start.80
  681.1 9.1 collective-permute-start.115
  682.4 9.5 collective-permute-start.116
  705.7 9.3 collective-permute-start.121
  707.0 9.8 collective-permute-start.122
  739.8 7.0 collective-permute-start.128
  762.8 6.9 collective-permute-start.134
  785.8 6.9 collective-permute-start.140
  808.7 6.9 collective-permute-start.146
  831.6 6.9 collective-permute-start.152
  854.5 6.9 collective-permute-start.158
  877.6 6.9 collective-permute-start.164
  907.0 9.2 collective-permute-start.169
  908.3 9.6 collective-permute-start.170
  931.6 9.3 collective-permute-start.175
  932.9 9.8 collective-permute-start.176
  (161 other events, 832.3 us)
where the time goes:
time: 1040 us; the launch traced here: 1030 us
  starting transfers between devices  452 us (43%)
  waiting for transfers between devices  282 us (27%)
  local copies, waits for them, and re-layouts  205 us (20%)
  other arithmetic  47 us (5%)
  matrix products  35.8 us (3%)
    ppermute x93, starting transfers between devices, with_halo(): before = lax.ppermute(last, axis, up)  303 us
    ppermute x93, waiting for transfers between devices, with_halo(): after = lax.ppermute(first, axis, down)  229 us
    ppermute x93, starting transfers between devices, with_halo(): after = lax.ppermute(first, axis, down)  143 us
    reshape x4, local copies, waits for them, and re-layouts, restrict_mean(): residual.reshape(size_x // 2, 2, size_y // 2, 2, size_z // 2, 2)  81.3 us
    reshape x4, local copies, waits for them, and re-layouts, prolong(): return spread.reshape(2 * size_x, 2 * size_y, 2 * size_z)  57.7 us
    ppermute x93, waiting for transfers between devices, with_halo(): before = lax.ppermute(last, axis, up)  43.1 us
    dot_general x2, matrix products, element_energy(): jnp.dot(element_stiffness, stacked, precision=lax.Precision.HIGHEST)  35.8 us
    reduce_sum x4, other arithmetic, restrict_mean(): residual.reshape(size_x // 2, 2, size_y // 2, 2, size_z // 2, 2)  29.6 us
  transfers between devices with their start and end apart: 189, of which 118 were waited for; matrix products, arithmetic and copies ran while one was open for 1% of the time, Pallas kernels for 0%

commit v1 on v0

v1 whole, which is shorter than its diff:
```python
import jax
import jax.numpy as jnp
from jax import lax
from jax.experimental import pallas as pl
from jax.experimental.pallas import tpu as pltpu
from jax.sharding import PartitionSpec as P

FILTER_COEF = 36.0
DAMPING = 0.95
S0 = FILTER_COEF
S1 = FILTER_COEF / 4.0
S2 = FILTER_COEF / 16.0
KEEP = 1.0 - DAMPING
HIGH = lax.Precision.HIGHEST
F32 = jnp.float32

PL0, R0 = 24, 160
PL1, R1 = 42, 128
PL2, R2 = 18, 72


def iota(shape, dim):
    return lax.broadcasted_iota(jnp.int32, shape, dim)


def next_lane(value):
    return pltpu.roll(value, 127, 1)


def prev_lane(value):
    return pltpu.roll(value, 1, 1)


def axis_count(place, total):
    return jnp.where(place > 0, 1.0, 0.0) + jnp.where(place < total - 1, 1.0, 0.0)


def make_tables(weight, diag, rows, row_off, lane_place, lane_ok, base_y, base_z, total, scale):
    y = iota((rows, 128), 0) - row_off + base_y
    z = lane_place + base_z
    inside = lane_ok & (y >= 0) & (y < total) & (z >= 0) & (z < total)
    count = axis_count(y, total) + axis_count(z, total)
    weight[0] = jnp.zeros((rows, 128), F32)
    for i in (1, 2):
        value = 1.0 + scale * (count + float(i))
        weight[i] = jnp.where(inside, DAMPING / value, 0.0)
        if diag is not None:
            diag[i] = value


def x_index(place, total):
    edge = (place == 0) | (place == total - 1)
    out = (place < 0) | (place >= total)
    return jnp.where(out, 0, jnp.where(edge, 1, 2))


def lanes_main():
    return iota((R0, 128), 1)


def level0_tables(pos, wm, ws, dm):
    lane = lanes_main()
    yes = lane >= 0
    make_tables(wm, dm, R0, 16, lane, yes, pos[1] * 128, pos[2] * 128, 512, S0)
    side = jnp.where(lane < 64, lane + 128, lane - 128)
    ok = (lane < 8) | (lane >= 120)
    make_tables(ws, None, R0, 16, side, ok, pos[1] * 128, pos[2] * 128, 512, S0)


def level0_sweep(pos, src, dst, fm, fs, wm, ws, first, last, side):
    lane = iota((48, 128), 1)

    def body(p, carry):
        i = x_index(pos[0] * 8 + p - 8, 64)
        for r in range(8, 152, 48):
            rows = pl.ds(r, 48)
            up, dn = pl.ds(r - 1, 48), pl.ds(r + 1, 48)
            m, s = src[0][p, rows], src[1][p, rows]
            mr, sr, ml, sl = next_lane(m), next_lane(s), prev_lane(m), prev_lane(s)
            tot = src[0][p - 1, rows] + src[0][p + 1, rows] + src[0][p, up] + src[0][p, dn]
            tot = tot + jnp.where(lane == 127, sr, mr) + jnp.where(lane == 0, sl, ml)
            dst[0][p, rows] = KEEP * m + wm[i, rows] * (fm[p, rows] + S0 * tot)
            if side:
                tot = src[1][p - 1, rows] + src[1][p + 1, rows] + src[1][p, up] + src[1][p, dn]
                tot = tot + jnp.where(lane == 127, mr, sr) + jnp.where(lane == 0, ml, sl)
                dst[1][p, rows] = KEEP * s + ws[i, rows] * (fs[p, rows] + S0 * tot)
        return carry

    lax.fori_loop(first, last + 1, body, 0)


def restrict_matrix(size):
    src, dst = iota((size, 128), 0), iota((size, 128), 1)
    col = jnp.where(dst < 64, dst, dst - 64)
    ok = (dst < 86) | (dst >= 106)
    return jnp.where(ok & (src // 2 == col), 0.125, 0.0)


def level0_restrict(pos, src, fm, dm, tmp, out):
    lane = iota((64, 128), 1)
    matrix = restrict_matrix(128)

    def body(k, carry):
        for r in (0, 64):
            both = None
            for q in (0, 1):
                p = 8 + 2 * k + q
                i = x_index(pos[0] * 8 + p - 8, 64)
                rows = pl.ds(r + 16, 64)
                m, s = src[0][p, rows], src[1][p, rows]
                tot = src[0][p - 1, rows] + src[0][p + 1, rows]
                tot = tot + src[0][p, pl.ds(r + 15, 64)] + src[0][p, pl.ds(r + 17, 64)]
                tot = tot + jnp.where(lane == 127, next_lane(s), next_lane(m))
                tot = tot + jnp.where(lane == 0, prev_lane(s), prev_lane(m))
                res = fm[p, rows] + S0 * tot - dm[i, rows] * m
                both = res if both is None else both + res
            tmp[pl.ds(r, 64)] = both
        pair = tmp[pl.ds(0, 64, stride=2)] + tmp[pl.ds(1, 64, stride=2)]
        out[k] = jnp.dot(pair, matrix, precision=HIGH, preferred_element_type=F32)
        return carry

    lax.fori_loop(0, 4, body, 0)


def plane_sweep(src, dst, f, w, first, last, x_off, total, rows, scale):
    def body(p, carry):
        i = x_index(p - x_off, total)
        n = rows - 16
        mid = pl.ds(8, n)
        m = src[p, mid]
        tot = src[p - 1, mid] + src[p + 1, mid] + src[p, pl.ds(7, n)] + src[p, pl.ds(9, n)]
        tot = tot + next_lane(m) + prev_lane(m)
        dst[p, mid] = KEEP * m + w[i, mid] * (f[p, mid] + scale * tot)
        return carry

    lax.fori_loop(first, last + 1, body, 0)


def coarse_levels(pos, blocks, f1, va, vb, f2, a2, b2, w1, d1, w2, tmp):
    gx = pos[0]
    lane1 = iota((R1, 128), 1)
    z1 = jnp.where(lane1 < 96, lane1, lane1 - 128)
    ok1 = (lane1 < 86) | (lane1 >= 106)
    make_tables(w1, d1, R1, 32, z1, ok1, pos[1] * 64, pos[2] * 64, 256, S1)
    lane2 = iota((R2, 128), 1)
    z2 = jnp.where(lane2 < 64, lane2, lane2 - 128)
    ok2 = (lane2 < 43) | (lane2 >= 117)
    make_tables(w2, None, R2, 20, z2, ok2, pos[1] * 32, pos[2] * 32, 128, S2)

    zero = jnp.zeros((R1, 128), F32)
    for p in list(range(0, 5)) + list(range(37, 42)):
        f1[p] = zero
        va[p] = zero
        vb[p] = zero
    for p in range(5, 37):
        for ref in (va, vb):
            ref[p, pl.ds(0, 8)] = jnp.zeros((8, 128), F32)
            ref[p, pl.ds(120, 8)] = jnp.zeros((8, 128), F32)
    for ref in (a2, b2):
        for p in (0, 17):
            ref[p] = jnp.zeros((R2, 128), F32)
        for p in range(1, 17):
            ref[p, pl.ds(0, 8)] = jnp.zeros((8, 128), F32)
            ref[p, pl.ds(64, 8)] = jnp.zeros((8, 128), F32)

    for m in range(4):
        for q in range(2):
            block = blocks[2 * m + q]
            own = gx if q == 0 else jnp.bitwise_xor(gx, 1)
            place = jnp.bitwise_and(own + 8 - 2 * m, 7)
            for j in range(4):
                p = 5 + 4 * place + j
                i = x_index(4 * place + j, 32)
                value = block[j]
                f1[p, pl.ds(8, 112)] = value
                va[p, pl.ds(8, 112)] = w1[i, pl.ds(8, 112)] * value

    plane_sweep(va, vb, f1, w1, 5, 36, 5, 32, R1, S1)

    src, dst = iota((128, 128), 0), iota((128, 128), 1)
    zs1 = jnp.where(src < 96, src, src - 128)
    ks1 = (src < 86) | (src >= 106)
    zd2 = jnp.where(dst < 64, dst, dst - 128)
    kd2 = (dst < 43) | (dst >= 117)
    down = jnp.where(ks1 & kd2 & (lax.shift_right_arithmetic(zs1, 1) == zd2), 0.125, 0.0)
    zs2 = jnp.where(src < 64, src, src - 128)
    ks2 = (src < 43) | (src >= 117)
    zd1 = jnp.where(dst < 96, dst, dst - 128)
    kd1 = (dst < 86) | (dst >= 106)
    up = jnp.where(ks2 & kd1 & (lax.shift_right_arithmetic(zd1, 1) == zs2), 1.0, 0.0)

    def restrict(k, carry):
        both = None
        mid = pl.ds(8, 112)
        for q in (0, 1):
            p = 5 + 2 * k + q
            i = x_index(p - 5, 32)
            m = vb[p, mid]
            tot = vb[p - 1, mid] + vb[p + 1, mid] + vb[p, pl.ds(7, 112)] + vb[p, pl.ds(9, 112)]
            tot = tot + next_lane(m) + prev_lane(m)
            res = f1[p, mid] + S1 * tot - d1[i, mid] * m
            both = res if both is None else both + res
        tmp[pl.ds(0, 112)] = both
        pair = tmp[pl.ds(0, 56, stride=2)] + tmp[pl.ds(1, 56, stride=2)]
        value = jnp.dot(pair, down, precision=HIGH, preferred_element_type=F32)
        f2[1 + k, pl.ds(8, 56)] = value
        a2[1 + k, pl.ds(8, 56)] = w2[x_index(k, 16), pl.ds(8, 56)] * value
        return carry

    lax.fori_loop(0, 16, restrict, 0)

    src2, dst2 = a2, b2
    for _ in range(7):
        plane_sweep(src2, dst2, f2, w2, 1, 16, 1, 16, R2, S2)
        src2, dst2 = dst2, src2

    def prolong(k, carry):
        e = jnp.dot(src2[1 + k, pl.ds(8, 56)], up, precision=HIGH, preferred_element_type=F32)
        for q in (0, 1):
            for h in (0, 1):
                rows = pl.ds(8 + h, 56, stride=2)
                vb[5 + 2 * k + q, rows] = vb[5 + 2 * k + q, rows] + e
        return carry

    lax.fori_loop(0, 16, prolong, 0)
    plane_sweep(vb, va, f1, w1, 4 * gx + 1, 4 * gx + 12, 5, 32, R1, S1)
    plane_sweep(va, vb, f1, w1, 4 * gx + 2, 4 * gx + 11, 5, 32, R1, S1)


def level0_prolong(pos, e1, old, new, first, last):
    src, dst = iota((128, 256), 0), iota((128, 256), 1)
    zs = jnp.where(src < 96, src, src - 128)
    side = dst - 128
    zd = jnp.where(dst < 128, dst, jnp.where(side < 64, side + 128, side - 128))
    ok = (dst < 128) | (side < 8) | (side >= 120)
    up = jnp.where(ok & (lax.shift_right_arithmetic(zd, 1) == zs), 1.0, 0.0)

    def body(k, carry):
        e = e1[4 * pos[0] + 1 + k, pl.ds(28, 72)]
        e = jnp.dot(e, up, precision=HIGH, preferred_element_type=F32)
        for q in (0, 1):
            p = 2 * k + q
            for h in (0, 1):
                rows = pl.ds(8 + h, 72, stride=2)
                new[0][p, rows] = old[0][p, rows] + e[:, :128]
                new[1][p, rows] = old[1][p, rows] + e[:, 128:]
        return carry

    lax.fori_loop(first // 2, last // 2 + 1, body, 0)


def zero_pads(refs, first, last):
    zero = jnp.zeros((8, 128), F32)
    for ref in refs:
        for p in range(first, last + 1):
            ref[p, pl.ds(0, 8)] = zero
            ref[p, pl.ds(152, 8)] = zero


def rim_kernel(u, cols, rows):
    lane = iota((128, 128), 1)
    acc = jnp.zeros((128, 128), F32)
    for d in range(3):
        for x in range(8):
            k = 8 * d + x
            value = u[d, x]
            acc = jnp.where(lane == k, pltpu.roll(value, k, 1) if k else value, acc)
            rows[pl.ds(k, 1)] = u[d, x, pl.ds(0, 1)]
    cols[...] = acc


def energy_kernel(pos, stiff, u, xface, yrim, zrim, xrim, rho, f, pack, u0, u1, table):
    gx, gy, gz = pos[0], pos[1], pos[2]
    keep_x = jnp.where(gx < 7, 1.0, 0.0)
    keep_y = jnp.where(gy < 3, 1.0, 0.0)
    keep_z = jnp.where(gz < 3, 1.0, 0.0)
    n = 0
    for i in range(24):
        for j in range(i, 24):
            value = stiff[i, j] if i == j else stiff[i, j] + stiff[j, i]
            table[n] = jnp.full((8, 128), value, F32)
            n += 1
    lane = iota((128, 128), 1)
    lane8 = iota((8, 128), 1)
    for d in range(3):
        for x in range(9):
            k = 8 * d + x
            if x < 8:
                body = u[d, x]
                col = zrim[...]
                row = yrim[pl.ds(k, 1)]
                corner = yrim[pl.ds(24, 8)]
            else:
                k = 8 * d
                body = xface[d] * keep_x
                col = xrim[pl.ds(32, 128)] * keep_x
                row = xrim[pl.ds(k, 1)] * keep_x
                corner = xrim[pl.ds(24, 8)] * keep_x
            row = jnp.broadcast_to(row, (8, 128)) * keep_y
            corner = jnp.broadcast_to(corner[0:1], (8, 128)) * (keep_y * keep_z)
            q = 9 * d + x
            u0[q, pl.ds(0, 128)] = body
            u0[q, pl.ds(128, 8)] = row
            u1[q, pl.ds(0, 128)] = jnp.where(
                lane == 127, pltpu.roll(col, 127 - k, 1) * keep_z, next_lane(body))
            u1[q, pl.ds(128, 8)] = jnp.where(
                lane8 == 127, pltpu.roll(corner, 127 - k, 1), next_lane(row))

    def chunk(c, carry):
        x, y = c // 16, pl.multiple_of((c % 16) * 8, 8)
        val = []
        for c_z in (0, 1):
            for b in (0, 1):
                for a in (0, 1):
                    for d in range(3):
                        ref = u1 if c_z else u0
                        val.append(ref[9 * d + x + a, pl.ds(y + b, 8)])
        energy = None
        n = 0
        for i in range(24):
            acc = None
            for j in range(i, 24):
                term = table[n] * val[j]
                acc = term if acc is None else acc + term
                n += 1
            acc = acc * val[i]
            energy = acc if energy is None else energy + acc
        r = rho[x, pl.ds(y, 8)]
        f[x, pl.ds(y, 8)] = -3.0 * r * r * energy
        return carry

    lax.fori_loop(0, 128, chunk, 0)
    acc = jnp.zeros((128, 128), F32)
    for x in range(8):
        value = f[x]
        low = pltpu.roll(value, 8 * x, 1) if x else value
        acc = jnp.where((lane >= 8 * x) & (lane < 8 * x + 8), low, acc)
        high = pltpu.roll(value, (8 * x + 72) % 128, 1)
        acc = jnp.where((lane >= 64 + 8 * x) & (lane < 72 + 8 * x), high, acc)
    pack[...] = acc


def spread(value, x):
    lane = iota(value.shape, 1)
    low = pltpu.roll(value, (128 - 8 * x) % 128, 1) if x else value
    high = pltpu.roll(value, (56 - 8 * x) % 128, 1)
    return jnp.where(lane < 64, low, high)


def first_kernel(pos, fl, fc, fr, hl, hc, hr, fm, fs, vm, vs, out, am, as_, wm, ws, dm, tmp):
    level0_tables(pos, wm, ws, dm)
    zero_pads((fm, fs, vm, vs, am, as_), 0, 23)
    for b, (blk, halo) in enumerate(((fl, hl), (fc, hc), (fr, hr))):
        for x in range(8):
            p = 8 * b + x
            i = x_index(pos[0] * 8 + p - 8, 64)
            parts = (
                (8, 8, halo[pl.ds(8 * x, 8)], spread(halo[pl.ds(64, 8)], x)),
                (16, 128, blk[x], spread(halo[pl.ds(144, 128)], x)),
                (144, 8, halo[pl.ds(72 + 8 * x, 8)], spread(halo[pl.ds(136, 8)], x)),
            )
            for start, size, main, side in parts:
                rows = pl.ds(start, size)
                fm[p, rows] = main
                fs[p, rows] = side
                am[p, rows] = wm[i, rows] * main
                as_[p, rows] = ws[i, rows] * side
    level0_sweep(pos, (am, as_), (vm, vs), fm, fs, wm, ws, 2, 21, True)
    level0_restrict(pos, (vm, vs), fm, dm, tmp, out)


def middle_kernel(pos, *refs):
    blocks = refs[:8]
    fm, fs, vm, vs, om, os_, out = refs[8:15]
    am, as_, bm, bs, wm, ws, dm, f1, va, vb, f2, a2, b2, w1, d1, w2, tmp = refs[15:]
    coarse_levels(pos, blocks, f1, va, vb, f2, a2, b2, w1, d1, w2, tmp)
    level0_tables(pos, wm, ws, dm)
    zero_pads((am, as_, bm, bs, om, os_), 0, 23)
    level0_prolong(pos, vb, (vm, vs), (am, as_), 2, 21)
    level0_sweep(pos, (am, as_), (bm, bs), fm, fs, wm, ws, 3, 20, True)
    level0_sweep(pos, (bm, bs), (am, as_), fm, fs, wm, ws, 4, 19, True)
    level0_sweep(pos, (am, as_), (bm, bs), fm, fs, wm, ws, 5, 18, True)
    level0_sweep(pos, (bm, bs), (om, os_), fm, fs, wm, ws, 6, 17, True)
    level0_restrict(pos, (om, os_), fm, dm, tmp, out)


def last_kernel(pos, *refs):
    blocks = refs[:8]
    fm, fs, vm, vs, out = refs[8:13]
    am, as_, bm, bs, wm, ws, f1, va, vb, f2, a2, b2, w1, d1, w2, tmp = refs[13:]
    coarse_levels(pos, blocks, f1, va, vb, f2, a2, b2, w1, d1, w2, tmp)
    level0_tables(pos, wm, ws, None)
    zero_pads((am, as_, bm, bs), 0, 23)
    level0_prolong(pos, vb, (vm, vs), (am, as_), 6, 17)
    level0_sweep(pos, (am, as_), (bm, bs), fm, fs, wm, ws, 7, 16, True)
    level0_sweep(pos, (bm, bs), (am, as_), fm, fs, wm, ws, 8, 15, False)
    for x in range(8):
        out[x] = am[8 + x, pl.ds(16, 128)]


SMEM = pl.BlockSpec(memory_space=pltpu.SMEM)
VM = pl.BlockSpec(memory_space=pltpu.VMEM)


def shape(*dims):
    return jax.ShapeDtypeStruct(dims, F32)


def vmem(*dims):
    return pltpu.VMEM(dims, F32)


def call(kernel, outs, scratch, scalars, args, name):
    specs = [SMEM] * scalars + [VM] * (len(args) - scalars)
    return pl.pallas_call(
        kernel,
        out_shape=outs,
        in_specs=specs,
        out_specs=[VM] * len(outs),
        scratch_shapes=scratch,
        compiler_params=pltpu.CompilerParams(vmem_limit_bytes=48 << 20),
        name=name,
    )(*args)


def shifted(value, axis, step):
    size = lax.axis_size(axis)
    return lax.ppermute(value, axis, [(i, (i + step) % size) for i in range(size)])


def swapped(value):
    return lax.ppermute(value, "gx", [(i, i ^ 1) for i in range(lax.axis_size("gx"))])


COARSE_SCRATCH = [
    vmem(PL1, R1, 128), vmem(PL1, R1, 128), vmem(PL1, R1, 128),
    vmem(PL2, R2, 128), vmem(PL2, R2, 128), vmem(PL2, R2, 128),
    vmem(3, R1, 128), vmem(3, R1, 128), vmem(3, R2, 128), vmem(128, 128),
]
TABLE = vmem(3, R0, 128)
WIDE = vmem(PL0, R0, 128)


def gather_level1(own):
    lane = lax.broadcasted_iota(jnp.int32, own.shape, 2)
    right, left = shifted(own, "gz", -1), shifted(own, "gz", 1)
    own = jnp.where(lane < 64, own, jnp.where(lane < 96, right, left))
    low, high = shifted(own[:, 40:], "gy", 1), shifted(own[:, :24], "gy", -1)
    own = jnp.concatenate([low, own, high], axis=1)
    blocks = []
    for m in range(4):
        part = own if m == 0 else shifted(own, "gx", 2 * m)
        blocks += [part, swapped(part)]
    return blocks


def per_device(u, rho, stiff):
    pos = jnp.stack([lax.axis_index(a) for a in ("gx", "gy", "gz")]).astype(jnp.int32)
    cols, rows = call(rim_kernel, [shape(128, 128), shape(24, 128)], [], 0, [u], "rims")
    xface = shifted(u[:, 0], "gx", -1)
    zrim = shifted(cols, "gz", -1)
    yrim = shifted(jnp.concatenate([rows, zrim[:8]], axis=0), "gy", -1)
    xrim = shifted(jnp.concatenate([yrim, zrim], axis=0), "gx", -1)
    f, pack = call(
        energy_kernel, [shape(8, 128, 128), shape(128, 128)],
        [vmem(27, 136, 128), vmem(27, 136, 128), vmem(300, 8, 128)], 2,
        [pos, stiff, u, xface, yrim, zrim, xrim, rho], "energy")

    fl, fr = shifted(f, "gx", 1), shifted(f, "gx", -1)
    lane = lax.broadcasted_iota(jnp.int32, pack.shape, 1)
    z = jnp.where(lane < 64, shifted(pack, "gz", -1), shifted(pack, "gz", 1))
    up = jnp.concatenate([f[:, 120:].reshape(64, 128), z[120:]], axis=0)
    down = jnp.concatenate([f[:, :8].reshape(64, 128), z[:8]], axis=0)
    h = jnp.concatenate([shifted(up, "gy", 1), shifted(down, "gy", -1), z], axis=0)
    hl, hr = shifted(h, "gx", 1), shifted(h, "gx", -1)

    wide = shape(PL0, R0, 128)
    fm, fs, vm, vs, f1 = call(
        first_kernel, [wide, wide, wide, wide, shape(4, 64, 128)],
        [WIDE, WIDE, TABLE, TABLE, TABLE, vmem(128, 128)], 1,
        [pos, fl, f, fr, hl, h, hr], "first")
    vm, vs, f1 = call(
        middle_kernel, [wide, wide, shape(4, 64, 128)],
        [WIDE] * 4 + [TABLE] * 3 + COARSE_SCRATCH, 1,
        [pos, *gather_level1(f1), fm, fs, vm, vs], "middle")
    (out,) = call(
        last_kernel, [shape(8, 128, 128)],
        [WIDE] * 4 + [TABLE] * 2 + COARSE_SCRATCH, 1,
        [pos, *gather_level1(f1), fm, fs, vm, vs], "last")
    return out


def solution(mesh):
    return jax.shard_map(
        per_device,
        mesh=mesh,
        in_specs=(P(None, "gx", "gy", "gz"), P("gx", "gy", "gz"), P()),
        out_specs=P("gx", "gy", "gz"),
        check_vma=False,
    )
```

time: 1040 us -> 192 us (0.18); the launches traced: 1030 us -> 192 us
  starting transfers between devices: 452 us -> 57.6 us
  waiting for transfers between devices: 282 us -> 30.4 us
  local copies, waits for them, and re-layouts: 205 us -> 6.71 us
  Pallas kernels: 0 us -> 96.5 us
  other arithmetic: 47 us -> 0.21 us
  matrix products: 35.8 us -> 0 us
    ppermute x189 -> x34, starting transfers between devices: 452 us -> 57.6 us  [the longest x26 38.7 us: shifted(): lax.ppermute(value, axis, [(i, (i + step) % size) for i in range(size)])]
    ppermute x189 -> x34, waiting for transfers between devices: 282 us -> 30.4 us  [the longest x26 28.2 us: shifted(): lax.ppermute(value, axis, [(i, (i + step) % size) for i in range(size)])]
    reshape x8 -> x1, local copies, waits for them, and re-layouts: 139 us -> 0.01 us  [per_device(): up = jnp.concatenate([f[:, 120:].reshape(64, 128), z[120:]], axis=0)]
    pallas_call x0 -> x5, Pallas kernels: none -> 96.5 us  [call(): pl.pallas_call(kernel, out_shape=outs, in_specs=specs, out_specs=[VM] * l...]
    dot_general x2 -> x0, matrix products: 35.8 us -> none  [element_energy(): jnp.dot(element_stiffness, stacked, precision=lax.Precision.HIGHEST)]
    reduce_sum x4 -> x0, other arithmetic: 29.6 us -> none  [restrict_mean(): residual.reshape(size_x // 2, 2, size_y // 2, 2, size_z // 2, 2)]
    broadcast_in_dim x4 -> x0, local copies, waits for them, and re-layouts: 28.3 us -> none  [prolong(): jnp.broadcast_to(coarse[:, None, :, None, :, None], (size_x, 2, size_y, 2...]
    slice x83 -> x4, local copies, waits for them, and re-layouts: 15.3 us -> 0.02 us  [the longest x2 0.02 us: gather_level1(): low, high = (shifted(own[:, 40:], 'gy', 1), shifted(own[:, :24], 'gy', -1))]
  transfers between devices with their start and end apart: 189 -> 34, of which waited for: 118 -> 17; matrix products, arithmetic and copies ran while one was open for 1% -> 0% of each run, Pallas kernels for 0% -> 0%
where the time goes in v1:
time: 192 us
  Pallas kernels  96.5 us (50%)
  starting transfers between devices  57.6 us (30%)
  waiting for transfers between devices  30.4 us (16%)
  local copies, waits for them, and re-layouts  6.71 us (3%)
    pallas_call x5, Pallas kernels, call(): pl.pallas_call(kernel, out_shape=outs, in_specs=specs, out_specs=[VM] * l...  96.5 us
    ppermute x26, starting transfers between devices, shifted(): lax.ppermute(value, axis, [(i, (i + step) % size) for i in range(size)])  38.7 us
    ppermute x26, waiting for transfers between devices, shifted(): lax.ppermute(value, axis, [(i, (i + step) % size) for i in range(size)])  28.2 us
    ppermute x8, starting transfers between devices, swapped(): lax.ppermute(value, 'gx', [(i, i ^ 1) for i in range(lax.axis_size('gx'))])  18.9 us
    unnamed x20, local copies, waits for them, and re-layouts  6.66 us
  transfers between devices with their start and end apart: 34, of which 17 were waited for; matrix products, arithmetic and copies ran while one was open for 0% of the time, Pallas kernels for 0%

profile of v1, /device:TPU:1, one launch (start us, length us, event | category | flops | bytes accessed | tf_op | source)
XLA Modules:
  0.0 191.6 jit_solution(13000559014490976636)
XLA Ops:
  0.0 1.4 copy-done.4
  1.9 3.4 %collective-permute-start.1 = (f32[128,128]{1,0:T(8,128)S(1)}, f32[128,128]{1,0:T(8,128)S(1)}, u32[]{:S(2)}, u32[]{:S(2)}) collective-permute-start(f32[128,128]{1,0:T(8,128)S(1)} %get-tuple-element.18), channel_id=1, source_target_pairs={{0,3},{1,0},{2,1},{3,2},{4,7},{5,4},{6,5},{7,6},{8,11},{9,8},{10,9... | collective-permute-start | bytes 196616 | tf_op jit(solution)/shard_map/ppermute | solution.py:428
  6.6 3.8 %collective-permute-start.2 = (f32[32,128]{1,0:T(8,128)S(1)}, f32[32,128]{1,0:T(8,128)S(1)}, u32[]{:S(2)}, u32[]{:S(2)}) collective-permute-start(f32[32,128]{1,0:T(8,128)S(1)} %pad_maximum_fusion.6), channel_id=1, source_target_pairs={{0,12},{4,0},{8,4},{12,8},{1,13},{5,1},{9,5},{13,9},{2,14},{6,2},{... | collective-permute-start | bytes 49160 | tf_op jit(solution)/shard_map/ppermute | solution.py:428
  11.2 2.7 %collective-permute-start.3 = (f32[160,128]{1,0:T(8,128)S(1)}, f32[160,128]{1,0:T(8,128)S(1)}, u32[]{:S(2)}, u32[]{:S(2)}) collective-permute-start(f32[160,128]{1,0:T(8,128)S(1)} %pad_maximum_fusion.3), channel_id=1, source_target_pairs={{0,112},{16,0},{32,16},{48,32},{64,48},{80,64},{96,80},{112,96},{1... | collective-permute-start | bytes 245768 | tf_op jit(solution)/shard_map/ppermute | solution.py:428
  14.0 2.9 %collective-permute-done.3.xrim = f32[160,128]{1,0:T(8,128)S(1)} collective-permute-done((f32[160,128]{1,0:T(8,128)S(1)}, f32[160,128]{1,0:T(8,128)S(1)}, u32[]{:S(2)}, u32[]{:S(2)}) %collective-permute-start.3) | collective-permute-done | bytes 81952 | tf_op jit(solution)/shard_map/ppermute | solution.py:428
  16.9 15.1 %energy.1 = (f32[8,128,128]{2,1,0:T(8,128)S(1)}, f32[128,128]{1,0:T(8,128)S(1)}) custom-call(s32[3]{0:T(128)S(1)} %pad_add_fusion.pos, f32[24,24]{1,0:T(8,128)S(1)} %copy-done.9, f32[3,8,128,128]{3,2,1,0:T(8,128)S(1)} %copy-done.5, f32[3,128,128]{2,1,0:T(8,128)S(1)} %collective-permute-done.xface, f32[32,128]{1,0:T(8,128)S(1)} %collective-permute-done.2.yrim, ...), custom_call_target="tpu_custom_call" | custom-call | tf_op jit(solution)/shard_map/energy/pallas_call | solution.py:415
  32.9 2.6 %collective-permute-start.6 = (f32[128,128]{1,0:T(8,128)S(1)}, f32[128,128]{1,0:T(8,128)S(1)}, u32[]{:S(2)}, u32[]{:S(2)}) collective-permute-start(f32[128,128]{1,0:T(8,128)S(1)} %get-tuple-element.20), channel_id=1, source_target_pairs={{0,3},{1,0},{2,1},{3,2},{4,7},{5,4},{6,5},{7,6},{8,11},{9,8},{10,9... | collective-permute-start | bytes 196616 | tf_op jit(solution)/shard_map/ppermute | solution.py:428
  35.5 1.7 collective-permute-start.4
  37.3 3.3 %collective-permute-start.9 = (f32[72,128]{1,0:T(8,128)S(1)}, f32[72,128]{1,0:T(8,128)S(1)}, u32[]{:S(2)}, u32[]{:S(2)}) collective-permute-start(f32[72,128]{1,0:T(8,128)S(1)} %pad_maximum_fusion.5), channel_id=1, source_target_pairs={{0,12},{4,0},{8,4},{12,8},{1,13},{5,1},{9,5},{13,9},{2,14},{6,2},{... | collective-permute-start | bytes 110600 | tf_op jit(solution)/shard_map/ppermute | solution.py:428
  41.6 3.3 %collective-permute-done.8 = f32[72,128]{1,0:T(8,128)S(1)} collective-permute-done((f32[72,128]{1,0:T(8,128)S(1)}, f32[72,128]{1,0:T(8,128)S(1)}, u32[]{:S(2)}, u32[]{:S(2)}) %collective-permute-start.8) | collective-permute-done | bytes 36896 | tf_op jit(solution)/shard_map/ppermute | solution.py:428
  44.9 1.3 collective-permute-start.11
  46.9 2.7 %collective-permute-done.11.hr = f32[272,128]{1,0:T(8,128)S(1)} collective-permute-done((f32[272,128]{1,0:T(8,128)S(1)}, f32[272,128]{1,0:T(8,128)S(1)}, u32[]{:S(2)}, u32[]{:S(2)}) %collective-permute-start.11) | collective-permute-done | bytes 139296 | tf_op jit(solution)/shard_map/ppermute | solution.py:428
  49.6 8.1 %first.1 = (f32[24,160,128]{2,1,0:T(8,128)S(1)}, f32[24,160,128]{2,1,0:T(8,128)S(1)}, f32[24,160,128]{2,1,0:T(8,128)}, f32[24,160,128]{2,1,0:T(8,128)}, f32[4,64,128]{2,1,0:T(8,128)S(1)}) custom-call(s32[3]{0:T(128)S(1)} %pad_add_fusion.pos, f32[8,128,128]{2,1,0:T(8,128)S(1)} %collective-permute-done.4.fl, f32[8,128,128]{2,1,0:T(8,128)S(1)} %get-tuple-element.19.fc, ...), custom_call_target="tpu_custom_call" | custom-call | tf_op jit(solution)/shard_map/first/pallas_call | solution.py:415
  57.7 1.3 copy-done
  61.3 1.8 collective-permute-start.12
  63.1 2.3 %collective-permute-done.13 = f32[4,64,128]{2,1,0:T(8,128)S(1)} collective-permute-done((f32[4,64,128]{2,1,0:T(8,128)S(1)}, f32[4,64,128]{2,1,0:T(8,128)S(1)}, u32[]{:S(2)}, u32[]{:S(2)}) %collective-permute-start.13) | collective-permute-done | bytes 131104 | tf_op jit(solution)/shard_map/ppermute | solution.py:428
  66.0 2.7 %collective-permute-start.15 = (f32[4,24,128]{2,1,0:T(8,128)S(1)}, f32[4,24,128]{2,1,0:T(8,128)S(1)}, u32[]{:S(2)}, u32[]{:S(2)}) collective-permute-start(f32[4,24,128]{2,1,0:T(8,128)S(1)} %get-tuple-element.34), channel_id=1, source_target_pairs={{0,12},{4,0},{8,4},{12,8},{1,13},{5,1},{9,5},{13,9},{2,14},{6,2},{... | collective-permute-start | bytes 147464 | tf_op jit(solution)/shard_map/ppermute | solution.py:428
  68.7 1.5 collective-permute-done.14
  70.2 4.0 %collective-permute-start.21 = (f32[4,112,128]{2,1,0:T(8,128)S(1)}, f32[4,112,128]{2,1,0:T(8,128)S(1)}, u32[]{:S(2)}, u32[]{:S(2)}) collective-permute-start(f32[4,112,128]{2,1,0:T(8,128)S(1)} %pad_maximum_fusion.refs_0_), channel_id=1, source_target_pairs={{0,96},{16,112},{32,0},{48,16},{64,32},{80,48},{96,64},{112,80},{1... | collective-permute-start | bytes 688136 | tf_op jit(solution)/shard_map/ppermute | solution.py:428
  74.9 3.1 %collective-permute-start.16 = (f32[4,112,128]{2,1,0:T(8,128)S(1)}, f32[4,112,128]{2,1,0:T(8,128)S(1)}, u32[]{:S(2)}, u32[]{:S(2)}) collective-permute-start(f32[4,112,128]{2,1,0:T(8,128)S(1)} %pad_maximum_fusion.refs_0_), channel_id=1, source_target_pairs={{0,16},{16,0},{32,48},{48,32},{64,80},{80,64},{96,112},{112,96},{1... | collective-permute-start | bytes 688136 | tf_op jit(solution)/shard_map/ppermute | solution.py:432
  78.0 5.7 %collective-permute-done.21.refs_6_ = f32[4,112,128]{2,1,0:T(8,128)S(1)} collective-permute-done((f32[4,112,128]{2,1,0:T(8,128)S(1)}, f32[4,112,128]{2,1,0:T(8,128)S(1)}, u32[]{:S(2)}, u32[]{:S(2)}) %collective-permute-start.21) | collective-permute-done | bytes 229408 | tf_op jit(solution)/shard_map/ppermute | solution.py:428
  84.9 1.3 collective-permute-start.20
  89.6 41.3 %middle.1 = (f32[24,160,128]{2,1,0:T(8,128)S(1)}, f32[24,160,128]{2,1,0:T(8,128)S(1)}, f32[4,64,128]{2,1,0:T(8,128)S(1)}) custom-call(s32[3]{0:T(128)S(1)} %pad_add_fusion.pos, f32[4,112,128]{2,1,0:T(8,128)S(1)} %pad_maximum_fusion.refs_0_, f32[4,112,128]{2,1,0:T(8,128)S(1)} %collective-permute-done.16.refs_1_, ...), custom_call_target="tpu_custom_call" | custom-call | tf_op jit(solution)/shard_map/middle/pallas_call | solution.py:415
  132.3 1.3 copy-done.7
  133.6 2.7 %collective-permute-start.23 = (f32[4,64,128]{2,1,0:T(8,128)S(1)}, f32[4,64,128]{2,1,0:T(8,128)S(1)}, u32[]{:S(2)}, u32[]{:S(2)}) collective-permute-start(f32[4,64,128]{2,1,0:T(8,128)S(1)} %get-tuple-element.26), channel_id=1, source_target_pairs={{0,3},{1,0},{2,1},{3,2},{4,7},{5,4},{6,5},{7,6},{8,11},{9,8},{10,9... | collective-permute-start | bytes 393224 | tf_op jit(solution)/shard_map/ppermute | solution.py:428
  136.3 3.2 %collective-permute-done.24 = f32[4,64,128]{2,1,0:T(8,128)S(1)} collective-permute-done((f32[4,64,128]{2,1,0:T(8,128)S(1)}, f32[4,64,128]{2,1,0:T(8,128)S(1)}, u32[]{:S(2)}, u32[]{:S(2)}) %collective-permute-start.24) | collective-permute-done | bytes 131104 | tf_op jit(solution)/shard_map/ppermute | solution.py:428
  139.6 2.8 %collective-permute-start.26 = (f32[4,24,128]{2,1,0:T(8,128)S(1)}, f32[4,24,128]{2,1,0:T(8,128)S(1)}, u32[]{:S(2)}, u32[]{:S(2)}) collective-permute-start(f32[4,24,128]{2,1,0:T(8,128)S(1)} %get-tuple-element.32), channel_id=1, source_target_pairs={{0,12},{4,0},{8,4},{12,8},{1,13},{5,1},{9,5},{13,9},{2,14},{6,2},{... | collective-permute-start | bytes 147464 | tf_op jit(solution)/shard_map/ppermute | solution.py:428
  142.4 1.4 collective-permute-done.25
  145.4 2.9 %collective-permute-start.27 = (f32[4,112,128]{2,1,0:T(8,128)S(1)}, f32[4,112,128]{2,1,0:T(8,128)S(1)}, u32[]{:S(2)}, u32[]{:S(2)}) collective-permute-start(f32[4,112,128]{2,1,0:T(8,128)S(1)} %pad_maximum_fusion.1.refs_0_), channel_id=1, source_target_pairs={{0,16},{16,0},{32,48},{48,32},{64,80},{80,64},{96,112},{112,96},{1... | collective-permute-start | bytes 688136 | tf_op jit(solution)/shard_map/ppermute | solution.py:432
  148.8 5.6 %collective-permute-start.33 = (f32[4,112,128]{2,1,0:T(8,128)S(1)}, f32[4,112,128]{2,1,0:T(8,128)S(1)}, u32[]{:S(2)}, u32[]{:S(2)}) collective-permute-start(f32[4,112,128]{2,1,0:T(8,128)S(1)} %collective-permute-done.32.refs_6_), channel_id=1, source_target_pairs={{0,16},{16,0},{32,48},{48,32},{64,80},{80,64},{96,112},{112,96},{1... | collective-permute-start | bytes 688136 | tf_op jit(solution)/shard_map/ppermute | solution.py:432
  154.4 2.2 %collective-permute-start.31 = (f32[4,112,128]{2,1,0:T(8,128)S(1)}, f32[4,112,128]{2,1,0:T(8,128)S(1)}, u32[]{:S(2)}, u32[]{:S(2)}) collective-permute-start(f32[4,112,128]{2,1,0:T(8,128)S(1)} %collective-permute-done.30.refs_4_), channel_id=1, source_target_pairs={{0,16},{16,0},{32,48},{48,32},{64,80},{80,64},{96,112},{112,96},{1... | collective-permute-start | bytes 688136 | tf_op jit(solution)/shard_map/ppermute | solution.py:432
  160.1 31.6 %last.1 = f32[8,128,128]{2,1,0:T(8,128)} custom-call(s32[3]{0:T(128)S(1)} %pad_add_fusion.pos, f32[4,112,128]{2,1,0:T(8,128)S(1)} %pad_maximum_fusion.1.refs_0_, f32[4,112,128]{2,1,0:T(8,128)S(1)} %collective-permute-done.27.refs_1_, f32[4,112,128]{2,1,0:T(8,128)S(1)} %collective-permute-done.28.refs_2_, f32[4,112,128]{2,1,0:T(8,128)S(1)} %collective-permute-done.29.refs_3_, ...), custom_call_target="tpu_custom_call" | custom-call | tf_op jit(solution)/shard_map/last/pallas_call | solution.py:415
  (80 shorter events, 20.5 us)
Async XLA Ops:
  1.9 4.7 %collective-permute-start.1 = (f32[128,128]{1,0:T(8,128)S(1)}, f32[128,128]{1,0:T(8,128)S(1)}, u32[]{:S(2)}, u32[]{:S(2)}) collective-permute-start(f32[128,128]{1,0:T(8,128)S(1)} %get-tuple-element.18), channel_id=1, source_target_pairs={{0,3},{1,0},{2,1},{3,2},{4,7},{5,4},{6,5},{7,6},{8,11},{9,8},{10,9... | collective-permute-start | bytes 196616 | tf_op jit(solution)/shard_map/ppermute | solution.py:428
  5.3 11.6 %collective-permute-start = (f32[3,128,128]{2,1,0:T(8,128)S(1)}, f32[3,128,128]{2,1,0:T(8,128)S(1)}, u32[]{:S(2)}, u32[]{:S(2)}) collective-permute-start(f32[3,128,128]{2,1,0:T(8,128)S(1)} %slice_bitcast_fusion), channel_id=1, source_target_pairs={{0,112},{16,0},{32,16},{48,32},{64,48},{80,64},{96,80},{112,96},{1... | collective-permute-start | bytes 589832 | tf_op jit(solution)/shard_map/ppermute | solution.py:428
  6.6 4.6 %collective-permute-start.2 = (f32[32,128]{1,0:T(8,128)S(1)}, f32[32,128]{1,0:T(8,128)S(1)}, u32[]{:S(2)}, u32[]{:S(2)}) collective-permute-start(f32[32,128]{1,0:T(8,128)S(1)} %pad_maximum_fusion.6), channel_id=1, source_target_pairs={{0,12},{4,0},{8,4},{12,8},{1,13},{5,1},{9,5},{13,9},{2,14},{6,2},{... | collective-permute-start | bytes 49160 | tf_op jit(solution)/shard_map/ppermute | solution.py:428
  11.2 5.7 %collective-permute-start.3 = (f32[160,128]{1,0:T(8,128)S(1)}, f32[160,128]{1,0:T(8,128)S(1)}, u32[]{:S(2)}, u32[]{:S(2)}) collective-permute-start(f32[160,128]{1,0:T(8,128)S(1)} %pad_maximum_fusion.3), channel_id=1, source_target_pairs={{0,112},{16,0},{32,16},{48,32},{64,48},{80,64},{96,80},{112,96},{1... | collective-permute-start | bytes 245768 | tf_op jit(solution)/shard_map/ppermute | solution.py:428
  32.0 5.2 %collective-permute-start.7 = (f32[128,128]{1,0:T(8,128)S(1)}, f32[128,128]{1,0:T(8,128)S(1)}, u32[]{:S(2)}, u32[]{:S(2)}) collective-permute-start(f32[128,128]{1,0:T(8,128)S(1)} %get-tuple-element.20), channel_id=1, source_target_pairs={{0,1},{1,2},{2,3},{3,0},{4,5},{5,6},{6,7},{7,4},{8,9},{9,10},{10,1... | collective-permute-start | bytes 196616 | tf_op jit(solution)/shard_map/ppermute | solution.py:428
  32.9 4.3 %collective-permute-start.6 = (f32[128,128]{1,0:T(8,128)S(1)}, f32[128,128]{1,0:T(8,128)S(1)}, u32[]{:S(2)}, u32[]{:S(2)}) collective-permute-start(f32[128,128]{1,0:T(8,128)S(1)} %get-tuple-element.20), channel_id=1, source_target_pairs={{0,3},{1,0},{2,1},{3,2},{4,7},{5,4},{6,5},{7,6},{8,11},{9,8},{10,9... | collective-permute-start | bytes 196616 | tf_op jit(solution)/shard_map/ppermute | solution.py:428
  35.5 14.1 %collective-permute-start.5 = (f32[8,128,128]{2,1,0:T(8,128)S(1)}, f32[8,128,128]{2,1,0:T(8,128)S(1)}, u32[]{:S(2)}, u32[]{:S(2)}) collective-permute-start(f32[8,128,128]{2,1,0:T(8,128)S(1)} %get-tuple-element.19.fc), channel_id=1, source_target_pairs={{0,112},{16,0},{32,16},{48,32},{64,48},{80,64},{96,80},{112,96},{1... | collective-permute-start | bytes 1572872 | tf_op jit(solution)/shard_map/ppermute | solution.py:428
  35.5 14.1 %collective-permute-start.4 = (f32[8,128,128]{2,1,0:T(8,128)S(1)}, f32[8,128,128]{2,1,0:T(8,128)S(1)}, u32[]{:S(2)}, u32[]{:S(2)}) collective-permute-start(f32[8,128,128]{2,1,0:T(8,128)S(1)} %get-tuple-element.19.fc), channel_id=1, source_target_pairs={{0,16},{16,32},{32,48},{48,64},{64,80},{80,96},{96,112},{112,0},{1... | collective-permute-start | bytes 1572872 | tf_op jit(solution)/shard_map/ppermute | solution.py:428
  37.3 4.4 %collective-permute-start.9 = (f32[72,128]{1,0:T(8,128)S(1)}, f32[72,128]{1,0:T(8,128)S(1)}, u32[]{:S(2)}, u32[]{:S(2)}) collective-permute-start(f32[72,128]{1,0:T(8,128)S(1)} %pad_maximum_fusion.5), channel_id=1, source_target_pairs={{0,12},{4,0},{8,4},{12,8},{1,13},{5,1},{9,5},{13,9},{2,14},{6,2},{... | collective-permute-start | bytes 110600 | tf_op jit(solution)/shard_map/ppermute | solution.py:428
  40.6 4.3 %collective-permute-start.8 = (f32[72,128]{1,0:T(8,128)S(1)}, f32[72,128]{1,0:T(8,128)S(1)}, u32[]{:S(2)}, u32[]{:S(2)}) collective-permute-start(f32[72,128]{1,0:T(8,128)S(1)} %pad_maximum_fusion.4), channel_id=1, source_target_pairs={{0,4},{4,8},{8,12},{12,0},{1,5},{5,9},{9,13},{13,1},{2,6},{6,10},{... | collective-permute-start | bytes 110600 | tf_op jit(solution)/shard_map/ppermute | solution.py:428
  44.9 4.7 %collective-permute-start.11 = (f32[272,128]{1,0:T(8,128)S(1)}, f32[272,128]{1,0:T(8,128)S(1)}, u32[]{:S(2)}, u32[]{:S(2)}) collective-permute-start(f32[272,128]{1,0:T(8,128)S(1)} %pad_maximum_fusion.2.hc), channel_id=1, source_target_pairs={{0,112},{16,0},{32,16},{48,32},{64,48},{80,64},{96,80},{112,96},{1... | collective-permute-start | bytes 417800 | tf_op jit(solution)/shard_map/ppermute | solution.py:428
  46.2 3.4 %collective-permute-start.10 = (f32[272,128]{1,0:T(8,128)S(1)}, f32[272,128]{1,0:T(8,128)S(1)}, u32[]{:S(2)}, u32[]{:S(2)}) collective-permute-start(f32[272,128]{1,0:T(8,128)S(1)} %pad_maximum_fusion.2.hc), channel_id=1, source_target_pairs={{0,16},{16,32},{32,48},{48,64},{64,80},{80,96},{96,112},{112,0},{1... | collective-permute-start | bytes 417800 | tf_op jit(solution)/shard_map/ppermute | solution.py:428
  60.3 5.2 %collective-permute-start.13 = (f32[4,64,128]{2,1,0:T(8,128)S(1)}, f32[4,64,128]{2,1,0:T(8,128)S(1)}, u32[]{:S(2)}, u32[]{:S(2)}) collective-permute-start(f32[4,64,128]{2,1,0:T(8,128)S(1)} %get-tuple-element.21), channel_id=1, source_target_pairs={{0,1},{1,2},{2,3},{3,0},{4,5},{5,6},{6,7},{7,4},{8,9},{9,10},{10,1... | collective-permute-start | bytes 393224 | tf_op jit(solution)/shard_map/ppermute | solution.py:428
  61.3 4.6 %collective-permute-start.12 = (f32[4,64,128]{2,1,0:T(8,128)S(1)}, f32[4,64,128]{2,1,0:T(8,128)S(1)}, u32[]{:S(2)}, u32[]{:S(2)}) collective-permute-start(f32[4,64,128]{2,1,0:T(8,128)S(1)} %get-tuple-element.21), channel_id=1, source_target_pairs={{0,3},{1,0},{2,1},{3,2},{4,7},{5,4},{6,5},{7,6},{8,11},{9,8},{10,9... | collective-permute-start | bytes 393224 | tf_op jit(solution)/shard_map/ppermute | solution.py:428
  65.9 4.2 %collective-permute-start.14 = (f32[4,24,128]{2,1,0:T(8,128)S(1)}, f32[4,24,128]{2,1,0:T(8,128)S(1)}, u32[]{:S(2)}, u32[]{:S(2)}) collective-permute-start(f32[4,24,128]{2,1,0:T(8,128)S(1)} %get-tuple-element.33), channel_id=1, source_target_pairs={{0,4},{4,8},{8,12},{12,0},{1,5},{5,9},{9,13},{13,1},{2,6},{6,10},{... | collective-permute-start | bytes 147464 | tf_op jit(solution)/shard_map/ppermute | solution.py:428
  66.0 4.1 %collective-permute-start.15 = (f32[4,24,128]{2,1,0:T(8,128)S(1)}, f32[4,24,128]{2,1,0:T(8,128)S(1)}, u32[]{:S(2)}, u32[]{:S(2)}) collective-permute-start(f32[4,24,128]{2,1,0:T(8,128)S(1)} %get-tuple-element.34), channel_id=1, source_target_pairs={{0,12},{4,0},{8,4},{12,8},{1,13},{5,1},{9,5},{13,9},{2,14},{6,2},{... | collective-permute-start | bytes 147464 | tf_op jit(solution)/shard_map/ppermute | solution.py:428
  70.2 13.5 %collective-permute-start.21 = (f32[4,112,128]{2,1,0:T(8,128)S(1)}, f32[4,112,128]{2,1,0:T(8,128)S(1)}, u32[]{:S(2)}, u32[]{:S(2)}) collective-permute-start(f32[4,112,128]{2,1,0:T(8,128)S(1)} %pad_maximum_fusion.refs_0_), channel_id=1, source_target_pairs={{0,96},{16,112},{32,0},{48,16},{64,32},{80,48},{96,64},{112,80},{1... | collective-permute-start | bytes 688136 | tf_op jit(solution)/shard_map/ppermute | solution.py:428
  74.2 10.7 %collective-permute-start.19 = (f32[4,112,128]{2,1,0:T(8,128)S(1)}, f32[4,112,128]{2,1,0:T(8,128)S(1)}, u32[]{:S(2)}, u32[]{:S(2)}) collective-permute-start(f32[4,112,128]{2,1,0:T(8,128)S(1)} %pad_maximum_fusion.refs_0_), channel_id=1, source_target_pairs={{0,64},{16,80},{32,96},{48,112},{64,0},{80,16},{96,32},{112,48},{1... | collective-permute-start | bytes 688136 | tf_op jit(solution)/shard_map/ppermute | solution.py:428
  74.3 12.9 %collective-permute-start.17 = (f32[4,112,128]{2,1,0:T(8,128)S(1)}, f32[4,112,128]{2,1,0:T(8,128)S(1)}, u32[]{:S(2)}, u32[]{:S(2)}) collective-permute-start(f32[4,112,128]{2,1,0:T(8,128)S(1)} %pad_maximum_fusion.refs_0_), channel_id=1, source_target_pairs={{0,32},{16,48},{32,64},{48,80},{64,96},{80,112},{96,0},{112,16},{1... | collective-permute-start | bytes 688136 | tf_op jit(solution)/shard_map/ppermute | solution.py:428
  74.9 13.6 %collective-permute-start.16 = (f32[4,112,128]{2,1,0:T(8,128)S(1)}, f32[4,112,128]{2,1,0:T(8,128)S(1)}, u32[]{:S(2)}, u32[]{:S(2)}) collective-permute-start(f32[4,112,128]{2,1,0:T(8,128)S(1)} %pad_maximum_fusion.refs_0_), channel_id=1, source_target_pairs={{0,16},{16,0},{32,48},{48,32},{64,80},{80,64},{96,112},{112,96},{1... | collective-permute-start | bytes 688136 | tf_op jit(solution)/shard_map/ppermute | solution.py:432
  83.7 4.8 %collective-permute-start.22 = (f32[4,112,128]{2,1,0:T(8,128)S(1)}, f32[4,112,128]{2,1,0:T(8,128)S(1)}, u32[]{:S(2)}, u32[]{:S(2)}) collective-permute-start(f32[4,112,128]{2,1,0:T(8,128)S(1)} %collective-permute-done.21.refs_6_), channel_id=1, source_target_pairs={{0,16},{16,0},{32,48},{48,32},{64,80},{80,64},{96,112},{112,96},{1... | collective-permute-start | bytes 688136 | tf_op jit(solution)/shard_map/ppermute | solution.py:432
  84.9 3.6 %collective-permute-start.20 = (f32[4,112,128]{2,1,0:T(8,128)S(1)}, f32[4,112,128]{2,1,0:T(8,128)S(1)}, u32[]{:S(2)}, u32[]{:S(2)}) collective-permute-start(f32[4,112,128]{2,1,0:T(8,128)S(1)} %collective-permute-done.19.refs_4_), channel_id=1, source_target_pairs={{0,16},{16,0},{32,48},{48,32},{64,80},{80,64},{96,112},{112,96},{1... | collective-permute-start | bytes 688136 | tf_op jit(solution)/shard_map/ppermute | solution.py:432
  133.6 5.9 %collective-permute-start.24 = (f32[4,64,128]{2,1,0:T(8,128)S(1)}, f32[4,64,128]{2,1,0:T(8,128)S(1)}, u32[]{:S(2)}, u32[]{:S(2)}) collective-permute-start(f32[4,64,128]{2,1,0:T(8,128)S(1)} %get-tuple-element.26), channel_id=1, source_target_pairs={{0,1},{1,2},{2,3},{3,0},{4,5},{5,6},{6,7},{7,4},{8,9},{9,10},{10,1... | collective-permute-start | bytes 393224 | tf_op jit(solution)/shard_map/ppermute | solution.py:428
  133.6 5.9 %collective-permute-start.23 = (f32[4,64,128]{2,1,0:T(8,128)S(1)}, f32[4,64,128]{2,1,0:T(8,128)S(1)}, u32[]{:S(2)}, u32[]{:S(2)}) collective-permute-start(f32[4,64,128]{2,1,0:T(8,128)S(1)} %get-tuple-element.26), channel_id=1, source_target_pairs={{0,3},{1,0},{2,1},{3,2},{4,7},{5,4},{6,5},{7,6},{8,11},{9,8},{10,9... | collective-permute-start | bytes 393224 | tf_op jit(solution)/shard_map/ppermute | solution.py:428
  139.6 4.2 %collective-permute-start.25 = (f32[4,24,128]{2,1,0:T(8,128)S(1)}, f32[4,24,128]{2,1,0:T(8,128)S(1)}, u32[]{:S(2)}, u32[]{:S(2)}) collective-permute-start(f32[4,24,128]{2,1,0:T(8,128)S(1)} %get-tuple-element.31), channel_id=1, source_target_pairs={{0,4},{4,8},{8,12},{12,0},{1,5},{5,9},{9,13},{13,1},{2,6},{6,10},{... | collective-permute-start | bytes 147464 | tf_op jit(solution)/shard_map/ppermute | solution.py:428
  139.6 4.2 %collective-permute-start.26 = (f32[4,24,128]{2,1,0:T(8,128)S(1)}, f32[4,24,128]{2,1,0:T(8,128)S(1)}, u32[]{:S(2)}, u32[]{:S(2)}) collective-permute-start(f32[4,24,128]{2,1,0:T(8,128)S(1)} %get-tuple-element.32), channel_id=1, source_target_pairs={{0,12},{4,0},{8,4},{12,8},{1,13},{5,1},{9,5},{13,9},{2,14},{6,2},{... | collective-permute-start | bytes 147464 | tf_op jit(solution)/shard_map/ppermute | solution.py:428
  143.8 4.9 %collective-permute-start.32 = (f32[4,112,128]{2,1,0:T(8,128)S(1)}, f32[4,112,128]{2,1,0:T(8,128)S(1)}, u32[]{:S(2)}, u32[]{:S(2)}) collective-permute-start(f32[4,112,128]{2,1,0:T(8,128)S(1)} %pad_maximum_fusion.1.refs_0_), channel_id=1, source_target_pairs={{0,96},{16,112},{32,0},{48,16},{64,32},{80,48},{96,64},{112,80},{1... | collective-permute-start | bytes 688136 | tf_op jit(solution)/shard_map/ppermute | solution.py:428
  144.5 9.9 %collective-permute-start.30 = (f32[4,112,128]{2,1,0:T(8,128)S(1)}, f32[4,112,128]{2,1,0:T(8,128)S(1)}, u32[]{:S(2)}, u32[]{:S(2)}) collective-permute-start(f32[4,112,128]{2,1,0:T(8,128)S(1)} %pad_maximum_fusion.1.refs_0_), channel_id=1, source_target_pairs={{0,64},{16,80},{32,96},{48,112},{64,0},{80,16},{96,32},{112,48},{1... | collective-permute-start | bytes 688136 | tf_op jit(solution)/shard_map/ppermute | solution.py:428
  144.5 13.2 %collective-permute-start.28 = (f32[4,112,128]{2,1,0:T(8,128)S(1)}, f32[4,112,128]{2,1,0:T(8,128)S(1)}, u32[]{:S(2)}, u32[]{:S(2)}) collective-permute-start(f32[4,112,128]{2,1,0:T(8,128)S(1)} %pad_maximum_fusion.1.refs_0_), channel_id=1, source_target_pairs={{0,32},{16,48},{32,64},{48,80},{64,96},{80,112},{96,0},{112,16},{1... | collective-permute-start | bytes 688136 | tf_op jit(solution)/shard_map/ppermute | solution.py:428
  145.4 13.6 %collective-permute-start.27 = (f32[4,112,128]{2,1,0:T(8,128)S(1)}, f32[4,112,128]{2,1,0:T(8,128)S(1)}, u32[]{:S(2)}, u32[]{:S(2)}) collective-permute-start(f32[4,112,128]{2,1,0:T(8,128)S(1)} %pad_maximum_fusion.1.refs_0_), channel_id=1, source_target_pairs={{0,16},{16,0},{32,48},{48,32},{64,80},{80,64},{96,112},{112,96},{1... | collective-permute-start | bytes 688136 | tf_op jit(solution)/shard_map/ppermute | solution.py:432
  148.8 10.2 %collective-permute-start.33 = (f32[4,112,128]{2,1,0:T(8,128)S(1)}, f32[4,112,128]{2,1,0:T(8,128)S(1)}, u32[]{:S(2)}, u32[]{:S(2)}) collective-permute-start(f32[4,112,128]{2,1,0:T(8,128)S(1)} %collective-permute-done.32.refs_6_), channel_id=1, source_target_pairs={{0,16},{16,0},{32,48},{48,32},{64,80},{80,64},{96,112},{112,96},{1... | collective-permute-start | bytes 688136 | tf_op jit(solution)/shard_map/ppermute | solution.py:432
  154.4 4.6 %collective-permute-start.31 = (f32[4,112,128]{2,1,0:T(8,128)S(1)}, f32[4,112,128]{2,1,0:T(8,128)S(1)}, u32[]{:S(2)}, u32[]{:S(2)}) collective-permute-start(f32[4,112,128]{2,1,0:T(8,128)S(1)} %collective-permute-done.30.refs_4_), channel_id=1, source_target_pairs={{0,16},{16,0},{32,48},{48,32},{64,80},{80,64},{96,112},{112,96},{1... | collective-permute-start | bytes 688136 | tf_op jit(solution)/shard_map/ppermute | solution.py:432
  (12 other events, 198.8 us)

commit v2 on v1

--- a/solution.py
+++ b/solution.py
@@ -10,6 +10,7 @@
 S0 = FILTER_COEF
 S1 = FILTER_COEF / 4.0
 S2 = FILTER_COEF / 16.0
+UN0 = 10
 KEEP = 1.0 - DAMPING
 HIGH = lax.Precision.HIGHEST
 F32 = jnp.float32
@@ -33,6 +34,21 @@
 
 def axis_count(place, total):
     return jnp.where(place > 0, 1.0, 0.0) + jnp.where(place < total - 1, 1.0, 0.0)
+
+
+def planes(start, count, unroll, body):
+    step = max(u for u in range(1, unroll + 1) if count % u == 0)
+    if step == count:
+        for j in range(count):
+            body(start + j)
+        return
+
+    def block(k, carry):
+        for j in range(step):
+            body(start + k * step + j)
+        return carry
+
+    lax.fori_loop(0, count // step, block, 0)
 
 
 def make_tables(weight, diag, rows, row_off, lane_place, lane_ok, base_y, base_z, total, scale):
@@ -70,7 +86,7 @@
 def level0_sweep(pos, src, dst, fm, fs, wm, ws, first, last, side):
     lane = iota((48, 128), 1)
 
-    def body(p, carry):
+    def body(p):
         i = x_index(pos[0] * 8 + p - 8, 64)
         for r in range(8, 152, 48):
             rows = pl.ds(r, 48)
@@ -84,9 +100,8 @@
                 tot = src[1][p - 1, rows] + src[1][p + 1, rows] + src[1][p, up] + src[1][p, dn]
                 tot = tot + jnp.where(lane == 127, mr, sr) + jnp.where(lane == 0, ml, sl)
                 dst[1][p, rows] = KEEP * s + ws[i, rows] * (fs[p, rows] + S0 * tot)
-        return carry
-
-    lax.fori_loop(first, last + 1, body, 0)
+
+    planes(first, last + 1 - first, UN0, body)
 
 
 def restrict_matrix(size):
@@ -100,7 +115,7 @@
     lane = iota((64, 128), 1)
     matrix = restrict_matrix(128)
 
-    def body(k, carry):
+    def body(k):
         for r in (0, 64):
             both = None
             for q in (0, 1):
@@ -114,16 +129,15 @@
                 tot = tot + jnp.where(lane == 0, prev_lane(s), prev_lane(m))
                 res = fm[p, rows] + S0 * tot - dm[i, rows] * m
                 both = res if both is None else both + res
-            tmp[pl.ds(r, 64)] = both
-        pair = tmp[pl.ds(0, 64, stride=2)] + tmp[pl.ds(1, 64, stride=2)]
+            tmp[k, pl.ds(r, 64)] = both
+        pair = tmp[k, pl.ds(0, 64, stride=2)] + tmp[k, pl.ds(1, 64, stride=2)]
         out[k] = jnp.dot(pair, matrix, precision=HIGH, preferred_element_type=F32)
-        return carry
-
-    lax.fori_loop(0, 4, body, 0)
-
-
-def plane_sweep(src, dst, f, w, first, last, x_off, total, rows, scale):
-    def body(p, carry):
+
+    planes(0, 4, 4, body)
+
+
+def plane_sweep(src, dst, f, w, first, count, x_off, total, rows, scale):
+    def body(p):
         i = x_index(p - x_off, total)
         n = rows - 16
         mid = pl.ds(8, n)
@@ -131,9 +145,8 @@
         tot = src[p - 1, mid] + src[p + 1, mid] + src[p, pl.ds(7, n)] + src[p, pl.ds(9, n)]
         tot = tot + next_lane(m) + prev_lane(m)
         dst[p, mid] = KEEP * m + w[i, mid] * (f[p, mid] + scale * tot)
-        return carry
-
-    lax.fori_loop(first, last + 1, body, 0)
+
+    planes(first, count, 16, body)
 
 
 def coarse_levels(pos, blocks, f1, va, vb, f2, a2, b2, w1, d1, w2, tmp):
@@ -175,7 +188,7 @@
                 f1[p, pl.ds(8, 112)] = value
                 va[p, pl.ds(8, 112)] = w1[i, pl.ds(8, 112)] * value
 
-    plane_sweep(va, vb, f1, w1, 5, 36, 5, 32, R1, S1)
+    plane_sweep(va, vb, f1, w1, 5, 32, 5, 32, R1, S1)
 
     src, dst = iota((128, 128), 0), iota((128, 128), 1)
     zs1 = jnp.where(src < 96, src, src - 128)
@@ -189,7 +202,7 @@
     kd1 = (dst < 86) | (dst >= 106)
     up = jnp.where(ks2 & kd1 & (lax.shift_right_arithmetic(zd1, 1) == zs2), 1.0, 0.0)
 
-    def restrict(k, carry):
+    def restrict(k):
         both = None
         mid = pl.ds(8, 112)
         for q in (0, 1):
@@ -200,31 +213,29 @@
             tot = tot + next_lane(m) + prev_lane(m)
             res = f1[p, mid] + S1 * tot - d1[i, mid] * m
             both = res if both is None else both + res
-        tmp[pl.ds(0, 112)] = both
-        pair = tmp[pl.ds(0, 56, stride=2)] + tmp[pl.ds(1, 56, stride=2)]
+        tmp[k, pl.ds(0, 112)] = both
+        pair = tmp[k, pl.ds(0, 56, stride=2)] + tmp[k, pl.ds(1, 56, stride=2)]
         value = jnp.dot(pair, down, precision=HIGH, preferred_element_type=F32)
         f2[1 + k, pl.ds(8, 56)] = value
         a2[1 + k, pl.ds(8, 56)] = w2[x_index(k, 16), pl.ds(8, 56)] * value
-        return carry
-
-    lax.fori_loop(0, 16, restrict, 0)
+
+    planes(0, 16, 8, restrict)
 
     src2, dst2 = a2, b2
     for _ in range(7):
         plane_sweep(src2, dst2, f2, w2, 1, 16, 1, 16, R2, S2)
         src2, dst2 = dst2, src2
 
-    def prolong(k, carry):
+    def prolong(k):
         e = jnp.dot(src2[1 + k, pl.ds(8, 56)], up, precision=HIGH, preferred_element_type=F32)
         for q in (0, 1):
             for h in (0, 1):
                 rows = pl.ds(8 + h, 56, stride=2)
                 vb[5 + 2 * k + q, rows] = vb[5 + 2 * k + q, rows] + e
-        return carry
-
-    lax.fori_loop(0, 16, prolong, 0)
-    plane_sweep(vb, va, f1, w1, 4 * gx + 1, 4 * gx + 12, 5, 32, R1, S1)
-    plane_sweep(va, vb, f1, w1, 4 * gx + 2, 4 * gx + 11, 5, 32, R1, S1)
+
+    planes(0, 16, 8, prolong)
+    plane_sweep(vb, va, f1, w1, 4 * gx + 1, 12, 5, 32, R1, S1)
+    plane_sweep(va, vb, f1, w1, 4 * gx + 2, 10, 5, 32, R1, S1)
 
 
 def level0_prolong(pos, e1, old, new, first, last):
@@ -235,7 +246,7 @@
     ok = (dst < 128) | (side < 8) | (side >= 120)
     up = jnp.where(ok & (lax.shift_right_arithmetic(zd, 1) == zs), 1.0, 0.0)
 
-    def body(k, carry):
+    def body(k):
         e = e1[4 * pos[0] + 1 + k, pl.ds(28, 72)]
         e = jnp.dot(e, up, precision=HIGH, preferred_element_type=F32)
         for q in (0, 1):
@@ -244,9 +255,8 @@
                 rows = pl.ds(8 + h, 72, stride=2)
                 new[0][p, rows] = old[0][p, rows] + e[:, :128]
                 new[1][p, rows] = old[1][p, rows] + e[:, 128:]
-        return carry
-
-    lax.fori_loop(first // 2, last // 2 + 1, body, 0)
+
+    planes(first // 2, last // 2 + 1 - first // 2, 10, body)
 
 
 def zero_pads(refs, first, last):
@@ -410,7 +420,7 @@
     return pltpu.VMEM(dims, F32)
 
 
-def call(kernel, outs, scratch, scalars, args, name):
+def call(kernel, outs, scratch, scalars, args, name, limit=12):
     specs = [SMEM] * scalars + [VM] * (len(args) - scalars)
     return pl.pallas_call(
         kernel,
@@ -418,7 +428,7 @@
         in_specs=specs,
         out_specs=[VM] * len(outs),
         scratch_shapes=scratch,
-        compiler_params=pltpu.CompilerParams(vmem_limit_bytes=48 << 20),
+        compiler_params=pltpu.CompilerParams(vmem_limit_bytes=limit << 20),
         name=name,
     )(*args)
 
@@ -435,7 +445,7 @@
 COARSE_SCRATCH = [
     vmem(PL1, R1, 128), vmem(PL1, R1, 128), vmem(PL1, R1, 128),
     vmem(PL2, R2, 128), vmem(PL2, R2, 128), vmem(PL2, R2, 128),
-    vmem(3, R1, 128), vmem(3, R1, 128), vmem(3, R2, 128), vmem(128, 128),
+    vmem(3, R1, 128), vmem(3, R1, 128), vmem(3, R2, 128), vmem(16, 128, 128),
 ]
 TABLE = vmem(3, R0, 128)
 WIDE = vmem(PL0, R0, 128)
@@ -477,16 +487,16 @@
     wide = shape(PL0, R0, 128)
     fm, fs, vm, vs, f1 = call(
         first_kernel, [wide, wide, wide, wide, shape(4, 64, 128)],
-        [WIDE, WIDE, TABLE, TABLE, TABLE, vmem(128, 128)], 1,
+        [WIDE, WIDE, TABLE, TABLE, TABLE, vmem(4, 128, 128)], 1,
         [pos, fl, f, fr, hl, h, hr], "first")
     vm, vs, f1 = call(
         middle_kernel, [wide, wide, shape(4, 64, 128)],
         [WIDE] * 4 + [TABLE] * 3 + COARSE_SCRATCH, 1,
-        [pos, *gather_level1(f1), fm, fs, vm, vs], "middle")
+        [pos, *gather_level1(f1), fm, fs, vm, vs], "middle", 24)
     (out,) = call(
         last_kernel, [shape(8, 128, 128)],
         [WIDE] * 4 + [TABLE] * 2 + COARSE_SCRATCH, 1,
-        [pos, *gather_level1(f1), fm, fs, vm, vs], "last")
+        [pos, *gather_level1(f1), fm, fs, vm, vs], "last", 24)
     return out
 
 

time: 192 us -> 136 us (0.71)
  Pallas kernels: 96.5 us -> 46 us
  local copies, waits for them, and re-layouts: 6.71 us -> 1.46 us
    pallas_call x5, Pallas kernels: 96.5 us -> 46 us  [call(): pl.pallas_call(kernel, out_shape=outs, in_specs=specs, out_specs=[VM] * l...]
    unnamed x20 -> x8, local copies, waits for them, and re-layouts: 6.66 us -> 1.42 us
where the time goes in v2:
time: 136 us
  starting transfers between devices  57.8 us (42%)
  Pallas kernels  46 us (34%)
  waiting for transfers between devices  30.4 us (22%)
  local copies, waits for them, and re-layouts  1.46 us (1%)
    pallas_call x5, Pallas kernels, call(): pl.pallas_call(kernel, out_shape=outs, in_specs=specs, out_specs=[VM] * l...  46 us
    ppermute x26, starting transfers between devices, shifted(): lax.ppermute(value, axis, [(i, (i + step) % size) for i in range(size)])  38.9 us
    ppermute x26, waiting for transfers between devices, shifted(): lax.ppermute(value, axis, [(i, (i + step) % size) for i in range(size)])  28.1 us
    ppermute x8, starting transfers between devices, swapped(): lax.ppermute(value, 'gx', [(i, i ^ 1) for i in range(lax.axis_size('gx'))])  18.9 us
  transfers between devices with their start and end apart: 34, of which 17 were waited for; matrix products, arithmetic and copies ran while one was open for 0% of the time, Pallas kernels for 0%

profile of v2, /device:TPU:1, one launch (start us, length us, event | category | flops | bytes accessed | tf_op | source)
XLA Modules:
  0.0 136.0 jit_solution(8883000270616264019)
XLA Ops:
  0.0 1.4 %copy-done = f32[3,8,128,128]{3,2,1,0:T(8,128)S(1)} copy-done((f32[3,8,128,128]{3,2,1,0:T(8,128)S(1)}, f32[3,8,128,128]{3,2,1,0:T(8,128)}, u32[]{:S(2)}) %copy-start) | copy-done | bytes 1572888
  1.9 3.4 %collective-permute-start.1 = (f32[128,128]{1,0:T(8,128)S(1)}, f32[128,128]{1,0:T(8,128)S(1)}, u32[]{:S(2)}, u32[]{:S(2)}) collective-permute-start(f32[128,128]{1,0:T(8,128)S(1)} %get-tuple-element.18), channel_id=1, source_target_pairs={{0,3},{1,0},{2,1},{3,2},{4,7},{5,4},{6,5},{7,6},{8,11},{9,8},{10,9... | collective-permute-start | bytes 196616 | tf_op jit(solution)/shard_map/ppermute | solution.py:438
  6.6 3.8 %collective-permute-start.2 = (f32[32,128]{1,0:T(8,128)S(1)}, f32[32,128]{1,0:T(8,128)S(1)}, u32[]{:S(2)}, u32[]{:S(2)}) collective-permute-start(f32[32,128]{1,0:T(8,128)S(1)} %pad_maximum_fusion.6), channel_id=1, source_target_pairs={{0,12},{4,0},{8,4},{12,8},{1,13},{5,1},{9,5},{13,9},{2,14},{6,2},{... | collective-permute-start | bytes 49160 | tf_op jit(solution)/shard_map/ppermute | solution.py:438
  11.2 2.7 %collective-permute-start.3 = (f32[160,128]{1,0:T(8,128)S(1)}, f32[160,128]{1,0:T(8,128)S(1)}, u32[]{:S(2)}, u32[]{:S(2)}) collective-permute-start(f32[160,128]{1,0:T(8,128)S(1)} %pad_maximum_fusion.3), channel_id=1, source_target_pairs={{0,112},{16,0},{32,16},{48,32},{64,48},{80,64},{96,80},{112,96},{1... | collective-permute-start | bytes 245768 | tf_op jit(solution)/shard_map/ppermute | solution.py:438
  14.0 2.9 %collective-permute-done.3.xrim = f32[160,128]{1,0:T(8,128)S(1)} collective-permute-done((f32[160,128]{1,0:T(8,128)S(1)}, f32[160,128]{1,0:T(8,128)S(1)}, u32[]{:S(2)}, u32[]{:S(2)}) %collective-permute-start.3) | collective-permute-done | bytes 81952 | tf_op jit(solution)/shard_map/ppermute | solution.py:438
  16.9 15.1 %energy.1 = (f32[8,128,128]{2,1,0:T(8,128)S(1)}, f32[128,128]{1,0:T(8,128)S(1)}) custom-call(s32[3]{0:T(128)S(1)} %pad_add_fusion.pos, f32[24,24]{1,0:T(8,128)S(1)} %copy-done.3, f32[3,8,128,128]{3,2,1,0:T(8,128)S(1)} %copy-done.1, f32[3,128,128]{2,1,0:T(8,128)S(1)} %collective-permute-done.xface, f32[32,128]{1,0:T(8,128)S(1)} %collective-permute-done.2.yrim, ...), custom_call_target="tpu_custom_call" | custom-call | tf_op jit(solution)/shard_map/energy/pallas_call | solution.py:425
  32.9 2.6 %collective-permute-start.6 = (f32[128,128]{1,0:T(8,128)S(1)}, f32[128,128]{1,0:T(8,128)S(1)}, u32[]{:S(2)}, u32[]{:S(2)}) collective-permute-start(f32[128,128]{1,0:T(8,128)S(1)} %get-tuple-element.20), channel_id=1, source_target_pairs={{0,3},{1,0},{2,1},{3,2},{4,7},{5,4},{6,5},{7,6},{8,11},{9,8},{10,9... | collective-permute-start | bytes 196616 | tf_op jit(solution)/shard_map/ppermute | solution.py:438
  35.5 1.7 %collective-permute-start.4 = (f32[8,128,128]{2,1,0:T(8,128)S(1)}, f32[8,128,128]{2,1,0:T(8,128)S(1)}, u32[]{:S(2)}, u32[]{:S(2)}) collective-permute-start(f32[8,128,128]{2,1,0:T(8,128)S(1)} %get-tuple-element.19.fc), channel_id=1, source_target_pairs={{0,16},{16,32},{32,48},{48,64},{64,80},{80,96},{96,112},{112,0},{1... | collective-permute-start | bytes 1572872 | tf_op jit(solution)/shard_map/ppermute | solution.py:438
  37.3 3.3 %collective-permute-start.9 = (f32[72,128]{1,0:T(8,128)S(1)}, f32[72,128]{1,0:T(8,128)S(1)}, u32[]{:S(2)}, u32[]{:S(2)}) collective-permute-start(f32[72,128]{1,0:T(8,128)S(1)} %pad_maximum_fusion.5), channel_id=1, source_target_pairs={{0,12},{4,0},{8,4},{12,8},{1,13},{5,1},{9,5},{13,9},{2,14},{6,2},{... | collective-permute-start | bytes 110600 | tf_op jit(solution)/shard_map/ppermute | solution.py:438
  41.6 3.3 %collective-permute-done.8 = f32[72,128]{1,0:T(8,128)S(1)} collective-permute-done((f32[72,128]{1,0:T(8,128)S(1)}, f32[72,128]{1,0:T(8,128)S(1)}, u32[]{:S(2)}, u32[]{:S(2)}) %collective-permute-start.8) | collective-permute-done | bytes 36896 | tf_op jit(solution)/shard_map/ppermute | solution.py:438
  44.9 1.3 collective-permute-start.11
  46.9 2.7 %collective-permute-done.11.hr = f32[272,128]{1,0:T(8,128)S(1)} collective-permute-done((f32[272,128]{1,0:T(8,128)S(1)}, f32[272,128]{1,0:T(8,128)S(1)}, u32[]{:S(2)}, u32[]{:S(2)}) %collective-permute-start.11) | collective-permute-done | bytes 139296 | tf_op jit(solution)/shard_map/ppermute | solution.py:438
  49.6 4.5 %first.1 = (f32[24,160,128]{2,1,0:T(8,128)S(1)}, f32[24,160,128]{2,1,0:T(8,128)S(1)}, f32[24,160,128]{2,1,0:T(8,128)S(1)}, f32[24,160,128]{2,1,0:T(8,128)S(1)}, f32[4,64,128]{2,1,0:T(8,128)S(1)}) custom-call(s32[3]{0:T(128)S(1)} %pad_add_fusion.pos, f32[8,128,128]{2,1,0:T(8,128)S(1)} %collective-permute-done.4.fl, f32[8,128,128]{2,1,0:T(8,128)S(1)} %get-tuple-element.19.fc, ...), custom_call_target="tpu_custom_call" | custom-call | tf_op jit(solution)/shard_map/first/pallas_call | solution.py:425
  55.2 1.9 %collective-permute-start.12 = (f32[4,64,128]{2,1,0:T(8,128)S(1)}, f32[4,64,128]{2,1,0:T(8,128)S(1)}, u32[]{:S(2)}, u32[]{:S(2)}) collective-permute-start(f32[4,64,128]{2,1,0:T(8,128)S(1)} %get-tuple-element.21), channel_id=1, source_target_pairs={{0,3},{1,0},{2,1},{3,2},{4,7},{5,4},{6,5},{7,6},{8,11},{9,8},{10,9... | collective-permute-start | bytes 393224 | tf_op jit(solution)/shard_map/ppermute | solution.py:438
  57.1 2.3 %collective-permute-done.13 = f32[4,64,128]{2,1,0:T(8,128)S(1)} collective-permute-done((f32[4,64,128]{2,1,0:T(8,128)S(1)}, f32[4,64,128]{2,1,0:T(8,128)S(1)}, u32[]{:S(2)}, u32[]{:S(2)}) %collective-permute-start.13) | collective-permute-done | bytes 131104 | tf_op jit(solution)/shard_map/ppermute | solution.py:438
  59.9 2.7 %collective-permute-start.15 = (f32[4,24,128]{2,1,0:T(8,128)S(1)}, f32[4,24,128]{2,1,0:T(8,128)S(1)}, u32[]{:S(2)}, u32[]{:S(2)}) collective-permute-start(f32[4,24,128]{2,1,0:T(8,128)S(1)} %get-tuple-element.34), channel_id=1, source_target_pairs={{0,12},{4,0},{8,4},{12,8},{1,13},{5,1},{9,5},{13,9},{2,14},{6,2},{... | collective-permute-start | bytes 147464 | tf_op jit(solution)/shard_map/ppermute | solution.py:438
  62.6 1.5 %collective-permute-done.14 = f32[4,24,128]{2,1,0:T(8,128)S(1)} collective-permute-done((f32[4,24,128]{2,1,0:T(8,128)S(1)}, f32[4,24,128]{2,1,0:T(8,128)S(1)}, u32[]{:S(2)}, u32[]{:S(2)}) %collective-permute-start.14) | collective-permute-done | bytes 49184 | tf_op jit(solution)/shard_map/ppermute | solution.py:438
  64.1 4.0 %collective-permute-start.21 = (f32[4,112,128]{2,1,0:T(8,128)S(1)}, f32[4,112,128]{2,1,0:T(8,128)S(1)}, u32[]{:S(2)}, u32[]{:S(2)}) collective-permute-start(f32[4,112,128]{2,1,0:T(8,128)S(1)} %pad_maximum_fusion.refs_0_), channel_id=1, source_target_pairs={{0,96},{16,112},{32,0},{48,16},{64,32},{80,48},{96,64},{112,80},{1... | collective-permute-start | bytes 688136 | tf_op jit(solution)/shard_map/ppermute | solution.py:438
  68.8 3.1 %collective-permute-start.16 = (f32[4,112,128]{2,1,0:T(8,128)S(1)}, f32[4,112,128]{2,1,0:T(8,128)S(1)}, u32[]{:S(2)}, u32[]{:S(2)}) collective-permute-start(f32[4,112,128]{2,1,0:T(8,128)S(1)} %pad_maximum_fusion.refs_0_), channel_id=1, source_target_pairs={{0,16},{16,0},{32,48},{48,32},{64,80},{80,64},{96,112},{112,96},{1... | collective-permute-start | bytes 688136 | tf_op jit(solution)/shard_map/ppermute | solution.py:442
  71.9 5.7 %collective-permute-done.21.refs_6_ = f32[4,112,128]{2,1,0:T(8,128)S(1)} collective-permute-done((f32[4,112,128]{2,1,0:T(8,128)S(1)}, f32[4,112,128]{2,1,0:T(8,128)S(1)}, u32[]{:S(2)}, u32[]{:S(2)}) %collective-permute-start.21) | collective-permute-done | bytes 229408 | tf_op jit(solution)/shard_map/ppermute | solution.py:438
  77.5 1.3 collective-permute-start.22
  78.8 1.3 collective-permute-start.20
  81.1 1.3 collective-permute-start.18
  83.5 15.5 %middle.1 = (f32[24,160,128]{2,1,0:T(8,128)S(1)}, f32[24,160,128]{2,1,0:T(8,128)S(1)}, f32[4,64,128]{2,1,0:T(8,128)S(1)}) custom-call(s32[3]{0:T(128)S(1)} %pad_add_fusion.pos, f32[4,112,128]{2,1,0:T(8,128)S(1)} %pad_maximum_fusion.refs_0_, f32[4,112,128]{2,1,0:T(8,128)S(1)} %collective-permute-done.16.refs_1_, ...), custom_call_target="tpu_custom_call" | custom-call | tf_op jit(solution)/shard_map/middle/pallas_call | solution.py:425
  99.1 2.7 %collective-permute-start.23 = (f32[4,64,128]{2,1,0:T(8,128)S(1)}, f32[4,64,128]{2,1,0:T(8,128)S(1)}, u32[]{:S(2)}, u32[]{:S(2)}) collective-permute-start(f32[4,64,128]{2,1,0:T(8,128)S(1)} %get-tuple-element.26), channel_id=1, source_target_pairs={{0,3},{1,0},{2,1},{3,2},{4,7},{5,4},{6,5},{7,6},{8,11},{9,8},{10,9... | collective-permute-start | bytes 393224 | tf_op jit(solution)/shard_map/ppermute | solution.py:438
  101.7 3.2 %collective-permute-done.24 = f32[4,64,128]{2,1,0:T(8,128)S(1)} collective-permute-done((f32[4,64,128]{2,1,0:T(8,128)S(1)}, f32[4,64,128]{2,1,0:T(8,128)S(1)}, u32[]{:S(2)}, u32[]{:S(2)}) %collective-permute-start.24) | collective-permute-done | bytes 131104 | tf_op jit(solution)/shard_map/ppermute | solution.py:438
  105.1 2.7 %collective-permute-start.26 = (f32[4,24,128]{2,1,0:T(8,128)S(1)}, f32[4,24,128]{2,1,0:T(8,128)S(1)}, u32[]{:S(2)}, u32[]{:S(2)}) collective-permute-start(f32[4,24,128]{2,1,0:T(8,128)S(1)} %get-tuple-element.32), channel_id=1, source_target_pairs={{0,12},{4,0},{8,4},{12,8},{1,13},{5,1},{9,5},{13,9},{2,14},{6,2},{... | collective-permute-start | bytes 147464 | tf_op jit(solution)/shard_map/ppermute | solution.py:438
  107.8 1.4 %collective-permute-done.25 = f32[4,24,128]{2,1,0:T(8,128)S(1)} collective-permute-done((f32[4,24,128]{2,1,0:T(8,128)S(1)}, f32[4,24,128]{2,1,0:T(8,128)S(1)}, u32[]{:S(2)}, u32[]{:S(2)}) %collective-permute-start.25) | collective-permute-done | bytes 49184 | tf_op jit(solution)/shard_map/ppermute | solution.py:438
  110.8 2.9 %collective-permute-start.27 = (f32[4,112,128]{2,1,0:T(8,128)S(1)}, f32[4,112,128]{2,1,0:T(8,128)S(1)}, u32[]{:S(2)}, u32[]{:S(2)}) collective-permute-start(f32[4,112,128]{2,1,0:T(8,128)S(1)} %pad_maximum_fusion.1.refs_0_), channel_id=1, source_target_pairs={{0,16},{16,0},{32,48},{48,32},{64,80},{80,64},{96,112},{112,96},{1... | collective-permute-start | bytes 688136 | tf_op jit(solution)/shard_map/ppermute | solution.py:442
  114.2 5.6 %collective-permute-start.33 = (f32[4,112,128]{2,1,0:T(8,128)S(1)}, f32[4,112,128]{2,1,0:T(8,128)S(1)}, u32[]{:S(2)}, u32[]{:S(2)}) collective-permute-start(f32[4,112,128]{2,1,0:T(8,128)S(1)} %collective-permute-done.32.refs_6_), channel_id=1, source_target_pairs={{0,16},{16,0},{32,48},{48,32},{64,80},{80,64},{96,112},{112,96},{1... | collective-permute-start | bytes 688136 | tf_op jit(solution)/shard_map/ppermute | solution.py:442
  119.8 2.2 %collective-permute-start.31 = (f32[4,112,128]{2,1,0:T(8,128)S(1)}, f32[4,112,128]{2,1,0:T(8,128)S(1)}, u32[]{:S(2)}, u32[]{:S(2)}) collective-permute-start(f32[4,112,128]{2,1,0:T(8,128)S(1)} %collective-permute-done.30.refs_4_), channel_id=1, source_target_pairs={{0,16},{16,0},{32,48},{48,32},{64,80},{80,64},{96,112},{112,96},{1... | collective-permute-start | bytes 688136 | tf_op jit(solution)/shard_map/ppermute | solution.py:442
  125.5 10.5 %last.1 = f32[8,128,128]{2,1,0:T(8,128)} custom-call(s32[3]{0:T(128)S(1)} %pad_add_fusion.pos, f32[4,112,128]{2,1,0:T(8,128)S(1)} %pad_maximum_fusion.1.refs_0_, f32[4,112,128]{2,1,0:T(8,128)S(1)} %collective-permute-done.27.refs_1_, f32[4,112,128]{2,1,0:T(8,128)S(1)} %collective-permute-done.28.refs_2_, f32[4,112,128]{2,1,0:T(8,128)S(1)} %collective-permute-done.29.refs_3_, ...), custom_call_target="tpu_custom_call" | custom-call | tf_op jit(solution)/shard_map/last/pallas_call | solution.py:425
  (68 shorter events, 15.5 us)
Async XLA Ops:
  1.9 4.7 %collective-permute-start.1 = (f32[128,128]{1,0:T(8,128)S(1)}, f32[128,128]{1,0:T(8,128)S(1)}, u32[]{:S(2)}, u32[]{:S(2)}) collective-permute-start(f32[128,128]{1,0:T(8,128)S(1)} %get-tuple-element.18), channel_id=1, source_target_pairs={{0,3},{1,0},{2,1},{3,2},{4,7},{5,4},{6,5},{7,6},{8,11},{9,8},{10,9... | collective-permute-start | bytes 196616 | tf_op jit(solution)/shard_map/ppermute | solution.py:438
  5.3 11.6 %collective-permute-start = (f32[3,128,128]{2,1,0:T(8,128)S(1)}, f32[3,128,128]{2,1,0:T(8,128)S(1)}, u32[]{:S(2)}, u32[]{:S(2)}) collective-permute-start(f32[3,128,128]{2,1,0:T(8,128)S(1)} %slice_bitcast_fusion), channel_id=1, source_target_pairs={{0,112},{16,0},{32,16},{48,32},{64,48},{80,64},{96,80},{112,96},{1... | collective-permute-start | bytes 589832 | tf_op jit(solution)/shard_map/ppermute | solution.py:438
  6.6 4.6 %collective-permute-start.2 = (f32[32,128]{1,0:T(8,128)S(1)}, f32[32,128]{1,0:T(8,128)S(1)}, u32[]{:S(2)}, u32[]{:S(2)}) collective-permute-start(f32[32,128]{1,0:T(8,128)S(1)} %pad_maximum_fusion.6), channel_id=1, source_target_pairs={{0,12},{4,0},{8,4},{12,8},{1,13},{5,1},{9,5},{13,9},{2,14},{6,2},{... | collective-permute-start | bytes 49160 | tf_op jit(solution)/shard_map/ppermute | solution.py:438
  11.2 5.7 %collective-permute-start.3 = (f32[160,128]{1,0:T(8,128)S(1)}, f32[160,128]{1,0:T(8,128)S(1)}, u32[]{:S(2)}, u32[]{:S(2)}) collective-permute-start(f32[160,128]{1,0:T(8,128)S(1)} %pad_maximum_fusion.3), channel_id=1, source_target_pairs={{0,112},{16,0},{32,16},{48,32},{64,48},{80,64},{96,80},{112,96},{1... | collective-permute-start | bytes 245768 | tf_op jit(solution)/shard_map/ppermute | solution.py:438
  32.0 5.2 %collective-permute-start.7 = (f32[128,128]{1,0:T(8,128)S(1)}, f32[128,128]{1,0:T(8,128)S(1)}, u32[]{:S(2)}, u32[]{:S(2)}) collective-permute-start(f32[128,128]{1,0:T(8,128)S(1)} %get-tuple-element.20), channel_id=1, source_target_pairs={{0,1},{1,2},{2,3},{3,0},{4,5},{5,6},{6,7},{7,4},{8,9},{9,10},{10,1... | collective-permute-start | bytes 196616 | tf_op jit(solution)/shard_map/ppermute | solution.py:438
  32.9 4.3 %collective-permute-start.6 = (f32[128,128]{1,0:T(8,128)S(1)}, f32[128,128]{1,0:T(8,128)S(1)}, u32[]{:S(2)}, u32[]{:S(2)}) collective-permute-start(f32[128,128]{1,0:T(8,128)S(1)} %get-tuple-element.20), channel_id=1, source_target_pairs={{0,3},{1,0},{2,1},{3,2},{4,7},{5,4},{6,5},{7,6},{8,11},{9,8},{10,9... | collective-permute-start | bytes 196616 | tf_op jit(solution)/shard_map/ppermute | solution.py:438
  35.5 14.1 %collective-permute-start.5 = (f32[8,128,128]{2,1,0:T(8,128)S(1)}, f32[8,128,128]{2,1,0:T(8,128)S(1)}, u32[]{:S(2)}, u32[]{:S(2)}) collective-permute-start(f32[8,128,128]{2,1,0:T(8,128)S(1)} %get-tuple-element.19.fc), channel_id=1, source_target_pairs={{0,112},{16,0},{32,16},{48,32},{64,48},{80,64},{96,80},{112,96},{1... | collective-permute-start | bytes 1572872 | tf_op jit(solution)/shard_map/ppermute | solution.py:438
  35.5 14.1 %collective-permute-start.4 = (f32[8,128,128]{2,1,0:T(8,128)S(1)}, f32[8,128,128]{2,1,0:T(8,128)S(1)}, u32[]{:S(2)}, u32[]{:S(2)}) collective-permute-start(f32[8,128,128]{2,1,0:T(8,128)S(1)} %get-tuple-element.19.fc), channel_id=1, source_target_pairs={{0,16},{16,32},{32,48},{48,64},{64,80},{80,96},{96,112},{112,0},{1... | collective-permute-start | bytes 1572872 | tf_op jit(solution)/shard_map/ppermute | solution.py:438
  37.3 4.4 %collective-permute-start.9 = (f32[72,128]{1,0:T(8,128)S(1)}, f32[72,128]{1,0:T(8,128)S(1)}, u32[]{:S(2)}, u32[]{:S(2)}) collective-permute-start(f32[72,128]{1,0:T(8,128)S(1)} %pad_maximum_fusion.5), channel_id=1, source_target_pairs={{0,12},{4,0},{8,4},{12,8},{1,13},{5,1},{9,5},{13,9},{2,14},{6,2},{... | collective-permute-start | bytes 110600 | tf_op jit(solution)/shard_map/ppermute | solution.py:438
  40.6 4.3 %collective-permute-start.8 = (f32[72,128]{1,0:T(8,128)S(1)}, f32[72,128]{1,0:T(8,128)S(1)}, u32[]{:S(2)}, u32[]{:S(2)}) collective-permute-start(f32[72,128]{1,0:T(8,128)S(1)} %pad_maximum_fusion.4), channel_id=1, source_target_pairs={{0,4},{4,8},{8,12},{12,0},{1,5},{5,9},{9,13},{13,1},{2,6},{6,10},{... | collective-permute-start | bytes 110600 | tf_op jit(solution)/shard_map/ppermute | solution.py:438
  44.9 4.7 %collective-permute-start.11 = (f32[272,128]{1,0:T(8,128)S(1)}, f32[272,128]{1,0:T(8,128)S(1)}, u32[]{:S(2)}, u32[]{:S(2)}) collective-permute-start(f32[272,128]{1,0:T(8,128)S(1)} %pad_maximum_fusion.2.hc), channel_id=1, source_target_pairs={{0,112},{16,0},{32,16},{48,32},{64,48},{80,64},{96,80},{112,96},{1... | collective-permute-start | bytes 417800 | tf_op jit(solution)/shard_map/ppermute | solution.py:438
  46.2 3.4 %collective-permute-start.10 = (f32[272,128]{1,0:T(8,128)S(1)}, f32[272,128]{1,0:T(8,128)S(1)}, u32[]{:S(2)}, u32[]{:S(2)}) collective-permute-start(f32[272,128]{1,0:T(8,128)S(1)} %pad_maximum_fusion.2.hc), channel_id=1, source_target_pairs={{0,16},{16,32},{32,48},{48,64},{64,80},{80,96},{96,112},{112,0},{1... | collective-permute-start | bytes 417800 | tf_op jit(solution)/shard_map/ppermute | solution.py:438
  54.1 5.2 %collective-permute-start.13 = (f32[4,64,128]{2,1,0:T(8,128)S(1)}, f32[4,64,128]{2,1,0:T(8,128)S(1)}, u32[]{:S(2)}, u32[]{:S(2)}) collective-permute-start(f32[4,64,128]{2,1,0:T(8,128)S(1)} %get-tuple-element.21), channel_id=1, source_target_pairs={{0,1},{1,2},{2,3},{3,0},{4,5},{5,6},{6,7},{7,4},{8,9},{9,10},{10,1... | collective-permute-start | bytes 393224 | tf_op jit(solution)/shard_map/ppermute | solution.py:438
  55.2 4.6 %collective-permute-start.12 = (f32[4,64,128]{2,1,0:T(8,128)S(1)}, f32[4,64,128]{2,1,0:T(8,128)S(1)}, u32[]{:S(2)}, u32[]{:S(2)}) collective-permute-start(f32[4,64,128]{2,1,0:T(8,128)S(1)} %get-tuple-element.21), channel_id=1, source_target_pairs={{0,3},{1,0},{2,1},{3,2},{4,7},{5,4},{6,5},{7,6},{8,11},{9,8},{10,9... | collective-permute-start | bytes 393224 | tf_op jit(solution)/shard_map/ppermute | solution.py:438
  59.8 4.2 %collective-permute-start.14 = (f32[4,24,128]{2,1,0:T(8,128)S(1)}, f32[4,24,128]{2,1,0:T(8,128)S(1)}, u32[]{:S(2)}, u32[]{:S(2)}) collective-permute-start(f32[4,24,128]{2,1,0:T(8,128)S(1)} %get-tuple-element.33), channel_id=1, source_target_pairs={{0,4},{4,8},{8,12},{12,0},{1,5},{5,9},{9,13},{13,1},{2,6},{6,10},{... | collective-permute-start | bytes 147464 | tf_op jit(solution)/shard_map/ppermute | solution.py:438
  59.9 4.1 %collective-permute-start.15 = (f32[4,24,128]{2,1,0:T(8,128)S(1)}, f32[4,24,128]{2,1,0:T(8,128)S(1)}, u32[]{:S(2)}, u32[]{:S(2)}) collective-permute-start(f32[4,24,128]{2,1,0:T(8,128)S(1)} %get-tuple-element.34), channel_id=1, source_target_pairs={{0,12},{4,0},{8,4},{12,8},{1,13},{5,1},{9,5},{13,9},{2,14},{6,2},{... | collective-permute-start | bytes 147464 | tf_op jit(solution)/shard_map/ppermute | solution.py:438
  64.1 13.5 %collective-permute-start.21 = (f32[4,112,128]{2,1,0:T(8,128)S(1)}, f32[4,112,128]{2,1,0:T(8,128)S(1)}, u32[]{:S(2)}, u32[]{:S(2)}) collective-permute-start(f32[4,112,128]{2,1,0:T(8,128)S(1)} %pad_maximum_fusion.refs_0_), channel_id=1, source_target_pairs={{0,96},{16,112},{32,0},{48,16},{64,32},{80,48},{96,64},{112,80},{1... | collective-permute-start | bytes 688136 | tf_op jit(solution)/shard_map/ppermute | solution.py:438
  68.1 10.7 %collective-permute-start.19 = (f32[4,112,128]{2,1,0:T(8,128)S(1)}, f32[4,112,128]{2,1,0:T(8,128)S(1)}, u32[]{:S(2)}, u32[]{:S(2)}) collective-permute-start(f32[4,112,128]{2,1,0:T(8,128)S(1)} %pad_maximum_fusion.refs_0_), channel_id=1, source_target_pairs={{0,64},{16,80},{32,96},{48,112},{64,0},{80,16},{96,32},{112,48},{1... | collective-permute-start | bytes 688136 | tf_op jit(solution)/shard_map/ppermute | solution.py:438
  68.2 12.9 %collective-permute-start.17 = (f32[4,112,128]{2,1,0:T(8,128)S(1)}, f32[4,112,128]{2,1,0:T(8,128)S(1)}, u32[]{:S(2)}, u32[]{:S(2)}) collective-permute-start(f32[4,112,128]{2,1,0:T(8,128)S(1)} %pad_maximum_fusion.refs_0_), channel_id=1, source_target_pairs={{0,32},{16,48},{32,64},{48,80},{64,96},{80,112},{96,0},{112,16},{1... | collective-permute-start | bytes 688136 | tf_op jit(solution)/shard_map/ppermute | solution.py:438
  68.8 13.6 %collective-permute-start.16 = (f32[4,112,128]{2,1,0:T(8,128)S(1)}, f32[4,112,128]{2,1,0:T(8,128)S(1)}, u32[]{:S(2)}, u32[]{:S(2)}) collective-permute-start(f32[4,112,128]{2,1,0:T(8,128)S(1)} %pad_maximum_fusion.refs_0_), channel_id=1, source_target_pairs={{0,16},{16,0},{32,48},{48,32},{64,80},{80,64},{96,112},{112,96},{1... | collective-permute-start | bytes 688136 | tf_op jit(solution)/shard_map/ppermute | solution.py:442
  77.5 4.8 %collective-permute-start.22 = (f32[4,112,128]{2,1,0:T(8,128)S(1)}, f32[4,112,128]{2,1,0:T(8,128)S(1)}, u32[]{:S(2)}, u32[]{:S(2)}) collective-permute-start(f32[4,112,128]{2,1,0:T(8,128)S(1)} %collective-permute-done.21.refs_6_), channel_id=1, source_target_pairs={{0,16},{16,0},{32,48},{48,32},{64,80},{80,64},{96,112},{112,96},{1... | collective-permute-start | bytes 688136 | tf_op jit(solution)/shard_map/ppermute | solution.py:442
  78.8 3.6 %collective-permute-start.20 = (f32[4,112,128]{2,1,0:T(8,128)S(1)}, f32[4,112,128]{2,1,0:T(8,128)S(1)}, u32[]{:S(2)}, u32[]{:S(2)}) collective-permute-start(f32[4,112,128]{2,1,0:T(8,128)S(1)} %collective-permute-done.19.refs_4_), channel_id=1, source_target_pairs={{0,16},{16,0},{32,48},{48,32},{64,80},{80,64},{96,112},{112,96},{1... | collective-permute-start | bytes 688136 | tf_op jit(solution)/shard_map/ppermute | solution.py:442
  99.0 6.0 %collective-permute-start.24 = (f32[4,64,128]{2,1,0:T(8,128)S(1)}, f32[4,64,128]{2,1,0:T(8,128)S(1)}, u32[]{:S(2)}, u32[]{:S(2)}) collective-permute-start(f32[4,64,128]{2,1,0:T(8,128)S(1)} %get-tuple-element.26), channel_id=1, source_target_pairs={{0,1},{1,2},{2,3},{3,0},{4,5},{5,6},{6,7},{7,4},{8,9},{9,10},{10,1... | collective-permute-start | bytes 393224 | tf_op jit(solution)/shard_map/ppermute | solution.py:438
  99.1 5.9 %collective-permute-start.23 = (f32[4,64,128]{2,1,0:T(8,128)S(1)}, f32[4,64,128]{2,1,0:T(8,128)S(1)}, u32[]{:S(2)}, u32[]{:S(2)}) collective-permute-start(f32[4,64,128]{2,1,0:T(8,128)S(1)} %get-tuple-element.26), channel_id=1, source_target_pairs={{0,3},{1,0},{2,1},{3,2},{4,7},{5,4},{6,5},{7,6},{8,11},{9,8},{10,9... | collective-permute-start | bytes 393224 | tf_op jit(solution)/shard_map/ppermute | solution.py:438
  105.0 4.2 %collective-permute-start.25 = (f32[4,24,128]{2,1,0:T(8,128)S(1)}, f32[4,24,128]{2,1,0:T(8,128)S(1)}, u32[]{:S(2)}, u32[]{:S(2)}) collective-permute-start(f32[4,24,128]{2,1,0:T(8,128)S(1)} %get-tuple-element.31), channel_id=1, source_target_pairs={{0,4},{4,8},{8,12},{12,0},{1,5},{5,9},{9,13},{13,1},{2,6},{6,10},{... | collective-permute-start | bytes 147464 | tf_op jit(solution)/shard_map/ppermute | solution.py:438
  105.1 4.1 %collective-permute-start.26 = (f32[4,24,128]{2,1,0:T(8,128)S(1)}, f32[4,24,128]{2,1,0:T(8,128)S(1)}, u32[]{:S(2)}, u32[]{:S(2)}) collective-permute-start(f32[4,24,128]{2,1,0:T(8,128)S(1)} %get-tuple-element.32), channel_id=1, source_target_pairs={{0,12},{4,0},{8,4},{12,8},{1,13},{5,1},{9,5},{13,9},{2,14},{6,2},{... | collective-permute-start | bytes 147464 | tf_op jit(solution)/shard_map/ppermute | solution.py:438
  109.3 4.9 %collective-permute-start.32 = (f32[4,112,128]{2,1,0:T(8,128)S(1)}, f32[4,112,128]{2,1,0:T(8,128)S(1)}, u32[]{:S(2)}, u32[]{:S(2)}) collective-permute-start(f32[4,112,128]{2,1,0:T(8,128)S(1)} %pad_maximum_fusion.1.refs_0_), channel_id=1, source_target_pairs={{0,96},{16,112},{32,0},{48,16},{64,32},{80,48},{96,64},{112,80},{1... | collective-permute-start | bytes 688136 | tf_op jit(solution)/shard_map/ppermute | solution.py:438
  109.9 9.9 %collective-permute-start.30 = (f32[4,112,128]{2,1,0:T(8,128)S(1)}, f32[4,112,128]{2,1,0:T(8,128)S(1)}, u32[]{:S(2)}, u32[]{:S(2)}) collective-permute-start(f32[4,112,128]{2,1,0:T(8,128)S(1)} %pad_maximum_fusion.1.refs_0_), channel_id=1, source_target_pairs={{0,64},{16,80},{32,96},{48,112},{64,0},{80,16},{96,32},{112,48},{1... | collective-permute-start | bytes 688136 | tf_op jit(solution)/shard_map/ppermute | solution.py:438
  109.9 13.2 %collective-permute-start.28 = (f32[4,112,128]{2,1,0:T(8,128)S(1)}, f32[4,112,128]{2,1,0:T(8,128)S(1)}, u32[]{:S(2)}, u32[]{:S(2)}) collective-permute-start(f32[4,112,128]{2,1,0:T(8,128)S(1)} %pad_maximum_fusion.1.refs_0_), channel_id=1, source_target_pairs={{0,32},{16,48},{32,64},{48,80},{64,96},{80,112},{96,0},{112,16},{1... | collective-permute-start | bytes 688136 | tf_op jit(solution)/shard_map/ppermute | solution.py:438
  110.8 13.6 %collective-permute-start.27 = (f32[4,112,128]{2,1,0:T(8,128)S(1)}, f32[4,112,128]{2,1,0:T(8,128)S(1)}, u32[]{:S(2)}, u32[]{:S(2)}) collective-permute-start(f32[4,112,128]{2,1,0:T(8,128)S(1)} %pad_maximum_fusion.1.refs_0_), channel_id=1, source_target_pairs={{0,16},{16,0},{32,48},{48,32},{64,80},{80,64},{96,112},{112,96},{1... | collective-permute-start | bytes 688136 | tf_op jit(solution)/shard_map/ppermute | solution.py:442
  114.2 10.2 %collective-permute-start.33 = (f32[4,112,128]{2,1,0:T(8,128)S(1)}, f32[4,112,128]{2,1,0:T(8,128)S(1)}, u32[]{:S(2)}, u32[]{:S(2)}) collective-permute-start(f32[4,112,128]{2,1,0:T(8,128)S(1)} %collective-permute-done.32.refs_6_), channel_id=1, source_target_pairs={{0,16},{16,0},{32,48},{48,32},{64,80},{80,64},{96,112},{112,96},{1... | collective-permute-start | bytes 688136 | tf_op jit(solution)/shard_map/ppermute | solution.py:442
  119.8 4.6 %collective-permute-start.31 = (f32[4,112,128]{2,1,0:T(8,128)S(1)}, f32[4,112,128]{2,1,0:T(8,128)S(1)}, u32[]{:S(2)}, u32[]{:S(2)}) collective-permute-start(f32[4,112,128]{2,1,0:T(8,128)S(1)} %collective-permute-done.30.refs_4_), channel_id=1, source_target_pairs={{0,16},{16,0},{32,48},{48,32},{64,80},{80,64},{96,112},{112,96},{1... | collective-permute-start | bytes 688136 | tf_op jit(solution)/shard_map/ppermute | solution.py:442
  (6 other events, 52.7 us)

commit v3 on v2

--- a/solution.py
+++ b/solution.py
@@ -14,6 +14,7 @@
 KEEP = 1.0 - DAMPING
 HIGH = lax.Precision.HIGHEST
 F32 = jnp.float32
+BF16 = jnp.bfloat16
 
 PL0, R0 = 24, 160
 PL1, R1 = 42, 128
@@ -279,74 +280,118 @@
     cols[...] = acc
 
 
-def energy_kernel(pos, stiff, u, xface, yrim, zrim, xrim, rho, f, pack, u0, u1, table):
+def form_matrix(stiff, high, low):
+    r, c = iota((192, 24), 0), iota((192, 24), 1)
+    wide = jnp.where(lax.shift_right_logical(r, 3) == c, 1.0, 0.0)
+    r, c = iota((24, 192), 0), iota((24, 192), 1)
+    tall = jnp.where(lax.shift_right_logical(c, 3) == r, 1.0, 0.0)
+    full = jnp.dot(wide, stiff, precision=HIGH, preferred_element_type=F32)
+    full = jnp.dot(full, tall, precision=HIGH, preferred_element_type=F32)
+    r, c = iota((192, 192), 0), iota((192, 192), 1)
+    full = jnp.where(jnp.bitwise_and(r, 7) == jnp.bitwise_and(c, 7), full, 0.0)
+    top = full.astype(BF16)
+    high[...] = top
+    low[...] = (full - top.astype(F32)).astype(BF16)
+
+
+def energy_group(u0, u1, high, low, rho, f, x, y, x_in, x_out):
+    cols = []
+    for q in range(4):
+        val = []
+        for ref in (u0, u1):
+            for b in (0, 1):
+                for a in (0, 1):
+                    for d in range(3):
+                        val.append(ref[9 * d + x + a, pl.ds(y + 8 * q + b, 8)])
+        cols.append(jnp.concatenate(val, axis=0))
+    u = jnp.concatenate(cols, axis=1)
+    top = u.astype(BF16)
+    pushed = jnp.dot(high[...], top, preferred_element_type=F32)
+    pushed = pushed + jnp.dot(low[...], top, preferred_element_type=F32)
+    prod = pushed * (u + (u - top.astype(F32)))
+    energy = prod[0:8]
+    for i in range(1, 24):
+        energy = energy + prod[8 * i:8 * i + 8]
+    for q in range(4):
+        rows = pl.ds(y + 8 * q, 8)
+        r = rho[x_in, rows]
+        f[x_out, rows] = -3.0 * r * r * energy[:, 128 * q:128 * q + 128]
+
+
+def energy_first(pos, stiff, u, zrim, rho, u0, u1, high, low, f):
+    keep_z = jnp.where(pos[2] < 3, 1.0, 0.0)
+    form_matrix(stiff[...], high, low)
+    lane = iota((128, 128), 1)
+    col = zrim[...] * keep_z
+    for d in range(3):
+        for x in range(8):
+            k, q = 8 * d + x, 9 * d + x
+            body = u[d, x]
+            u0[q] = body
+            u1[q] = jnp.where(lane == 127, pltpu.roll(col, 127 - k, 1), next_lane(body))
+
+    def group(c):
+        x = c // 3
+        y = pl.multiple_of((c - 3 * x) * 32, 32)
+        energy_group(u0, u1, high, low, rho, f, x, y, x, x)
+
+    planes(0, 12, 4, group)
+
+
+def energy_second(u0, u1, high, low, rho, f):
+    def group(c):
+        x = c // 3
+        y = pl.multiple_of((c - 3 * x) * 32, 32)
+        energy_group(u0, u1, high, low, rho, f, x + 4, y, x + 4, x)
+
+    planes(0, 9, 3, group)
+
+
+def energy_last(pos, u0, u1, high, low, rho, xface, yrim, zrim, xrim, fa, fb, f, pack, w0, w1):
     gx, gy, gz = pos[0], pos[1], pos[2]
     keep_x = jnp.where(gx < 7, 1.0, 0.0)
     keep_y = jnp.where(gy < 3, 1.0, 0.0)
     keep_z = jnp.where(gz < 3, 1.0, 0.0)
-    n = 0
-    for i in range(24):
-        for j in range(i, 24):
-            value = stiff[i, j] if i == j else stiff[i, j] + stiff[j, i]
-            table[n] = jnp.full((8, 128), value, F32)
-            n += 1
     lane = iota((128, 128), 1)
     lane8 = iota((8, 128), 1)
     for d in range(3):
         for x in range(9):
-            k = 8 * d + x
+            k, q = 8 * d + x, 9 * d + x
             if x < 8:
-                body = u[d, x]
-                col = zrim[...]
+                rows = pl.ds(0, 128) if x == 7 else pl.ds(96, 32)
+                w0[q, rows] = u0[q, rows]
+                w1[q, rows] = u1[q, rows]
                 row = yrim[pl.ds(k, 1)]
                 corner = yrim[pl.ds(24, 8)]
             else:
                 k = 8 * d
                 body = xface[d] * keep_x
-                col = xrim[pl.ds(32, 128)] * keep_x
+                col = xrim[pl.ds(32, 128)] * (keep_x * keep_z)
+                w0[q, pl.ds(0, 128)] = body
+                w1[q, pl.ds(0, 128)] = jnp.where(
+                    lane == 127, pltpu.roll(col, 127 - k, 1), next_lane(body))
                 row = xrim[pl.ds(k, 1)] * keep_x
                 corner = xrim[pl.ds(24, 8)] * keep_x
             row = jnp.broadcast_to(row, (8, 128)) * keep_y
             corner = jnp.broadcast_to(corner[0:1], (8, 128)) * (keep_y * keep_z)
-            q = 9 * d + x
-            u0[q, pl.ds(0, 128)] = body
-            u0[q, pl.ds(128, 8)] = row
-            u1[q, pl.ds(0, 128)] = jnp.where(
-                lane == 127, pltpu.roll(col, 127 - k, 1) * keep_z, next_lane(body))
-            u1[q, pl.ds(128, 8)] = jnp.where(
+            w0[q, pl.ds(128, 8)] = row
+            w1[q, pl.ds(128, 8)] = jnp.where(
                 lane8 == 127, pltpu.roll(corner, 127 - k, 1), next_lane(row))
-
-    def chunk(c, carry):
-        x, y = c // 16, pl.multiple_of((c % 16) * 8, 8)
-        val = []
-        for c_z in (0, 1):
-            for b in (0, 1):
-                for a in (0, 1):
-                    for d in range(3):
-                        ref = u1 if c_z else u0
-                        val.append(ref[9 * d + x + a, pl.ds(y + b, 8)])
-        energy = None
-        n = 0
-        for i in range(24):
-            acc = None
-            for j in range(i, 24):
-                term = table[n] * val[j]
-                acc = term if acc is None else acc + term
-                n += 1
-            acc = acc * val[i]
-            energy = acc if energy is None else energy + acc
-        r = rho[x, pl.ds(y, 8)]
-        f[x, pl.ds(y, 8)] = -3.0 * r * r * energy
-        return carry
-
-    lax.fori_loop(0, 128, chunk, 0)
+    for x in range(4):
+        f[x, pl.ds(0, 96)] = fa[x, pl.ds(0, 96)]
+    for x in range(3):
+        f[4 + x, pl.ds(0, 96)] = fb[x, pl.ds(0, 96)]
+    for x in range(7):
+        energy_group(w0, w1, high, low, rho, f, x, 96, x, x)
+    for q in range(4):
+        energy_group(w0, w1, high, low, rho, f, 7, 32 * q, 7, 7)
     acc = jnp.zeros((128, 128), F32)
     for x in range(8):
         value = f[x]
-        low = pltpu.roll(value, 8 * x, 1) if x else value
-        acc = jnp.where((lane >= 8 * x) & (lane < 8 * x + 8), low, acc)
-        high = pltpu.roll(value, (8 * x + 72) % 128, 1)
-        acc = jnp.where((lane >= 64 + 8 * x) & (lane < 72 + 8 * x), high, acc)
+        low_z = pltpu.roll(value, 8 * x, 1) if x else value
+        acc = jnp.where((lane >= 8 * x) & (lane < 8 * x + 8), low_z, acc)
+        high_z = pltpu.roll(value, (8 * x + 72) % 128, 1)
+        acc = jnp.where((lane >= 64 + 8 * x) & (lane < 72 + 8 * x), high_z, acc)
     pack[...] = acc
 
 
@@ -470,11 +515,18 @@
     xface = shifted(u[:, 0], "gx", -1)
     zrim = shifted(cols, "gz", -1)
     yrim = shifted(jnp.concatenate([rows, zrim[:8]], axis=0), "gy", -1)
+    mat = jax.ShapeDtypeStruct((192, 192), BF16)
+    u0, u1, high, low, fa = call(
+        energy_first, [shape(27, 128, 128), shape(27, 128, 128), mat, mat, shape(4, 128, 128)],
+        [], 1, [pos, stiff, u, zrim, rho], "energy_first")
+    yrim, fa = lax.optimization_barrier((yrim, fa))
     xrim = shifted(jnp.concatenate([yrim, zrim], axis=0), "gx", -1)
+    (fb,) = call(
+        energy_second, [shape(3, 128, 128)], [], 0, [u0, u1, high, low, rho], "energy_second")
     f, pack = call(
-        energy_kernel, [shape(8, 128, 128), shape(128, 128)],
-        [vmem(27, 136, 128), vmem(27, 136, 128), vmem(300, 8, 128)], 2,
-        [pos, stiff, u, xface, yrim, zrim, xrim, rho], "energy")
+        energy_last, [shape(8, 128, 128), shape(128, 128)],
+        [vmem(27, 136, 128), vmem(27, 136, 128)], 1,
+        [pos, u0, u1, high, low, rho, xface, yrim, zrim, xrim, fa, fb], "energy_last")
 
     fl, fr = shifted(f, "gx", 1), shifted(f, "gx", -1)
     lane = lax.broadcasted_iota(jnp.int32, pack.shape, 1)

time: 136 us -> 125 us (0.919)
  Pallas kernels: 46 us -> 38 us
  starting transfers between devices: 57.8 us -> 54.4 us
    pallas_call x5 -> x7, Pallas kernels: 46 us -> 38 us  [call(): pl.pallas_call(kernel, out_shape=outs, in_specs=specs, out_specs=[VM] * l...]
    ppermute x26, starting transfers between devices: 38.9 us -> 36.9 us  [shifted(): lax.ppermute(value, axis, [(i, (i + step) % size) for i in range(size)])]
    ppermute x8, starting transfers between devices: 18.9 us -> 17.5 us  [swapped(): lax.ppermute(value, 'gx', [(i, i ^ 1) for i in range(lax.axis_size('gx'))])]
  transfers between devices with their start and end apart: 34 -> 34, of which waited for: 17 -> 16; matrix products, arithmetic and copies ran while one was open for 0% -> 0% of each run, Pallas kernels for 0% -> 4%
where the time goes in v3:
time: 125 us
  starting transfers between devices  54.4 us (44%)
  Pallas kernels  38 us (30%)
  waiting for transfers between devices  29.2 us (23%)
  local copies, waits for them, and re-layouts  2.5 us (2%)
    pallas_call x7, Pallas kernels, call(): pl.pallas_call(kernel, out_shape=outs, in_specs=specs, out_specs=[VM] * l...  38 us
    ppermute x26, starting transfers between devices, shifted(): lax.ppermute(value, axis, [(i, (i + step) % size) for i in range(size)])  36.9 us
    ppermute x26, waiting for transfers between devices, shifted(): lax.ppermute(value, axis, [(i, (i + step) % size) for i in range(size)])  27 us
    ppermute x8, starting transfers between devices, swapped(): lax.ppermute(value, 'gx', [(i, i ^ 1) for i in range(lax.axis_size('gx'))])  17.5 us
  transfers between devices with their start and end apart: 34, of which 16 were waited for; matrix products, arithmetic and copies ran while one was open for 0% of the time, Pallas kernels for 4%

profile of v3, /device:TPU:1, one launch (start us, length us, event | category | flops | bytes accessed | tf_op | source)
XLA Modules:
  0.0 124.5 jit_solution(13573639242158442532)
XLA Ops:
  0.0 1.4 %copy-done = f32[3,8,128,128]{3,2,1,0:T(8,128)S(1)} copy-done((f32[3,8,128,128]{3,2,1,0:T(8,128)S(1)}, f32[3,8,128,128]{3,2,1,0:T(8,128)}, u32[]{:S(2)}) %copy-start) | copy-done | bytes 1572888
  1.9 3.4 %collective-permute-start = (f32[128,128]{1,0:T(8,128)S(1)}, f32[128,128]{1,0:T(8,128)S(1)}, u32[]{:S(2)}, u32[]{:S(2)}) collective-permute-start(f32[128,128]{1,0:T(8,128)S(1)} %get-tuple-element.24), channel_id=1, source_target_pairs={{0,3},{1,0},{2,1},{3,2},{4,7},{5,4},{6,5},{7,6},{8,11},{9,8},{10,9... | collective-permute-start | bytes 196616 | tf_op jit(solution)/shard_map/ppermute | solution.py:483
  6.6 3.8 %collective-permute-start.2 = (f32[32,128]{1,0:T(8,128)S(1)}, f32[32,128]{1,0:T(8,128)S(1)}, u32[]{:S(2)}, u32[]{:S(2)}) collective-permute-start(f32[32,128]{1,0:T(8,128)S(1)} %pad_maximum_fusion.6), channel_id=1, source_target_pairs={{0,12},{4,0},{8,4},{12,8},{1,13},{5,1},{9,5},{13,9},{2,14},{6,2},{... | collective-permute-start | bytes 49160 | tf_op jit(solution)/shard_map/ppermute | solution.py:483
  11.5 3.3 %energy_first.1 = (f32[27,128,128]{2,1,0:T(8,128)S(1)}, f32[27,128,128]{2,1,0:T(8,128)S(1)}, bf16[192,192]{1,0:T(8,128)(2,1)S(1)}, bf16[192,192]{1,0:T(8,128)(2,1)S(1)}, f32[4,128,128]{2,1,0:T(8,128)S(1)}) custom-call(s32[3]{0:T(128)S(1)} %pad_add_fusion.pos, f32[24,24]{1,0:T(8,128)S(1)} %copy-done.4, f32[3,8,128,128]{3,2,1,0:T(8,128)S(1)} %copy-done.1, ...), custom_call_target="tpu_custom_call" | custom-call | tf_op jit(solution)/shard_map/energy_first/pallas_call | solution.py:470
  14.8 2.2 %collective-permute-start.3 = (f32[160,128]{1,0:T(8,128)S(1)}, f32[160,128]{1,0:T(8,128)S(1)}, u32[]{:S(2)}, u32[]{:S(2)}) collective-permute-start(f32[160,128]{1,0:T(8,128)S(1)} %pad_maximum_fusion.3), channel_id=1, source_target_pairs={{0,112},{16,0},{32,16},{48,32},{64,48},{80,64},{96,80},{112,96},{1... | collective-permute-start | bytes 245768 | tf_op jit(solution)/shard_map/ppermute | solution.py:483
  17.0 1.5 %energy_second.1.fb = f32[3,128,128]{2,1,0:T(8,128)S(1)} custom-call(f32[27,128,128]{2,1,0:T(8,128)S(1)} %get-tuple-element.25.u0, f32[27,128,128]{2,1,0:T(8,128)S(1)} %get-tuple-element.26.u1, bf16[192,192]{1,0:T(8,128)(2,1)S(1)} %get-tuple-element.27.high, bf16[192,192]{1,0:T(8,128)(2,1)S(1)} %get-tuple-element.28.low, f32[8,128,128]{2,1,0:T(8,128)S(1)} %copy-done.2), custom_call_target="tpu_custom_call" | custom-call | tf_op jit(solution)/shard_map/energy_second/pallas_call | solution.py:470
  18.5 1.4 %collective-permute-done.3.xrim = f32[160,128]{1,0:T(8,128)S(1)} collective-permute-done((f32[160,128]{1,0:T(8,128)S(1)}, f32[160,128]{1,0:T(8,128)S(1)}, u32[]{:S(2)}, u32[]{:S(2)}) %collective-permute-start.3) | collective-permute-done | bytes 81952 | tf_op jit(solution)/shard_map/ppermute | solution.py:483
  19.9 2.2 %energy_last.1 = (f32[8,128,128]{2,1,0:T(8,128)S(1)}, f32[128,128]{1,0:T(8,128)S(1)}) custom-call(s32[3]{0:T(128)S(1)} %pad_add_fusion.pos, f32[27,128,128]{2,1,0:T(8,128)S(1)} %get-tuple-element.25.u0, f32[27,128,128]{2,1,0:T(8,128)S(1)} %get-tuple-element.26.u1, bf16[192,192]{1,0:T(8,128)(2,1)S(1)} %get-tuple-element.27.high, ...), custom_call_target="tpu_custom_call" | custom-call | tf_op jit(solution)/shard_map/energy_last/pallas_call | solution.py:470
  23.0 2.6 %collective-permute-start.6 = (f32[128,128]{1,0:T(8,128)S(1)}, f32[128,128]{1,0:T(8,128)S(1)}, u32[]{:S(2)}, u32[]{:S(2)}) collective-permute-start(f32[128,128]{1,0:T(8,128)S(1)} %get-tuple-element.34), channel_id=1, source_target_pairs={{0,3},{1,0},{2,1},{3,2},{4,7},{5,4},{6,5},{7,6},{8,11},{9,8},{10,9... | collective-permute-start | bytes 196616 | tf_op jit(solution)/shard_map/ppermute | solution.py:483
  25.6 1.7 %collective-permute-start.4 = (f32[8,128,128]{2,1,0:T(8,128)S(1)}, f32[8,128,128]{2,1,0:T(8,128)S(1)}, u32[]{:S(2)}, u32[]{:S(2)}) collective-permute-start(f32[8,128,128]{2,1,0:T(8,128)S(1)} %get-tuple-element.33.fc), channel_id=1, source_target_pairs={{0,16},{16,32},{32,48},{48,64},{64,80},{80,96},{96,112},{112,0},{1... | collective-permute-start | bytes 1572872 | tf_op jit(solution)/shard_map/ppermute | solution.py:483
  28.2 1.4 %collective-permute-start.8 = (f32[72,128]{1,0:T(8,128)S(1)}, f32[72,128]{1,0:T(8,128)S(1)}, u32[]{:S(2)}, u32[]{:S(2)}) collective-permute-start(f32[72,128]{1,0:T(8,128)S(1)} %pad_maximum_fusion.4), channel_id=1, source_target_pairs={{0,4},{4,8},{8,12},{12,0},{1,5},{5,9},{9,13},{13,1},{2,6},{6,10},{... | collective-permute-start | bytes 110600 | tf_op jit(solution)/shard_map/ppermute | solution.py:483
  30.9 1.6 %collective-permute-done.8 = f32[72,128]{1,0:T(8,128)S(1)} collective-permute-done((f32[72,128]{1,0:T(8,128)S(1)}, f32[72,128]{1,0:T(8,128)S(1)}, u32[]{:S(2)}, u32[]{:S(2)}) %collective-permute-start.8) | collective-permute-done | bytes 36896 | tf_op jit(solution)/shard_map/ppermute | solution.py:483
  32.6 1.5 %collective-permute-start.11 = (f32[272,128]{1,0:T(8,128)S(1)}, f32[272,128]{1,0:T(8,128)S(1)}, u32[]{:S(2)}, u32[]{:S(2)}) collective-permute-start(f32[272,128]{1,0:T(8,128)S(1)} %pad_maximum_fusion.2.hc), channel_id=1, source_target_pairs={{0,112},{16,0},{32,16},{48,32},{64,48},{80,64},{96,80},{112,96},{1... | collective-permute-start | bytes 417800 | tf_op jit(solution)/shard_map/ppermute | solution.py:483
  34.3 3.0 %collective-permute-done.11.hr = f32[272,128]{1,0:T(8,128)S(1)} collective-permute-done((f32[272,128]{1,0:T(8,128)S(1)}, f32[272,128]{1,0:T(8,128)S(1)}, u32[]{:S(2)}, u32[]{:S(2)}) %collective-permute-start.11) | collective-permute-done | bytes 139296 | tf_op jit(solution)/shard_map/ppermute | solution.py:483
  37.4 4.5 %first.1 = (f32[24,160,128]{2,1,0:T(8,128)S(1)}, f32[24,160,128]{2,1,0:T(8,128)S(1)}, f32[24,160,128]{2,1,0:T(8,128)S(1)}, f32[24,160,128]{2,1,0:T(8,128)S(1)}, f32[4,64,128]{2,1,0:T(8,128)S(1)}) custom-call(s32[3]{0:T(128)S(1)} %pad_add_fusion.pos, f32[8,128,128]{2,1,0:T(8,128)S(1)} %collective-permute-done.4.fl, f32[8,128,128]{2,1,0:T(8,128)S(1)} %get-tuple-element.33.fc, ...), custom_call_target="tpu_custom_call" | custom-call | tf_op jit(solution)/shard_map/first/pallas_call | solution.py:470
  42.5 2.1 %collective-permute-start.12 = (f32[4,64,128]{2,1,0:T(8,128)S(1)}, f32[4,64,128]{2,1,0:T(8,128)S(1)}, u32[]{:S(2)}, u32[]{:S(2)}) collective-permute-start(f32[4,64,128]{2,1,0:T(8,128)S(1)} %get-tuple-element.35), channel_id=1, source_target_pairs={{0,3},{1,0},{2,1},{3,2},{4,7},{5,4},{6,5},{7,6},{8,11},{9,8},{10,9... | collective-permute-start | bytes 393224 | tf_op jit(solution)/shard_map/ppermute | solution.py:483
  44.6 2.3 %collective-permute-done.13 = f32[4,64,128]{2,1,0:T(8,128)S(1)} collective-permute-done((f32[4,64,128]{2,1,0:T(8,128)S(1)}, f32[4,64,128]{2,1,0:T(8,128)S(1)}, u32[]{:S(2)}, u32[]{:S(2)}) %collective-permute-start.13) | collective-permute-done | bytes 131104 | tf_op jit(solution)/shard_map/ppermute | solution.py:483
  47.1 2.7 %collective-permute-start.15 = (f32[4,24,128]{2,1,0:T(8,128)S(1)}, f32[4,24,128]{2,1,0:T(8,128)S(1)}, u32[]{:S(2)}, u32[]{:S(2)}) collective-permute-start(f32[4,24,128]{2,1,0:T(8,128)S(1)} %get-tuple-element.48), channel_id=1, source_target_pairs={{0,12},{4,0},{8,4},{12,8},{1,13},{5,1},{9,5},{13,9},{2,14},{6,2},{... | collective-permute-start | bytes 147464 | tf_op jit(solution)/shard_map/ppermute | solution.py:483
  49.8 1.8 %collective-permute-done.14 = f32[4,24,128]{2,1,0:T(8,128)S(1)} collective-permute-done((f32[4,24,128]{2,1,0:T(8,128)S(1)}, f32[4,24,128]{2,1,0:T(8,128)S(1)}, u32[]{:S(2)}, u32[]{:S(2)}) %collective-permute-start.14) | collective-permute-done | bytes 49184 | tf_op jit(solution)/shard_map/ppermute | solution.py:483
  51.6 4.7 %collective-permute-start.21 = (f32[4,112,128]{2,1,0:T(8,128)S(1)}, f32[4,112,128]{2,1,0:T(8,128)S(1)}, u32[]{:S(2)}, u32[]{:S(2)}) collective-permute-start(f32[4,112,128]{2,1,0:T(8,128)S(1)} %pad_maximum_fusion.refs_0_), channel_id=1, source_target_pairs={{0,96},{16,112},{32,0},{48,16},{64,32},{80,48},{96,64},{112,80},{1... | collective-permute-start | bytes 688136 | tf_op jit(solution)/shard_map/ppermute | solution.py:483
  56.9 2.7 %collective-permute-start.16 = (f32[4,112,128]{2,1,0:T(8,128)S(1)}, f32[4,112,128]{2,1,0:T(8,128)S(1)}, u32[]{:S(2)}, u32[]{:S(2)}) collective-permute-start(f32[4,112,128]{2,1,0:T(8,128)S(1)} %pad_maximum_fusion.refs_0_), channel_id=1, source_target_pairs={{0,16},{16,0},{32,48},{48,32},{64,80},{80,64},{96,112},{112,96},{1... | collective-permute-start | bytes 688136 | tf_op jit(solution)/shard_map/ppermute | solution.py:487
  59.6 6.3 %collective-permute-done.21.refs_6_ = f32[4,112,128]{2,1,0:T(8,128)S(1)} collective-permute-done((f32[4,112,128]{2,1,0:T(8,128)S(1)}, f32[4,112,128]{2,1,0:T(8,128)S(1)}, u32[]{:S(2)}, u32[]{:S(2)}) %collective-permute-start.21) | collective-permute-done | bytes 229408 | tf_op jit(solution)/shard_map/ppermute | solution.py:483
  71.5 15.5 %middle.1 = (f32[24,160,128]{2,1,0:T(8,128)S(1)}, f32[24,160,128]{2,1,0:T(8,128)S(1)}, f32[4,64,128]{2,1,0:T(8,128)S(1)}) custom-call(s32[3]{0:T(128)S(1)} %pad_add_fusion.pos, f32[4,112,128]{2,1,0:T(8,128)S(1)} %pad_maximum_fusion.refs_0_, f32[4,112,128]{2,1,0:T(8,128)S(1)} %collective-permute-done.16.refs_1_, ...), custom_call_target="tpu_custom_call" | custom-call | tf_op jit(solution)/shard_map/middle/pallas_call | solution.py:470
  87.1 2.9 %collective-permute-start.23 = (f32[4,64,128]{2,1,0:T(8,128)S(1)}, f32[4,64,128]{2,1,0:T(8,128)S(1)}, u32[]{:S(2)}, u32[]{:S(2)}) collective-permute-start(f32[4,64,128]{2,1,0:T(8,128)S(1)} %get-tuple-element.40), channel_id=1, source_target_pairs={{0,3},{1,0},{2,1},{3,2},{4,7},{5,4},{6,5},{7,6},{8,11},{9,8},{10,9... | collective-permute-start | bytes 393224 | tf_op jit(solution)/shard_map/ppermute | solution.py:483
  90.0 3.3 %collective-permute-done.24 = f32[4,64,128]{2,1,0:T(8,128)S(1)} collective-permute-done((f32[4,64,128]{2,1,0:T(8,128)S(1)}, f32[4,64,128]{2,1,0:T(8,128)S(1)}, u32[]{:S(2)}, u32[]{:S(2)}) %collective-permute-start.24) | collective-permute-done | bytes 131104 | tf_op jit(solution)/shard_map/ppermute | solution.py:483
  93.4 2.7 %collective-permute-start.26 = (f32[4,24,128]{2,1,0:T(8,128)S(1)}, f32[4,24,128]{2,1,0:T(8,128)S(1)}, u32[]{:S(2)}, u32[]{:S(2)}) collective-permute-start(f32[4,24,128]{2,1,0:T(8,128)S(1)} %get-tuple-element.46), channel_id=1, source_target_pairs={{0,12},{4,0},{8,4},{12,8},{1,13},{5,1},{9,5},{13,9},{2,14},{6,2},{... | collective-permute-start | bytes 147464 | tf_op jit(solution)/shard_map/ppermute | solution.py:483
  96.2 1.4 %collective-permute-done.25 = f32[4,24,128]{2,1,0:T(8,128)S(1)} collective-permute-done((f32[4,24,128]{2,1,0:T(8,128)S(1)}, f32[4,24,128]{2,1,0:T(8,128)S(1)}, u32[]{:S(2)}, u32[]{:S(2)}) %collective-permute-start.25) | collective-permute-done | bytes 49184 | tf_op jit(solution)/shard_map/ppermute | solution.py:483
  99.2 2.7 %collective-permute-start.27 = (f32[4,112,128]{2,1,0:T(8,128)S(1)}, f32[4,112,128]{2,1,0:T(8,128)S(1)}, u32[]{:S(2)}, u32[]{:S(2)}) collective-permute-start(f32[4,112,128]{2,1,0:T(8,128)S(1)} %pad_maximum_fusion.1.refs_0_), channel_id=1, source_target_pairs={{0,16},{16,0},{32,48},{48,32},{64,80},{80,64},{96,112},{112,96},{1... | collective-permute-start | bytes 688136 | tf_op jit(solution)/shard_map/ppermute | solution.py:487
  102.6 5.6 %collective-permute-start.33 = (f32[4,112,128]{2,1,0:T(8,128)S(1)}, f32[4,112,128]{2,1,0:T(8,128)S(1)}, u32[]{:S(2)}, u32[]{:S(2)}) collective-permute-start(f32[4,112,128]{2,1,0:T(8,128)S(1)} %collective-permute-done.32.refs_6_), channel_id=1, source_target_pairs={{0,16},{16,0},{32,48},{48,32},{64,80},{80,64},{96,112},{112,96},{1... | collective-permute-start | bytes 688136 | tf_op jit(solution)/shard_map/ppermute | solution.py:487
  108.2 2.4 %collective-permute-start.31 = (f32[4,112,128]{2,1,0:T(8,128)S(1)}, f32[4,112,128]{2,1,0:T(8,128)S(1)}, u32[]{:S(2)}, u32[]{:S(2)}) collective-permute-start(f32[4,112,128]{2,1,0:T(8,128)S(1)} %collective-permute-done.30.refs_4_), channel_id=1, source_target_pairs={{0,16},{16,0},{32,48},{48,32},{64,80},{80,64},{96,112},{112,96},{1... | collective-permute-start | bytes 688136 | tf_op jit(solution)/shard_map/ppermute | solution.py:487
  110.5 1.4 %collective-permute-done.28.refs_2_ = f32[4,112,128]{2,1,0:T(8,128)S(1)} collective-permute-done((f32[4,112,128]{2,1,0:T(8,128)S(1)}, f32[4,112,128]{2,1,0:T(8,128)S(1)}, u32[]{:S(2)}, u32[]{:S(2)}) %collective-permute-start.28) | collective-permute-done | bytes 229408 | tf_op jit(solution)/shard_map/ppermute | solution.py:483
  114.0 10.5 %last.1 = f32[8,128,128]{2,1,0:T(8,128)} custom-call(s32[3]{0:T(128)S(1)} %pad_add_fusion.pos, f32[4,112,128]{2,1,0:T(8,128)S(1)} %pad_maximum_fusion.1.refs_0_, f32[4,112,128]{2,1,0:T(8,128)S(1)} %collective-permute-done.27.refs_1_, f32[4,112,128]{2,1,0:T(8,128)S(1)} %collective-permute-done.28.refs_2_, f32[4,112,128]{2,1,0:T(8,128)S(1)} %collective-permute-done.29.refs_3_, ...), custom_call_target="tpu_custom_call" | custom-call | tf_op jit(solution)/shard_map/last/pallas_call | solution.py:470
  (72 shorter events, 17.9 us)
Async XLA Ops:
  1.9 4.7 %collective-permute-start = (f32[128,128]{1,0:T(8,128)S(1)}, f32[128,128]{1,0:T(8,128)S(1)}, u32[]{:S(2)}, u32[]{:S(2)}) collective-permute-start(f32[128,128]{1,0:T(8,128)S(1)} %get-tuple-element.24), channel_id=1, source_target_pairs={{0,3},{1,0},{2,1},{3,2},{4,7},{5,4},{6,5},{7,6},{8,11},{9,8},{10,9... | collective-permute-start | bytes 196616 | tf_op jit(solution)/shard_map/ppermute | solution.py:483
  5.3 14.7 %collective-permute-start.1 = (f32[3,128,128]{2,1,0:T(8,128)S(1)}, f32[3,128,128]{2,1,0:T(8,128)S(1)}, u32[]{:S(2)}, u32[]{:S(2)}) collective-permute-start(f32[3,128,128]{2,1,0:T(8,128)S(1)} %slice_bitcast_fusion), channel_id=1, source_target_pairs={{0,112},{16,0},{32,16},{48,32},{64,48},{80,64},{96,80},{112,96},{1... | collective-permute-start | bytes 589832 | tf_op jit(solution)/shard_map/ppermute | solution.py:483
  6.6 8.2 %collective-permute-start.2 = (f32[32,128]{1,0:T(8,128)S(1)}, f32[32,128]{1,0:T(8,128)S(1)}, u32[]{:S(2)}, u32[]{:S(2)}) collective-permute-start(f32[32,128]{1,0:T(8,128)S(1)} %pad_maximum_fusion.6), channel_id=1, source_target_pairs={{0,12},{4,0},{8,4},{12,8},{1,13},{5,1},{9,5},{13,9},{2,14},{6,2},{... | collective-permute-start | bytes 49160 | tf_op jit(solution)/shard_map/ppermute | solution.py:483
  14.8 5.1 %collective-permute-start.3 = (f32[160,128]{1,0:T(8,128)S(1)}, f32[160,128]{1,0:T(8,128)S(1)}, u32[]{:S(2)}, u32[]{:S(2)}) collective-permute-start(f32[160,128]{1,0:T(8,128)S(1)} %pad_maximum_fusion.3), channel_id=1, source_target_pairs={{0,112},{16,0},{32,16},{48,32},{64,48},{80,64},{96,80},{112,96},{1... | collective-permute-start | bytes 245768 | tf_op jit(solution)/shard_map/ppermute | solution.py:483
  22.2 5.9 %collective-permute-start.7 = (f32[128,128]{1,0:T(8,128)S(1)}, f32[128,128]{1,0:T(8,128)S(1)}, u32[]{:S(2)}, u32[]{:S(2)}) collective-permute-start(f32[128,128]{1,0:T(8,128)S(1)} %get-tuple-element.34), channel_id=1, source_target_pairs={{0,1},{1,2},{2,3},{3,0},{4,5},{5,6},{6,7},{7,4},{8,9},{9,10},{10,1... | collective-permute-start | bytes 196616 | tf_op jit(solution)/shard_map/ppermute | solution.py:483
  23.0 5.0 %collective-permute-start.6 = (f32[128,128]{1,0:T(8,128)S(1)}, f32[128,128]{1,0:T(8,128)S(1)}, u32[]{:S(2)}, u32[]{:S(2)}) collective-permute-start(f32[128,128]{1,0:T(8,128)S(1)} %get-tuple-element.34), channel_id=1, source_target_pairs={{0,3},{1,0},{2,1},{3,2},{4,7},{5,4},{6,5},{7,6},{8,11},{9,8},{10,9... | collective-permute-start | bytes 196616 | tf_op jit(solution)/shard_map/ppermute | solution.py:483
  25.6 11.8 %collective-permute-start.5 = (f32[8,128,128]{2,1,0:T(8,128)S(1)}, f32[8,128,128]{2,1,0:T(8,128)S(1)}, u32[]{:S(2)}, u32[]{:S(2)}) collective-permute-start(f32[8,128,128]{2,1,0:T(8,128)S(1)} %get-tuple-element.33.fc), channel_id=1, source_target_pairs={{0,112},{16,0},{32,16},{48,32},{64,48},{80,64},{96,80},{112,96},{1... | collective-permute-start | bytes 1572872 | tf_op jit(solution)/shard_map/ppermute | solution.py:483
  25.6 11.7 %collective-permute-start.4 = (f32[8,128,128]{2,1,0:T(8,128)S(1)}, f32[8,128,128]{2,1,0:T(8,128)S(1)}, u32[]{:S(2)}, u32[]{:S(2)}) collective-permute-start(f32[8,128,128]{2,1,0:T(8,128)S(1)} %get-tuple-element.33.fc), channel_id=1, source_target_pairs={{0,16},{16,32},{32,48},{48,64},{64,80},{80,96},{96,112},{112,0},{1... | collective-permute-start | bytes 1572872 | tf_op jit(solution)/shard_map/ppermute | solution.py:483
  28.1 2.9 %collective-permute-start.9 = (f32[72,128]{1,0:T(8,128)S(1)}, f32[72,128]{1,0:T(8,128)S(1)}, u32[]{:S(2)}, u32[]{:S(2)}) collective-permute-start(f32[72,128]{1,0:T(8,128)S(1)} %pad_maximum_fusion.5), channel_id=1, source_target_pairs={{0,12},{4,0},{8,4},{12,8},{1,13},{5,1},{9,5},{13,9},{2,14},{6,2},{... | collective-permute-start | bytes 110600 | tf_op jit(solution)/shard_map/ppermute | solution.py:483
  28.2 4.3 %collective-permute-start.8 = (f32[72,128]{1,0:T(8,128)S(1)}, f32[72,128]{1,0:T(8,128)S(1)}, u32[]{:S(2)}, u32[]{:S(2)}) collective-permute-start(f32[72,128]{1,0:T(8,128)S(1)} %pad_maximum_fusion.4), channel_id=1, source_target_pairs={{0,4},{4,8},{8,12},{12,0},{1,5},{5,9},{9,13},{13,1},{2,6},{6,10},{... | collective-permute-start | bytes 110600 | tf_op jit(solution)/shard_map/ppermute | solution.py:483
  32.6 4.8 %collective-permute-start.11 = (f32[272,128]{1,0:T(8,128)S(1)}, f32[272,128]{1,0:T(8,128)S(1)}, u32[]{:S(2)}, u32[]{:S(2)}) collective-permute-start(f32[272,128]{1,0:T(8,128)S(1)} %pad_maximum_fusion.2.hc), channel_id=1, source_target_pairs={{0,112},{16,0},{32,16},{48,32},{64,48},{80,64},{96,80},{112,96},{1... | collective-permute-start | bytes 417800 | tf_op jit(solution)/shard_map/ppermute | solution.py:483
  34.1 3.3 %collective-permute-start.10 = (f32[272,128]{1,0:T(8,128)S(1)}, f32[272,128]{1,0:T(8,128)S(1)}, u32[]{:S(2)}, u32[]{:S(2)}) collective-permute-start(f32[272,128]{1,0:T(8,128)S(1)} %pad_maximum_fusion.2.hc), channel_id=1, source_target_pairs={{0,16},{16,32},{32,48},{48,64},{64,80},{80,96},{96,112},{112,0},{1... | collective-permute-start | bytes 417800 | tf_op jit(solution)/shard_map/ppermute | solution.py:483
  41.9 5.1 %collective-permute-start.13 = (f32[4,64,128]{2,1,0:T(8,128)S(1)}, f32[4,64,128]{2,1,0:T(8,128)S(1)}, u32[]{:S(2)}, u32[]{:S(2)}) collective-permute-start(f32[4,64,128]{2,1,0:T(8,128)S(1)} %get-tuple-element.35), channel_id=1, source_target_pairs={{0,1},{1,2},{2,3},{3,0},{4,5},{5,6},{6,7},{7,4},{8,9},{9,10},{10,1... | collective-permute-start | bytes 393224 | tf_op jit(solution)/shard_map/ppermute | solution.py:483
  42.5 4.4 %collective-permute-start.12 = (f32[4,64,128]{2,1,0:T(8,128)S(1)}, f32[4,64,128]{2,1,0:T(8,128)S(1)}, u32[]{:S(2)}, u32[]{:S(2)}) collective-permute-start(f32[4,64,128]{2,1,0:T(8,128)S(1)} %get-tuple-element.35), channel_id=1, source_target_pairs={{0,3},{1,0},{2,1},{3,2},{4,7},{5,4},{6,5},{7,6},{8,11},{9,8},{10,9... | collective-permute-start | bytes 393224 | tf_op jit(solution)/shard_map/ppermute | solution.py:483
  47.0 4.5 %collective-permute-start.14 = (f32[4,24,128]{2,1,0:T(8,128)S(1)}, f32[4,24,128]{2,1,0:T(8,128)S(1)}, u32[]{:S(2)}, u32[]{:S(2)}) collective-permute-start(f32[4,24,128]{2,1,0:T(8,128)S(1)} %get-tuple-element.47), channel_id=1, source_target_pairs={{0,4},{4,8},{8,12},{12,0},{1,5},{5,9},{9,13},{13,1},{2,6},{6,10},{... | collective-permute-start | bytes 147464 | tf_op jit(solution)/shard_map/ppermute | solution.py:483
  47.1 4.4 %collective-permute-start.15 = (f32[4,24,128]{2,1,0:T(8,128)S(1)}, f32[4,24,128]{2,1,0:T(8,128)S(1)}, u32[]{:S(2)}, u32[]{:S(2)}) collective-permute-start(f32[4,24,128]{2,1,0:T(8,128)S(1)} %get-tuple-element.48), channel_id=1, source_target_pairs={{0,12},{4,0},{8,4},{12,8},{1,13},{5,1},{9,5},{13,9},{2,14},{6,2},{... | collective-permute-start | bytes 147464 | tf_op jit(solution)/shard_map/ppermute | solution.py:483
  51.6 14.3 %collective-permute-start.21 = (f32[4,112,128]{2,1,0:T(8,128)S(1)}, f32[4,112,128]{2,1,0:T(8,128)S(1)}, u32[]{:S(2)}, u32[]{:S(2)}) collective-permute-start(f32[4,112,128]{2,1,0:T(8,128)S(1)} %pad_maximum_fusion.refs_0_), channel_id=1, source_target_pairs={{0,96},{16,112},{32,0},{48,16},{64,32},{80,48},{96,64},{112,80},{1... | collective-permute-start | bytes 688136 | tf_op jit(solution)/shard_map/ppermute | solution.py:483
  56.2 10.7 %collective-permute-start.19 = (f32[4,112,128]{2,1,0:T(8,128)S(1)}, f32[4,112,128]{2,1,0:T(8,128)S(1)}, u32[]{:S(2)}, u32[]{:S(2)}) collective-permute-start(f32[4,112,128]{2,1,0:T(8,128)S(1)} %pad_maximum_fusion.refs_0_), channel_id=1, source_target_pairs={{0,64},{16,80},{32,96},{48,112},{64,0},{80,16},{96,32},{112,48},{1... | collective-permute-start | bytes 688136 | tf_op jit(solution)/shard_map/ppermute | solution.py:483
  56.2 13.2 %collective-permute-start.17 = (f32[4,112,128]{2,1,0:T(8,128)S(1)}, f32[4,112,128]{2,1,0:T(8,128)S(1)}, u32[]{:S(2)}, u32[]{:S(2)}) collective-permute-start(f32[4,112,128]{2,1,0:T(8,128)S(1)} %pad_maximum_fusion.refs_0_), channel_id=1, source_target_pairs={{0,32},{16,48},{32,64},{48,80},{64,96},{80,112},{96,0},{112,16},{1... | collective-permute-start | bytes 688136 | tf_op jit(solution)/shard_map/ppermute | solution.py:483
  56.9 13.5 %collective-permute-start.16 = (f32[4,112,128]{2,1,0:T(8,128)S(1)}, f32[4,112,128]{2,1,0:T(8,128)S(1)}, u32[]{:S(2)}, u32[]{:S(2)}) collective-permute-start(f32[4,112,128]{2,1,0:T(8,128)S(1)} %pad_maximum_fusion.refs_0_), channel_id=1, source_target_pairs={{0,16},{16,0},{32,48},{48,32},{64,80},{80,64},{96,112},{112,96},{1... | collective-permute-start | bytes 688136 | tf_op jit(solution)/shard_map/ppermute | solution.py:487
  65.9 4.5 %collective-permute-start.22 = (f32[4,112,128]{2,1,0:T(8,128)S(1)}, f32[4,112,128]{2,1,0:T(8,128)S(1)}, u32[]{:S(2)}, u32[]{:S(2)}) collective-permute-start(f32[4,112,128]{2,1,0:T(8,128)S(1)} %collective-permute-done.21.refs_6_), channel_id=1, source_target_pairs={{0,16},{16,0},{32,48},{48,32},{64,80},{80,64},{96,112},{112,96},{1... | collective-permute-start | bytes 688136 | tf_op jit(solution)/shard_map/ppermute | solution.py:487
  67.0 3.4 %collective-permute-start.20 = (f32[4,112,128]{2,1,0:T(8,128)S(1)}, f32[4,112,128]{2,1,0:T(8,128)S(1)}, u32[]{:S(2)}, u32[]{:S(2)}) collective-permute-start(f32[4,112,128]{2,1,0:T(8,128)S(1)} %collective-permute-done.19.refs_4_), channel_id=1, source_target_pairs={{0,16},{16,0},{32,48},{48,32},{64,80},{80,64},{96,112},{112,96},{1... | collective-permute-start | bytes 688136 | tf_op jit(solution)/shard_map/ppermute | solution.py:487
  87.0 6.3 %collective-permute-start.24 = (f32[4,64,128]{2,1,0:T(8,128)S(1)}, f32[4,64,128]{2,1,0:T(8,128)S(1)}, u32[]{:S(2)}, u32[]{:S(2)}) collective-permute-start(f32[4,64,128]{2,1,0:T(8,128)S(1)} %get-tuple-element.40), channel_id=1, source_target_pairs={{0,1},{1,2},{2,3},{3,0},{4,5},{5,6},{6,7},{7,4},{8,9},{9,10},{10,1... | collective-permute-start | bytes 393224 | tf_op jit(solution)/shard_map/ppermute | solution.py:483
  87.1 6.3 %collective-permute-start.23 = (f32[4,64,128]{2,1,0:T(8,128)S(1)}, f32[4,64,128]{2,1,0:T(8,128)S(1)}, u32[]{:S(2)}, u32[]{:S(2)}) collective-permute-start(f32[4,64,128]{2,1,0:T(8,128)S(1)} %get-tuple-element.40), channel_id=1, source_target_pairs={{0,3},{1,0},{2,1},{3,2},{4,7},{5,4},{6,5},{7,6},{8,11},{9,8},{10,9... | collective-permute-start | bytes 393224 | tf_op jit(solution)/shard_map/ppermute | solution.py:483
  93.4 4.2 %collective-permute-start.25 = (f32[4,24,128]{2,1,0:T(8,128)S(1)}, f32[4,24,128]{2,1,0:T(8,128)S(1)}, u32[]{:S(2)}, u32[]{:S(2)}) collective-permute-start(f32[4,24,128]{2,1,0:T(8,128)S(1)} %get-tuple-element.45), channel_id=1, source_target_pairs={{0,4},{4,8},{8,12},{12,0},{1,5},{5,9},{9,13},{13,1},{2,6},{6,10},{... | collective-permute-start | bytes 147464 | tf_op jit(solution)/shard_map/ppermute | solution.py:483
  93.4 4.1 %collective-permute-start.26 = (f32[4,24,128]{2,1,0:T(8,128)S(1)}, f32[4,24,128]{2,1,0:T(8,128)S(1)}, u32[]{:S(2)}, u32[]{:S(2)}) collective-permute-start(f32[4,24,128]{2,1,0:T(8,128)S(1)} %get-tuple-element.46), channel_id=1, source_target_pairs={{0,12},{4,0},{8,4},{12,8},{1,13},{5,1},{9,5},{13,9},{2,14},{6,2},{... | collective-permute-start | bytes 147464 | tf_op jit(solution)/shard_map/ppermute | solution.py:483
  97.6 4.9 %collective-permute-start.32 = (f32[4,112,128]{2,1,0:T(8,128)S(1)}, f32[4,112,128]{2,1,0:T(8,128)S(1)}, u32[]{:S(2)}, u32[]{:S(2)}) collective-permute-start(f32[4,112,128]{2,1,0:T(8,128)S(1)} %pad_maximum_fusion.1.refs_0_), channel_id=1, source_target_pairs={{0,96},{16,112},{32,0},{48,16},{64,32},{80,48},{96,64},{112,80},{1... | collective-permute-start | bytes 688136 | tf_op jit(solution)/shard_map/ppermute | solution.py:483
  98.4 9.7 %collective-permute-start.30 = (f32[4,112,128]{2,1,0:T(8,128)S(1)}, f32[4,112,128]{2,1,0:T(8,128)S(1)}, u32[]{:S(2)}, u32[]{:S(2)}) collective-permute-start(f32[4,112,128]{2,1,0:T(8,128)S(1)} %pad_maximum_fusion.1.refs_0_), channel_id=1, source_target_pairs={{0,64},{16,80},{32,96},{48,112},{64,0},{80,16},{96,32},{112,48},{1... | collective-permute-start | bytes 688136 | tf_op jit(solution)/shard_map/ppermute | solution.py:483
  98.4 13.5 %collective-permute-start.28 = (f32[4,112,128]{2,1,0:T(8,128)S(1)}, f32[4,112,128]{2,1,0:T(8,128)S(1)}, u32[]{:S(2)}, u32[]{:S(2)}) collective-permute-start(f32[4,112,128]{2,1,0:T(8,128)S(1)} %pad_maximum_fusion.1.refs_0_), channel_id=1, source_target_pairs={{0,32},{16,48},{32,64},{48,80},{64,96},{80,112},{96,0},{112,16},{1... | collective-permute-start | bytes 688136 | tf_op jit(solution)/shard_map/ppermute | solution.py:483
  99.2 13.7 %collective-permute-start.27 = (f32[4,112,128]{2,1,0:T(8,128)S(1)}, f32[4,112,128]{2,1,0:T(8,128)S(1)}, u32[]{:S(2)}, u32[]{:S(2)}) collective-permute-start(f32[4,112,128]{2,1,0:T(8,128)S(1)} %pad_maximum_fusion.1.refs_0_), channel_id=1, source_target_pairs={{0,16},{16,0},{32,48},{48,32},{64,80},{80,64},{96,112},{112,96},{1... | collective-permute-start | bytes 688136 | tf_op jit(solution)/shard_map/ppermute | solution.py:487
  102.6 10.3 %collective-permute-start.33 = (f32[4,112,128]{2,1,0:T(8,128)S(1)}, f32[4,112,128]{2,1,0:T(8,128)S(1)}, u32[]{:S(2)}, u32[]{:S(2)}) collective-permute-start(f32[4,112,128]{2,1,0:T(8,128)S(1)} %collective-permute-done.32.refs_6_), channel_id=1, source_target_pairs={{0,16},{16,0},{32,48},{48,32},{64,80},{80,64},{96,112},{112,96},{1... | collective-permute-start | bytes 688136 | tf_op jit(solution)/shard_map/ppermute | solution.py:487
  108.2 4.7 %collective-permute-start.31 = (f32[4,112,128]{2,1,0:T(8,128)S(1)}, f32[4,112,128]{2,1,0:T(8,128)S(1)}, u32[]{:S(2)}, u32[]{:S(2)}) collective-permute-start(f32[4,112,128]{2,1,0:T(8,128)S(1)} %collective-permute-done.30.refs_4_), channel_id=1, source_target_pairs={{0,16},{16,0},{32,48},{48,32},{64,80},{80,64},{96,112},{112,96},{1... | collective-permute-start | bytes 688136 | tf_op jit(solution)/shard_map/ppermute | solution.py:487
  (7 other events, 27.6 us)

commit v4 on v3

v4 whole, which is shorter than its diff:
```python
import jax
import jax.numpy as jnp
from jax import lax
from jax.experimental import pallas as pl
from jax.experimental.pallas import tpu as pltpu
from jax.sharding import PartitionSpec as P

FILTER_COEF = 36.0
DAMPING = 0.95
S0 = FILTER_COEF
S1 = FILTER_COEF / 4.0
S2 = FILTER_COEF / 16.0
KEEP = 1.0 - DAMPING
HIGH = lax.Precision.HIGHEST
F32 = jnp.float32
BF16 = jnp.bfloat16

PL0, R0 = 24, 160
PL1, R1 = 42, 128
R2 = 72


def iota(shape, dim):
    return lax.broadcasted_iota(jnp.int32, shape, dim)


def next_lane(value):
    return pltpu.roll(value, 127, 1)


def prev_lane(value):
    return pltpu.roll(value, 1, 1)


def axis_count(place, total):
    return jnp.where(place > 0, 1.0, 0.0) + jnp.where(place < total - 1, 1.0, 0.0)


def planes(start, count, unroll, body):
    step = max(u for u in range(1, unroll + 1) if count % u == 0)
    if step == count:
        for j in range(count):
            body(start + j, j)
        return

    def block(k, carry):
        for j in range(step):
            body(start + k * step + j, j)
        return carry

    lax.fori_loop(0, count // step, block, 0)


def make_tables(weight, diag, rows, row_off, lane_place, lane_ok, base_y, base_z, total, scale):
    y = iota((rows, 128), 0) - row_off + base_y
    z = lane_place + base_z
    inside = lane_ok & (y >= 0) & (y < total) & (z >= 0) & (z < total)
    count = axis_count(y, total) + axis_count(z, total)
    weight[0] = jnp.zeros((rows, 128), F32)
    for i in (1, 2):
        value = 1.0 + scale * (count + float(i))
        weight[i] = jnp.where(inside, DAMPING / value, 0.0)
        if diag is not None:
            diag[i] = value


def x_index(place, total):
    edge = (place == 0) | (place == total - 1)
    out = (place < 0) | (place >= total)
    return jnp.where(out, 0, jnp.where(edge, 1, 2))


def side_place(lane):
    return jnp.where(lane < 64, lane + 128, lane - 128)


def level1_place(lane):
    return jnp.where(lane < 96, lane, lane - 128)


def level1_ok(place):
    return (place >= -22) & (place < 86)


def half(place):
    return lax.shift_right_arithmetic(place, 1)


def hits(cond):
    return jnp.where(cond, 1.0, 0.0)


def level0_place(index):
    side = index - 128
    ok = (index < 128) | (side < 8) | (side >= 120)
    return jnp.where(index < 128, index, side_place(side)), ok


def setup_kernel(pos, wm, ws, dm, w1, d1, w2, t0, t1, r0, tr0, dd, tdd, uu, up0):
    gy, gz = pos[1], pos[2]
    lane = iota((R0, 128), 1)
    make_tables(wm, dm, R0, 16, lane, lane >= 0, gy * 128, gz * 128, 512, S0)
    ok = (lane < 8) | (lane >= 120)
    make_tables(ws, None, R0, 16, side_place(lane), ok, gy * 128, gz * 128, 512, S0)
    z = level1_place(iota((R1, 128), 1))
    make_tables(w1, d1, R1, 32, z, level1_ok(z), gy * 64, gz * 64, 256, S1)

    lane = iota((R2, 128), 1)
    part = jnp.bitwise_and(lane, 63)
    y, z = iota((R2, 128), 0) - 20 + gy * 32, part - 11 + gz * 32
    inside = (part < 54) & (y >= 0) & (y < 128) & (z >= 0) & (z < 128)
    count = axis_count(y, 128) + axis_count(z, 128)
    for i in range(3):
        edge = {0: lane < 64, 1: lane < 0, 2: lane >= 64}[i]
        value = 1.0 + S2 * (count + jnp.where(edge, 1.0, 2.0))
        w2[i] = jnp.where(inside, DAMPING / value, 0.0)

    src, dst = iota((256, 256), 0), iota((256, 256), 1)
    step = jnp.bitwise_and(src - dst, 255)
    t0[...] = hits((step == 1) | (step == 255)).astype(BF16)
    src, dst = iota((256, 128), 0), iota((256, 128), 1)
    step = jnp.bitwise_and(src - dst, 127)
    t1[...] = hits((step == 1) | (step == 127)).astype(BF16)

    col = jnp.where(dst < 64, dst, dst - 64)
    good = (dst < 86) | (dst >= 106)
    z, ok = level0_place(src)
    total = jnp.zeros((256, 128), F32)
    for dz in (-1, 1):
        total = total + hits(ok & good & (z + dz >= 0) & (z + dz < 128) & (half(z + dz) == col))
    tr0[...] = 0.125 * total
    r0[...] = 0.125 * hits(good & (half(src) == col) & (src < 128))[0:128]

    z = level1_place(jnp.bitwise_and(src, 127))
    part = jnp.bitwise_and(dst, 63)
    good = (part < 54) & ((src < 128) == (dst < 64))
    dd[...] = 0.125 * hits(good & level1_ok(z) & (half(z) == part - 11))
    total = jnp.zeros((256, 128), F32)
    for dz in (-1, 1):
        total = total + hits(good & level1_ok(z + dz) & (half(z + dz) == part - 11))
    tdd[...] = 0.125 * total

    src, dst = iota((128, 256), 0), iota((128, 256), 1)
    z = level1_place(jnp.bitwise_and(dst, 127))
    part = jnp.bitwise_and(src, 63)
    good = (part < 54) & ((dst < 128) == (src < 64))
    uu[...] = hits(good & level1_ok(z) & (half(z) == part - 11))
    z, ok = level0_place(dst)
    up0[...] = hits(ok & (half(z) == level1_place(src)))


def two_parts(value):
    top = value.astype(BF16)
    return top, (value - top.astype(F32)).astype(BF16)


def level0_sweep(pos, src, dst, fm, fs, wm, ws, t0, first, last, side):
    lane = iota((144, 128), 1)
    rows, up, dn = pl.ds(8, 144), pl.ds(7, 144), pl.ds(9, 144)

    def body(p, j):
        i = x_index(pos[0] * 8 + p - 8, 64)
        m, s = src[0][p, rows], src[1][p, rows]
        if j % 2:
            a, b = two_parts(jnp.concatenate([m, s], axis=1))
            near = jnp.dot(a, t0[...], preferred_element_type=F32)
            near = near + jnp.dot(b, t0[...], preferred_element_type=F32)
            near_m, near_s = near[:, :128], near[:, 128:]
        else:
            mr, sr, ml, sl = next_lane(m), next_lane(s), prev_lane(m), prev_lane(s)
            near_m = jnp.where(lane == 127, sr, mr) + jnp.where(lane == 0, sl, ml)
            near_s = jnp.where(lane == 127, mr, sr) + jnp.where(lane == 0, ml, sl)
        tot = src[0][p - 1, rows] + src[0][p + 1, rows] + src[0][p, up] + src[0][p, dn]
        dst[0][p, rows] = KEEP * m + wm[i, rows] * (fm[p, rows] + S0 * (tot + near_m))
        if side:
            tot = src[1][p - 1, rows] + src[1][p + 1, rows] + src[1][p, up] + src[1][p, dn]
            dst[1][p, rows] = KEEP * s + ws[i, rows] * (fs[p, rows] + S0 * (tot + near_s))

    planes(first, last + 1 - first, 10, body)


def level0_restrict(pos, src, fm, dm, r0, tr0, tmp, out):
    rows, up, dn = pl.ds(16, 128), pl.ds(15, 128), pl.ds(17, 128)

    def body(k, j):
        sums = [None, None, None]
        for q in (0, 1):
            p = 8 + 2 * k + q
            i = x_index(pos[0] * 8 + p - 8, 64)
            m = src[0][p, rows]
            tot = src[0][p - 1, rows] + src[0][p + 1, rows] + src[0][p, up] + src[0][p, dn]
            parts = (fm[p, rows] + S0 * tot - dm[i, rows] * m, m, src[1][p, rows])
            sums = [v if t is None else t + v for t, v in zip(sums, parts)]
        pairs = []
        for n in range(3):
            tmp[3 * k + n] = sums[n]
            pairs.append(tmp[3 * k + n, pl.ds(0, 64, stride=2)] + tmp[3 * k + n, pl.ds(1, 64, stride=2)])
        value = jnp.dot(pairs[0], r0[...], precision=HIGH, preferred_element_type=F32)
        near = jnp.concatenate(pairs[1:], axis=1)
        near = jnp.dot(near, tr0[...], precision=HIGH, preferred_element_type=F32)
        out[k] = value + S0 * near

    planes(0, 4, 4, body)


def level1_sweep(src, dst, f, w, t1, first, count):
    mid, up, dn = pl.ds(8, 112), pl.ds(7, 112), pl.ds(9, 112)

    def body(p, j):
        i = x_index(p - 5, 32)
        m = src[p, mid]
        if j % 2:
            near = jnp.concatenate(two_parts(m), axis=1)
            near = jnp.dot(near, t1[...], preferred_element_type=F32)
        else:
            near = next_lane(m) + prev_lane(m)
        tot = src[p - 1, mid] + src[p + 1, mid] + src[p, up] + src[p, dn] + near
        dst[p, mid] = KEEP * m + w[i, mid] * (f[p, mid] + S1 * tot)

    planes(first, count, 16, body)


def level2_sweep(src, dst, f, w):
    lane = iota((56, 128), 1)
    mid, up, dn = pl.ds(8, 56), pl.ds(7, 56), pl.ds(9, 56)
    for p in range(1, 9):
        m = src[p, mid]
        if p == 1:
            before = jnp.where(lane >= 64, pltpu.roll(src[8, mid], 64, 1), 0.0)
        else:
            before = src[p - 1, mid]
        if p == 8:
            after = jnp.where(lane < 64, pltpu.roll(src[1, mid], 64, 1), 0.0)
        else:
            after = src[p + 1, mid]
        tot = before + after + src[p, up] + src[p, dn] + next_lane(m) + prev_lane(m)
        dst[p, mid] = KEEP * m + w[{1: 0, 8: 2}.get(p, 1), mid] * (f[p, mid] + S2 * tot)


def coarse_levels(pos, blocks, tables, f1, va, vb, f2, a2, b2, tmp):
    w1, d1, w2, t1, dd, tdd, uu = tables
    gx = pos[0]
    zero = jnp.zeros((R1, 128), F32)
    for p in list(range(0, 5)) + list(range(37, 42)):
        f1[p] = zero
        va[p] = zero
        vb[p] = zero
    for p in range(5, 37):
        for ref in (va, vb):
            ref[p, pl.ds(0, 8)] = jnp.zeros((8, 128), F32)
            ref[p, pl.ds(120, 8)] = jnp.zeros((8, 128), F32)
    for ref in (a2, b2):
        for p in range(1, 9):
            ref[p, pl.ds(0, 8)] = jnp.zeros((8, 128), F32)
            ref[p, pl.ds(64, 8)] = jnp.zeros((8, 128), F32)

    for m in range(4):
        for q in range(2):
            block = blocks[2 * m + q]
            own = gx if q == 0 else jnp.bitwise_xor(gx, 1)
            place = jnp.bitwise_and(own + 8 - 2 * m, 7)
            for j in range(4):
                p = 5 + 4 * place + j
                i = x_index(4 * place + j, 32)
                value = block[j]
                f1[p, pl.ds(8, 112)] = value
                va[p, pl.ds(8, 112)] = w1[i, pl.ds(8, 112)] * value

    level1_sweep(va, vb, f1, w1, t1, 5, 32)

    def residual(k):
        mid = pl.ds(8, 112)
        sums = [None, None]
        for q in (0, 1):
            p = 5 + 2 * k + q
            i = x_index(p - 5, 32)
            m = vb[p, mid]
            tot = vb[p - 1, mid] + vb[p + 1, mid] + vb[p, pl.ds(7, 112)] + vb[p, pl.ds(9, 112)]
            parts = (f1[p, mid] + S1 * tot - d1[i, mid] * m, m)
            sums = [v if t is None else t + v for t, v in zip(sums, parts)]
        pairs = []
        for n in range(2):
            tmp[2 * k + n, pl.ds(0, 112)] = sums[n]
            pairs.append(tmp[2 * k + n, pl.ds(0, 56, stride=2)] + tmp[2 * k + n, pl.ds(1, 56, stride=2)])
        return pairs

    def restrict(p, j):
        low, high = residual(p - 1), residual(p + 7)
        value = jnp.dot(jnp.concatenate([low[0], high[0]], axis=1), dd[...],
                        precision=HIGH, preferred_element_type=F32)
        near = jnp.dot(jnp.concatenate([low[1], high[1]], axis=1), tdd[...],
                       precision=HIGH, preferred_element_type=F32)
        value = value + S1 * near
        f2[p, pl.ds(8, 56)] = value
        i = jnp.where(p == 1, 0, jnp.where(p == 8, 2, 1))
        a2[p, pl.ds(8, 56)] = w2[i, pl.ds(8, 56)] * value

    planes(1, 8, 8, restrict)

    src2, dst2 = a2, b2
    for _ in range(7):
        level2_sweep(src2, dst2, f2, w2)
        src2, dst2 = dst2, src2

    def prolong(p, j):
        both = jnp.dot(src2[p, pl.ds(8, 56)], uu[...], precision=HIGH, preferred_element_type=F32)
        for n, k in ((0, p - 1), (1, p + 7)):
            e = both[:, 128 * n:128 * n + 128]
            for q in (0, 1):
                for h in (0, 1):
                    rows = pl.ds(8 + h, 56, stride=2)
                    vb[5 + 2 * k + q, rows] = vb[5 + 2 * k + q, rows] + e

    planes(1, 8, 8, prolong)
    level1_sweep(vb, va, f1, w1, t1, 4 * gx + 1, 12)
    level1_sweep(va, vb, f1, w1, t1, 4 * gx + 2, 10)


def level0_prolong(pos, e1, up0, old, new, first, last):
    def body(k, j):
        e = e1[4 * pos[0] + 1 + k, pl.ds(28, 72)]
        e = jnp.dot(e, up0[...], precision=HIGH, preferred_element_type=F32)
        for q in (0, 1):
            p = 2 * k + q
            for h in (0, 1):
                rows = pl.ds(8 + h, 72, stride=2)
                new[0][p, rows] = old[0][p, rows] + e[:, :128]
                new[1][p, rows] = old[1][p, rows] + e[:, 128:]

    planes(first // 2, last // 2 + 1 - first // 2, 10, body)


def zero_pads(refs, first, last):
    zero = jnp.zeros((8, 128), F32)
    for ref in refs:
        for p in range(first, last + 1):
            ref[p, pl.ds(0, 8)] = zero
            ref[p, pl.ds(152, 8)] = zero


def rim_kernel(u, cols, rows):
    lane = iota((128, 128), 1)
    acc = jnp.zeros((128, 128), F32)
    for d in range(3):
        for x in range(8):
            k = 8 * d + x
            value = u[d, x]
            acc = jnp.where(lane == k, pltpu.roll(value, k, 1) if k else value, acc)
            rows[pl.ds(k, 1)] = u[d, x, pl.ds(0, 1)]
    cols[...] = acc


def form_matrix(stiff, high, low):
    r, c = iota((192, 24), 0), iota((192, 24), 1)
    wide = jnp.where(lax.shift_right_logical(r, 3) == c, 1.0, 0.0)
    r, c = iota((24, 192), 0), iota((24, 192), 1)
    tall = jnp.where(lax.shift_right_logical(c, 3) == r, 1.0, 0.0)
    full = jnp.dot(wide, stiff, precision=HIGH, preferred_element_type=F32)
    full = jnp.dot(full, tall, precision=HIGH, preferred_element_type=F32)
    r, c = iota((192, 192), 0), iota((192, 192), 1)
    full = jnp.where(jnp.bitwise_and(r, 7) == jnp.bitwise_and(c, 7), full, 0.0)
    top = full.astype(BF16)
    high[...] = top
    low[...] = (full - top.astype(F32)).astype(BF16)


def energy_group(u0, u1, high, low, rho, f, x, y, x_in, x_out):
    cols = []
    for q in range(4):
        val = []
        for ref in (u0, u1):
            for b in (0, 1):
                for a in (0, 1):
                    for d in range(3):
                        val.append(ref[9 * d + x + a, pl.ds(y + 8 * q + b, 8)])
        cols.append(jnp.concatenate(val, axis=0))
    u = jnp.concatenate(cols, axis=1)
    top = u.astype(BF16)
    pushed = jnp.dot(high[...], top, preferred_element_type=F32)
    pushed = pushed + jnp.dot(low[...], top, preferred_element_type=F32)
    prod = pushed * (u + (u - top.astype(F32)))
    energy = prod[0:8]
    for i in range(1, 24):
        energy = energy + prod[8 * i:8 * i + 8]
    for q in range(4):
        rows = pl.ds(y + 8 * q, 8)
        r = rho[x_in, rows]
        f[x_out, rows] = -3.0 * r * r * energy[:, 128 * q:128 * q + 128]


def energy_first(pos, stiff, u, zrim, rho, u0, u1, high, low, f):
    keep_z = jnp.where(pos[2] < 3, 1.0, 0.0)
    form_matrix(stiff[...], high, low)
    lane = iota((128, 128), 1)
    col = zrim[...] * keep_z
    for d in range(3):
        for x in range(8):
            k, q = 8 * d + x, 9 * d + x
            body = u[d, x]
            u0[q] = body
            u1[q] = jnp.where(lane == 127, pltpu.roll(col, 127 - k, 1), next_lane(body))

    def group(c, j):
        x = c // 3
        y = pl.multiple_of((c - 3 * x) * 32, 32)
        energy_group(u0, u1, high, low, rho, f, x, y, x, x)

    planes(0, 12, 4, group)


def energy_second(u0, u1, high, low, rho, f):
    def group(c, j):
        x = c // 3
        y = pl.multiple_of((c - 3 * x) * 32, 32)
        energy_group(u0, u1, high, low, rho, f, x + 4, y, x + 4, x)

    planes(0, 9, 3, group)


def energy_last(pos, u0, u1, high, low, rho, xface, yrim, zrim, xrim, fa, fb, f, lead, tail, pack, w0, w1):
    gx, gy, gz = pos[0], pos[1], pos[2]
    keep_x = jnp.where(gx < 7, 1.0, 0.0)
    keep_y = jnp.where(gy < 3, 1.0, 0.0)
    keep_z = jnp.where(gz < 3, 1.0, 0.0)
    lane = iota((128, 128), 1)
    lane8 = iota((8, 128), 1)
    for d in range(3):
        for x in range(9):
            k, q = 8 * d + x, 9 * d + x
            if x < 8:
                rows = pl.ds(0, 128) if x == 7 else pl.ds(96, 32)
                w0[q, rows] = u0[q, rows]
                w1[q, rows] = u1[q, rows]
                row = yrim[pl.ds(k, 1)]
                corner = yrim[pl.ds(24, 8)]
            else:
                k = 8 * d
                body = xface[d] * keep_x
                col = xrim[pl.ds(32, 128)] * (keep_x * keep_z)
                w0[q, pl.ds(0, 128)] = body
                w1[q, pl.ds(0, 128)] = jnp.where(
                    lane == 127, pltpu.roll(col, 127 - k, 1), next_lane(body))
                row = xrim[pl.ds(k, 1)] * keep_x
                corner = xrim[pl.ds(24, 8)] * keep_x
            row = jnp.broadcast_to(row, (8, 128)) * keep_y
            corner = jnp.broadcast_to(corner[0:1], (8, 128)) * (keep_y * keep_z)
            w0[q, pl.ds(128, 8)] = row
            w1[q, pl.ds(128, 8)] = jnp.where(
                lane8 == 127, pltpu.roll(corner, 127 - k, 1), next_lane(row))
    for x in range(4):
        f[x, pl.ds(0, 96)] = fa[x, pl.ds(0, 96)]
    for x in range(3):
        f[4 + x, pl.ds(0, 96)] = fb[x, pl.ds(0, 96)]
    for x in range(7):
        energy_group(w0, w1, high, low, rho, f, x, 96, x, x)
    for q in range(4):
        energy_group(w0, w1, high, low, rho, f, 7, 32 * q, 7, 7)
    acc = jnp.zeros((128, 128), F32)
    for x in range(8):
        value = f[x]
        if x < 7:
            lead[x] = value
        if x > 0:
            tail[x - 1] = value
        low_z = pltpu.roll(value, 8 * x, 1) if x else value
        acc = jnp.where((lane >= 8 * x) & (lane < 8 * x + 8), low_z, acc)
        high_z = pltpu.roll(value, (8 * x + 72) % 128, 1)
        acc = jnp.where((lane >= 64 + 8 * x) & (lane < 72 + 8 * x), high_z, acc)
    pack[...] = acc


def spread(value, x):
    lane = iota(value.shape, 1)
    low = pltpu.roll(value, (128 - 8 * x) % 128, 1) if x else value
    high = pltpu.roll(value, (56 - 8 * x) % 128, 1)
    return jnp.where(lane < 64, low, high)


def first_kernel(pos, fl, fc, fr, hl, hc, hr, wm, ws, dm, t0, r0, tr0,
                 fm, fs, vm, vs, out, am, as_, tmp):
    zero_pads((fm, fs, vm, vs, am, as_), 1, 22)
    for b, (blk, halo) in enumerate(((fl, hl), (fc, hc), (fr, hr))):
        for x in range(1 if b == 0 else 0, 7 if b == 2 else 8):
            p = 8 * b + x
            i = x_index(pos[0] * 8 + p - 8, 64)
            parts = (
                (8, 8, halo[pl.ds(8 * x, 8)], spread(halo[pl.ds(64, 8)], x)),
                (16, 128, blk[x - 1 if b == 0 else x], spread(halo[pl.ds(144, 128)], x)),
                (144, 8, halo[pl.ds(72 + 8 * x, 8)], spread(halo[pl.ds(136, 8)], x)),
            )
            for start, size, main, side in parts:
                rows = pl.ds(start, size)
                fm[p, rows] = main
                fs[p, rows] = side
                am[p, rows] = wm[i, rows] * main
                as_[p, rows] = ws[i, rows] * side
    level0_sweep(pos, (am, as_), (vm, vs), fm, fs, wm, ws, t0, 2, 21, True)
    level0_restrict(pos, (vm, vs), fm, dm, r0, tr0, tmp, out)


def middle_kernel(pos, *refs):
    blocks, tables = refs[:8], refs[8:15]
    up0, wm, ws, dm, t0, r0, tr0, fm, fs, vm, vs, om, os_, out = refs[15:29]
    am, as_, bm, bs, f1, va, vb, f2, a2, b2, tmp = refs[29:]
    zero_pads((am, as_, bm, bs, om, os_), 2, 21)
    coarse_levels(pos, blocks, tables, f1, va, vb, f2, a2, b2, tmp)
    level0_prolong(pos, vb, up0, (vm, vs), (am, as_), 2, 21)
    level0_sweep(pos, (am, as_), (bm, bs), fm, fs, wm, ws, t0, 3, 20, True)
    level0_sweep(pos, (bm, bs), (am, as_), fm, fs, wm, ws, t0, 4, 19, True)
    level0_sweep(pos, (am, as_), (bm, bs), fm, fs, wm, ws, t0, 5, 18, True)
    level0_sweep(pos, (bm, bs), (om, os_), fm, fs, wm, ws, t0, 6, 17, True)
    level0_restrict(pos, (om, os_), fm, dm, r0, tr0, tmp, out)


def last_kernel(pos, *refs):
    blocks, tables = refs[:8], refs[8:15]
    up0, wm, ws, t0, fm, fs, vm, vs, out = refs[15:24]
    am, as_, bm, bs, f1, va, vb, f2, a2, b2, tmp = refs[24:]
    zero_pads((am, as_, bm, bs), 6, 17)
    coarse_levels(pos, blocks, tables, f1, va, vb, f2, a2, b2, tmp)
    level0_prolong(pos, vb, up0, (vm, vs), (am, as_), 6, 17)
    level0_sweep(pos, (am, as_), (bm, bs), fm, fs, wm, ws, t0, 7, 16, True)
    level0_sweep(pos, (bm, bs), (am, as_), fm, fs, wm, ws, t0, 8, 15, False)
    for x in range(8):
        out[x] = am[8 + x, pl.ds(16, 128)]


SMEM = pl.BlockSpec(memory_space=pltpu.SMEM)
VM = pl.BlockSpec(memory_space=pltpu.VMEM)


def shape(*dims):
    return jax.ShapeDtypeStruct(dims, F32)


def vmem(*dims):
    return pltpu.VMEM(dims, F32)


def call(kernel, outs, scratch, scalars, args, name, limit=12):
    specs = [SMEM] * scalars + [VM] * (len(args) - scalars)
    return pl.pallas_call(
        kernel,
        out_shape=outs,
        in_specs=specs,
        out_specs=[VM] * len(outs),
        scratch_shapes=scratch,
        compiler_params=pltpu.CompilerParams(vmem_limit_bytes=limit << 20),
        name=name,
    )(*args)


def shifted(value, axis, step):
    size = lax.axis_size(axis)
    return lax.ppermute(value, axis, [(i, (i + step) % size) for i in range(size)])


def swapped(value):
    return lax.ppermute(value, "gx", [(i, i ^ 1) for i in range(lax.axis_size("gx"))])


COARSE_SCRATCH = [
    vmem(PL1, R1, 128), vmem(PL1, R1, 128), vmem(PL1, R1, 128),
    vmem(10, R2, 128), vmem(10, R2, 128), vmem(10, R2, 128), vmem(32, 128, 128),
]
WIDE = vmem(PL0, R0, 128)


def gather_level1(own):
    lane = lax.broadcasted_iota(jnp.int32, own.shape, 2)
    right, left = shifted(own, "gz", -1), shifted(own, "gz", 1)
    own = jnp.where(lane < 64, own, jnp.where(lane < 96, right, left))
    low, high = shifted(own[:, 40:], "gy", 1), shifted(own[:, :24], "gy", -1)
    own = jnp.concatenate([low, own, high], axis=1)
    blocks = []
    for m in range(4):
        part = own if m == 0 else shifted(own, "gx", 2 * m)
        blocks += [part, swapped(part)]
    return blocks


def per_device(u, rho, stiff):
    pos = jnp.stack([lax.axis_index(a) for a in ("gx", "gy", "gz")]).astype(jnp.int32)
    t = shape(3, R0, 128)
    wm, ws, dm, w1, d1, w2, t0, t1, r0, tr0, dd, tdd, uu, up0 = call(
        setup_kernel,
        [t, t, t, shape(3, R1, 128), shape(3, R1, 128), shape(3, R2, 128),
         jax.ShapeDtypeStruct((256, 256), BF16), jax.ShapeDtypeStruct((256, 128), BF16),
         shape(128, 128), shape(256, 128), shape(256, 128), shape(256, 128),
         shape(128, 256), shape(128, 256)], [], 1, [pos], "setup")
    cols, rows = call(rim_kernel, [shape(128, 128), shape(24, 128)], [], 0, [u], "rims")
    xface = shifted(u[:, 0], "gx", -1)
    zrim = shifted(cols, "gz", -1)
    yrim = shifted(jnp.concatenate([rows, zrim[:8]], axis=0), "gy", -1)
    mat = jax.ShapeDtypeStruct((192, 192), BF16)
    u0, u1, high, low, fa = call(
        energy_first, [shape(27, 128, 128), shape(27, 128, 128), mat, mat, shape(4, 128, 128)],
        [], 1, [pos, stiff, u, zrim, rho], "energy_first")
    yrim, fa = lax.optimization_barrier((yrim, fa))
    xrim = shifted(jnp.concatenate([yrim, zrim], axis=0), "gx", -1)
    (fb,) = call(
        energy_second, [shape(3, 128, 128)], [], 0, [u0, u1, high, low, rho], "energy_second")
    f, lead, tail, pack = call(
        energy_last, [shape(8, 128, 128), shape(7, 128, 128), shape(7, 128, 128), shape(128, 128)],
        [vmem(27, 136, 128), vmem(27, 136, 128)], 1,
        [pos, u0, u1, high, low, rho, xface, yrim, zrim, xrim, fa, fb], "energy_last")

    fl, fr = shifted(tail, "gx", 1), shifted(lead, "gx", -1)
    lane = lax.broadcasted_iota(jnp.int32, pack.shape, 1)
    z = jnp.where(lane < 64, shifted(pack, "gz", -1), shifted(pack, "gz", 1))
    up = jnp.concatenate([f[:, 120:].reshape(64, 128), z[120:]], axis=0)
    down = jnp.concatenate([f[:, :8].reshape(64, 128), z[:8]], axis=0)
    h = jnp.concatenate([shifted(up, "gy", 1), shifted(down, "gy", -1), z], axis=0)
    hl, hr = shifted(h, "gx", 1), shifted(h, "gx", -1)

    wide = shape(PL0, R0, 128)
    fm, fs, vm, vs, f1 = call(
        first_kernel, [wide, wide, wide, wide, shape(4, 64, 128)],
        [WIDE, WIDE, vmem(12, 128, 128)], 1,
        [pos, fl, f, fr, hl, h, hr, wm, ws, dm, t0, r0, tr0], "first")
    tables = [w1, d1, w2, t1, dd, tdd, uu, up0]
    vm, vs, f1 = call(
        middle_kernel, [wide, wide, shape(4, 64, 128)], [WIDE] * 4 + COARSE_SCRATCH, 1,
        [pos, *gather_level1(f1), *tables, wm, ws, dm, t0, r0, tr0, fm, fs, vm, vs], "middle", 24)
    (out,) = call(
        last_kernel, [shape(8, 128, 128)], [WIDE] * 4 + COARSE_SCRATCH, 1,
        [pos, *gather_level1(f1), *tables, wm, ws, t0, fm, fs, vm, vs], "last", 24)
    return out


def solution(mesh):
    return jax.shard_map(
        per_device,
        mesh=mesh,
        in_specs=(P(None, "gx", "gy", "gz"), P("gx", "gy", "gz"), P()),
        out_specs=P("gx", "gy", "gz"),
        check_vma=False,
    )
```

time: 125 us -> 119 us (0.952)
  waiting for transfers between devices: 29.2 us -> 23.8 us
  Pallas kernels: 38 us -> 35.1 us
  starting transfers between devices: 54.4 us -> 57.1 us
    ppermute x26, waiting for transfers between devices: 27 us -> 21.5 us  [shifted(): lax.ppermute(value, axis, [(i, (i + step) % size) for i in range(size)])]
    ppermute x8, starting transfers between devices: 17.5 us -> 21.9 us  [swapped(): lax.ppermute(value, 'gx', [(i, i ^ 1) for i in range(lax.axis_size('gx'))])]
    pallas_call x7 -> x8, Pallas kernels: 38 us -> 35.1 us  [call(): pl.pallas_call(kernel, out_shape=outs, in_specs=specs, out_specs=[VM] * l...]
    ppermute x26, starting transfers between devices: 36.9 us -> 35.2 us  [shifted(): lax.ppermute(value, axis, [(i, (i + step) % size) for i in range(size)])]
  transfers between devices with their start and end apart: 34 -> 34, of which waited for: 16 -> 16; matrix products, arithmetic and copies ran while one was open for 0% -> 0% of each run, Pallas kernels for 4% -> 5%
where the time goes in v4:
time: 119 us
  starting transfers between devices  57.1 us (48%)
  Pallas kernels  35.1 us (29%)
  waiting for transfers between devices  23.8 us (20%)
  local copies, waits for them, and re-layouts  2.5 us (2%)
    ppermute x26, starting transfers between devices, shifted(): lax.ppermute(value, axis, [(i, (i + step) % size) for i in range(size)])  35.2 us
    pallas_call x8, Pallas kernels, call(): pl.pallas_call(kernel, out_shape=outs, in_specs=specs, out_specs=[VM] * l...  35.1 us
    ppermute x8, starting transfers between devices, swapped(): lax.ppermute(value, 'gx', [(i, i ^ 1) for i in range(lax.axis_size('gx'))])  21.9 us
    ppermute x26, waiting for transfers between devices, shifted(): lax.ppermute(value, axis, [(i, (i + step) % size) for i in range(size)])  21.5 us
    unnamed x10, local copies, waits for them, and re-layouts  2.46 us
  transfers between devices with their start and end apart: 34, of which 16 were waited for; matrix products, arithmetic and copies ran while one was open for 0% of the time, Pallas kernels for 5%

profile of v4, /device:TPU:1, one launch (start us, length us, event | category | flops | bytes accessed | tf_op | source)
XLA Modules:
  0.0 118.9 jit_solution(7446714574881483867)
XLA Ops:
  0.0 1.4 %copy-done = f32[3,8,128,128]{3,2,1,0:T(8,128)S(1)} copy-done((f32[3,8,128,128]{3,2,1,0:T(8,128)S(1)}, f32[3,8,128,128]{3,2,1,0:T(8,128)}, u32[]{:S(2)}) %copy-start) | copy-done | bytes 1572888
  1.9 3.4 %collective-permute-start = (f32[128,128]{1,0:T(8,128)S(1)}, f32[128,128]{1,0:T(8,128)S(1)}, u32[]{:S(2)}, u32[]{:S(2)}) collective-permute-start(f32[128,128]{1,0:T(8,128)S(1)} %get-tuple-element.40), channel_id=1, source_target_pairs={{0,3},{1,0},{2,1},{3,2},{4,7},{5,4},{6,5},{7,6},{8,11},{9,8},{10,9... | collective-permute-start | bytes 196616 | tf_op jit(solution)/shard_map/ppermute | solution.py:555
  6.6 3.8 %collective-permute-start.2 = (f32[32,128]{1,0:T(8,128)S(1)}, f32[32,128]{1,0:T(8,128)S(1)}, u32[]{:S(2)}, u32[]{:S(2)}) collective-permute-start(f32[32,128]{1,0:T(8,128)S(1)} %pad_maximum_fusion.6), channel_id=1, source_target_pairs={{0,12},{4,0},{8,4},{12,8},{1,13},{5,1},{9,5},{13,9},{2,14},{6,2},{... | collective-permute-start | bytes 49160 | tf_op jit(solution)/shard_map/ppermute | solution.py:555
  11.5 3.3 %energy_first.1 = (f32[27,128,128]{2,1,0:T(8,128)S(1)}, f32[27,128,128]{2,1,0:T(8,128)S(1)}, bf16[192,192]{1,0:T(8,128)(2,1)S(1)}, bf16[192,192]{1,0:T(8,128)(2,1)S(1)}, f32[4,128,128]{2,1,0:T(8,128)S(1)}) custom-call(s32[3]{0:T(128)S(1)} %pad_add_fusion.pos, f32[24,24]{1,0:T(8,128)S(1)} %copy-done.4, f32[3,8,128,128]{3,2,1,0:T(8,128)S(1)} %copy-done.1, ...), custom_call_target="tpu_custom_call" | custom-call | tf_op jit(solution)/shard_map/energy_first/pallas_call | solution.py:542
  14.8 2.2 %collective-permute-start.3 = (f32[160,128]{1,0:T(8,128)S(1)}, f32[160,128]{1,0:T(8,128)S(1)}, u32[]{:S(2)}, u32[]{:S(2)}) collective-permute-start(f32[160,128]{1,0:T(8,128)S(1)} %pad_maximum_fusion.3), channel_id=1, source_target_pairs={{0,112},{16,0},{32,16},{48,32},{64,48},{80,64},{96,80},{112,96},{1... | collective-permute-start | bytes 245768 | tf_op jit(solution)/shard_map/ppermute | solution.py:555
  17.0 1.5 %energy_second.1.fb = f32[3,128,128]{2,1,0:T(8,128)S(1)} custom-call(f32[27,128,128]{2,1,0:T(8,128)S(1)} %get-tuple-element.41.u0, f32[27,128,128]{2,1,0:T(8,128)S(1)} %get-tuple-element.42.u1, bf16[192,192]{1,0:T(8,128)(2,1)S(1)} %get-tuple-element.43.high, bf16[192,192]{1,0:T(8,128)(2,1)S(1)} %get-tuple-element.44.low, f32[8,128,128]{2,1,0:T(8,128)S(1)} %copy-done.2), custom_call_target="tpu_custom_call" | custom-call | tf_op jit(solution)/shard_map/energy_second/pallas_call | solution.py:542
  18.5 1.4 %collective-permute-done.3.xrim = f32[160,128]{1,0:T(8,128)S(1)} collective-permute-done((f32[160,128]{1,0:T(8,128)S(1)}, f32[160,128]{1,0:T(8,128)S(1)}, u32[]{:S(2)}, u32[]{:S(2)}) %collective-permute-start.3) | collective-permute-done | bytes 81952 | tf_op jit(solution)/shard_map/ppermute | solution.py:555
  20.0 2.1 %energy_last.1 = (f32[8,128,128]{2,1,0:T(8,128)S(1)}, f32[7,128,128]{2,1,0:T(8,128)S(1)}, f32[7,128,128]{2,1,0:T(8,128)S(1)}, f32[128,128]{1,0:T(8,128)S(1)}) custom-call(s32[3]{0:T(128)S(1)} %pad_add_fusion.pos, f32[27,128,128]{2,1,0:T(8,128)S(1)} %get-tuple-element.41.u0, f32[27,128,128]{2,1,0:T(8,128)S(1)} %get-tuple-element.42.u1, ...), custom_call_target="tpu_custom_call" | custom-call | tf_op jit(solution)/shard_map/energy_last/pallas_call | solution.py:542
  22.8 2.6 %collective-permute-start.6 = (f32[128,128]{1,0:T(8,128)S(1)}, f32[128,128]{1,0:T(8,128)S(1)}, u32[]{:S(2)}, u32[]{:S(2)}) collective-permute-start(f32[128,128]{1,0:T(8,128)S(1)} %get-tuple-element.52), channel_id=1, source_target_pairs={{0,3},{1,0},{2,1},{3,2},{4,7},{5,4},{6,5},{7,6},{8,11},{9,8},{10,9... | collective-permute-start | bytes 196616 | tf_op jit(solution)/shard_map/ppermute | solution.py:555
  25.9 2.0 %collective-permute-done.7 = f32[128,128]{1,0:T(8,128)S(1)} collective-permute-done((f32[128,128]{1,0:T(8,128)S(1)}, f32[128,128]{1,0:T(8,128)S(1)}, u32[]{:S(2)}, u32[]{:S(2)}) %collective-permute-start.7) | collective-permute-done | bytes 65568 | tf_op jit(solution)/shard_map/ppermute | solution.py:555
  28.1 1.4 %collective-permute-start.8 = (f32[72,128]{1,0:T(8,128)S(1)}, f32[72,128]{1,0:T(8,128)S(1)}, u32[]{:S(2)}, u32[]{:S(2)}) collective-permute-start(f32[72,128]{1,0:T(8,128)S(1)} %pad_maximum_fusion.4), channel_id=1, source_target_pairs={{0,4},{4,8},{8,12},{12,0},{1,5},{5,9},{9,13},{13,1},{2,6},{6,10},{... | collective-permute-start | bytes 110600 | tf_op jit(solution)/shard_map/ppermute | solution.py:555
  29.5 1.6 %collective-permute-done.9 = f32[72,128]{1,0:T(8,128)S(1)} collective-permute-done((f32[72,128]{1,0:T(8,128)S(1)}, f32[72,128]{1,0:T(8,128)S(1)}, u32[]{:S(2)}, u32[]{:S(2)}) %collective-permute-start.9) | collective-permute-done | bytes 36896 | tf_op jit(solution)/shard_map/ppermute | solution.py:555
  32.4 1.7 %collective-permute-start.11 = (f32[272,128]{1,0:T(8,128)S(1)}, f32[272,128]{1,0:T(8,128)S(1)}, u32[]{:S(2)}, u32[]{:S(2)}) collective-permute-start(f32[272,128]{1,0:T(8,128)S(1)} %pad_maximum_fusion.2.hc), channel_id=1, source_target_pairs={{0,112},{16,0},{32,16},{48,32},{64,48},{80,64},{96,80},{112,96},{1... | collective-permute-start | bytes 417800 | tf_op jit(solution)/shard_map/ppermute | solution.py:555
  35.2 1.8 %collective-permute-done.11.hr = f32[272,128]{1,0:T(8,128)S(1)} collective-permute-done((f32[272,128]{1,0:T(8,128)S(1)}, f32[272,128]{1,0:T(8,128)S(1)}, u32[]{:S(2)}, u32[]{:S(2)}) %collective-permute-start.11) | collective-permute-done | bytes 139296 | tf_op jit(solution)/shard_map/ppermute | solution.py:555
  36.9 4.2 %first.1 = (f32[24,160,128]{2,1,0:T(8,128)S(1)}, f32[24,160,128]{2,1,0:T(8,128)S(1)}, f32[24,160,128]{2,1,0:T(8,128)S(1)}, f32[24,160,128]{2,1,0:T(8,128)S(1)}, f32[4,64,128]{2,1,0:T(8,128)S(1)}) custom-call(s32[3]{0:T(128)S(1)} %pad_add_fusion.pos, f32[7,128,128]{2,1,0:T(8,128)S(1)} %collective-permute-done.4.fl, f32[8,128,128]{2,1,0:T(8,128)S(1)} %get-tuple-element.50.fc, ...), custom_call_target="tpu_custom_call" | custom-call | tf_op jit(solution)/shard_map/first/pallas_call | solution.py:542
  42.1 2.0 %collective-permute-start.12 = (f32[4,64,128]{2,1,0:T(8,128)S(1)}, f32[4,64,128]{2,1,0:T(8,128)S(1)}, u32[]{:S(2)}, u32[]{:S(2)}) collective-permute-start(f32[4,64,128]{2,1,0:T(8,128)S(1)} %get-tuple-element.59), channel_id=1, source_target_pairs={{0,3},{1,0},{2,1},{3,2},{4,7},{5,4},{6,5},{7,6},{8,11},{9,8},{10,9... | collective-permute-start | bytes 393224 | tf_op jit(solution)/shard_map/ppermute | solution.py:555
  44.1 2.3 %collective-permute-done.13 = f32[4,64,128]{2,1,0:T(8,128)S(1)} collective-permute-done((f32[4,64,128]{2,1,0:T(8,128)S(1)}, f32[4,64,128]{2,1,0:T(8,128)S(1)}, u32[]{:S(2)}, u32[]{:S(2)}) %collective-permute-start.13) | collective-permute-done | bytes 131104 | tf_op jit(solution)/shard_map/ppermute | solution.py:555
  46.5 2.7 %collective-permute-start.15 = (f32[4,24,128]{2,1,0:T(8,128)S(1)}, f32[4,24,128]{2,1,0:T(8,128)S(1)}, u32[]{:S(2)}, u32[]{:S(2)}) collective-permute-start(f32[4,24,128]{2,1,0:T(8,128)S(1)} %get-tuple-element.80), channel_id=1, source_target_pairs={{0,12},{4,0},{8,4},{12,8},{1,13},{5,1},{9,5},{13,9},{2,14},{6,2},{... | collective-permute-start | bytes 147464 | tf_op jit(solution)/shard_map/ppermute | solution.py:555
  49.1 1.5 %collective-permute-done.14 = f32[4,24,128]{2,1,0:T(8,128)S(1)} collective-permute-done((f32[4,24,128]{2,1,0:T(8,128)S(1)}, f32[4,24,128]{2,1,0:T(8,128)S(1)}, u32[]{:S(2)}, u32[]{:S(2)}) %collective-permute-start.14) | collective-permute-done | bytes 49184 | tf_op jit(solution)/shard_map/ppermute | solution.py:555
  50.6 3.7 %collective-permute-start.21 = (f32[4,112,128]{2,1,0:T(8,128)S(1)}, f32[4,112,128]{2,1,0:T(8,128)S(1)}, u32[]{:S(2)}, u32[]{:S(2)}) collective-permute-start(f32[4,112,128]{2,1,0:T(8,128)S(1)} %pad_maximum_fusion.refs_0_), channel_id=1, source_target_pairs={{0,96},{16,112},{32,0},{48,16},{64,32},{80,48},{96,64},{112,80},{1... | collective-permute-start | bytes 688136 | tf_op jit(solution)/shard_map/ppermute | solution.py:555
  55.7 3.0 %collective-permute-start.16 = (f32[4,112,128]{2,1,0:T(8,128)S(1)}, f32[4,112,128]{2,1,0:T(8,128)S(1)}, u32[]{:S(2)}, u32[]{:S(2)}) collective-permute-start(f32[4,112,128]{2,1,0:T(8,128)S(1)} %pad_maximum_fusion.refs_0_), channel_id=1, source_target_pairs={{0,16},{16,0},{32,48},{48,32},{64,80},{80,64},{96,112},{112,96},{1... | collective-permute-start | bytes 688136 | tf_op jit(solution)/shard_map/ppermute | solution.py:559
  58.7 2.4 %collective-permute-done.21.refs_6_ = f32[4,112,128]{2,1,0:T(8,128)S(1)} collective-permute-done((f32[4,112,128]{2,1,0:T(8,128)S(1)}, f32[4,112,128]{2,1,0:T(8,128)S(1)}, u32[]{:S(2)}, u32[]{:S(2)}) %collective-permute-start.21) | collective-permute-done | bytes 229408 | tf_op jit(solution)/shard_map/ppermute | solution.py:555
  61.1 4.0 %collective-permute-start.22 = (f32[4,112,128]{2,1,0:T(8,128)S(1)}, f32[4,112,128]{2,1,0:T(8,128)S(1)}, u32[]{:S(2)}, u32[]{:S(2)}) collective-permute-start(f32[4,112,128]{2,1,0:T(8,128)S(1)} %collective-permute-done.21.refs_6_), channel_id=1, source_target_pairs={{0,16},{16,0},{32,48},{48,32},{64,80},{80,64},{96,112},{112,96},{1... | collective-permute-start | bytes 688136 | tf_op jit(solution)/shard_map/ppermute | solution.py:559
  67.4 1.4 %collective-permute-start.18 = (f32[4,112,128]{2,1,0:T(8,128)S(1)}, f32[4,112,128]{2,1,0:T(8,128)S(1)}, u32[]{:S(2)}, u32[]{:S(2)}) collective-permute-start(f32[4,112,128]{2,1,0:T(8,128)S(1)} %collective-permute-done.17.refs_2_), channel_id=1, source_target_pairs={{0,16},{16,0},{32,48},{48,32},{64,80},{80,64},{96,112},{112,96},{1... | collective-permute-start | bytes 688136 | tf_op jit(solution)/shard_map/ppermute | solution.py:559
  69.9 13.9 %middle.1 = (f32[24,160,128]{2,1,0:T(8,128)S(1)}, f32[24,160,128]{2,1,0:T(8,128)S(1)}, f32[4,64,128]{2,1,0:T(8,128)S(1)}) custom-call(s32[3]{0:T(128)S(1)} %pad_add_fusion.pos, f32[4,112,128]{2,1,0:T(8,128)S(1)} %pad_maximum_fusion.refs_0_, f32[4,112,128]{2,1,0:T(8,128)S(1)} %collective-permute-done.16.refs_1_, ...), custom_call_target="tpu_custom_call" | custom-call | tf_op jit(solution)/shard_map/middle/pallas_call | solution.py:542
  85.0 1.6 %collective-permute-start.23 = (f32[4,64,128]{2,1,0:T(8,128)S(1)}, f32[4,64,128]{2,1,0:T(8,128)S(1)}, u32[]{:S(2)}, u32[]{:S(2)}) collective-permute-start(f32[4,64,128]{2,1,0:T(8,128)S(1)} %get-tuple-element.72), channel_id=1, source_target_pairs={{0,3},{1,0},{2,1},{3,2},{4,7},{5,4},{6,5},{7,6},{8,11},{9,8},{10,9... | collective-permute-start | bytes 393224 | tf_op jit(solution)/shard_map/ppermute | solution.py:555
  86.6 3.2 %collective-permute-done.24 = f32[4,64,128]{2,1,0:T(8,128)S(1)} collective-permute-done((f32[4,64,128]{2,1,0:T(8,128)S(1)}, f32[4,64,128]{2,1,0:T(8,128)S(1)}, u32[]{:S(2)}, u32[]{:S(2)}) %collective-permute-start.24) | collective-permute-done | bytes 131104 | tf_op jit(solution)/shard_map/ppermute | solution.py:555
  89.9 2.7 %collective-permute-start.26 = (f32[4,24,128]{2,1,0:T(8,128)S(1)}, f32[4,24,128]{2,1,0:T(8,128)S(1)}, u32[]{:S(2)}, u32[]{:S(2)}) collective-permute-start(f32[4,24,128]{2,1,0:T(8,128)S(1)} %get-tuple-element.78), channel_id=1, source_target_pairs={{0,12},{4,0},{8,4},{12,8},{1,13},{5,1},{9,5},{13,9},{2,14},{6,2},{... | collective-permute-start | bytes 147464 | tf_op jit(solution)/shard_map/ppermute | solution.py:555
  95.6 3.1 %collective-permute-start.27 = (f32[4,112,128]{2,1,0:T(8,128)S(1)}, f32[4,112,128]{2,1,0:T(8,128)S(1)}, u32[]{:S(2)}, u32[]{:S(2)}) collective-permute-start(f32[4,112,128]{2,1,0:T(8,128)S(1)} %pad_maximum_fusion.1.refs_0_), channel_id=1, source_target_pairs={{0,16},{16,0},{32,48},{48,32},{64,80},{80,64},{96,112},{112,96},{1... | collective-permute-start | bytes 688136 | tf_op jit(solution)/shard_map/ppermute | solution.py:559
  99.0 5.6 %collective-permute-start.33 = (f32[4,112,128]{2,1,0:T(8,128)S(1)}, f32[4,112,128]{2,1,0:T(8,128)S(1)}, u32[]{:S(2)}, u32[]{:S(2)}) collective-permute-start(f32[4,112,128]{2,1,0:T(8,128)S(1)} %collective-permute-done.32.refs_6_), channel_id=1, source_target_pairs={{0,16},{16,0},{32,48},{48,32},{64,80},{80,64},{96,112},{112,96},{1... | collective-permute-start | bytes 688136 | tf_op jit(solution)/shard_map/ppermute | solution.py:559
  104.7 2.1 %collective-permute-start.31 = (f32[4,112,128]{2,1,0:T(8,128)S(1)}, f32[4,112,128]{2,1,0:T(8,128)S(1)}, u32[]{:S(2)}, u32[]{:S(2)}) collective-permute-start(f32[4,112,128]{2,1,0:T(8,128)S(1)} %collective-permute-done.30.refs_4_), channel_id=1, source_target_pairs={{0,16},{16,0},{32,48},{48,32},{64,80},{80,64},{96,112},{112,96},{1... | collective-permute-start | bytes 688136 | tf_op jit(solution)/shard_map/ppermute | solution.py:559
  110.2 8.7 %last.1 = f32[8,128,128]{2,1,0:T(8,128)} custom-call(s32[3]{0:T(128)S(1)} %pad_add_fusion.pos, f32[4,112,128]{2,1,0:T(8,128)S(1)} %pad_maximum_fusion.1.refs_0_, f32[4,112,128]{2,1,0:T(8,128)S(1)} %collective-permute-done.27.refs_1_, f32[4,112,128]{2,1,0:T(8,128)S(1)} %collective-permute-done.28.refs_2_, f32[4,112,128]{2,1,0:T(8,128)S(1)} %collective-permute-done.29.refs_3_, ...), custom_call_target="tpu_custom_call" | custom-call | tf_op jit(solution)/shard_map/last/pallas_call | solution.py:542
  (73 shorter events, 20.4 us)
Async XLA Ops:
  1.9 4.7 %collective-permute-start = (f32[128,128]{1,0:T(8,128)S(1)}, f32[128,128]{1,0:T(8,128)S(1)}, u32[]{:S(2)}, u32[]{:S(2)}) collective-permute-start(f32[128,128]{1,0:T(8,128)S(1)} %get-tuple-element.40), channel_id=1, source_target_pairs={{0,3},{1,0},{2,1},{3,2},{4,7},{5,4},{6,5},{7,6},{8,11},{9,8},{10,9... | collective-permute-start | bytes 196616 | tf_op jit(solution)/shard_map/ppermute | solution.py:555
  5.3 14.7 %collective-permute-start.1 = (f32[3,128,128]{2,1,0:T(8,128)S(1)}, f32[3,128,128]{2,1,0:T(8,128)S(1)}, u32[]{:S(2)}, u32[]{:S(2)}) collective-permute-start(f32[3,128,128]{2,1,0:T(8,128)S(1)} %slice_bitcast_fusion), channel_id=1, source_target_pairs={{0,112},{16,0},{32,16},{48,32},{64,48},{80,64},{96,80},{112,96},{1... | collective-permute-start | bytes 589832 | tf_op jit(solution)/shard_map/ppermute | solution.py:555
  6.6 8.2 %collective-permute-start.2 = (f32[32,128]{1,0:T(8,128)S(1)}, f32[32,128]{1,0:T(8,128)S(1)}, u32[]{:S(2)}, u32[]{:S(2)}) collective-permute-start(f32[32,128]{1,0:T(8,128)S(1)} %pad_maximum_fusion.6), channel_id=1, source_target_pairs={{0,12},{4,0},{8,4},{12,8},{1,13},{5,1},{9,5},{13,9},{2,14},{6,2},{... | collective-permute-start | bytes 49160 | tf_op jit(solution)/shard_map/ppermute | solution.py:555
  14.8 5.1 %collective-permute-start.3 = (f32[160,128]{1,0:T(8,128)S(1)}, f32[160,128]{1,0:T(8,128)S(1)}, u32[]{:S(2)}, u32[]{:S(2)}) collective-permute-start(f32[160,128]{1,0:T(8,128)S(1)} %pad_maximum_fusion.3), channel_id=1, source_target_pairs={{0,112},{16,0},{32,16},{48,32},{64,48},{80,64},{96,80},{112,96},{1... | collective-permute-start | bytes 245768 | tf_op jit(solution)/shard_map/ppermute | solution.py:555
  22.0 5.9 %collective-permute-start.7 = (f32[128,128]{1,0:T(8,128)S(1)}, f32[128,128]{1,0:T(8,128)S(1)}, u32[]{:S(2)}, u32[]{:S(2)}) collective-permute-start(f32[128,128]{1,0:T(8,128)S(1)} %get-tuple-element.52), channel_id=1, source_target_pairs={{0,1},{1,2},{2,3},{3,0},{4,5},{5,6},{6,7},{7,4},{8,9},{9,10},{10,1... | collective-permute-start | bytes 196616 | tf_op jit(solution)/shard_map/ppermute | solution.py:555
  22.8 5.0 %collective-permute-start.6 = (f32[128,128]{1,0:T(8,128)S(1)}, f32[128,128]{1,0:T(8,128)S(1)}, u32[]{:S(2)}, u32[]{:S(2)}) collective-permute-start(f32[128,128]{1,0:T(8,128)S(1)} %get-tuple-element.52), channel_id=1, source_target_pairs={{0,3},{1,0},{2,1},{3,2},{4,7},{5,4},{6,5},{7,6},{8,11},{9,8},{10,9... | collective-permute-start | bytes 196616 | tf_op jit(solution)/shard_map/ppermute | solution.py:555
  25.4 11.5 %collective-permute-start.4 = (f32[7,128,128]{2,1,0:T(8,128)S(1)}, f32[7,128,128]{2,1,0:T(8,128)S(1)}, u32[]{:S(2)}, u32[]{:S(2)}) collective-permute-start(f32[7,128,128]{2,1,0:T(8,128)S(1)} %get-tuple-element.49), channel_id=1, source_target_pairs={{0,16},{16,32},{32,48},{48,64},{64,80},{80,96},{96,112},{112,0},{1... | collective-permute-start | bytes 1376264 | tf_op jit(solution)/shard_map/ppermute | solution.py:555
  25.6 11.3 %collective-permute-start.5 = (f32[7,128,128]{2,1,0:T(8,128)S(1)}, f32[7,128,128]{2,1,0:T(8,128)S(1)}, u32[]{:S(2)}, u32[]{:S(2)}) collective-permute-start(f32[7,128,128]{2,1,0:T(8,128)S(1)} %get-tuple-element.51), channel_id=1, source_target_pairs={{0,112},{16,0},{32,16},{48,32},{64,48},{80,64},{96,80},{112,96},{1... | collective-permute-start | bytes 1376264 | tf_op jit(solution)/shard_map/ppermute | solution.py:555
  27.9 3.2 %collective-permute-start.9 = (f32[72,128]{1,0:T(8,128)S(1)}, f32[72,128]{1,0:T(8,128)S(1)}, u32[]{:S(2)}, u32[]{:S(2)}) collective-permute-start(f32[72,128]{1,0:T(8,128)S(1)} %pad_maximum_fusion.5), channel_id=1, source_target_pairs={{0,12},{4,0},{8,4},{12,8},{1,13},{5,1},{9,5},{13,9},{2,14},{6,2},{... | collective-permute-start | bytes 110600 | tf_op jit(solution)/shard_map/ppermute | solution.py:555
  28.1 4.4 %collective-permute-start.8 = (f32[72,128]{1,0:T(8,128)S(1)}, f32[72,128]{1,0:T(8,128)S(1)}, u32[]{:S(2)}, u32[]{:S(2)}) collective-permute-start(f32[72,128]{1,0:T(8,128)S(1)} %pad_maximum_fusion.4), channel_id=1, source_target_pairs={{0,4},{4,8},{8,12},{12,0},{1,5},{5,9},{9,13},{13,1},{2,6},{6,10},{... | collective-permute-start | bytes 110600 | tf_op jit(solution)/shard_map/ppermute | solution.py:555
  32.4 4.5 %collective-permute-start.11 = (f32[272,128]{1,0:T(8,128)S(1)}, f32[272,128]{1,0:T(8,128)S(1)}, u32[]{:S(2)}, u32[]{:S(2)}) collective-permute-start(f32[272,128]{1,0:T(8,128)S(1)} %pad_maximum_fusion.2.hc), channel_id=1, source_target_pairs={{0,112},{16,0},{32,16},{48,32},{64,48},{80,64},{96,80},{112,96},{1... | collective-permute-start | bytes 417800 | tf_op jit(solution)/shard_map/ppermute | solution.py:555
  34.1 2.8 %collective-permute-start.10 = (f32[272,128]{1,0:T(8,128)S(1)}, f32[272,128]{1,0:T(8,128)S(1)}, u32[]{:S(2)}, u32[]{:S(2)}) collective-permute-start(f32[272,128]{1,0:T(8,128)S(1)} %pad_maximum_fusion.2.hc), channel_id=1, source_target_pairs={{0,16},{16,32},{32,48},{48,64},{64,80},{80,96},{96,112},{112,0},{1... | collective-permute-start | bytes 417800 | tf_op jit(solution)/shard_map/ppermute | solution.py:555
  41.2 5.2 %collective-permute-start.13 = (f32[4,64,128]{2,1,0:T(8,128)S(1)}, f32[4,64,128]{2,1,0:T(8,128)S(1)}, u32[]{:S(2)}, u32[]{:S(2)}) collective-permute-start(f32[4,64,128]{2,1,0:T(8,128)S(1)} %get-tuple-element.59), channel_id=1, source_target_pairs={{0,1},{1,2},{2,3},{3,0},{4,5},{5,6},{6,7},{7,4},{8,9},{9,10},{10,1... | collective-permute-start | bytes 393224 | tf_op jit(solution)/shard_map/ppermute | solution.py:555
  42.1 4.3 %collective-permute-start.12 = (f32[4,64,128]{2,1,0:T(8,128)S(1)}, f32[4,64,128]{2,1,0:T(8,128)S(1)}, u32[]{:S(2)}, u32[]{:S(2)}) collective-permute-start(f32[4,64,128]{2,1,0:T(8,128)S(1)} %get-tuple-element.59), channel_id=1, source_target_pairs={{0,3},{1,0},{2,1},{3,2},{4,7},{5,4},{6,5},{7,6},{8,11},{9,8},{10,9... | collective-permute-start | bytes 393224 | tf_op jit(solution)/shard_map/ppermute | solution.py:555
  46.4 4.2 %collective-permute-start.14 = (f32[4,24,128]{2,1,0:T(8,128)S(1)}, f32[4,24,128]{2,1,0:T(8,128)S(1)}, u32[]{:S(2)}, u32[]{:S(2)}) collective-permute-start(f32[4,24,128]{2,1,0:T(8,128)S(1)} %get-tuple-element.79), channel_id=1, source_target_pairs={{0,4},{4,8},{8,12},{12,0},{1,5},{5,9},{9,13},{13,1},{2,6},{6,10},{... | collective-permute-start | bytes 147464 | tf_op jit(solution)/shard_map/ppermute | solution.py:555
  46.5 4.1 %collective-permute-start.15 = (f32[4,24,128]{2,1,0:T(8,128)S(1)}, f32[4,24,128]{2,1,0:T(8,128)S(1)}, u32[]{:S(2)}, u32[]{:S(2)}) collective-permute-start(f32[4,24,128]{2,1,0:T(8,128)S(1)} %get-tuple-element.80), channel_id=1, source_target_pairs={{0,12},{4,0},{8,4},{12,8},{1,13},{5,1},{9,5},{13,9},{2,14},{6,2},{... | collective-permute-start | bytes 147464 | tf_op jit(solution)/shard_map/ppermute | solution.py:555
  50.6 10.5 %collective-permute-start.21 = (f32[4,112,128]{2,1,0:T(8,128)S(1)}, f32[4,112,128]{2,1,0:T(8,128)S(1)}, u32[]{:S(2)}, u32[]{:S(2)}) collective-permute-start(f32[4,112,128]{2,1,0:T(8,128)S(1)} %pad_maximum_fusion.refs_0_), channel_id=1, source_target_pairs={{0,96},{16,112},{32,0},{48,16},{64,32},{80,48},{96,64},{112,80},{1... | collective-permute-start | bytes 688136 | tf_op jit(solution)/shard_map/ppermute | solution.py:555
  54.4 10.7 %collective-permute-start.19 = (f32[4,112,128]{2,1,0:T(8,128)S(1)}, f32[4,112,128]{2,1,0:T(8,128)S(1)}, u32[]{:S(2)}, u32[]{:S(2)}) collective-permute-start(f32[4,112,128]{2,1,0:T(8,128)S(1)} %pad_maximum_fusion.refs_0_), channel_id=1, source_target_pairs={{0,64},{16,80},{32,96},{48,112},{64,0},{80,16},{96,32},{112,48},{1... | collective-permute-start | bytes 688136 | tf_op jit(solution)/shard_map/ppermute | solution.py:555
  55.0 12.5 %collective-permute-start.17 = (f32[4,112,128]{2,1,0:T(8,128)S(1)}, f32[4,112,128]{2,1,0:T(8,128)S(1)}, u32[]{:S(2)}, u32[]{:S(2)}) collective-permute-start(f32[4,112,128]{2,1,0:T(8,128)S(1)} %pad_maximum_fusion.refs_0_), channel_id=1, source_target_pairs={{0,32},{16,48},{32,64},{48,80},{64,96},{80,112},{96,0},{112,16},{1... | collective-permute-start | bytes 688136 | tf_op jit(solution)/shard_map/ppermute | solution.py:555
  55.7 13.2 %collective-permute-start.16 = (f32[4,112,128]{2,1,0:T(8,128)S(1)}, f32[4,112,128]{2,1,0:T(8,128)S(1)}, u32[]{:S(2)}, u32[]{:S(2)}) collective-permute-start(f32[4,112,128]{2,1,0:T(8,128)S(1)} %pad_maximum_fusion.refs_0_), channel_id=1, source_target_pairs={{0,16},{16,0},{32,48},{48,32},{64,80},{80,64},{96,112},{112,96},{1... | collective-permute-start | bytes 688136 | tf_op jit(solution)/shard_map/ppermute | solution.py:559
  61.1 7.7 %collective-permute-start.22 = (f32[4,112,128]{2,1,0:T(8,128)S(1)}, f32[4,112,128]{2,1,0:T(8,128)S(1)}, u32[]{:S(2)}, u32[]{:S(2)}) collective-permute-start(f32[4,112,128]{2,1,0:T(8,128)S(1)} %collective-permute-done.21.refs_6_), channel_id=1, source_target_pairs={{0,16},{16,0},{32,48},{48,32},{64,80},{80,64},{96,112},{112,96},{1... | collective-permute-start | bytes 688136 | tf_op jit(solution)/shard_map/ppermute | solution.py:559
  65.1 3.7 %collective-permute-start.20 = (f32[4,112,128]{2,1,0:T(8,128)S(1)}, f32[4,112,128]{2,1,0:T(8,128)S(1)}, u32[]{:S(2)}, u32[]{:S(2)}) collective-permute-start(f32[4,112,128]{2,1,0:T(8,128)S(1)} %collective-permute-done.19.refs_4_), channel_id=1, source_target_pairs={{0,16},{16,0},{32,48},{48,32},{64,80},{80,64},{96,112},{112,96},{1... | collective-permute-start | bytes 688136 | tf_op jit(solution)/shard_map/ppermute | solution.py:559
  83.8 6.0 %collective-permute-start.24 = (f32[4,64,128]{2,1,0:T(8,128)S(1)}, f32[4,64,128]{2,1,0:T(8,128)S(1)}, u32[]{:S(2)}, u32[]{:S(2)}) collective-permute-start(f32[4,64,128]{2,1,0:T(8,128)S(1)} %get-tuple-element.72), channel_id=1, source_target_pairs={{0,1},{1,2},{2,3},{3,0},{4,5},{5,6},{6,7},{7,4},{8,9},{9,10},{10,1... | collective-permute-start | bytes 393224 | tf_op jit(solution)/shard_map/ppermute | solution.py:555
  85.0 4.9 %collective-permute-start.23 = (f32[4,64,128]{2,1,0:T(8,128)S(1)}, f32[4,64,128]{2,1,0:T(8,128)S(1)}, u32[]{:S(2)}, u32[]{:S(2)}) collective-permute-start(f32[4,64,128]{2,1,0:T(8,128)S(1)} %get-tuple-element.72), channel_id=1, source_target_pairs={{0,3},{1,0},{2,1},{3,2},{4,7},{5,4},{6,5},{7,6},{8,11},{9,8},{10,9... | collective-permute-start | bytes 393224 | tf_op jit(solution)/shard_map/ppermute | solution.py:555
  89.9 4.2 %collective-permute-start.25 = (f32[4,24,128]{2,1,0:T(8,128)S(1)}, f32[4,24,128]{2,1,0:T(8,128)S(1)}, u32[]{:S(2)}, u32[]{:S(2)}) collective-permute-start(f32[4,24,128]{2,1,0:T(8,128)S(1)} %get-tuple-element.77), channel_id=1, source_target_pairs={{0,4},{4,8},{8,12},{12,0},{1,5},{5,9},{9,13},{13,1},{2,6},{6,10},{... | collective-permute-start | bytes 147464 | tf_op jit(solution)/shard_map/ppermute | solution.py:555
  89.9 4.1 %collective-permute-start.26 = (f32[4,24,128]{2,1,0:T(8,128)S(1)}, f32[4,24,128]{2,1,0:T(8,128)S(1)}, u32[]{:S(2)}, u32[]{:S(2)}) collective-permute-start(f32[4,24,128]{2,1,0:T(8,128)S(1)} %get-tuple-element.78), channel_id=1, source_target_pairs={{0,12},{4,0},{8,4},{12,8},{1,13},{5,1},{9,5},{13,9},{2,14},{6,2},{... | collective-permute-start | bytes 147464 | tf_op jit(solution)/shard_map/ppermute | solution.py:555
  94.1 4.9 %collective-permute-start.32 = (f32[4,112,128]{2,1,0:T(8,128)S(1)}, f32[4,112,128]{2,1,0:T(8,128)S(1)}, u32[]{:S(2)}, u32[]{:S(2)}) collective-permute-start(f32[4,112,128]{2,1,0:T(8,128)S(1)} %pad_maximum_fusion.1.refs_0_), channel_id=1, source_target_pairs={{0,96},{16,112},{32,0},{48,16},{64,32},{80,48},{96,64},{112,80},{1... | collective-permute-start | bytes 688136 | tf_op jit(solution)/shard_map/ppermute | solution.py:555
  94.6 10.0 %collective-permute-start.30 = (f32[4,112,128]{2,1,0:T(8,128)S(1)}, f32[4,112,128]{2,1,0:T(8,128)S(1)}, u32[]{:S(2)}, u32[]{:S(2)}) collective-permute-start(f32[4,112,128]{2,1,0:T(8,128)S(1)} %pad_maximum_fusion.1.refs_0_), channel_id=1, source_target_pairs={{0,64},{16,80},{32,96},{48,112},{64,0},{80,16},{96,32},{112,48},{1... | collective-permute-start | bytes 688136 | tf_op jit(solution)/shard_map/ppermute | solution.py:555
  95.1 12.7 %collective-permute-start.28 = (f32[4,112,128]{2,1,0:T(8,128)S(1)}, f32[4,112,128]{2,1,0:T(8,128)S(1)}, u32[]{:S(2)}, u32[]{:S(2)}) collective-permute-start(f32[4,112,128]{2,1,0:T(8,128)S(1)} %pad_maximum_fusion.1.refs_0_), channel_id=1, source_target_pairs={{0,32},{16,48},{32,64},{48,80},{64,96},{80,112},{96,0},{112,16},{1... | collective-permute-start | bytes 688136 | tf_op jit(solution)/shard_map/ppermute | solution.py:555
  95.6 13.4 %collective-permute-start.27 = (f32[4,112,128]{2,1,0:T(8,128)S(1)}, f32[4,112,128]{2,1,0:T(8,128)S(1)}, u32[]{:S(2)}, u32[]{:S(2)}) collective-permute-start(f32[4,112,128]{2,1,0:T(8,128)S(1)} %pad_maximum_fusion.1.refs_0_), channel_id=1, source_target_pairs={{0,16},{16,0},{32,48},{48,32},{64,80},{80,64},{96,112},{112,96},{1... | collective-permute-start | bytes 688136 | tf_op jit(solution)/shard_map/ppermute | solution.py:559
  99.0 10.0 %collective-permute-start.33 = (f32[4,112,128]{2,1,0:T(8,128)S(1)}, f32[4,112,128]{2,1,0:T(8,128)S(1)}, u32[]{:S(2)}, u32[]{:S(2)}) collective-permute-start(f32[4,112,128]{2,1,0:T(8,128)S(1)} %collective-permute-done.32.refs_6_), channel_id=1, source_target_pairs={{0,16},{16,0},{32,48},{48,32},{64,80},{80,64},{96,112},{112,96},{1... | collective-permute-start | bytes 688136 | tf_op jit(solution)/shard_map/ppermute | solution.py:559
  104.7 4.4 %collective-permute-start.31 = (f32[4,112,128]{2,1,0:T(8,128)S(1)}, f32[4,112,128]{2,1,0:T(8,128)S(1)}, u32[]{:S(2)}, u32[]{:S(2)}) collective-permute-start(f32[4,112,128]{2,1,0:T(8,128)S(1)} %collective-permute-done.30.refs_4_), channel_id=1, source_target_pairs={{0,16},{16,0},{32,48},{48,32},{64,80},{80,64},{96,112},{112,96},{1... | collective-permute-start | bytes 688136 | tf_op jit(solution)/shard_map/ppermute | solution.py:559
  (7 other events, 28.4 us)

commit v5 on v4

--- a/solution.py
+++ b/solution.py
@@ -96,7 +96,7 @@
     return jnp.where(index < 128, index, side_place(side)), ok
 
 
-def setup_kernel(pos, wm, ws, dm, w1, d1, w2, t0, t1, r0, tr0, dd, tdd, uu, up0):
+def setup_kernel(pos, wm, ws, dm, w1, d1, w2, t0, t1, r0, tr0, dd, tdd, uu, up0, zz):
     gy, gz = pos[1], pos[2]
     lane = iota((R0, 128), 1)
     make_tables(wm, dm, R0, 16, lane, lane >= 0, gy * 128, gz * 128, 512, S0)
@@ -122,36 +122,48 @@
     step = jnp.bitwise_and(src - dst, 127)
     t1[...] = hits((step == 1) | (step == 127)).astype(BF16)
 
-    col = jnp.where(dst < 64, dst, dst - 64)
-    good = (dst < 86) | (dst >= 106)
+    col, good = dst, dst < 64
     z, ok = level0_place(src)
     total = jnp.zeros((256, 128), F32)
     for dz in (-1, 1):
         total = total + hits(ok & good & (z + dz >= 0) & (z + dz < 128) & (half(z + dz) == col))
-    tr0[...] = 0.125 * total
-    r0[...] = 0.125 * hits(good & (half(src) == col) & (src < 128))[0:128]
+    tr0[...] = (0.125 * total).astype(BF16)
+    r0[...] = (0.125 * hits(good & (half(src) == col) & (src < 128)))[0:128].astype(BF16)
+
+    src5, dst5 = iota((512, 256), 0), iota((512, 256), 1)
+    slot = jnp.bitwise_and(dst5, 31)
+    same = lax.shift_right_logical(src5, 7) == lax.shift_right_logical(jnp.bitwise_and(dst5, 127), 5)
+    edge = src5 == jnp.bitwise_and(src5, 384) + slot + jnp.where(dst5 < 128, 0, 32)
+    used = (slot >= jnp.where(dst5 < 128, 0, 10)) & (slot < jnp.where(dst5 < 128, 22, 32))
+    zz[...] = hits(same & edge & used).astype(BF16)
 
     z = level1_place(jnp.bitwise_and(src, 127))
     part = jnp.bitwise_and(dst, 63)
     good = (part < 54) & ((src < 128) == (dst < 64))
-    dd[...] = 0.125 * hits(good & level1_ok(z) & (half(z) == part - 11))
+    dd[...] = (0.125 * hits(good & level1_ok(z) & (half(z) == part - 11))).astype(BF16)
     total = jnp.zeros((256, 128), F32)
     for dz in (-1, 1):
         total = total + hits(good & level1_ok(z + dz) & (half(z + dz) == part - 11))
-    tdd[...] = 0.125 * total
+    tdd[...] = (0.125 * total).astype(BF16)
 
     src, dst = iota((128, 256), 0), iota((128, 256), 1)
     z = level1_place(jnp.bitwise_and(dst, 127))
     part = jnp.bitwise_and(src, 63)
     good = (part < 54) & ((dst < 128) == (src < 64))
-    uu[...] = hits(good & level1_ok(z) & (half(z) == part - 11))
+    uu[...] = hits(good & level1_ok(z) & (half(z) == part - 11)).astype(BF16)
     z, ok = level0_place(dst)
-    up0[...] = hits(ok & (half(z) == level1_place(src)))
+    up0[...] = hits(ok & (half(z) == level1_place(src))).astype(BF16)
 
 
 def two_parts(value):
     top = value.astype(BF16)
     return top, (value - top.astype(F32)).astype(BF16)
+
+
+def select(value, matrix):
+    top, rest = two_parts(value)
+    out = jnp.dot(top, matrix, preferred_element_type=F32)
+    return out + jnp.dot(rest, matrix, preferred_element_type=F32)
 
 
 def level0_sweep(pos, src, dst, fm, fs, wm, ws, t0, first, last, side):
@@ -162,9 +174,7 @@
         i = x_index(pos[0] * 8 + p - 8, 64)
         m, s = src[0][p, rows], src[1][p, rows]
         if j % 2:
-            a, b = two_parts(jnp.concatenate([m, s], axis=1))
-            near = jnp.dot(a, t0[...], preferred_element_type=F32)
-            near = near + jnp.dot(b, t0[...], preferred_element_type=F32)
+            near = select(jnp.concatenate([m, s], axis=1), t0[...])
             near_m, near_s = near[:, :128], near[:, 128:]
         else:
             mr, sr, ml, sl = next_lane(m), next_lane(s), prev_lane(m), prev_lane(s)
@@ -179,10 +189,10 @@
     planes(first, last + 1 - first, 10, body)
 
 
-def level0_restrict(pos, src, fm, dm, r0, tr0, tmp, out):
+def level0_restrict(pos, src, fm, dm, r0, tr0, zz, tmp, out, z_low, z_high):
     rows, up, dn = pl.ds(16, 128), pl.ds(15, 128), pl.ds(17, 128)
-
-    def body(k, j):
+    values = []
+    for k in range(4):
         sums = [None, None, None]
         for q in (0, 1):
             p = 8 + 2 * k + q
@@ -195,12 +205,12 @@
         for n in range(3):
             tmp[3 * k + n] = sums[n]
             pairs.append(tmp[3 * k + n, pl.ds(0, 64, stride=2)] + tmp[3 * k + n, pl.ds(1, 64, stride=2)])
-        value = jnp.dot(pairs[0], r0[...], precision=HIGH, preferred_element_type=F32)
-        near = jnp.concatenate(pairs[1:], axis=1)
-        near = jnp.dot(near, tr0[...], precision=HIGH, preferred_element_type=F32)
-        out[k] = value + S0 * near
-
-    planes(0, 4, 4, body)
+        near = select(jnp.concatenate(pairs[1:], axis=1), tr0[...])
+        values.append(select(pairs[0], r0[...]) + S0 * near)
+        out[k] = values[k]
+    edges = select(jnp.concatenate(values, axis=1), zz[...])
+    z_low[...] = edges[:, :128]
+    z_high[...] = edges[:, 128:]
 
 
 def level1_sweep(src, dst, f, w, t1, first, count):
@@ -286,11 +296,8 @@
 
     def restrict(p, j):
         low, high = residual(p - 1), residual(p + 7)
-        value = jnp.dot(jnp.concatenate([low[0], high[0]], axis=1), dd[...],
-                        precision=HIGH, preferred_element_type=F32)
-        near = jnp.dot(jnp.concatenate([low[1], high[1]], axis=1), tdd[...],
-                       precision=HIGH, preferred_element_type=F32)
-        value = value + S1 * near
+        value = select(jnp.concatenate([low[0], high[0]], axis=1), dd[...])
+        value = value + S1 * select(jnp.concatenate([low[1], high[1]], axis=1), tdd[...])
         f2[p, pl.ds(8, 56)] = value
         i = jnp.where(p == 1, 0, jnp.where(p == 8, 2, 1))
         a2[p, pl.ds(8, 56)] = w2[i, pl.ds(8, 56)] * value
@@ -303,7 +310,7 @@
         src2, dst2 = dst2, src2
 
     def prolong(p, j):
-        both = jnp.dot(src2[p, pl.ds(8, 56)], uu[...], precision=HIGH, preferred_element_type=F32)
+        both = select(src2[p, pl.ds(8, 56)], uu[...])
         for n, k in ((0, p - 1), (1, p + 7)):
             e = both[:, 128 * n:128 * n + 128]
             for q in (0, 1):
@@ -319,7 +326,7 @@
 def level0_prolong(pos, e1, up0, old, new, first, last):
     def body(k, j):
         e = e1[4 * pos[0] + 1 + k, pl.ds(28, 72)]
-        e = jnp.dot(e, up0[...], precision=HIGH, preferred_element_type=F32)
+        e = select(e, up0[...])
         for q in (0, 1):
             p = 2 * k + q
             for h in (0, 1):
@@ -338,13 +345,14 @@
             ref[p, pl.ds(152, 8)] = zero
 
 
-def rim_kernel(u, cols, rows):
+def rim_kernel(u, u0, cols, rows):
     lane = iota((128, 128), 1)
     acc = jnp.zeros((128, 128), F32)
     for d in range(3):
         for x in range(8):
             k = 8 * d + x
             value = u[d, x]
+            u0[9 * d + x] = value
             acc = jnp.where(lane == k, pltpu.roll(value, k, 1) if k else value, acc)
             rows[pl.ds(k, 1)] = u[d, x, pl.ds(0, 1)]
     cols[...] = acc
@@ -388,7 +396,7 @@
         f[x_out, rows] = -3.0 * r * r * energy[:, 128 * q:128 * q + 128]
 
 
-def energy_first(pos, stiff, u, zrim, rho, u0, u1, high, low, f):
+def energy_first(pos, stiff, u0, zrim, rho, u1, high, low, f):
     keep_z = jnp.where(pos[2] < 3, 1.0, 0.0)
     form_matrix(stiff[...], high, low)
     lane = iota((128, 128), 1)
@@ -396,9 +404,7 @@
     for d in range(3):
         for x in range(8):
             k, q = 8 * d + x, 9 * d + x
-            body = u[d, x]
-            u0[q] = body
-            u1[q] = jnp.where(lane == 127, pltpu.roll(col, 127 - k, 1), next_lane(body))
+            u1[q] = jnp.where(lane == 127, pltpu.roll(col, 127 - k, 1), next_lane(u0[q]))
 
     def group(c, j):
         x = c // 3
@@ -462,22 +468,17 @@
             lead[x] = value
         if x > 0:
             tail[x - 1] = value
-        low_z = pltpu.roll(value, 8 * x, 1) if x else value
-        acc = jnp.where((lane >= 8 * x) & (lane < 8 * x + 8), low_z, acc)
-        high_z = pltpu.roll(value, (8 * x + 72) % 128, 1)
-        acc = jnp.where((lane >= 64 + 8 * x) & (lane < 72 + 8 * x), high_z, acc)
+        here = (lane >= 16 * x) & (lane < 16 * x + 16)
+        acc = jnp.where(here, pltpu.roll(value, (16 * x + 8) % 128, 1), acc)
     pack[...] = acc
 
 
 def spread(value, x):
-    lane = iota(value.shape, 1)
-    low = pltpu.roll(value, (128 - 8 * x) % 128, 1) if x else value
-    high = pltpu.roll(value, (56 - 8 * x) % 128, 1)
-    return jnp.where(lane < 64, low, high)
-
-
-def first_kernel(pos, fl, fc, fr, hl, hc, hr, wm, ws, dm, t0, r0, tr0,
-                 fm, fs, vm, vs, out, am, as_, tmp):
+    return pltpu.roll(value, (248 - 16 * x) % 128, 1)
+
+
+def first_kernel(pos, fl, fc, fr, hl, hc, hr, wm, ws, dm, t0, r0, tr0, zz,
+                 fm, fs, vm, vs, out, z_low, z_high, am, as_, tmp):
     zero_pads((fm, fs, vm, vs, am, as_), 1, 22)
     for b, (blk, halo) in enumerate(((fl, hl), (fc, hc), (fr, hr))):
         for x in range(1 if b == 0 else 0, 7 if b == 2 else 8):
@@ -495,13 +496,13 @@
                 am[p, rows] = wm[i, rows] * main
                 as_[p, rows] = ws[i, rows] * side
     level0_sweep(pos, (am, as_), (vm, vs), fm, fs, wm, ws, t0, 2, 21, True)
-    level0_restrict(pos, (vm, vs), fm, dm, r0, tr0, tmp, out)
+    level0_restrict(pos, (vm, vs), fm, dm, r0, tr0, zz, tmp, out, z_low, z_high)
 
 
 def middle_kernel(pos, *refs):
     blocks, tables = refs[:8], refs[8:15]
-    up0, wm, ws, dm, t0, r0, tr0, fm, fs, vm, vs, om, os_, out = refs[15:29]
-    am, as_, bm, bs, f1, va, vb, f2, a2, b2, tmp = refs[29:]
+    up0, wm, ws, dm, t0, r0, tr0, zz, fm, fs, vm, vs = refs[15:27]
+    om, os_, out, z_low, z_high, am, as_, bm, bs, f1, va, vb, f2, a2, b2, tmp = refs[27:]
     zero_pads((am, as_, bm, bs, om, os_), 2, 21)
     coarse_levels(pos, blocks, tables, f1, va, vb, f2, a2, b2, tmp)
     level0_prolong(pos, vb, up0, (vm, vs), (am, as_), 2, 21)
@@ -509,7 +510,7 @@
     level0_sweep(pos, (bm, bs), (am, as_), fm, fs, wm, ws, t0, 4, 19, True)
     level0_sweep(pos, (am, as_), (bm, bs), fm, fs, wm, ws, t0, 5, 18, True)
     level0_sweep(pos, (bm, bs), (om, os_), fm, fs, wm, ws, t0, 6, 17, True)
-    level0_restrict(pos, (om, os_), fm, dm, r0, tr0, tmp, out)
+    level0_restrict(pos, (om, os_), fm, dm, r0, tr0, zz, tmp, out, z_low, z_high)
 
 
 def last_kernel(pos, *refs):
@@ -533,6 +534,10 @@
     return jax.ShapeDtypeStruct(dims, F32)
 
 
+def half_shape(*dims):
+    return jax.ShapeDtypeStruct(dims, BF16)
+
+
 def vmem(*dims):
     return pltpu.VMEM(dims, F32)
 
@@ -566,10 +571,14 @@
 WIDE = vmem(PL0, R0, 128)
 
 
-def gather_level1(own):
-    lane = lax.broadcasted_iota(jnp.int32, own.shape, 2)
-    right, left = shifted(own, "gz", -1), shifted(own, "gz", 1)
-    own = jnp.where(lane < 64, own, jnp.where(lane < 96, right, left))
+def gather_level1(own, z_low, z_high):
+    lane = lax.broadcasted_iota(jnp.int32, (64, 128), 1)
+    right, left = shifted(z_low, "gz", -1), shifted(z_high, "gz", 1)
+    wide = []
+    for k in range(4):
+        rim = jnp.where(lane < 96, jnp.roll(right, 64 - 32 * k, 1), jnp.roll(left, 96 - 32 * k, 1))
+        wide.append(jnp.where(lane < 64, own[k], rim))
+    own = jnp.stack(wide)
     low, high = shifted(own[:, 40:], "gy", 1), shifted(own[:, :24], "gy", -1)
     own = jnp.concatenate([low, own, high], axis=1)
     blocks = []
@@ -582,20 +591,22 @@
 def per_device(u, rho, stiff):
     pos = jnp.stack([lax.axis_index(a) for a in ("gx", "gy", "gz")]).astype(jnp.int32)
     t = shape(3, R0, 128)
-    wm, ws, dm, w1, d1, w2, t0, t1, r0, tr0, dd, tdd, uu, up0 = call(
+    wm, ws, dm, w1, d1, w2, t0, t1, r0, tr0, dd, tdd, uu, up0, zz = call(
         setup_kernel,
         [t, t, t, shape(3, R1, 128), shape(3, R1, 128), shape(3, R2, 128),
-         jax.ShapeDtypeStruct((256, 256), BF16), jax.ShapeDtypeStruct((256, 128), BF16),
-         shape(128, 128), shape(256, 128), shape(256, 128), shape(256, 128),
-         shape(128, 256), shape(128, 256)], [], 1, [pos], "setup")
-    cols, rows = call(rim_kernel, [shape(128, 128), shape(24, 128)], [], 0, [u], "rims")
+         half_shape(256, 256), half_shape(256, 128), half_shape(128, 128), half_shape(256, 128),
+         half_shape(256, 128), half_shape(256, 128), half_shape(128, 256), half_shape(128, 256),
+         half_shape(512, 256)],
+        [], 1, [pos], "setup")
+    u0, cols, rows = call(
+        rim_kernel, [shape(27, 128, 128), shape(128, 128), shape(24, 128)], [], 0, [u], "rims")
     xface = shifted(u[:, 0], "gx", -1)
     zrim = shifted(cols, "gz", -1)
     yrim = shifted(jnp.concatenate([rows, zrim[:8]], axis=0), "gy", -1)
-    mat = jax.ShapeDtypeStruct((192, 192), BF16)
-    u0, u1, high, low, fa = call(
-        energy_first, [shape(27, 128, 128), shape(27, 128, 128), mat, mat, shape(4, 128, 128)],
-        [], 1, [pos, stiff, u, zrim, rho], "energy_first")
+    mat = half_shape(192, 192)
+    u1, high, low, fa = call(
+        energy_first, [shape(27, 128, 128), mat, mat, shape(4, 128, 128)],
+        [], 1, [pos, stiff, u0, zrim, rho], "energy_first")
     yrim, fa = lax.optimization_barrier((yrim, fa))
     xrim = shifted(jnp.concatenate([yrim, zrim], axis=0), "gx", -1)
     (fb,) = call(
@@ -607,24 +618,26 @@
 
     fl, fr = shifted(tail, "gx", 1), shifted(lead, "gx", -1)
     lane = lax.broadcasted_iota(jnp.int32, pack.shape, 1)
-    z = jnp.where(lane < 64, shifted(pack, "gz", -1), shifted(pack, "gz", 1))
+    from_left = jnp.bitwise_and(lane, 15) < 8
+    z = jnp.where(from_left, shifted(pack, "gz", 1), shifted(pack, "gz", -1))
     up = jnp.concatenate([f[:, 120:].reshape(64, 128), z[120:]], axis=0)
     down = jnp.concatenate([f[:, :8].reshape(64, 128), z[:8]], axis=0)
     h = jnp.concatenate([shifted(up, "gy", 1), shifted(down, "gy", -1), z], axis=0)
     hl, hr = shifted(h, "gx", 1), shifted(h, "gx", -1)
 
     wide = shape(PL0, R0, 128)
-    fm, fs, vm, vs, f1 = call(
-        first_kernel, [wide, wide, wide, wide, shape(4, 64, 128)],
+    level1 = [shape(4, 64, 128), shape(64, 128), shape(64, 128)]
+    fm, fs, vm, vs, *f1 = call(
+        first_kernel, [wide, wide, wide, wide, *level1],
         [WIDE, WIDE, vmem(12, 128, 128)], 1,
-        [pos, fl, f, fr, hl, h, hr, wm, ws, dm, t0, r0, tr0], "first")
+        [pos, fl, f, fr, hl, h, hr, wm, ws, dm, t0, r0, tr0, zz], "first")
     tables = [w1, d1, w2, t1, dd, tdd, uu, up0]
-    vm, vs, f1 = call(
-        middle_kernel, [wide, wide, shape(4, 64, 128)], [WIDE] * 4 + COARSE_SCRATCH, 1,
-        [pos, *gather_level1(f1), *tables, wm, ws, dm, t0, r0, tr0, fm, fs, vm, vs], "middle", 24)
+    vm, vs, *f1 = call(
+        middle_kernel, [wide, wide, *level1], [WIDE] * 4 + COARSE_SCRATCH, 1,
+        [pos, *gather_level1(*f1), *tables, wm, ws, dm, t0, r0, tr0, zz, fm, fs, vm, vs], "middle", 24)
     (out,) = call(
         last_kernel, [shape(8, 128, 128)], [WIDE] * 4 + COARSE_SCRATCH, 1,
-        [pos, *gather_level1(f1), *tables, wm, ws, t0, fm, fs, vm, vs], "last", 24)
+        [pos, *gather_level1(*f1), *tables, wm, ws, t0, fm, fs, vm, vs], "last", 24)
     return out
 
 

time: 119 us -> 114 us (0.958)
  waiting for transfers between devices: 23.8 us -> 20 us
  Pallas kernels: 35.1 us -> 31.4 us
  starting transfers between devices: 57.1 us -> 59.7 us
    ppermute x26, waiting for transfers between devices: 21.5 us -> 17.7 us  [shifted(): lax.ppermute(value, axis, [(i, (i + step) % size) for i in range(size)])]
    pallas_call x8, Pallas kernels: 35.1 us -> 31.4 us  [call(): pl.pallas_call(kernel, out_shape=outs, in_specs=specs, out_specs=[VM] * l...]
    ppermute x8, starting transfers between devices: 21.9 us -> 24.9 us  [swapped(): lax.ppermute(value, 'gx', [(i, i ^ 1) for i in range(lax.axis_size('gx'))])]
    unnamed x10 -> x6, local copies, waits for them, and re-layouts: 2.46 us -> 1.47 us
  transfers between devices with their start and end apart: 34 -> 34, of which waited for: 16 -> 14; matrix products, arithmetic and copies ran while one was open for 0% -> 1% of each run, Pallas kernels for 5% -> 5%
where the time goes in v5:
time: 114 us
  starting transfers between devices  59.7 us (52%)
  Pallas kernels  31.4 us (28%)
  waiting for transfers between devices  20 us (18%)
  local copies, waits for them, and re-layouts  2.41 us (2%)
    ppermute x26, starting transfers between devices, shifted(): lax.ppermute(value, axis, [(i, (i + step) % size) for i in range(size)])  34.8 us
    pallas_call x8, Pallas kernels, call(): pl.pallas_call(kernel, out_shape=outs, in_specs=specs, out_specs=[VM] * l...  31.4 us
    ppermute x8, starting transfers between devices, swapped(): lax.ppermute(value, 'gx', [(i, i ^ 1) for i in range(lax.axis_size('gx'))])  24.9 us
    ppermute x26, waiting for transfers between devices, shifted(): lax.ppermute(value, axis, [(i, (i + step) % size) for i in range(size)])  17.7 us
  transfers between devices with their start and end apart: 34, of which 14 were waited for; matrix products, arithmetic and copies ran while one was open for 1% of the time, Pallas kernels for 5%

profile of v5, /device:TPU:1, one launch (start us, length us, event | category | flops | bytes accessed | tf_op | source)
XLA Modules:
  0.0 114.3 jit_solution(6424740726310788360)
XLA Ops:
  0.0 1.5 %copy-done.1 = f32[3,8,128,128]{3,2,1,0:T(8,128)S(1)} copy-done((f32[3,8,128,128]{3,2,1,0:T(8,128)S(1)}, f32[3,8,128,128]{3,2,1,0:T(8,128)}, u32[]{:S(2)}) %copy-start.1) | copy-done | bytes 1572888
  1.9 3.4 %collective-permute-start = (f32[128,128]{1,0:T(8,128)S(1)}, f32[128,128]{1,0:T(8,128)S(1)}, u32[]{:S(2)}, u32[]{:S(2)}) collective-permute-start(f32[128,128]{1,0:T(8,128)S(1)} %get-tuple-element.46), channel_id=1, source_target_pairs={{0,3},{1,0},{2,1},{3,2},{4,7},{5,4},{6,5},{7,6},{8,11},{9,8},{10,9... | collective-permute-start | bytes 196616 | tf_op jit(solution)/shard_map/ppermute | solution.py:560
  6.7 3.8 %collective-permute-start.2 = (f32[32,128]{1,0:T(8,128)S(1)}, f32[32,128]{1,0:T(8,128)S(1)}, u32[]{:S(2)}, u32[]{:S(2)}) collective-permute-start(f32[32,128]{1,0:T(8,128)S(1)} %pad_maximum_fusion.14), channel_id=1, source_target_pairs={{0,12},{4,0},{8,4},{12,8},{1,13},{5,1},{9,5},{13,9},{2,14},{6,2},{... | collective-permute-start | bytes 49160 | tf_op jit(solution)/shard_map/ppermute | solution.py:560
  10.5 3.2 %energy_first.1 = (f32[27,128,128]{2,1,0:T(8,128)S(1)}, bf16[192,192]{1,0:T(8,128)(2,1)S(1)}, bf16[192,192]{1,0:T(8,128)(2,1)S(1)}, f32[4,128,128]{2,1,0:T(8,128)S(1)}) custom-call(s32[3]{0:T(128)S(1)} %pad_add_fusion.pos, f32[24,24]{1,0:T(8,128)S(1)} %copy-done.2, f32[27,128,128]{2,1,0:T(8,128)S(1)} %get-tuple-element.45.u0, ...), custom_call_target="tpu_custom_call" | custom-call | tf_op jit(solution)/shard_map/energy_first/pallas_call | solution.py:547
  13.8 2.2 %collective-permute-start.3 = (f32[160,128]{1,0:T(8,128)S(1)}, f32[160,128]{1,0:T(8,128)S(1)}, u32[]{:S(2)}, u32[]{:S(2)}) collective-permute-start(f32[160,128]{1,0:T(8,128)S(1)} %pad_maximum_fusion.3), channel_id=1, source_target_pairs={{0,112},{16,0},{32,16},{48,32},{64,48},{80,64},{96,80},{112,96},{1... | collective-permute-start | bytes 245768 | tf_op jit(solution)/shard_map/ppermute | solution.py:560
  16.0 1.5 %energy_second.1.fb = f32[3,128,128]{2,1,0:T(8,128)S(1)} custom-call(f32[27,128,128]{2,1,0:T(8,128)S(1)} %get-tuple-element.45.u0, f32[27,128,128]{2,1,0:T(8,128)S(1)} %get-tuple-element.47.u1, bf16[192,192]{1,0:T(8,128)(2,1)S(1)} %get-tuple-element.48.high, bf16[192,192]{1,0:T(8,128)(2,1)S(1)} %get-tuple-element.49.low, f32[8,128,128]{2,1,0:T(8,128)S(1)} %copy-done), custom_call_target="tpu_custom_call" | custom-call | tf_op jit(solution)/shard_map/energy_second/pallas_call | solution.py:547
  18.9 2.0 %energy_last.1 = (f32[8,128,128]{2,1,0:T(8,128)S(1)}, f32[7,128,128]{2,1,0:T(8,128)S(1)}, f32[7,128,128]{2,1,0:T(8,128)S(1)}, f32[128,128]{1,0:T(8,128)S(1)}) custom-call(s32[3]{0:T(128)S(1)} %pad_add_fusion.pos, f32[27,128,128]{2,1,0:T(8,128)S(1)} %get-tuple-element.45.u0, f32[27,128,128]{2,1,0:T(8,128)S(1)} %get-tuple-element.47.u1, ...), custom_call_target="tpu_custom_call" | custom-call | tf_op jit(solution)/shard_map/energy_last/pallas_call | solution.py:547
  20.9 3.3 %collective-permute-start.7 = (f32[128,128]{1,0:T(8,128)S(1)}, f32[128,128]{1,0:T(8,128)S(1)}, u32[]{:S(2)}, u32[]{:S(2)}) collective-permute-start(f32[128,128]{1,0:T(8,128)S(1)} %get-tuple-element.57), channel_id=1, source_target_pairs={{0,3},{1,0},{2,1},{3,2},{4,7},{5,4},{6,5},{7,6},{8,11},{9,8},{10,9... | collective-permute-start | bytes 196616 | tf_op jit(solution)/shard_map/ppermute | solution.py:560
  25.9 3.2 %collective-permute-done.6 = f32[128,128]{1,0:T(8,128)S(1)} collective-permute-done((f32[128,128]{1,0:T(8,128)S(1)}, f32[128,128]{1,0:T(8,128)S(1)}, u32[]{:S(2)}, u32[]{:S(2)}) %collective-permute-start.6) | collective-permute-done | bytes 65568 | tf_op jit(solution)/shard_map/ppermute | solution.py:560
  30.7 1.6 %collective-permute-done.9 = f32[72,128]{1,0:T(8,128)S(1)} collective-permute-done((f32[72,128]{1,0:T(8,128)S(1)}, f32[72,128]{1,0:T(8,128)S(1)}, u32[]{:S(2)}, u32[]{:S(2)}) %collective-permute-start.9) | collective-permute-done | bytes 36896 | tf_op jit(solution)/shard_map/ppermute | solution.py:560
  32.3 2.3 %collective-permute-done.8 = f32[72,128]{1,0:T(8,128)S(1)} collective-permute-done((f32[72,128]{1,0:T(8,128)S(1)}, f32[72,128]{1,0:T(8,128)S(1)}, u32[]{:S(2)}, u32[]{:S(2)}) %collective-permute-start.8) | collective-permute-done | bytes 36896 | tf_op jit(solution)/shard_map/ppermute | solution.py:560
  34.7 1.6 %collective-permute-start.11 = (f32[272,128]{1,0:T(8,128)S(1)}, f32[272,128]{1,0:T(8,128)S(1)}, u32[]{:S(2)}, u32[]{:S(2)}) collective-permute-start(f32[272,128]{1,0:T(8,128)S(1)} %pad_maximum_fusion.2.hc), channel_id=1, source_target_pairs={{0,112},{16,0},{32,16},{48,32},{64,48},{80,64},{96,80},{112,96},{1... | collective-permute-start | bytes 417800 | tf_op jit(solution)/shard_map/ppermute | solution.py:560
  38.2 1.9 %collective-permute-done.11.hr = f32[272,128]{1,0:T(8,128)S(1)} collective-permute-done((f32[272,128]{1,0:T(8,128)S(1)}, f32[272,128]{1,0:T(8,128)S(1)}, u32[]{:S(2)}, u32[]{:S(2)}) %collective-permute-start.11) | collective-permute-done | bytes 139296 | tf_op jit(solution)/shard_map/ppermute | solution.py:560
  40.1 3.7 %first.1 = (f32[24,160,128]{2,1,0:T(8,128)S(1)}, f32[24,160,128]{2,1,0:T(8,128)S(1)}, f32[24,160,128]{2,1,0:T(8,128)S(1)}, f32[24,160,128]{2,1,0:T(8,128)S(1)}, ...) custom-call(s32[3]{0:T(128)S(1)} %pad_add_fusion.pos, ...), custom_call_target="tpu_custom_call" | custom-call | tf_op jit(solution)/shard_map/first/pallas_call | solution.py:547
  44.0 2.7 %collective-permute-start.12 = (f32[64,128]{1,0:T(8,128)S(1)}, f32[64,128]{1,0:T(8,128)S(1)}, u32[]{:S(2)}, u32[]{:S(2)}) collective-permute-start(f32[64,128]{1,0:T(8,128)S(1)} %get-tuple-element.66), channel_id=1, source_target_pairs={{0,3},{1,0},{2,1},{3,2},{4,7},{5,4},{6,5},{7,6},{8,11},{9,8},{10,9... | collective-permute-start | bytes 98312 | tf_op jit(solution)/shard_map/ppermute | solution.py:560
  48.7 2.7 %collective-permute-start.15 = (f32[4,24,128]{2,1,0:T(8,128)S(1)}, f32[4,24,128]{2,1,0:T(8,128)S(1)}, u32[]{:S(2)}, u32[]{:S(2)}) collective-permute-start(f32[4,24,128]{2,1,0:T(8,128)S(1)} %get-tuple-element.98), channel_id=1, source_target_pairs={{0,12},{4,0},{8,4},{12,8},{1,13},{5,1},{9,5},{13,9},{2,14},{6,2},{... | collective-permute-start | bytes 147464 | tf_op jit(solution)/shard_map/ppermute | solution.py:560
  51.4 1.5 %collective-permute-done.14 = f32[4,24,128]{2,1,0:T(8,128)S(1)} collective-permute-done((f32[4,24,128]{2,1,0:T(8,128)S(1)}, f32[4,24,128]{2,1,0:T(8,128)S(1)}, u32[]{:S(2)}, u32[]{:S(2)}) %collective-permute-start.14) | collective-permute-done | bytes 49184 | tf_op jit(solution)/shard_map/ppermute | solution.py:560
  52.9 1.5 %collective-permute-start.21 = (f32[4,112,128]{2,1,0:T(8,128)S(1)}, f32[4,112,128]{2,1,0:T(8,128)S(1)}, u32[]{:S(2)}, u32[]{:S(2)}) collective-permute-start(f32[4,112,128]{2,1,0:T(8,128)S(1)} %pad_maximum_fusion.refs_0_), channel_id=1, source_target_pairs={{0,96},{16,112},{32,0},{48,16},{64,32},{80,48},{96,64},{112,80},{1... | collective-permute-start | bytes 688136 | tf_op jit(solution)/shard_map/ppermute | solution.py:560
  54.3 1.6 %collective-permute-start.19 = (f32[4,112,128]{2,1,0:T(8,128)S(1)}, f32[4,112,128]{2,1,0:T(8,128)S(1)}, u32[]{:S(2)}, u32[]{:S(2)}) collective-permute-start(f32[4,112,128]{2,1,0:T(8,128)S(1)} %pad_maximum_fusion.refs_0_), channel_id=1, source_target_pairs={{0,64},{16,80},{32,96},{48,112},{64,0},{80,16},{96,32},{112,48},{1... | collective-permute-start | bytes 688136 | tf_op jit(solution)/shard_map/ppermute | solution.py:560
  56.1 4.2 %collective-permute-start.16 = (f32[4,112,128]{2,1,0:T(8,128)S(1)}, f32[4,112,128]{2,1,0:T(8,128)S(1)}, u32[]{:S(2)}, u32[]{:S(2)}) collective-permute-start(f32[4,112,128]{2,1,0:T(8,128)S(1)} %pad_maximum_fusion.refs_0_), channel_id=1, source_target_pairs={{0,16},{16,0},{32,48},{48,32},{64,80},{80,64},{96,112},{112,96},{1... | collective-permute-start | bytes 688136 | tf_op jit(solution)/shard_map/ppermute | solution.py:564
  60.3 3.1 %collective-permute-start.22 = (f32[4,112,128]{2,1,0:T(8,128)S(1)}, f32[4,112,128]{2,1,0:T(8,128)S(1)}, u32[]{:S(2)}, u32[]{:S(2)}) collective-permute-start(f32[4,112,128]{2,1,0:T(8,128)S(1)} %collective-permute-done.21.refs_6_), channel_id=1, source_target_pairs={{0,16},{16,0},{32,48},{48,32},{64,80},{80,64},{96,112},{112,96},{1... | collective-permute-start | bytes 688136 | tf_op jit(solution)/shard_map/ppermute | solution.py:564
  63.4 3.0 %collective-permute-start.20 = (f32[4,112,128]{2,1,0:T(8,128)S(1)}, f32[4,112,128]{2,1,0:T(8,128)S(1)}, u32[]{:S(2)}, u32[]{:S(2)}) collective-permute-start(f32[4,112,128]{2,1,0:T(8,128)S(1)} %collective-permute-done.19.refs_4_), channel_id=1, source_target_pairs={{0,16},{16,0},{32,48},{48,32},{64,80},{80,64},{96,112},{112,96},{1... | collective-permute-start | bytes 688136 | tf_op jit(solution)/shard_map/ppermute | solution.py:564
  66.4 2.3 %collective-permute-start.18 = (f32[4,112,128]{2,1,0:T(8,128)S(1)}, f32[4,112,128]{2,1,0:T(8,128)S(1)}, u32[]{:S(2)}, u32[]{:S(2)}) collective-permute-start(f32[4,112,128]{2,1,0:T(8,128)S(1)} %collective-permute-done.17.refs_2_), channel_id=1, source_target_pairs={{0,16},{16,0},{32,48},{48,32},{64,80},{80,64},{96,112},{112,96},{1... | collective-permute-start | bytes 688136 | tf_op jit(solution)/shard_map/ppermute | solution.py:564
  69.9 12.1 %middle.1 = (f32[24,160,128]{2,1,0:T(8,128)S(1)}, f32[24,160,128]{2,1,0:T(8,128)S(1)}, f32[4,64,128]{2,1,0:T(8,128)S(1)}, f32[64,128]{1,0:T(8,128)S(1)}, f32[64,128]{1,0:T(8,128)S(1)}) custom-call(s32[3]{0:T(128)S(1)} %pad_add_fusion.pos, f32[4,112,128]{2,1,0:T(8,128)S(1)} %pad_maximum_fusion.refs_0_, f32[4,112,128]{2,1,0:T(8,128)S(1)} %collective-permute-done.16.refs_1_, ...), custom_call_target="tpu_custom_call" | custom-call | tf_op jit(solution)/shard_map/middle/pallas_call | solution.py:547
  82.1 2.7 %collective-permute-start.23 = (f32[64,128]{1,0:T(8,128)S(1)}, f32[64,128]{1,0:T(8,128)S(1)}, u32[]{:S(2)}, u32[]{:S(2)}) collective-permute-start(f32[64,128]{1,0:T(8,128)S(1)} %get-tuple-element.81), channel_id=1, source_target_pairs={{0,3},{1,0},{2,1},{3,2},{4,7},{5,4},{6,5},{7,6},{8,11},{9,8},{10,9... | collective-permute-start | bytes 98312 | tf_op jit(solution)/shard_map/ppermute | solution.py:560
  86.8 2.7 %collective-permute-start.26 = (f32[4,24,128]{2,1,0:T(8,128)S(1)}, f32[4,24,128]{2,1,0:T(8,128)S(1)}, u32[]{:S(2)}, u32[]{:S(2)}) collective-permute-start(f32[4,24,128]{2,1,0:T(8,128)S(1)} %get-tuple-element.96), channel_id=1, source_target_pairs={{0,12},{4,0},{8,4},{12,8},{1,13},{5,1},{9,5},{13,9},{2,14},{6,2},{... | collective-permute-start | bytes 147464 | tf_op jit(solution)/shard_map/ppermute | solution.py:560
  91.5 1.5 %collective-permute-start.30 = (f32[4,112,128]{2,1,0:T(8,128)S(1)}, f32[4,112,128]{2,1,0:T(8,128)S(1)}, u32[]{:S(2)}, u32[]{:S(2)}) collective-permute-start(f32[4,112,128]{2,1,0:T(8,128)S(1)} %pad_maximum_fusion.1.refs_0_), channel_id=1, source_target_pairs={{0,64},{16,80},{32,96},{48,112},{64,0},{80,16},{96,32},{112,48},{1... | collective-permute-start | bytes 688136 | tf_op jit(solution)/shard_map/ppermute | solution.py:560
  93.4 3.5 %collective-permute-start.27 = (f32[4,112,128]{2,1,0:T(8,128)S(1)}, f32[4,112,128]{2,1,0:T(8,128)S(1)}, u32[]{:S(2)}, u32[]{:S(2)}) collective-permute-start(f32[4,112,128]{2,1,0:T(8,128)S(1)} %pad_maximum_fusion.1.refs_0_), channel_id=1, source_target_pairs={{0,16},{16,0},{32,48},{48,32},{64,80},{80,64},{96,112},{112,96},{1... | collective-permute-start | bytes 688136 | tf_op jit(solution)/shard_map/ppermute | solution.py:564
  96.9 4.6 %collective-permute-start.33 = (f32[4,112,128]{2,1,0:T(8,128)S(1)}, f32[4,112,128]{2,1,0:T(8,128)S(1)}, u32[]{:S(2)}, u32[]{:S(2)}) collective-permute-start(f32[4,112,128]{2,1,0:T(8,128)S(1)} %collective-permute-done.32.refs_6_), channel_id=1, source_target_pairs={{0,16},{16,0},{32,48},{48,32},{64,80},{80,64},{96,112},{112,96},{1... | collective-permute-start | bytes 688136 | tf_op jit(solution)/shard_map/ppermute | solution.py:564
  101.5 2.0 %collective-permute-start.31 = (f32[4,112,128]{2,1,0:T(8,128)S(1)}, f32[4,112,128]{2,1,0:T(8,128)S(1)}, u32[]{:S(2)}, u32[]{:S(2)}) collective-permute-start(f32[4,112,128]{2,1,0:T(8,128)S(1)} %collective-permute-done.30.refs_4_), channel_id=1, source_target_pairs={{0,16},{16,0},{32,48},{48,32},{64,80},{80,64},{96,112},{112,96},{1... | collective-permute-start | bytes 688136 | tf_op jit(solution)/shard_map/ppermute | solution.py:564
  103.7 2.2 %collective-permute-start.29 = (f32[4,112,128]{2,1,0:T(8,128)S(1)}, f32[4,112,128]{2,1,0:T(8,128)S(1)}, u32[]{:S(2)}, u32[]{:S(2)}) collective-permute-start(f32[4,112,128]{2,1,0:T(8,128)S(1)} %collective-permute-done.28.refs_2_), channel_id=1, source_target_pairs={{0,16},{16,0},{32,48},{48,32},{64,80},{80,64},{96,112},{112,96},{1... | collective-permute-start | bytes 688136 | tf_op jit(solution)/shard_map/ppermute | solution.py:564
  107.0 7.3 %last.1 = f32[8,128,128]{2,1,0:T(8,128)} custom-call(s32[3]{0:T(128)S(1)} %pad_add_fusion.pos, f32[4,112,128]{2,1,0:T(8,128)S(1)} %pad_maximum_fusion.1.refs_0_, f32[4,112,128]{2,1,0:T(8,128)S(1)} %collective-permute-done.27.refs_1_, f32[4,112,128]{2,1,0:T(8,128)S(1)} %collective-permute-done.28.refs_2_, f32[4,112,128]{2,1,0:T(8,128)S(1)} %collective-permute-done.29.refs_3_, ...), custom_call_target="tpu_custom_call" | custom-call | tf_op jit(solution)/shard_map/last/pallas_call | solution.py:547
  (83 shorter events, 17.8 us)
Async XLA Ops:
  1.9 4.7 %collective-permute-start = (f32[128,128]{1,0:T(8,128)S(1)}, f32[128,128]{1,0:T(8,128)S(1)}, u32[]{:S(2)}, u32[]{:S(2)}) collective-permute-start(f32[128,128]{1,0:T(8,128)S(1)} %get-tuple-element.46), channel_id=1, source_target_pairs={{0,3},{1,0},{2,1},{3,2},{4,7},{5,4},{6,5},{7,6},{8,11},{9,8},{10,9... | collective-permute-start | bytes 196616 | tf_op jit(solution)/shard_map/ppermute | solution.py:560
  5.3 13.6 %collective-permute-start.1 = (f32[3,128,128]{2,1,0:T(8,128)S(1)}, f32[3,128,128]{2,1,0:T(8,128)S(1)}, u32[]{:S(2)}, u32[]{:S(2)}) collective-permute-start(f32[3,128,128]{2,1,0:T(8,128)S(1)} %slice_bitcast_fusion), channel_id=1, source_target_pairs={{0,112},{16,0},{32,16},{48,32},{64,48},{80,64},{96,80},{112,96},{1... | collective-permute-start | bytes 589832 | tf_op jit(solution)/shard_map/ppermute | solution.py:560
  6.7 7.1 %collective-permute-start.2 = (f32[32,128]{1,0:T(8,128)S(1)}, f32[32,128]{1,0:T(8,128)S(1)}, u32[]{:S(2)}, u32[]{:S(2)}) collective-permute-start(f32[32,128]{1,0:T(8,128)S(1)} %pad_maximum_fusion.14), channel_id=1, source_target_pairs={{0,12},{4,0},{8,4},{12,8},{1,13},{5,1},{9,5},{13,9},{2,14},{6,2},{... | collective-permute-start | bytes 49160 | tf_op jit(solution)/shard_map/ppermute | solution.py:560
  13.8 5.1 %collective-permute-start.3 = (f32[160,128]{1,0:T(8,128)S(1)}, f32[160,128]{1,0:T(8,128)S(1)}, u32[]{:S(2)}, u32[]{:S(2)}) collective-permute-start(f32[160,128]{1,0:T(8,128)S(1)} %pad_maximum_fusion.3), channel_id=1, source_target_pairs={{0,112},{16,0},{32,16},{48,32},{64,48},{80,64},{96,80},{112,96},{1... | collective-permute-start | bytes 245768 | tf_op jit(solution)/shard_map/ppermute | solution.py:560
  20.9 5.0 %collective-permute-start.7 = (f32[128,128]{1,0:T(8,128)S(1)}, f32[128,128]{1,0:T(8,128)S(1)}, u32[]{:S(2)}, u32[]{:S(2)}) collective-permute-start(f32[128,128]{1,0:T(8,128)S(1)} %get-tuple-element.57), channel_id=1, source_target_pairs={{0,3},{1,0},{2,1},{3,2},{4,7},{5,4},{6,5},{7,6},{8,11},{9,8},{10,9... | collective-permute-start | bytes 196616 | tf_op jit(solution)/shard_map/ppermute | solution.py:560
  24.2 4.9 %collective-permute-start.6 = (f32[128,128]{1,0:T(8,128)S(1)}, f32[128,128]{1,0:T(8,128)S(1)}, u32[]{:S(2)}, u32[]{:S(2)}) collective-permute-start(f32[128,128]{1,0:T(8,128)S(1)} %get-tuple-element.57), channel_id=1, source_target_pairs={{0,1},{1,2},{2,3},{3,0},{4,5},{5,6},{6,7},{7,4},{8,9},{9,10},{10,1... | collective-permute-start | bytes 196616 | tf_op jit(solution)/shard_map/ppermute | solution.py:560
  24.2 15.9 %collective-permute-start.4 = (f32[7,128,128]{2,1,0:T(8,128)S(1)}, f32[7,128,128]{2,1,0:T(8,128)S(1)}, u32[]{:S(2)}, u32[]{:S(2)}) collective-permute-start(f32[7,128,128]{2,1,0:T(8,128)S(1)} %get-tuple-element.54), channel_id=1, source_target_pairs={{0,16},{16,32},{32,48},{48,64},{64,80},{80,96},{96,112},{112,0},{1... | collective-permute-start | bytes 1376264 | tf_op jit(solution)/shard_map/ppermute | solution.py:560
  24.5 15.7 %collective-permute-start.5 = (f32[7,128,128]{2,1,0:T(8,128)S(1)}, f32[7,128,128]{2,1,0:T(8,128)S(1)}, u32[]{:S(2)}, u32[]{:S(2)}) collective-permute-start(f32[7,128,128]{2,1,0:T(8,128)S(1)} %get-tuple-element.56), channel_id=1, source_target_pairs={{0,112},{16,0},{32,16},{48,32},{64,48},{80,64},{96,80},{112,96},{1... | collective-permute-start | bytes 1376264 | tf_op jit(solution)/shard_map/ppermute | solution.py:560
  30.6 4.0 %collective-permute-start.8 = (f32[72,128]{1,0:T(8,128)S(1)}, f32[72,128]{1,0:T(8,128)S(1)}, u32[]{:S(2)}, u32[]{:S(2)}) collective-permute-start(f32[72,128]{1,0:T(8,128)S(1)} %pad_maximum_fusion.12), channel_id=1, source_target_pairs={{0,4},{4,8},{8,12},{12,0},{1,5},{5,9},{9,13},{13,1},{2,6},{6,10},{... | collective-permute-start | bytes 110600 | tf_op jit(solution)/shard_map/ppermute | solution.py:560
  34.7 5.5 %collective-permute-start.11 = (f32[272,128]{1,0:T(8,128)S(1)}, f32[272,128]{1,0:T(8,128)S(1)}, u32[]{:S(2)}, u32[]{:S(2)}) collective-permute-start(f32[272,128]{1,0:T(8,128)S(1)} %pad_maximum_fusion.2.hc), channel_id=1, source_target_pairs={{0,112},{16,0},{32,16},{48,32},{64,48},{80,64},{96,80},{112,96},{1... | collective-permute-start | bytes 417800 | tf_op jit(solution)/shard_map/ppermute | solution.py:560
  36.2 3.9 %collective-permute-start.10 = (f32[272,128]{1,0:T(8,128)S(1)}, f32[272,128]{1,0:T(8,128)S(1)}, u32[]{:S(2)}, u32[]{:S(2)}) collective-permute-start(f32[272,128]{1,0:T(8,128)S(1)} %pad_maximum_fusion.2.hc), channel_id=1, source_target_pairs={{0,16},{16,32},{32,48},{48,64},{64,80},{80,96},{96,112},{112,0},{1... | collective-permute-start | bytes 417800 | tf_op jit(solution)/shard_map/ppermute | solution.py:560
  43.9 4.0 %collective-permute-start.13 = (f32[64,128]{1,0:T(8,128)S(1)}, f32[64,128]{1,0:T(8,128)S(1)}, u32[]{:S(2)}, u32[]{:S(2)}) collective-permute-start(f32[64,128]{1,0:T(8,128)S(1)} %get-tuple-element.67), channel_id=1, source_target_pairs={{0,1},{1,2},{2,3},{3,0},{4,5},{5,6},{6,7},{7,4},{8,9},{9,10},{10,1... | collective-permute-start | bytes 98312 | tf_op jit(solution)/shard_map/ppermute | solution.py:560
  44.0 4.2 %collective-permute-start.12 = (f32[64,128]{1,0:T(8,128)S(1)}, f32[64,128]{1,0:T(8,128)S(1)}, u32[]{:S(2)}, u32[]{:S(2)}) collective-permute-start(f32[64,128]{1,0:T(8,128)S(1)} %get-tuple-element.66), channel_id=1, source_target_pairs={{0,3},{1,0},{2,1},{3,2},{4,7},{5,4},{6,5},{7,6},{8,11},{9,8},{10,9... | collective-permute-start | bytes 98312 | tf_op jit(solution)/shard_map/ppermute | solution.py:560
  48.6 4.2 %collective-permute-start.14 = (f32[4,24,128]{2,1,0:T(8,128)S(1)}, f32[4,24,128]{2,1,0:T(8,128)S(1)}, u32[]{:S(2)}, u32[]{:S(2)}) collective-permute-start(f32[4,24,128]{2,1,0:T(8,128)S(1)} %get-tuple-element.97), channel_id=1, source_target_pairs={{0,4},{4,8},{8,12},{12,0},{1,5},{5,9},{9,13},{13,1},{2,6},{6,10},{... | collective-permute-start | bytes 147464 | tf_op jit(solution)/shard_map/ppermute | solution.py:560
  48.7 4.1 %collective-permute-start.15 = (f32[4,24,128]{2,1,0:T(8,128)S(1)}, f32[4,24,128]{2,1,0:T(8,128)S(1)}, u32[]{:S(2)}, u32[]{:S(2)}) collective-permute-start(f32[4,24,128]{2,1,0:T(8,128)S(1)} %get-tuple-element.98), channel_id=1, source_target_pairs={{0,12},{4,0},{8,4},{12,8},{1,13},{5,1},{9,5},{13,9},{2,14},{6,2},{... | collective-permute-start | bytes 147464 | tf_op jit(solution)/shard_map/ppermute | solution.py:560
  52.9 7.5 %collective-permute-start.21 = (f32[4,112,128]{2,1,0:T(8,128)S(1)}, f32[4,112,128]{2,1,0:T(8,128)S(1)}, u32[]{:S(2)}, u32[]{:S(2)}) collective-permute-start(f32[4,112,128]{2,1,0:T(8,128)S(1)} %pad_maximum_fusion.refs_0_), channel_id=1, source_target_pairs={{0,96},{16,112},{32,0},{48,16},{64,32},{80,48},{96,64},{112,80},{1... | collective-permute-start | bytes 688136 | tf_op jit(solution)/shard_map/ppermute | solution.py:560
  54.3 9.1 %collective-permute-start.19 = (f32[4,112,128]{2,1,0:T(8,128)S(1)}, f32[4,112,128]{2,1,0:T(8,128)S(1)}, u32[]{:S(2)}, u32[]{:S(2)}) collective-permute-start(f32[4,112,128]{2,1,0:T(8,128)S(1)} %pad_maximum_fusion.refs_0_), channel_id=1, source_target_pairs={{0,64},{16,80},{32,96},{48,112},{64,0},{80,16},{96,32},{112,48},{1... | collective-permute-start | bytes 688136 | tf_op jit(solution)/shard_map/ppermute | solution.py:560
  55.9 10.5 %collective-permute-start.17 = (f32[4,112,128]{2,1,0:T(8,128)S(1)}, f32[4,112,128]{2,1,0:T(8,128)S(1)}, u32[]{:S(2)}, u32[]{:S(2)}) collective-permute-start(f32[4,112,128]{2,1,0:T(8,128)S(1)} %pad_maximum_fusion.refs_0_), channel_id=1, source_target_pairs={{0,32},{16,48},{32,64},{48,80},{64,96},{80,112},{96,0},{112,16},{1... | collective-permute-start | bytes 688136 | tf_op jit(solution)/shard_map/ppermute | solution.py:560
  56.1 12.7 %collective-permute-start.16 = (f32[4,112,128]{2,1,0:T(8,128)S(1)}, f32[4,112,128]{2,1,0:T(8,128)S(1)}, u32[]{:S(2)}, u32[]{:S(2)}) collective-permute-start(f32[4,112,128]{2,1,0:T(8,128)S(1)} %pad_maximum_fusion.refs_0_), channel_id=1, source_target_pairs={{0,16},{16,0},{32,48},{48,32},{64,80},{80,64},{96,112},{112,96},{1... | collective-permute-start | bytes 688136 | tf_op jit(solution)/shard_map/ppermute | solution.py:564
  60.3 8.5 %collective-permute-start.22 = (f32[4,112,128]{2,1,0:T(8,128)S(1)}, f32[4,112,128]{2,1,0:T(8,128)S(1)}, u32[]{:S(2)}, u32[]{:S(2)}) collective-permute-start(f32[4,112,128]{2,1,0:T(8,128)S(1)} %collective-permute-done.21.refs_6_), channel_id=1, source_target_pairs={{0,16},{16,0},{32,48},{48,32},{64,80},{80,64},{96,112},{112,96},{1... | collective-permute-start | bytes 688136 | tf_op jit(solution)/shard_map/ppermute | solution.py:564
  63.4 5.3 %collective-permute-start.20 = (f32[4,112,128]{2,1,0:T(8,128)S(1)}, f32[4,112,128]{2,1,0:T(8,128)S(1)}, u32[]{:S(2)}, u32[]{:S(2)}) collective-permute-start(f32[4,112,128]{2,1,0:T(8,128)S(1)} %collective-permute-done.19.refs_4_), channel_id=1, source_target_pairs={{0,16},{16,0},{32,48},{48,32},{64,80},{80,64},{96,112},{112,96},{1... | collective-permute-start | bytes 688136 | tf_op jit(solution)/shard_map/ppermute | solution.py:564
  66.4 3.5 %collective-permute-start.18 = (f32[4,112,128]{2,1,0:T(8,128)S(1)}, f32[4,112,128]{2,1,0:T(8,128)S(1)}, u32[]{:S(2)}, u32[]{:S(2)}) collective-permute-start(f32[4,112,128]{2,1,0:T(8,128)S(1)} %collective-permute-done.17.refs_2_), channel_id=1, source_target_pairs={{0,16},{16,0},{32,48},{48,32},{64,80},{80,64},{96,112},{112,96},{1... | collective-permute-start | bytes 688136 | tf_op jit(solution)/shard_map/ppermute | solution.py:564
  82.0 4.0 %collective-permute-start.24 = (f32[64,128]{1,0:T(8,128)S(1)}, f32[64,128]{1,0:T(8,128)S(1)}, u32[]{:S(2)}, u32[]{:S(2)}) collective-permute-start(f32[64,128]{1,0:T(8,128)S(1)} %get-tuple-element.82), channel_id=1, source_target_pairs={{0,1},{1,2},{2,3},{3,0},{4,5},{5,6},{6,7},{7,4},{8,9},{9,10},{10,1... | collective-permute-start | bytes 98312 | tf_op jit(solution)/shard_map/ppermute | solution.py:560
  82.1 4.2 %collective-permute-start.23 = (f32[64,128]{1,0:T(8,128)S(1)}, f32[64,128]{1,0:T(8,128)S(1)}, u32[]{:S(2)}, u32[]{:S(2)}) collective-permute-start(f32[64,128]{1,0:T(8,128)S(1)} %get-tuple-element.81), channel_id=1, source_target_pairs={{0,3},{1,0},{2,1},{3,2},{4,7},{5,4},{6,5},{7,6},{8,11},{9,8},{10,9... | collective-permute-start | bytes 98312 | tf_op jit(solution)/shard_map/ppermute | solution.py:560
  86.7 4.2 %collective-permute-start.25 = (f32[4,24,128]{2,1,0:T(8,128)S(1)}, f32[4,24,128]{2,1,0:T(8,128)S(1)}, u32[]{:S(2)}, u32[]{:S(2)}) collective-permute-start(f32[4,24,128]{2,1,0:T(8,128)S(1)} %get-tuple-element.95), channel_id=1, source_target_pairs={{0,4},{4,8},{8,12},{12,0},{1,5},{5,9},{9,13},{13,1},{2,6},{6,10},{... | collective-permute-start | bytes 147464 | tf_op jit(solution)/shard_map/ppermute | solution.py:560
  86.8 4.1 %collective-permute-start.26 = (f32[4,24,128]{2,1,0:T(8,128)S(1)}, f32[4,24,128]{2,1,0:T(8,128)S(1)}, u32[]{:S(2)}, u32[]{:S(2)}) collective-permute-start(f32[4,24,128]{2,1,0:T(8,128)S(1)} %get-tuple-element.96), channel_id=1, source_target_pairs={{0,12},{4,0},{8,4},{12,8},{1,13},{5,1},{9,5},{13,9},{2,14},{6,2},{... | collective-permute-start | bytes 147464 | tf_op jit(solution)/shard_map/ppermute | solution.py:560
  91.0 5.9 %collective-permute-start.32 = (f32[4,112,128]{2,1,0:T(8,128)S(1)}, f32[4,112,128]{2,1,0:T(8,128)S(1)}, u32[]{:S(2)}, u32[]{:S(2)}) collective-permute-start(f32[4,112,128]{2,1,0:T(8,128)S(1)} %pad_maximum_fusion.1.refs_0_), channel_id=1, source_target_pairs={{0,96},{16,112},{32,0},{48,16},{64,32},{80,48},{96,64},{112,80},{1... | collective-permute-start | bytes 688136 | tf_op jit(solution)/shard_map/ppermute | solution.py:560
  91.5 10.1 %collective-permute-start.30 = (f32[4,112,128]{2,1,0:T(8,128)S(1)}, f32[4,112,128]{2,1,0:T(8,128)S(1)}, u32[]{:S(2)}, u32[]{:S(2)}) collective-permute-start(f32[4,112,128]{2,1,0:T(8,128)S(1)} %pad_maximum_fusion.1.refs_0_), channel_id=1, source_target_pairs={{0,64},{16,80},{32,96},{48,112},{64,0},{80,16},{96,32},{112,48},{1... | collective-permute-start | bytes 688136 | tf_op jit(solution)/shard_map/ppermute | solution.py:560
  93.0 10.7 %collective-permute-start.28 = (f32[4,112,128]{2,1,0:T(8,128)S(1)}, f32[4,112,128]{2,1,0:T(8,128)S(1)}, u32[]{:S(2)}, u32[]{:S(2)}) collective-permute-start(f32[4,112,128]{2,1,0:T(8,128)S(1)} %pad_maximum_fusion.1.refs_0_), channel_id=1, source_target_pairs={{0,32},{16,48},{32,64},{48,80},{64,96},{80,112},{96,0},{112,16},{1... | collective-permute-start | bytes 688136 | tf_op jit(solution)/shard_map/ppermute | solution.py:560
  93.4 12.5 %collective-permute-start.27 = (f32[4,112,128]{2,1,0:T(8,128)S(1)}, f32[4,112,128]{2,1,0:T(8,128)S(1)}, u32[]{:S(2)}, u32[]{:S(2)}) collective-permute-start(f32[4,112,128]{2,1,0:T(8,128)S(1)} %pad_maximum_fusion.1.refs_0_), channel_id=1, source_target_pairs={{0,16},{16,0},{32,48},{48,32},{64,80},{80,64},{96,112},{112,96},{1... | collective-permute-start | bytes 688136 | tf_op jit(solution)/shard_map/ppermute | solution.py:564
  96.9 9.0 %collective-permute-start.33 = (f32[4,112,128]{2,1,0:T(8,128)S(1)}, f32[4,112,128]{2,1,0:T(8,128)S(1)}, u32[]{:S(2)}, u32[]{:S(2)}) collective-permute-start(f32[4,112,128]{2,1,0:T(8,128)S(1)} %collective-permute-done.32.refs_6_), channel_id=1, source_target_pairs={{0,16},{16,0},{32,48},{48,32},{64,80},{80,64},{96,112},{112,96},{1... | collective-permute-start | bytes 688136 | tf_op jit(solution)/shard_map/ppermute | solution.py:564
  101.5 4.4 %collective-permute-start.31 = (f32[4,112,128]{2,1,0:T(8,128)S(1)}, f32[4,112,128]{2,1,0:T(8,128)S(1)}, u32[]{:S(2)}, u32[]{:S(2)}) collective-permute-start(f32[4,112,128]{2,1,0:T(8,128)S(1)} %collective-permute-done.30.refs_4_), channel_id=1, source_target_pairs={{0,16},{16,0},{32,48},{48,32},{64,80},{80,64},{96,112},{112,96},{1... | collective-permute-start | bytes 688136 | tf_op jit(solution)/shard_map/ppermute | solution.py:564
  (5 other events, 27.4 us)

commit v6 on v5

--- a/solution.py
+++ b/solution.py
@@ -372,7 +372,7 @@
     low[...] = (full - top.astype(F32)).astype(BF16)
 
 
-def energy_group(u0, u1, high, low, rho, f, x, y, x_in, x_out):
+def energy_group(u0, u1, high, low, rho, f, x, y, x_in, x_out, shift=0):
     cols = []
     for q in range(4):
         val = []
@@ -391,20 +391,25 @@
     for i in range(1, 24):
         energy = energy + prod[8 * i:8 * i + 8]
     for q in range(4):
-        rows = pl.ds(y + 8 * q, 8)
+        rows = pl.ds(y + shift + 8 * q, 8)
         r = rho[x_in, rows]
         f[x_out, rows] = -3.0 * r * r * energy[:, 128 * q:128 * q + 128]
 
 
-def energy_first(pos, stiff, u0, zrim, rho, u1, high, low, f):
-    keep_z = jnp.where(pos[2] < 3, 1.0, 0.0)
+def energy_setup(stiff, u0, u1, high, low):
     form_matrix(stiff[...], high, low)
+    for q in range(27):
+        if q % 9 < 8:
+            u1[q] = next_lane(u0[q])
+
+
+def energy_first(pos, u0, bare, high, low, zrim, rho, u1, f):
     lane = iota((128, 128), 1)
-    col = zrim[...] * keep_z
+    col = zrim[...] * jnp.where(pos[2] < 3, 1.0, 0.0)
     for d in range(3):
         for x in range(8):
             k, q = 8 * d + x, 9 * d + x
-            u1[q] = jnp.where(lane == 127, pltpu.roll(col, 127 - k, 1), next_lane(u0[q]))
+            u1[q] = jnp.where(lane == 127, pltpu.roll(col, 127 - k, 1), bare[q])
 
     def group(c, j):
         x = c // 3
@@ -414,53 +419,62 @@
     planes(0, 12, 4, group)
 
 
-def energy_second(u0, u1, high, low, rho, f):
+def rim_row(row, corner, k, w0, w1, q, start):
+    lane = iota((8, 128), 1)
+    row = jnp.broadcast_to(row, (8, 128))
+    corner = jnp.broadcast_to(corner, (8, 128))
+    w0[q, pl.ds(start, 8)] = row
+    w1[q, pl.ds(start, 8)] = jnp.where(
+        lane == 127, pltpu.roll(corner, 127 - k, 1), next_lane(row))
+
+
+def energy_second(pos, u0, u1, high, low, rho, yrim, fa, f, w0, w1):
+    keep_y = jnp.where(pos[1] < 3, 1.0, 0.0)
+    keep_z = jnp.where(pos[2] < 3, 1.0, 0.0)
+    corner = yrim[pl.ds(24, 1)] * (keep_y * keep_z)
+    for d in range(3):
+        for x in range(8):
+            k, q = 8 * d + x, 9 * d + x
+            w0[q, pl.ds(0, 32)] = u0[q, pl.ds(96, 32)]
+            w1[q, pl.ds(0, 32)] = u1[q, pl.ds(96, 32)]
+            rim_row(yrim[pl.ds(k, 1)] * keep_y, corner, k, w0, w1, q, 32)
+    for x in range(4):
+        f[x, pl.ds(0, 96)] = fa[x, pl.ds(0, 96)]
+
     def group(c, j):
         x = c // 3
         y = pl.multiple_of((c - 3 * x) * 32, 32)
-        energy_group(u0, u1, high, low, rho, f, x + 4, y, x + 4, x)
+        energy_group(u0, u1, high, low, rho, f, x + 4, y, x + 4, x + 4)
 
     planes(0, 9, 3, group)
-
-
-def energy_last(pos, u0, u1, high, low, rho, xface, yrim, zrim, xrim, fa, fb, f, lead, tail, pack, w0, w1):
-    gx, gy, gz = pos[0], pos[1], pos[2]
-    keep_x = jnp.where(gx < 7, 1.0, 0.0)
-    keep_y = jnp.where(gy < 3, 1.0, 0.0)
-    keep_z = jnp.where(gz < 3, 1.0, 0.0)
+    for x in range(7):
+        energy_group(w0, w1, high, low, rho, f, x, 0, x, x, 96)
+
+
+def energy_last(pos, u0, u1, high, low, rho, xface, yrim, zrim, xrim, fb,
+                f, lead, tail, pack, w0, w1):
+    keep_x = jnp.where(pos[0] < 7, 1.0, 0.0)
+    keep_y = jnp.where(pos[1] < 3, 1.0, 0.0)
+    keep_z = jnp.where(pos[2] < 3, 1.0, 0.0)
     lane = iota((128, 128), 1)
-    lane8 = iota((8, 128), 1)
+    col = xrim[pl.ds(32, 128)] * (keep_x * keep_z)
     for d in range(3):
-        for x in range(9):
-            k, q = 8 * d + x, 9 * d + x
-            if x < 8:
-                rows = pl.ds(0, 128) if x == 7 else pl.ds(96, 32)
-                w0[q, rows] = u0[q, rows]
-                w1[q, rows] = u1[q, rows]
-                row = yrim[pl.ds(k, 1)]
-                corner = yrim[pl.ds(24, 8)]
-            else:
-                k = 8 * d
-                body = xface[d] * keep_x
-                col = xrim[pl.ds(32, 128)] * (keep_x * keep_z)
-                w0[q, pl.ds(0, 128)] = body
-                w1[q, pl.ds(0, 128)] = jnp.where(
-                    lane == 127, pltpu.roll(col, 127 - k, 1), next_lane(body))
-                row = xrim[pl.ds(k, 1)] * keep_x
-                corner = xrim[pl.ds(24, 8)] * keep_x
-            row = jnp.broadcast_to(row, (8, 128)) * keep_y
-            corner = jnp.broadcast_to(corner[0:1], (8, 128)) * (keep_y * keep_z)
-            w0[q, pl.ds(128, 8)] = row
-            w1[q, pl.ds(128, 8)] = jnp.where(
-                lane8 == 127, pltpu.roll(corner, 127 - k, 1), next_lane(row))
-    for x in range(4):
-        f[x, pl.ds(0, 96)] = fa[x, pl.ds(0, 96)]
-    for x in range(3):
-        f[4 + x, pl.ds(0, 96)] = fb[x, pl.ds(0, 96)]
+        k, q = 8 * d + 7, 9 * d
+        w0[q, pl.ds(0, 128)] = u0[9 * d + 7]
+        w1[q, pl.ds(0, 128)] = u1[9 * d + 7]
+        corner = yrim[pl.ds(24, 1)] * (keep_y * keep_z)
+        rim_row(yrim[pl.ds(k, 1)] * keep_y, corner, k, w0, w1, q, 128)
+        k, q = 8 * d, 9 * d + 1
+        body = xface[d] * keep_x
+        w0[q, pl.ds(0, 128)] = body
+        w1[q, pl.ds(0, 128)] = jnp.where(
+            lane == 127, pltpu.roll(col, 127 - k, 1), next_lane(body))
+        corner = xrim[pl.ds(24, 1)] * (keep_x * keep_y * keep_z)
+        rim_row(xrim[pl.ds(k, 1)] * (keep_x * keep_y), corner, k, w0, w1, q, 128)
     for x in range(7):
-        energy_group(w0, w1, high, low, rho, f, x, 96, x, x)
+        f[x] = fb[x]
     for q in range(4):
-        energy_group(w0, w1, high, low, rho, f, 7, 32 * q, 7, 7)
+        energy_group(w0, w1, high, low, rho, f, 0, 32 * q, 7, 7)
     acc = jnp.zeros((128, 128), F32)
     for x in range(8):
         value = f[x]
@@ -477,26 +491,45 @@
     return pltpu.roll(value, (248 - 16 * x) % 128, 1)
 
 
-def first_kernel(pos, fl, fc, fr, hl, hc, hr, wm, ws, dm, t0, r0, tr0, zz,
-                 fm, fs, vm, vs, out, z_low, z_high, am, as_, tmp):
-    zero_pads((fm, fs, vm, vs, am, as_), 1, 22)
-    for b, (blk, halo) in enumerate(((fl, hl), (fc, hc), (fr, hr))):
-        for x in range(1 if b == 0 else 0, 7 if b == 2 else 8):
-            p = 8 * b + x
-            i = x_index(pos[0] * 8 + p - 8, 64)
-            parts = (
-                (8, 8, halo[pl.ds(8 * x, 8)], spread(halo[pl.ds(64, 8)], x)),
-                (16, 128, blk[x - 1 if b == 0 else x], spread(halo[pl.ds(144, 128)], x)),
-                (144, 8, halo[pl.ds(72 + 8 * x, 8)], spread(halo[pl.ds(136, 8)], x)),
-            )
-            for start, size, main, side in parts:
-                rows = pl.ds(start, size)
-                fm[p, rows] = main
-                fs[p, rows] = side
-                am[p, rows] = wm[i, rows] * main
-                as_[p, rows] = ws[i, rows] * side
-    level0_sweep(pos, (am, as_), (vm, vs), fm, fs, wm, ws, t0, 2, 21, True)
+def lay_out(pos, blk, halo, base, first, last, skip, wm, ws, fm, fs, am, as_):
+    for p in range(first, last + 1):
+        x = p - base
+        i = x_index(pos[0] * 8 + p - 8, 64)
+        parts = (
+            (8, 8, halo[pl.ds(8 * x, 8)], spread(halo[pl.ds(64, 8)], x)),
+            (16, 128, blk[x - skip], spread(halo[pl.ds(144, 128)], x)),
+            (144, 8, halo[pl.ds(72 + 8 * x, 8)], spread(halo[pl.ds(136, 8)], x)),
+        )
+        for start, size, main, side in parts:
+            rows = pl.ds(start, size)
+            fm[p, rows] = main
+            fs[p, rows] = side
+            am[p, rows] = wm[i, rows] * main
+            as_[p, rows] = ws[i, rows] * side
+
+
+def own_kernel(pos, fc, hc, wm, ws, fm, fs, am, as_):
+    zero_pads((fm, fs, am, as_), 1, 22)
+    lay_out(pos, fc, hc, 8, 8, 15, 0, wm, ws, fm, fs, am, as_)
+
+
+def first_kernel(pos, fl, fr, hl, hr, wm, ws, dm, t0, r0, tr0, zz, *refs):
+    fm, fs, am, as_, vm, vs, out, z_low, z_high, tmp = refs[4:]
+    lay_out(pos, fl, hl, 0, 6, 7, 1, wm, ws, fm, fs, am, as_)
+    lay_out(pos, fr, hr, 16, 16, 17, 0, wm, ws, fm, fs, am, as_)
+    zero_pads((vm, vs), 7, 16)
+    level0_sweep(pos, (am, as_), (vm, vs), fm, fs, wm, ws, t0, 7, 16, True)
     level0_restrict(pos, (vm, vs), fm, dm, r0, tr0, zz, tmp, out, z_low, z_high)
+
+
+def outer_kernel(pos, fl, fr, hl, hr, wm, ws, t0, *refs):
+    fm, fs, am, as_, vm, vs = refs[6:]
+    lay_out(pos, fl, hl, 0, 1, 5, 1, wm, ws, fm, fs, am, as_)
+    lay_out(pos, fr, hr, 16, 18, 22, 0, wm, ws, fm, fs, am, as_)
+    zero_pads((vm, vs), 2, 6)
+    zero_pads((vm, vs), 17, 21)
+    level0_sweep(pos, (am, as_), (vm, vs), fm, fs, wm, ws, t0, 2, 6, True)
+    level0_sweep(pos, (am, as_), (vm, vs), fm, fs, wm, ws, t0, 17, 21, True)
 
 
 def middle_kernel(pos, *refs):
@@ -542,7 +575,7 @@
     return pltpu.VMEM(dims, F32)
 
 
-def call(kernel, outs, scratch, scalars, args, name, limit=12):
+def call(kernel, outs, scratch, scalars, args, name, limit=12, in_place=None):
     specs = [SMEM] * scalars + [VM] * (len(args) - scalars)
     return pl.pallas_call(
         kernel,
@@ -550,6 +583,7 @@
         in_specs=specs,
         out_specs=[VM] * len(outs),
         scratch_shapes=scratch,
+        input_output_aliases=in_place or {},
         compiler_params=pltpu.CompilerParams(vmem_limit_bytes=limit << 20),
         name=name,
     )(*args)
@@ -571,7 +605,7 @@
 WIDE = vmem(PL0, R0, 128)
 
 
-def gather_level1(own, z_low, z_high):
+def extend_level1(own, z_low, z_high):
     lane = lax.broadcasted_iota(jnp.int32, (64, 128), 1)
     right, left = shifted(z_low, "gz", -1), shifted(z_high, "gz", 1)
     wide = []
@@ -580,12 +614,14 @@
         wide.append(jnp.where(lane < 64, own[k], rim))
     own = jnp.stack(wide)
     low, high = shifted(own[:, 40:], "gy", 1), shifted(own[:, :24], "gy", -1)
-    own = jnp.concatenate([low, own, high], axis=1)
-    blocks = []
-    for m in range(4):
-        part = own if m == 0 else shifted(own, "gx", 2 * m)
-        blocks += [part, swapped(part)]
-    return blocks
+    return jnp.concatenate([low, own, high], axis=1)
+
+
+def gather_level1(own, meanwhile):
+    parts = [own] + [shifted(own, "gx", 2 * m) for m in range(1, 4)]
+    if meanwhile:
+        parts[3], meanwhile = lax.optimization_barrier((parts[3], meanwhile))
+    return [v for part in parts for v in (part, swapped(part))], meanwhile
 
 
 def per_device(u, rho, stiff):
@@ -602,19 +638,23 @@
         rim_kernel, [shape(27, 128, 128), shape(128, 128), shape(24, 128)], [], 0, [u], "rims")
     xface = shifted(u[:, 0], "gx", -1)
     zrim = shifted(cols, "gz", -1)
+    mat = half_shape(192, 192)
+    bare, high, low = call(
+        energy_setup, [shape(27, 128, 128), mat, mat], [], 0, [stiff, u0], "energy_setup")
+    zrim, bare = lax.optimization_barrier((zrim, bare))
     yrim = shifted(jnp.concatenate([rows, zrim[:8]], axis=0), "gy", -1)
-    mat = half_shape(192, 192)
-    u1, high, low, fa = call(
-        energy_first, [shape(27, 128, 128), mat, mat, shape(4, 128, 128)],
-        [], 1, [pos, stiff, u0, zrim, rho], "energy_first")
+    u1, fa = call(
+        energy_first, [shape(27, 128, 128), shape(4, 128, 128)],
+        [], 1, [pos, u0, bare, high, low, zrim, rho], "energy_first")
     yrim, fa = lax.optimization_barrier((yrim, fa))
     xrim = shifted(jnp.concatenate([yrim, zrim], axis=0), "gx", -1)
     (fb,) = call(
-        energy_second, [shape(3, 128, 128)], [], 0, [u0, u1, high, low, rho], "energy_second")
+        energy_second, [shape(7, 128, 128)], [vmem(27, 40, 128), vmem(27, 40, 128)], 1,
+        [pos, u0, u1, high, low, rho, yrim, fa], "energy_second")
     f, lead, tail, pack = call(
         energy_last, [shape(8, 128, 128), shape(7, 128, 128), shape(7, 128, 128), shape(128, 128)],
         [vmem(27, 136, 128), vmem(27, 136, 128)], 1,
-        [pos, u0, u1, high, low, rho, xface, yrim, zrim, xrim, fa, fb], "energy_last")
+        [pos, u0, u1, high, low, rho, xface, yrim, zrim, xrim, fb], "energy_last")
 
     fl, fr = shifted(tail, "gx", 1), shifted(lead, "gx", -1)
     lane = lax.broadcasted_iota(jnp.int32, pack.shape, 1)
@@ -623,21 +663,29 @@
     up = jnp.concatenate([f[:, 120:].reshape(64, 128), z[120:]], axis=0)
     down = jnp.concatenate([f[:, :8].reshape(64, 128), z[:8]], axis=0)
     h = jnp.concatenate([shifted(up, "gy", 1), shifted(down, "gy", -1), z], axis=0)
-    hl, hr = shifted(h, "gx", 1), shifted(h, "gx", -1)
-
     wide = shape(PL0, R0, 128)
     level1 = [shape(4, 64, 128), shape(64, 128), shape(64, 128)]
-    fm, fs, vm, vs, *f1 = call(
-        first_kernel, [wide, wide, wide, wide, *level1],
-        [WIDE, WIDE, vmem(12, 128, 128)], 1,
-        [pos, fl, f, fr, hl, h, hr, wm, ws, dm, t0, r0, tr0, zz], "first")
+    state = call(own_kernel, [wide] * 4, [], 1, [pos, f, h, wm, ws], "own")
+    hl, hr = shifted(h, "gx", 1), shifted(h, "gx", -1)
+    *state, vm, vs, f1, z_low, z_high = call(
+        first_kernel, [wide] * 6 + level1, [vmem(12, 128, 128)], 1,
+        [pos, fl, fr, hl, hr, wm, ws, dm, t0, r0, tr0, zz, *state], "first",
+        in_place={12 + n: n for n in range(4)})
+    own = extend_level1(f1, z_low, z_high)
+    own, hl = lax.optimization_barrier((own, hl))
+    fm, fs, _, _, vm, vs = call(
+        outer_kernel, [wide] * 6, [], 1,
+        [pos, fl, fr, hl, hr, wm, ws, t0, *state, vm, vs], "outer",
+        in_place={8 + n: n for n in range(6)})
+    blocks, (fm, fs, vm, vs) = gather_level1(own, (fm, fs, vm, vs))
     tables = [w1, d1, w2, t1, dd, tdd, uu, up0]
     vm, vs, *f1 = call(
         middle_kernel, [wide, wide, *level1], [WIDE] * 4 + COARSE_SCRATCH, 1,
-        [pos, *gather_level1(*f1), *tables, wm, ws, dm, t0, r0, tr0, zz, fm, fs, vm, vs], "middle", 24)
+        [pos, *blocks, *tables, wm, ws, dm, t0, r0, tr0, zz, fm, fs, vm, vs], "middle", 24)
+    blocks, _ = gather_level1(extend_level1(*f1), ())
     (out,) = call(
         last_kernel, [shape(8, 128, 128)], [WIDE] * 4 + COARSE_SCRATCH, 1,
-        [pos, *gather_level1(*f1), *tables, wm, ws, t0, fm, fs, vm, vs], "last", 24)
+        [pos, *blocks, *tables, wm, ws, t0, fm, fs, vm, vs], "last", 24)
     return out
 
 

time: 114 us -> 113 us (level)
  waiting for transfers between devices: 20 us -> 16 us
  Pallas kernels: 31.4 us -> 33.9 us
    ppermute x26, waiting for transfers between devices: 17.7 us -> 13.8 us  [shifted(): lax.ppermute(value, axis, [(i, (i + step) % size) for i in range(size)])]
    pallas_call x8 -> x11, Pallas kernels: 31.4 us -> 33.9 us  [call(): pl.pallas_call(kernel, out_shape=outs, in_specs=specs, out_specs=[VM] * l...]
    ppermute x26, starting transfers between devices: 34.8 us -> 37 us  [shifted(): lax.ppermute(value, axis, [(i, (i + step) % size) for i in range(size)])]
    ppermute x8, starting transfers between devices: 24.9 us -> 22.8 us  [swapped(): lax.ppermute(value, 'gx', [(i, i ^ 1) for i in range(lax.axis_size('gx'))])]
  transfers between devices with their start and end apart: 34 -> 34, of which waited for: 14 -> 11; matrix products, arithmetic and copies ran while one was open for 1% -> 1% of each run, Pallas kernels for 5% -> 9%
where the time goes in v6:
time: 113 us
  starting transfers between devices  59.8 us (53%)
  Pallas kernels  33.9 us (30%)
  waiting for transfers between devices  16 us (14%)
  local copies, waits for them, and re-layouts  2.35 us (2%)
    ppermute x26, starting transfers between devices, shifted(): lax.ppermute(value, axis, [(i, (i + step) % size) for i in range(size)])  37 us
    pallas_call x11, Pallas kernels, call(): pl.pallas_call(kernel, out_shape=outs, in_specs=specs, out_specs=[VM] * l...  33.9 us
    ppermute x8, starting transfers between devices, swapped(): lax.ppermute(value, 'gx', [(i, i ^ 1) for i in range(lax.axis_size('gx'))])  22.8 us
    ppermute x26, waiting for transfers between devices, shifted(): lax.ppermute(value, axis, [(i, (i + step) % size) for i in range(size)])  13.8 us
  transfers between devices with their start and end apart: 34, of which 11 were waited for; matrix products, arithmetic and copies ran while one was open for 1% of the time, Pallas kernels for 9%

profile of v6, /device:TPU:1, one launch (start us, length us, event | category | flops | bytes accessed | tf_op | source)
XLA Modules:
  0.0 113.1 jit_solution(5721303789547870089)
XLA Ops:
  0.0 1.4 %copy-done.1 = f32[3,8,128,128]{3,2,1,0:T(8,128)S(1)} copy-done((f32[3,8,128,128]{3,2,1,0:T(8,128)S(1)}, f32[3,8,128,128]{3,2,1,0:T(8,128)}, u32[]{:S(2)}) %copy-start.1) | copy-done | bytes 1572888
  1.9 3.4 %collective-permute-start = (f32[128,128]{1,0:T(8,128)S(1)}, f32[128,128]{1,0:T(8,128)S(1)}, u32[]{:S(2)}, u32[]{:S(2)}) collective-permute-start(f32[128,128]{1,0:T(8,128)S(1)} %get-tuple-element.66), channel_id=1, source_target_pairs={{0,3},{1,0},{2,1},{3,2},{4,7},{5,4},{6,5},{7,6},{8,11},{9,8},{10,9... | collective-permute-start | bytes 196616 | tf_op jit(solution)/shard_map/ppermute | solution.py:594
  6.9 3.8 %collective-permute-start.2 = (f32[32,128]{1,0:T(8,128)S(1)}, f32[32,128]{1,0:T(8,128)S(1)}, u32[]{:S(2)}, u32[]{:S(2)}) collective-permute-start(f32[32,128]{1,0:T(8,128)S(1)} %pad_maximum_fusion.14), channel_id=1, source_target_pairs={{0,12},{4,0},{8,4},{12,8},{1,13},{5,1},{9,5},{13,9},{2,14},{6,2},{... | collective-permute-start | bytes 49160 | tf_op jit(solution)/shard_map/ppermute | solution.py:594
  10.8 2.9 %energy_first.1 = (f32[27,128,128]{2,1,0:T(8,128)S(1)}, f32[4,128,128]{2,1,0:T(8,128)S(1)}) custom-call(s32[3]{0:T(128)S(1)} %pad_add_fusion.pos, f32[27,128,128]{2,1,0:T(8,128)S(1)} %get-tuple-element.65.u0, f32[27,128,128]{2,1,0:T(8,128)S(1)} %get-tuple-element.68.bare, bf16[192,192]{1,0:T(8,128)(2,1)S(1)} %get-tuple-element.69.high, ...), custom_call_target="tpu_custom_call" | custom-call | tf_op jit(solution)/shard_map/energy_first/pallas_call | solution.py:580
  13.7 2.5 %collective-permute-start.3 = (f32[160,128]{1,0:T(8,128)S(1)}, f32[160,128]{1,0:T(8,128)S(1)}, u32[]{:S(2)}, u32[]{:S(2)}) collective-permute-start(f32[160,128]{1,0:T(8,128)S(1)} %pad_maximum_fusion.3), channel_id=1, source_target_pairs={{0,112},{16,0},{32,16},{48,32},{64,48},{80,64},{96,80},{112,96},{1... | collective-permute-start | bytes 245768 | tf_op jit(solution)/shard_map/ppermute | solution.py:594
  16.2 3.1 %energy_second.1.fb = f32[7,128,128]{2,1,0:T(8,128)S(1)} custom-call(s32[3]{0:T(128)S(1)} %pad_add_fusion.pos, f32[27,128,128]{2,1,0:T(8,128)S(1)} %get-tuple-element.65.u0, f32[27,128,128]{2,1,0:T(8,128)S(1)} %get-tuple-element.72.u1, bf16[192,192]{1,0:T(8,128)(2,1)S(1)} %get-tuple-element.69.high, bf16[192,192]{1,0:T(8,128)(2,1)S(1)} %get-tuple-element.70.low, ...), custom_call_target="tpu_custom_call" | custom-call | tf_op jit(solution)/shard_map/energy_second/pallas_call | solution.py:580
  19.3 1.3 %energy_last.1 = (f32[8,128,128]{2,1,0:T(8,128)S(1)}, f32[7,128,128]{2,1,0:T(8,128)S(1)}, f32[7,128,128]{2,1,0:T(8,128)S(1)}, f32[128,128]{1,0:T(8,128)S(1)}) custom-call(s32[3]{0:T(128)S(1)} %pad_add_fusion.pos, f32[27,128,128]{2,1,0:T(8,128)S(1)} %get-tuple-element.65.u0, f32[27,128,128]{2,1,0:T(8,128)S(1)} %get-tuple-element.72.u1, ...), custom_call_target="tpu_custom_call" | custom-call | tf_op jit(solution)/shard_map/energy_last/pallas_call | solution.py:580
  20.6 2.5 %collective-permute-start.7 = (f32[128,128]{1,0:T(8,128)S(1)}, f32[128,128]{1,0:T(8,128)S(1)}, u32[]{:S(2)}, u32[]{:S(2)}) collective-permute-start(f32[128,128]{1,0:T(8,128)S(1)} %get-tuple-element.80), channel_id=1, source_target_pairs={{0,3},{1,0},{2,1},{3,2},{4,7},{5,4},{6,5},{7,6},{8,11},{9,8},{10,9... | collective-permute-start | bytes 196616 | tf_op jit(solution)/shard_map/ppermute | solution.py:594
  24.4 3.0 %collective-permute-done.6 = f32[128,128]{1,0:T(8,128)S(1)} collective-permute-done((f32[128,128]{1,0:T(8,128)S(1)}, f32[128,128]{1,0:T(8,128)S(1)}, u32[]{:S(2)}, u32[]{:S(2)}) %collective-permute-start.6) | collective-permute-done | bytes 65568 | tf_op jit(solution)/shard_map/ppermute | solution.py:594
  27.5 2.0 %collective-permute-start.9 = (f32[72,128]{1,0:T(8,128)S(1)}, f32[72,128]{1,0:T(8,128)S(1)}, u32[]{:S(2)}, u32[]{:S(2)}) collective-permute-start(f32[72,128]{1,0:T(8,128)S(1)} %pad_maximum_fusion.13), channel_id=1, source_target_pairs={{0,12},{4,0},{8,4},{12,8},{1,13},{5,1},{9,5},{13,9},{2,14},{6,2},{... | collective-permute-start | bytes 110600 | tf_op jit(solution)/shard_map/ppermute | solution.py:594
  30.7 2.9 %collective-permute-done.8 = f32[72,128]{1,0:T(8,128)S(1)} collective-permute-done((f32[72,128]{1,0:T(8,128)S(1)}, f32[72,128]{1,0:T(8,128)S(1)}, u32[]{:S(2)}, u32[]{:S(2)}) %collective-permute-start.8) | collective-permute-done | bytes 36896 | tf_op jit(solution)/shard_map/ppermute | solution.py:594
  33.6 2.5 %collective-permute-start.11 = (f32[272,128]{1,0:T(8,128)S(1)}, f32[272,128]{1,0:T(8,128)S(1)}, u32[]{:S(2)}, u32[]{:S(2)}) collective-permute-start(f32[272,128]{1,0:T(8,128)S(1)} %pad_maximum_fusion.2.hc), channel_id=1, source_target_pairs={{0,112},{16,0},{32,16},{48,32},{64,48},{80,64},{96,80},{112,96},{1... | collective-permute-start | bytes 417800 | tf_op jit(solution)/shard_map/ppermute | solution.py:594
  40.4 2.5 %first.1 = (f32[24,160,128]{2,1,0:T(8,128)S(1)}, f32[24,160,128]{2,1,0:T(8,128)S(1)}, f32[24,160,128]{2,1,0:T(8,128)S(1)}, f32[24,160,128]{2,1,0:T(8,128)S(1)}, ...) custom-call(s32[3]{0:T(128)S(1)} %pad_add_fusion.pos, ...), custom_call_target="tpu_custom_call", output_to_operand_aliasing={{0}: (12, {}), {1}: (13, {}), {2}: (14, {}), {3}: (15, {})} | custom-call | tf_op jit(solution)/shard_map/first/pallas_call | solution.py:580
  42.9 2.7 %collective-permute-start.12 = (f32[64,128]{1,0:T(8,128)S(1)}, f32[64,128]{1,0:T(8,128)S(1)}, u32[]{:S(2)}, u32[]{:S(2)}) collective-permute-start(f32[64,128]{1,0:T(8,128)S(1)} %get-tuple-element.93), channel_id=1, source_target_pairs={{0,3},{1,0},{2,1},{3,2},{4,7},{5,4},{6,5},{7,6},{8,11},{9,8},{10,9... | collective-permute-start | bytes 98312 | tf_op jit(solution)/shard_map/ppermute | solution.py:594
  47.6 2.7 %collective-permute-start.15 = (f32[4,24,128]{2,1,0:T(8,128)S(1)}, f32[4,24,128]{2,1,0:T(8,128)S(1)}, u32[]{:S(2)}, u32[]{:S(2)}) collective-permute-start(f32[4,24,128]{2,1,0:T(8,128)S(1)} %get-tuple-element.138), channel_id=1, source_target_pairs={{0,12},{4,0},{8,4},{12,8},{1,13},{5,1},{9,5},{13,9},{2,14},{6,2},{... | collective-permute-start | bytes 147464 | tf_op jit(solution)/shard_map/ppermute | solution.py:594
  50.3 1.5 %collective-permute-done.14 = f32[4,24,128]{2,1,0:T(8,128)S(1)} collective-permute-done((f32[4,24,128]{2,1,0:T(8,128)S(1)}, f32[4,24,128]{2,1,0:T(8,128)S(1)}, u32[]{:S(2)}, u32[]{:S(2)}) %collective-permute-start.14) | collective-permute-done | bytes 49184 | tf_op jit(solution)/shard_map/ppermute | solution.py:594
  53.1 1.7 %collective-permute-start.19 = (f32[4,112,128]{2,1,0:T(8,128)S(1)}, f32[4,112,128]{2,1,0:T(8,128)S(1)}, u32[]{:S(2)}, u32[]{:S(2)}) collective-permute-start(f32[4,112,128]{2,1,0:T(8,128)S(1)} %pad_maximum_fusion.refs_0_), channel_id=1, source_target_pairs={{0,64},{16,80},{32,96},{48,112},{64,0},{80,16},{96,32},{112,48},{1... | collective-permute-start | bytes 688136 | tf_op jit(solution)/shard_map/ppermute | solution.py:594
  55.2 3.7 %collective-permute-start.16 = (f32[4,112,128]{2,1,0:T(8,128)S(1)}, f32[4,112,128]{2,1,0:T(8,128)S(1)}, u32[]{:S(2)}, u32[]{:S(2)}) collective-permute-start(f32[4,112,128]{2,1,0:T(8,128)S(1)} %pad_maximum_fusion.refs_0_), channel_id=1, source_target_pairs={{0,16},{16,0},{32,48},{48,32},{64,80},{80,64},{96,112},{112,96},{1... | collective-permute-start | bytes 688136 | tf_op jit(solution)/shard_map/ppermute | solution.py:598
  58.9 1.8 %outer.1 = (f32[24,160,128]{2,1,0:T(8,128)S(1)}, f32[24,160,128]{2,1,0:T(8,128)S(1)}, f32[24,160,128]{2,1,0:T(8,128)S(1)}, f32[24,160,128]{2,1,0:T(8,128)S(1)}, ...) custom-call(s32[3]{0:T(128)S(1)} %pad_add_fusion.pos, ...), custom_call_target="tpu_custom_call", output_to_operand_aliasing={{0}: (8, {}), {1}: (9, {}), {2}: (10, {}), {3}: (11, {}), {... | custom-call | tf_op jit(solution)/shard_map/outer/pallas_call | solution.py:580
  60.8 1.6 %collective-permute-start.22 = (f32[4,112,128]{2,1,0:T(8,128)S(1)}, f32[4,112,128]{2,1,0:T(8,128)S(1)}, u32[]{:S(2)}, u32[]{:S(2)}) collective-permute-start(f32[4,112,128]{2,1,0:T(8,128)S(1)} %collective-permute-done.21.refs_6_), channel_id=1, source_target_pairs={{0,16},{16,0},{32,48},{48,32},{64,80},{80,64},{96,112},{112,96},{1... | collective-permute-start | bytes 688136 | tf_op jit(solution)/shard_map/ppermute | solution.py:598
  62.4 2.8 %collective-permute-start.20 = (f32[4,112,128]{2,1,0:T(8,128)S(1)}, f32[4,112,128]{2,1,0:T(8,128)S(1)}, u32[]{:S(2)}, u32[]{:S(2)}) collective-permute-start(f32[4,112,128]{2,1,0:T(8,128)S(1)} %collective-permute-done.19.refs_4_), channel_id=1, source_target_pairs={{0,16},{16,0},{32,48},{48,32},{64,80},{80,64},{96,112},{112,96},{1... | collective-permute-start | bytes 688136 | tf_op jit(solution)/shard_map/ppermute | solution.py:598
  65.1 2.3 %collective-permute-start.18 = (f32[4,112,128]{2,1,0:T(8,128)S(1)}, f32[4,112,128]{2,1,0:T(8,128)S(1)}, u32[]{:S(2)}, u32[]{:S(2)}) collective-permute-start(f32[4,112,128]{2,1,0:T(8,128)S(1)} %collective-permute-done.17.refs_2_), channel_id=1, source_target_pairs={{0,16},{16,0},{32,48},{48,32},{64,80},{80,64},{96,112},{112,96},{1... | collective-permute-start | bytes 688136 | tf_op jit(solution)/shard_map/ppermute | solution.py:598
  68.6 12.1 %middle.1 = (f32[24,160,128]{2,1,0:T(8,128)S(1)}, f32[24,160,128]{2,1,0:T(8,128)S(1)}, f32[4,64,128]{2,1,0:T(8,128)S(1)}, f32[64,128]{1,0:T(8,128)S(1)}, f32[64,128]{1,0:T(8,128)S(1)}) custom-call(s32[3]{0:T(128)S(1)} %pad_add_fusion.pos, f32[4,112,128]{2,1,0:T(8,128)S(1)} %pad_maximum_fusion.refs_0_, f32[4,112,128]{2,1,0:T(8,128)S(1)} %collective-permute-done.16.refs_1_, ...), custom_call_target="tpu_custom_call" | custom-call | tf_op jit(solution)/shard_map/middle/pallas_call | solution.py:580
  80.8 2.7 %collective-permute-start.23 = (f32[64,128]{1,0:T(8,128)S(1)}, f32[64,128]{1,0:T(8,128)S(1)}, u32[]{:S(2)}, u32[]{:S(2)}) collective-permute-start(f32[64,128]{1,0:T(8,128)S(1)} %get-tuple-element.121), channel_id=1, source_target_pairs={{0,3},{1,0},{2,1},{3,2},{4,7},{5,4},{6,5},{7,6},{8,11},{9,8},{10,9... | collective-permute-start | bytes 98312 | tf_op jit(solution)/shard_map/ppermute | solution.py:594
  85.5 2.9 %collective-permute-start.26 = (f32[4,24,128]{2,1,0:T(8,128)S(1)}, f32[4,24,128]{2,1,0:T(8,128)S(1)}, u32[]{:S(2)}, u32[]{:S(2)}) collective-permute-start(f32[4,24,128]{2,1,0:T(8,128)S(1)} %get-tuple-element.136), channel_id=1, source_target_pairs={{0,12},{4,0},{8,4},{12,8},{1,13},{5,1},{9,5},{13,9},{2,14},{6,2},{... | collective-permute-start | bytes 147464 | tf_op jit(solution)/shard_map/ppermute | solution.py:594
  88.4 1.4 %collective-permute-done.25 = f32[4,24,128]{2,1,0:T(8,128)S(1)} collective-permute-done((f32[4,24,128]{2,1,0:T(8,128)S(1)}, f32[4,24,128]{2,1,0:T(8,128)S(1)}, u32[]{:S(2)}, u32[]{:S(2)}) %collective-permute-start.25) | collective-permute-done | bytes 49184 | tf_op jit(solution)/shard_map/ppermute | solution.py:594
  90.2 1.7 %collective-permute-start.30 = (f32[4,112,128]{2,1,0:T(8,128)S(1)}, f32[4,112,128]{2,1,0:T(8,128)S(1)}, u32[]{:S(2)}, u32[]{:S(2)}) collective-permute-start(f32[4,112,128]{2,1,0:T(8,128)S(1)} %pad_maximum_fusion.1.refs_0_), channel_id=1, source_target_pairs={{0,64},{16,80},{32,96},{48,112},{64,0},{80,16},{96,32},{112,48},{1... | collective-permute-start | bytes 688136 | tf_op jit(solution)/shard_map/ppermute | solution.py:594
  92.1 3.5 %collective-permute-start.27 = (f32[4,112,128]{2,1,0:T(8,128)S(1)}, f32[4,112,128]{2,1,0:T(8,128)S(1)}, u32[]{:S(2)}, u32[]{:S(2)}) collective-permute-start(f32[4,112,128]{2,1,0:T(8,128)S(1)} %pad_maximum_fusion.1.refs_0_), channel_id=1, source_target_pairs={{0,16},{16,0},{32,48},{48,32},{64,80},{80,64},{96,112},{112,96},{1... | collective-permute-start | bytes 688136 | tf_op jit(solution)/shard_map/ppermute | solution.py:598
  95.6 4.8 %collective-permute-start.33 = (f32[4,112,128]{2,1,0:T(8,128)S(1)}, f32[4,112,128]{2,1,0:T(8,128)S(1)}, u32[]{:S(2)}, u32[]{:S(2)}) collective-permute-start(f32[4,112,128]{2,1,0:T(8,128)S(1)} %collective-permute-done.32.refs_6_), channel_id=1, source_target_pairs={{0,16},{16,0},{32,48},{48,32},{64,80},{80,64},{96,112},{112,96},{1... | collective-permute-start | bytes 688136 | tf_op jit(solution)/shard_map/ppermute | solution.py:598
  100.4 1.9 %collective-permute-start.31 = (f32[4,112,128]{2,1,0:T(8,128)S(1)}, f32[4,112,128]{2,1,0:T(8,128)S(1)}, u32[]{:S(2)}, u32[]{:S(2)}) collective-permute-start(f32[4,112,128]{2,1,0:T(8,128)S(1)} %collective-permute-done.30.refs_4_), channel_id=1, source_target_pairs={{0,16},{16,0},{32,48},{48,32},{64,80},{80,64},{96,112},{112,96},{1... | collective-permute-start | bytes 688136 | tf_op jit(solution)/shard_map/ppermute | solution.py:598
  102.4 2.2 %collective-permute-start.29 = (f32[4,112,128]{2,1,0:T(8,128)S(1)}, f32[4,112,128]{2,1,0:T(8,128)S(1)}, u32[]{:S(2)}, u32[]{:S(2)}) collective-permute-start(f32[4,112,128]{2,1,0:T(8,128)S(1)} %collective-permute-done.28.refs_2_), channel_id=1, source_target_pairs={{0,16},{16,0},{32,48},{48,32},{64,80},{80,64},{96,112},{112,96},{1... | collective-permute-start | bytes 688136 | tf_op jit(solution)/shard_map/ppermute | solution.py:598
  105.7 7.3 %last.1 = f32[8,128,128]{2,1,0:T(8,128)} custom-call(s32[3]{0:T(128)S(1)} %pad_add_fusion.pos, f32[4,112,128]{2,1,0:T(8,128)S(1)} %pad_maximum_fusion.1.refs_0_, f32[4,112,128]{2,1,0:T(8,128)S(1)} %collective-permute-done.27.refs_1_, f32[4,112,128]{2,1,0:T(8,128)S(1)} %collective-permute-done.28.refs_2_, f32[4,112,128]{2,1,0:T(8,128)S(1)} %collective-permute-done.29.refs_3_, ...), custom_call_target="tpu_custom_call" | custom-call | tf_op jit(solution)/shard_map/last/pallas_call | solution.py:580
  (86 shorter events, 17.8 us)
Async XLA Ops:
  1.9 5.0 %collective-permute-start = (f32[128,128]{1,0:T(8,128)S(1)}, f32[128,128]{1,0:T(8,128)S(1)}, u32[]{:S(2)}, u32[]{:S(2)}) collective-permute-start(f32[128,128]{1,0:T(8,128)S(1)} %get-tuple-element.66), channel_id=1, source_target_pairs={{0,3},{1,0},{2,1},{3,2},{4,7},{5,4},{6,5},{7,6},{8,11},{9,8},{10,9... | collective-permute-start | bytes 196616 | tf_op jit(solution)/shard_map/ppermute | solution.py:594
  5.3 14.0 %collective-permute-start.1 = (f32[3,128,128]{2,1,0:T(8,128)S(1)}, f32[3,128,128]{2,1,0:T(8,128)S(1)}, u32[]{:S(2)}, u32[]{:S(2)}) collective-permute-start(f32[3,128,128]{2,1,0:T(8,128)S(1)} %slice_bitcast_fusion), channel_id=1, source_target_pairs={{0,112},{16,0},{32,16},{48,32},{64,48},{80,64},{96,80},{112,96},{1... | collective-permute-start | bytes 589832 | tf_op jit(solution)/shard_map/ppermute | solution.py:594
  6.9 6.8 %collective-permute-start.2 = (f32[32,128]{1,0:T(8,128)S(1)}, f32[32,128]{1,0:T(8,128)S(1)}, u32[]{:S(2)}, u32[]{:S(2)}) collective-permute-start(f32[32,128]{1,0:T(8,128)S(1)} %pad_maximum_fusion.14), channel_id=1, source_target_pairs={{0,12},{4,0},{8,4},{12,8},{1,13},{5,1},{9,5},{13,9},{2,14},{6,2},{... | collective-permute-start | bytes 49160 | tf_op jit(solution)/shard_map/ppermute | solution.py:594
  13.7 5.6 %collective-permute-start.3 = (f32[160,128]{1,0:T(8,128)S(1)}, f32[160,128]{1,0:T(8,128)S(1)}, u32[]{:S(2)}, u32[]{:S(2)}) collective-permute-start(f32[160,128]{1,0:T(8,128)S(1)} %pad_maximum_fusion.3), channel_id=1, source_target_pairs={{0,112},{16,0},{32,16},{48,32},{64,48},{80,64},{96,80},{112,96},{1... | collective-permute-start | bytes 245768 | tf_op jit(solution)/shard_map/ppermute | solution.py:594
  20.6 3.8 %collective-permute-start.7 = (f32[128,128]{1,0:T(8,128)S(1)}, f32[128,128]{1,0:T(8,128)S(1)}, u32[]{:S(2)}, u32[]{:S(2)}) collective-permute-start(f32[128,128]{1,0:T(8,128)S(1)} %get-tuple-element.80), channel_id=1, source_target_pairs={{0,3},{1,0},{2,1},{3,2},{4,7},{5,4},{6,5},{7,6},{8,11},{9,8},{10,9... | collective-permute-start | bytes 196616 | tf_op jit(solution)/shard_map/ppermute | solution.py:594
  23.1 4.3 %collective-permute-start.6 = (f32[128,128]{1,0:T(8,128)S(1)}, f32[128,128]{1,0:T(8,128)S(1)}, u32[]{:S(2)}, u32[]{:S(2)}) collective-permute-start(f32[128,128]{1,0:T(8,128)S(1)} %get-tuple-element.80), channel_id=1, source_target_pairs={{0,1},{1,2},{2,3},{3,0},{4,5},{5,6},{6,7},{7,4},{8,9},{9,10},{10,1... | collective-permute-start | bytes 196616 | tf_op jit(solution)/shard_map/ppermute | solution.py:594
  23.1 17.2 %collective-permute-start.4 = (f32[7,128,128]{2,1,0:T(8,128)S(1)}, f32[7,128,128]{2,1,0:T(8,128)S(1)}, u32[]{:S(2)}, u32[]{:S(2)}) collective-permute-start(f32[7,128,128]{2,1,0:T(8,128)S(1)} %get-tuple-element.77), channel_id=1, source_target_pairs={{0,16},{16,32},{32,48},{48,64},{64,80},{80,96},{96,112},{112,0},{1... | collective-permute-start | bytes 1376264 | tf_op jit(solution)/shard_map/ppermute | solution.py:594
  24.4 15.9 %collective-permute-start.5 = (f32[7,128,128]{2,1,0:T(8,128)S(1)}, f32[7,128,128]{2,1,0:T(8,128)S(1)}, u32[]{:S(2)}, u32[]{:S(2)}) collective-permute-start(f32[7,128,128]{2,1,0:T(8,128)S(1)} %get-tuple-element.78), channel_id=1, source_target_pairs={{0,112},{16,0},{32,16},{48,32},{64,48},{80,64},{96,80},{112,96},{1... | collective-permute-start | bytes 1376264 | tf_op jit(solution)/shard_map/ppermute | solution.py:594
  29.5 4.0 %collective-permute-start.8 = (f32[72,128]{1,0:T(8,128)S(1)}, f32[72,128]{1,0:T(8,128)S(1)}, u32[]{:S(2)}, u32[]{:S(2)}) collective-permute-start(f32[72,128]{1,0:T(8,128)S(1)} %pad_maximum_fusion.12), channel_id=1, source_target_pairs={{0,4},{4,8},{8,12},{12,0},{1,5},{5,9},{9,13},{13,1},{2,6},{6,10},{... | collective-permute-start | bytes 110600 | tf_op jit(solution)/shard_map/ppermute | solution.py:594
  33.6 6.8 %collective-permute-start.11 = (f32[272,128]{1,0:T(8,128)S(1)}, f32[272,128]{1,0:T(8,128)S(1)}, u32[]{:S(2)}, u32[]{:S(2)}) collective-permute-start(f32[272,128]{1,0:T(8,128)S(1)} %pad_maximum_fusion.2.hc), channel_id=1, source_target_pairs={{0,112},{16,0},{32,16},{48,32},{64,48},{80,64},{96,80},{112,96},{1... | collective-permute-start | bytes 417800 | tf_op jit(solution)/shard_map/ppermute | solution.py:594
  36.1 4.2 %collective-permute-start.10 = (f32[272,128]{1,0:T(8,128)S(1)}, f32[272,128]{1,0:T(8,128)S(1)}, u32[]{:S(2)}, u32[]{:S(2)}) collective-permute-start(f32[272,128]{1,0:T(8,128)S(1)} %pad_maximum_fusion.2.hc), channel_id=1, source_target_pairs={{0,16},{16,32},{32,48},{48,64},{64,80},{80,96},{96,112},{112,0},{1... | collective-permute-start | bytes 417800 | tf_op jit(solution)/shard_map/ppermute | solution.py:594
  42.8 4.0 %collective-permute-start.13 = (f32[64,128]{1,0:T(8,128)S(1)}, f32[64,128]{1,0:T(8,128)S(1)}, u32[]{:S(2)}, u32[]{:S(2)}) collective-permute-start(f32[64,128]{1,0:T(8,128)S(1)} %get-tuple-element.94), channel_id=1, source_target_pairs={{0,1},{1,2},{2,3},{3,0},{4,5},{5,6},{6,7},{7,4},{8,9},{9,10},{10,1... | collective-permute-start | bytes 98312 | tf_op jit(solution)/shard_map/ppermute | solution.py:594
  42.9 4.2 %collective-permute-start.12 = (f32[64,128]{1,0:T(8,128)S(1)}, f32[64,128]{1,0:T(8,128)S(1)}, u32[]{:S(2)}, u32[]{:S(2)}) collective-permute-start(f32[64,128]{1,0:T(8,128)S(1)} %get-tuple-element.93), channel_id=1, source_target_pairs={{0,3},{1,0},{2,1},{3,2},{4,7},{5,4},{6,5},{7,6},{8,11},{9,8},{10,9... | collective-permute-start | bytes 98312 | tf_op jit(solution)/shard_map/ppermute | solution.py:594
  47.6 4.2 %collective-permute-start.14 = (f32[4,24,128]{2,1,0:T(8,128)S(1)}, f32[4,24,128]{2,1,0:T(8,128)S(1)}, u32[]{:S(2)}, u32[]{:S(2)}) collective-permute-start(f32[4,24,128]{2,1,0:T(8,128)S(1)} %get-tuple-element.137), channel_id=1, source_target_pairs={{0,4},{4,8},{8,12},{12,0},{1,5},{5,9},{9,13},{13,1},{2,6},{6,10},{... | collective-permute-start | bytes 147464 | tf_op jit(solution)/shard_map/ppermute | solution.py:594
  47.6 4.1 %collective-permute-start.15 = (f32[4,24,128]{2,1,0:T(8,128)S(1)}, f32[4,24,128]{2,1,0:T(8,128)S(1)}, u32[]{:S(2)}, u32[]{:S(2)}) collective-permute-start(f32[4,24,128]{2,1,0:T(8,128)S(1)} %get-tuple-element.138), channel_id=1, source_target_pairs={{0,12},{4,0},{8,4},{12,8},{1,13},{5,1},{9,5},{13,9},{2,14},{6,2},{... | collective-permute-start | bytes 147464 | tf_op jit(solution)/shard_map/ppermute | solution.py:594
  51.8 8.9 %collective-permute-start.21 = (f32[4,112,128]{2,1,0:T(8,128)S(1)}, f32[4,112,128]{2,1,0:T(8,128)S(1)}, u32[]{:S(2)}, u32[]{:S(2)}) collective-permute-start(f32[4,112,128]{2,1,0:T(8,128)S(1)} %pad_maximum_fusion.refs_0_), channel_id=1, source_target_pairs={{0,96},{16,112},{32,0},{48,16},{64,32},{80,48},{96,64},{112,80},{1... | collective-permute-start | bytes 688136 | tf_op jit(solution)/shard_map/ppermute | solution.py:594
  53.1 9.3 %collective-permute-start.19 = (f32[4,112,128]{2,1,0:T(8,128)S(1)}, f32[4,112,128]{2,1,0:T(8,128)S(1)}, u32[]{:S(2)}, u32[]{:S(2)}) collective-permute-start(f32[4,112,128]{2,1,0:T(8,128)S(1)} %pad_maximum_fusion.refs_0_), channel_id=1, source_target_pairs={{0,64},{16,80},{32,96},{48,112},{64,0},{80,16},{96,32},{112,48},{1... | collective-permute-start | bytes 688136 | tf_op jit(solution)/shard_map/ppermute | solution.py:594
  54.8 10.3 %collective-permute-start.17 = (f32[4,112,128]{2,1,0:T(8,128)S(1)}, f32[4,112,128]{2,1,0:T(8,128)S(1)}, u32[]{:S(2)}, u32[]{:S(2)}) collective-permute-start(f32[4,112,128]{2,1,0:T(8,128)S(1)} %pad_maximum_fusion.refs_0_), channel_id=1, source_target_pairs={{0,32},{16,48},{32,64},{48,80},{64,96},{80,112},{96,0},{112,16},{1... | collective-permute-start | bytes 688136 | tf_op jit(solution)/shard_map/ppermute | solution.py:594
  55.2 12.3 %collective-permute-start.16 = (f32[4,112,128]{2,1,0:T(8,128)S(1)}, f32[4,112,128]{2,1,0:T(8,128)S(1)}, u32[]{:S(2)}, u32[]{:S(2)}) collective-permute-start(f32[4,112,128]{2,1,0:T(8,128)S(1)} %pad_maximum_fusion.refs_0_), channel_id=1, source_target_pairs={{0,16},{16,0},{32,48},{48,32},{64,80},{80,64},{96,112},{112,96},{1... | collective-permute-start | bytes 688136 | tf_op jit(solution)/shard_map/ppermute | solution.py:598
  60.8 6.7 %collective-permute-start.22 = (f32[4,112,128]{2,1,0:T(8,128)S(1)}, f32[4,112,128]{2,1,0:T(8,128)S(1)}, u32[]{:S(2)}, u32[]{:S(2)}) collective-permute-start(f32[4,112,128]{2,1,0:T(8,128)S(1)} %collective-permute-done.21.refs_6_), channel_id=1, source_target_pairs={{0,16},{16,0},{32,48},{48,32},{64,80},{80,64},{96,112},{112,96},{1... | collective-permute-start | bytes 688136 | tf_op jit(solution)/shard_map/ppermute | solution.py:598
  62.4 5.1 %collective-permute-start.20 = (f32[4,112,128]{2,1,0:T(8,128)S(1)}, f32[4,112,128]{2,1,0:T(8,128)S(1)}, u32[]{:S(2)}, u32[]{:S(2)}) collective-permute-start(f32[4,112,128]{2,1,0:T(8,128)S(1)} %collective-permute-done.19.refs_4_), channel_id=1, source_target_pairs={{0,16},{16,0},{32,48},{48,32},{64,80},{80,64},{96,112},{112,96},{1... | collective-permute-start | bytes 688136 | tf_op jit(solution)/shard_map/ppermute | solution.py:598
  65.1 3.5 %collective-permute-start.18 = (f32[4,112,128]{2,1,0:T(8,128)S(1)}, f32[4,112,128]{2,1,0:T(8,128)S(1)}, u32[]{:S(2)}, u32[]{:S(2)}) collective-permute-start(f32[4,112,128]{2,1,0:T(8,128)S(1)} %collective-permute-done.17.refs_2_), channel_id=1, source_target_pairs={{0,16},{16,0},{32,48},{48,32},{64,80},{80,64},{96,112},{112,96},{1... | collective-permute-start | bytes 688136 | tf_op jit(solution)/shard_map/ppermute | solution.py:598
  80.7 4.0 %collective-permute-start.24 = (f32[64,128]{1,0:T(8,128)S(1)}, f32[64,128]{1,0:T(8,128)S(1)}, u32[]{:S(2)}, u32[]{:S(2)}) collective-permute-start(f32[64,128]{1,0:T(8,128)S(1)} %get-tuple-element.122), channel_id=1, source_target_pairs={{0,1},{1,2},{2,3},{3,0},{4,5},{5,6},{6,7},{7,4},{8,9},{9,10},{10,1... | collective-permute-start | bytes 98312 | tf_op jit(solution)/shard_map/ppermute | solution.py:594
  80.8 4.2 %collective-permute-start.23 = (f32[64,128]{1,0:T(8,128)S(1)}, f32[64,128]{1,0:T(8,128)S(1)}, u32[]{:S(2)}, u32[]{:S(2)}) collective-permute-start(f32[64,128]{1,0:T(8,128)S(1)} %get-tuple-element.121), channel_id=1, source_target_pairs={{0,3},{1,0},{2,1},{3,2},{4,7},{5,4},{6,5},{7,6},{8,11},{9,8},{10,9... | collective-permute-start | bytes 98312 | tf_op jit(solution)/shard_map/ppermute | solution.py:594
  85.4 4.3 %collective-permute-start.25 = (f32[4,24,128]{2,1,0:T(8,128)S(1)}, f32[4,24,128]{2,1,0:T(8,128)S(1)}, u32[]{:S(2)}, u32[]{:S(2)}) collective-permute-start(f32[4,24,128]{2,1,0:T(8,128)S(1)} %get-tuple-element.135), channel_id=1, source_target_pairs={{0,4},{4,8},{8,12},{12,0},{1,5},{5,9},{9,13},{13,1},{2,6},{6,10},{... | collective-permute-start | bytes 147464 | tf_op jit(solution)/shard_map/ppermute | solution.py:594
  85.5 4.3 %collective-permute-start.26 = (f32[4,24,128]{2,1,0:T(8,128)S(1)}, f32[4,24,128]{2,1,0:T(8,128)S(1)}, u32[]{:S(2)}, u32[]{:S(2)}) collective-permute-start(f32[4,24,128]{2,1,0:T(8,128)S(1)} %get-tuple-element.136), channel_id=1, source_target_pairs={{0,12},{4,0},{8,4},{12,8},{1,13},{5,1},{9,5},{13,9},{2,14},{6,2},{... | collective-permute-start | bytes 147464 | tf_op jit(solution)/shard_map/ppermute | solution.py:594
  89.8 5.8 %collective-permute-start.32 = (f32[4,112,128]{2,1,0:T(8,128)S(1)}, f32[4,112,128]{2,1,0:T(8,128)S(1)}, u32[]{:S(2)}, u32[]{:S(2)}) collective-permute-start(f32[4,112,128]{2,1,0:T(8,128)S(1)} %pad_maximum_fusion.1.refs_0_), channel_id=1, source_target_pairs={{0,96},{16,112},{32,0},{48,16},{64,32},{80,48},{96,64},{112,80},{1... | collective-permute-start | bytes 688136 | tf_op jit(solution)/shard_map/ppermute | solution.py:594
  90.2 10.2 %collective-permute-start.30 = (f32[4,112,128]{2,1,0:T(8,128)S(1)}, f32[4,112,128]{2,1,0:T(8,128)S(1)}, u32[]{:S(2)}, u32[]{:S(2)}) collective-permute-start(f32[4,112,128]{2,1,0:T(8,128)S(1)} %pad_maximum_fusion.1.refs_0_), channel_id=1, source_target_pairs={{0,64},{16,80},{32,96},{48,112},{64,0},{80,16},{96,32},{112,48},{1... | collective-permute-start | bytes 688136 | tf_op jit(solution)/shard_map/ppermute | solution.py:594
  91.9 10.5 %collective-permute-start.28 = (f32[4,112,128]{2,1,0:T(8,128)S(1)}, f32[4,112,128]{2,1,0:T(8,128)S(1)}, u32[]{:S(2)}, u32[]{:S(2)}) collective-permute-start(f32[4,112,128]{2,1,0:T(8,128)S(1)} %pad_maximum_fusion.1.refs_0_), channel_id=1, source_target_pairs={{0,32},{16,48},{32,64},{48,80},{64,96},{80,112},{96,0},{112,16},{1... | collective-permute-start | bytes 688136 | tf_op jit(solution)/shard_map/ppermute | solution.py:594
  92.1 12.6 %collective-permute-start.27 = (f32[4,112,128]{2,1,0:T(8,128)S(1)}, f32[4,112,128]{2,1,0:T(8,128)S(1)}, u32[]{:S(2)}, u32[]{:S(2)}) collective-permute-start(f32[4,112,128]{2,1,0:T(8,128)S(1)} %pad_maximum_fusion.1.refs_0_), channel_id=1, source_target_pairs={{0,16},{16,0},{32,48},{48,32},{64,80},{80,64},{96,112},{112,96},{1... | collective-permute-start | bytes 688136 | tf_op jit(solution)/shard_map/ppermute | solution.py:598
  95.6 9.0 %collective-permute-start.33 = (f32[4,112,128]{2,1,0:T(8,128)S(1)}, f32[4,112,128]{2,1,0:T(8,128)S(1)}, u32[]{:S(2)}, u32[]{:S(2)}) collective-permute-start(f32[4,112,128]{2,1,0:T(8,128)S(1)} %collective-permute-done.32.refs_6_), channel_id=1, source_target_pairs={{0,16},{16,0},{32,48},{48,32},{64,80},{80,64},{96,112},{112,96},{1... | collective-permute-start | bytes 688136 | tf_op jit(solution)/shard_map/ppermute | solution.py:598
  100.4 4.3 %collective-permute-start.31 = (f32[4,112,128]{2,1,0:T(8,128)S(1)}, f32[4,112,128]{2,1,0:T(8,128)S(1)}, u32[]{:S(2)}, u32[]{:S(2)}) collective-permute-start(f32[4,112,128]{2,1,0:T(8,128)S(1)} %collective-permute-done.30.refs_4_), channel_id=1, source_target_pairs={{0,16},{16,0},{32,48},{48,32},{64,80},{80,64},{96,112},{112,96},{1... | collective-permute-start | bytes 688136 | tf_op jit(solution)/shard_map/ppermute | solution.py:598
  (5 other events, 22.2 us)

commit v7 on v6

--- a/solution.py
+++ b/solution.py
@@ -203,7 +203,7 @@
             sums = [v if t is None else t + v for t, v in zip(sums, parts)]
         pairs = []
         for n in range(3):
-            tmp[3 * k + n] = sums[n]
+            tmp[3 * k + n, pl.ds(0, 128)] = sums[n]
             pairs.append(tmp[3 * k + n, pl.ds(0, 64, stride=2)] + tmp[3 * k + n, pl.ds(1, 64, stride=2)])
         near = select(jnp.concatenate(pairs[1:], axis=1), tr0[...])
         values.append(select(pairs[0], r0[...]) + S0 * near)
@@ -268,7 +268,7 @@
         for q in range(2):
             block = blocks[2 * m + q]
             own = gx if q == 0 else jnp.bitwise_xor(gx, 1)
-            place = jnp.bitwise_and(own + 8 - 2 * m, 7)
+            place = jnp.bitwise_and(own + 8 - 2 * (0, 1, 3, 2)[m], 7)
             for j in range(4):
                 p = 5 + 4 * place + j
                 i = x_index(4 * place + j, 32)
@@ -600,7 +600,7 @@
 
 COARSE_SCRATCH = [
     vmem(PL1, R1, 128), vmem(PL1, R1, 128), vmem(PL1, R1, 128),
-    vmem(10, R2, 128), vmem(10, R2, 128), vmem(10, R2, 128), vmem(32, 128, 128),
+    vmem(10, R2, 128), vmem(10, R2, 128), vmem(10, R2, 128), vmem(32, 136, 128),
 ]
 WIDE = vmem(PL0, R0, 128)
 
@@ -618,7 +618,7 @@
 
 
 def gather_level1(own, meanwhile):
-    parts = [own] + [shifted(own, "gx", 2 * m) for m in range(1, 4)]
+    parts = [own] + [shifted(own, "gx", 2 * m) for m in (1, 3, 2)]
     if meanwhile:
         parts[3], meanwhile = lax.optimization_barrier((parts[3], meanwhile))
     return [v for part in parts for v in (part, swapped(part))], meanwhile
@@ -668,7 +668,7 @@
     state = call(own_kernel, [wide] * 4, [], 1, [pos, f, h, wm, ws], "own")
     hl, hr = shifted(h, "gx", 1), shifted(h, "gx", -1)
     *state, vm, vs, f1, z_low, z_high = call(
-        first_kernel, [wide] * 6 + level1, [vmem(12, 128, 128)], 1,
+        first_kernel, [wide] * 6 + level1, [vmem(12, 136, 128)], 1,
         [pos, fl, fr, hl, hr, wm, ws, dm, t0, r0, tr0, zz, *state], "first",
         in_place={12 + n: n for n in range(4)})
     own = extend_level1(f1, z_low, z_high)

time: 113 us -> 112 us (level)
    ppermute x8, starting transfers between devices: 22.8 us -> 20.7 us  [swapped(): lax.ppermute(value, 'gx', [(i, i ^ 1) for i in range(lax.axis_size('gx'))])]
    ppermute x26, starting transfers between devices: 37 us -> 38.5 us  [shifted(): lax.ppermute(value, axis, [(i, (i + step) % size) for i in range(size)])]
  transfers between devices with their start and end apart: 34 -> 34, of which waited for: 11 -> 10; matrix products, arithmetic and copies ran while one was open for 1% -> 1% of each run, Pallas kernels for 9% -> 9%
where the time goes in v7:
time: 112 us
  starting transfers between devices  59.2 us (53%)
  Pallas kernels  33.9 us (30%)
  waiting for transfers between devices  15.9 us (14%)
  local copies, waits for them, and re-layouts  2.35 us (2%)
    ppermute x26, starting transfers between devices, shifted(): lax.ppermute(value, axis, [(i, (i + step) % size) for i in range(size)])  38.5 us
    pallas_call x11, Pallas kernels, call(): pl.pallas_call(kernel, out_shape=outs, in_specs=specs, out_specs=[VM] * l...  33.9 us
    ppermute x8, starting transfers between devices, swapped(): lax.ppermute(value, 'gx', [(i, i ^ 1) for i in range(lax.axis_size('gx'))])  20.7 us
    ppermute x26, waiting for transfers between devices, shifted(): lax.ppermute(value, axis, [(i, (i + step) % size) for i in range(size)])  13.7 us
  transfers between devices with their start and end apart: 34, of which 10 were waited for; matrix products, arithmetic and copies ran while one was open for 1% of the time, Pallas kernels for 9%

profile of v7, /device:TPU:1, one launch (start us, length us, event | category | flops | bytes accessed | tf_op | source)
XLA Modules:
  0.0 112.2 jit_solution(10038754625311895562)
XLA Ops:
  0.0 1.4 %copy-done.1 = f32[3,8,128,128]{3,2,1,0:T(8,128)S(1)} copy-done((f32[3,8,128,128]{3,2,1,0:T(8,128)S(1)}, f32[3,8,128,128]{3,2,1,0:T(8,128)}, u32[]{:S(2)}) %copy-start.1) | copy-done | bytes 1572888
  1.9 3.4 %collective-permute-start = (f32[128,128]{1,0:T(8,128)S(1)}, f32[128,128]{1,0:T(8,128)S(1)}, u32[]{:S(2)}, u32[]{:S(2)}) collective-permute-start(f32[128,128]{1,0:T(8,128)S(1)} %get-tuple-element.66), channel_id=1, source_target_pairs={{0,3},{1,0},{2,1},{3,2},{4,7},{5,4},{6,5},{7,6},{8,11},{9,8},{10,9... | collective-permute-start | bytes 196616 | tf_op jit(solution)/shard_map/ppermute | solution.py:594
  6.9 3.8 %collective-permute-start.2 = (f32[32,128]{1,0:T(8,128)S(1)}, f32[32,128]{1,0:T(8,128)S(1)}, u32[]{:S(2)}, u32[]{:S(2)}) collective-permute-start(f32[32,128]{1,0:T(8,128)S(1)} %pad_maximum_fusion.14), channel_id=1, source_target_pairs={{0,12},{4,0},{8,4},{12,8},{1,13},{5,1},{9,5},{13,9},{2,14},{6,2},{... | collective-permute-start | bytes 49160 | tf_op jit(solution)/shard_map/ppermute | solution.py:594
  10.8 2.9 %energy_first.1 = (f32[27,128,128]{2,1,0:T(8,128)S(1)}, f32[4,128,128]{2,1,0:T(8,128)S(1)}) custom-call(s32[3]{0:T(128)S(1)} %pad_add_fusion.pos, f32[27,128,128]{2,1,0:T(8,128)S(1)} %get-tuple-element.65.u0, f32[27,128,128]{2,1,0:T(8,128)S(1)} %get-tuple-element.68.bare, bf16[192,192]{1,0:T(8,128)(2,1)S(1)} %get-tuple-element.69.high, ...), custom_call_target="tpu_custom_call" | custom-call | tf_op jit(solution)/shard_map/energy_first/pallas_call | solution.py:580
  13.7 2.5 %collective-permute-start.3 = (f32[160,128]{1,0:T(8,128)S(1)}, f32[160,128]{1,0:T(8,128)S(1)}, u32[]{:S(2)}, u32[]{:S(2)}) collective-permute-start(f32[160,128]{1,0:T(8,128)S(1)} %pad_maximum_fusion.3), channel_id=1, source_target_pairs={{0,112},{16,0},{32,16},{48,32},{64,48},{80,64},{96,80},{112,96},{1... | collective-permute-start | bytes 245768 | tf_op jit(solution)/shard_map/ppermute | solution.py:594
  16.2 3.1 %energy_second.1.fb = f32[7,128,128]{2,1,0:T(8,128)S(1)} custom-call(s32[3]{0:T(128)S(1)} %pad_add_fusion.pos, f32[27,128,128]{2,1,0:T(8,128)S(1)} %get-tuple-element.65.u0, f32[27,128,128]{2,1,0:T(8,128)S(1)} %get-tuple-element.72.u1, bf16[192,192]{1,0:T(8,128)(2,1)S(1)} %get-tuple-element.69.high, bf16[192,192]{1,0:T(8,128)(2,1)S(1)} %get-tuple-element.70.low, ...), custom_call_target="tpu_custom_call" | custom-call | tf_op jit(solution)/shard_map/energy_second/pallas_call | solution.py:580
  19.3 1.3 %energy_last.1 = (f32[8,128,128]{2,1,0:T(8,128)S(1)}, f32[7,128,128]{2,1,0:T(8,128)S(1)}, f32[7,128,128]{2,1,0:T(8,128)S(1)}, f32[128,128]{1,0:T(8,128)S(1)}) custom-call(s32[3]{0:T(128)S(1)} %pad_add_fusion.pos, f32[27,128,128]{2,1,0:T(8,128)S(1)} %get-tuple-element.65.u0, f32[27,128,128]{2,1,0:T(8,128)S(1)} %get-tuple-element.72.u1, ...), custom_call_target="tpu_custom_call" | custom-call | tf_op jit(solution)/shard_map/energy_last/pallas_call | solution.py:580
  20.6 2.5 %collective-permute-start.7 = (f32[128,128]{1,0:T(8,128)S(1)}, f32[128,128]{1,0:T(8,128)S(1)}, u32[]{:S(2)}, u32[]{:S(2)}) collective-permute-start(f32[128,128]{1,0:T(8,128)S(1)} %get-tuple-element.80), channel_id=1, source_target_pairs={{0,3},{1,0},{2,1},{3,2},{4,7},{5,4},{6,5},{7,6},{8,11},{9,8},{10,9... | collective-permute-start | bytes 196616 | tf_op jit(solution)/shard_map/ppermute | solution.py:594
  23.1 1.3 %collective-permute-start.4 = (f32[7,128,128]{2,1,0:T(8,128)S(1)}, f32[7,128,128]{2,1,0:T(8,128)S(1)}, u32[]{:S(2)}, u32[]{:S(2)}) collective-permute-start(f32[7,128,128]{2,1,0:T(8,128)S(1)} %get-tuple-element.77), channel_id=1, source_target_pairs={{0,16},{16,32},{32,48},{48,64},{64,80},{80,96},{96,112},{112,0},{1... | collective-permute-start | bytes 1376264 | tf_op jit(solution)/shard_map/ppermute | solution.py:594
  24.4 3.0 %collective-permute-done.6 = f32[128,128]{1,0:T(8,128)S(1)} collective-permute-done((f32[128,128]{1,0:T(8,128)S(1)}, f32[128,128]{1,0:T(8,128)S(1)}, u32[]{:S(2)}, u32[]{:S(2)}) %collective-permute-start.6) | collective-permute-done | bytes 65568 | tf_op jit(solution)/shard_map/ppermute | solution.py:594
  27.5 2.0 %collective-permute-start.9 = (f32[72,128]{1,0:T(8,128)S(1)}, f32[72,128]{1,0:T(8,128)S(1)}, u32[]{:S(2)}, u32[]{:S(2)}) collective-permute-start(f32[72,128]{1,0:T(8,128)S(1)} %pad_maximum_fusion.13), channel_id=1, source_target_pairs={{0,12},{4,0},{8,4},{12,8},{1,13},{5,1},{9,5},{13,9},{2,14},{6,2},{... | collective-permute-start | bytes 110600 | tf_op jit(solution)/shard_map/ppermute | solution.py:594
  30.7 2.9 %collective-permute-done.8 = f32[72,128]{1,0:T(8,128)S(1)} collective-permute-done((f32[72,128]{1,0:T(8,128)S(1)}, f32[72,128]{1,0:T(8,128)S(1)}, u32[]{:S(2)}, u32[]{:S(2)}) %collective-permute-start.8) | collective-permute-done | bytes 36896 | tf_op jit(solution)/shard_map/ppermute | solution.py:594
  33.6 2.5 %collective-permute-start.11 = (f32[272,128]{1,0:T(8,128)S(1)}, f32[272,128]{1,0:T(8,128)S(1)}, u32[]{:S(2)}, u32[]{:S(2)}) collective-permute-start(f32[272,128]{1,0:T(8,128)S(1)} %pad_maximum_fusion.2.hc), channel_id=1, source_target_pairs={{0,112},{16,0},{32,16},{48,32},{64,48},{80,64},{96,80},{112,96},{1... | collective-permute-start | bytes 417800 | tf_op jit(solution)/shard_map/ppermute | solution.py:594
  40.4 2.4 %first.1 = (f32[24,160,128]{2,1,0:T(8,128)S(1)}, f32[24,160,128]{2,1,0:T(8,128)S(1)}, f32[24,160,128]{2,1,0:T(8,128)S(1)}, f32[24,160,128]{2,1,0:T(8,128)S(1)}, ...) custom-call(s32[3]{0:T(128)S(1)} %pad_add_fusion.pos, ...), custom_call_target="tpu_custom_call", output_to_operand_aliasing={{0}: (12, {}), {1}: (13, {}), {2}: (14, {}), {3}: (15, {})} | custom-call | tf_op jit(solution)/shard_map/first/pallas_call | solution.py:580
  42.9 2.7 %collective-permute-start.12 = (f32[64,128]{1,0:T(8,128)S(1)}, f32[64,128]{1,0:T(8,128)S(1)}, u32[]{:S(2)}, u32[]{:S(2)}) collective-permute-start(f32[64,128]{1,0:T(8,128)S(1)} %get-tuple-element.93), channel_id=1, source_target_pairs={{0,3},{1,0},{2,1},{3,2},{4,7},{5,4},{6,5},{7,6},{8,11},{9,8},{10,9... | collective-permute-start | bytes 98312 | tf_op jit(solution)/shard_map/ppermute | solution.py:594
  47.6 2.7 %collective-permute-start.15 = (f32[4,24,128]{2,1,0:T(8,128)S(1)}, f32[4,24,128]{2,1,0:T(8,128)S(1)}, u32[]{:S(2)}, u32[]{:S(2)}) collective-permute-start(f32[4,24,128]{2,1,0:T(8,128)S(1)} %get-tuple-element.138), channel_id=1, source_target_pairs={{0,12},{4,0},{8,4},{12,8},{1,13},{5,1},{9,5},{13,9},{2,14},{6,2},{... | collective-permute-start | bytes 147464 | tf_op jit(solution)/shard_map/ppermute | solution.py:594
  50.3 1.5 %collective-permute-done.14 = f32[4,24,128]{2,1,0:T(8,128)S(1)} collective-permute-done((f32[4,24,128]{2,1,0:T(8,128)S(1)}, f32[4,24,128]{2,1,0:T(8,128)S(1)}, u32[]{:S(2)}, u32[]{:S(2)}) %collective-permute-start.14) | collective-permute-done | bytes 49184 | tf_op jit(solution)/shard_map/ppermute | solution.py:594
  51.8 2.5 %collective-permute-start.21 = (f32[4,112,128]{2,1,0:T(8,128)S(1)}, f32[4,112,128]{2,1,0:T(8,128)S(1)}, u32[]{:S(2)}, u32[]{:S(2)}) collective-permute-start(f32[4,112,128]{2,1,0:T(8,128)S(1)} %pad_maximum_fusion.refs_0_), channel_id=1, source_target_pairs={{0,64},{16,80},{32,96},{48,112},{64,0},{80,16},{96,32},{112,48},{1... | collective-permute-start | bytes 688136 | tf_op jit(solution)/shard_map/ppermute | solution.py:594
  55.8 3.7 %collective-permute-start.16 = (f32[4,112,128]{2,1,0:T(8,128)S(1)}, f32[4,112,128]{2,1,0:T(8,128)S(1)}, u32[]{:S(2)}, u32[]{:S(2)}) collective-permute-start(f32[4,112,128]{2,1,0:T(8,128)S(1)} %pad_maximum_fusion.refs_0_), channel_id=1, source_target_pairs={{0,16},{16,0},{32,48},{48,32},{64,80},{80,64},{96,112},{112,96},{1... | collective-permute-start | bytes 688136 | tf_op jit(solution)/shard_map/ppermute | solution.py:598
  59.5 1.8 %outer.1 = (f32[24,160,128]{2,1,0:T(8,128)S(1)}, f32[24,160,128]{2,1,0:T(8,128)S(1)}, f32[24,160,128]{2,1,0:T(8,128)S(1)}, f32[24,160,128]{2,1,0:T(8,128)S(1)}, ...) custom-call(s32[3]{0:T(128)S(1)} %pad_add_fusion.pos, ...), custom_call_target="tpu_custom_call", output_to_operand_aliasing={{0}: (8, {}), {1}: (9, {}), {2}: (10, {}), {3}: (11, {}), {... | custom-call | tf_op jit(solution)/shard_map/outer/pallas_call | solution.py:580
  61.4 2.6 %collective-permute-start.22 = (f32[4,112,128]{2,1,0:T(8,128)S(1)}, f32[4,112,128]{2,1,0:T(8,128)S(1)}, u32[]{:S(2)}, u32[]{:S(2)}) collective-permute-start(f32[4,112,128]{2,1,0:T(8,128)S(1)} %collective-permute-done.21.refs_6_), channel_id=1, source_target_pairs={{0,16},{16,0},{32,48},{48,32},{64,80},{80,64},{96,112},{112,96},{1... | collective-permute-start | bytes 688136 | tf_op jit(solution)/shard_map/ppermute | solution.py:598
  65.1 2.0 %collective-permute-start.18 = (f32[4,112,128]{2,1,0:T(8,128)S(1)}, f32[4,112,128]{2,1,0:T(8,128)S(1)}, u32[]{:S(2)}, u32[]{:S(2)}) collective-permute-start(f32[4,112,128]{2,1,0:T(8,128)S(1)} %collective-permute-done.17.refs_2_), channel_id=1, source_target_pairs={{0,16},{16,0},{32,48},{48,32},{64,80},{80,64},{96,112},{112,96},{1... | collective-permute-start | bytes 688136 | tf_op jit(solution)/shard_map/ppermute | solution.py:598
  68.2 12.1 %middle.1 = (f32[24,160,128]{2,1,0:T(8,128)S(1)}, f32[24,160,128]{2,1,0:T(8,128)S(1)}, f32[4,64,128]{2,1,0:T(8,128)S(1)}, f32[64,128]{1,0:T(8,128)S(1)}, f32[64,128]{1,0:T(8,128)S(1)}) custom-call(s32[3]{0:T(128)S(1)} %pad_add_fusion.pos, f32[4,112,128]{2,1,0:T(8,128)S(1)} %pad_maximum_fusion.refs_0_, f32[4,112,128]{2,1,0:T(8,128)S(1)} %collective-permute-done.16.refs_1_, ...), custom_call_target="tpu_custom_call" | custom-call | tf_op jit(solution)/shard_map/middle/pallas_call | solution.py:580
  80.4 2.7 %collective-permute-start.23 = (f32[64,128]{1,0:T(8,128)S(1)}, f32[64,128]{1,0:T(8,128)S(1)}, u32[]{:S(2)}, u32[]{:S(2)}) collective-permute-start(f32[64,128]{1,0:T(8,128)S(1)} %get-tuple-element.121), channel_id=1, source_target_pairs={{0,3},{1,0},{2,1},{3,2},{4,7},{5,4},{6,5},{7,6},{8,11},{9,8},{10,9... | collective-permute-start | bytes 98312 | tf_op jit(solution)/shard_map/ppermute | solution.py:594
  83.0 1.3 %collective-permute-done.24 = f32[64,128]{1,0:T(8,128)S(1)} collective-permute-done((f32[64,128]{1,0:T(8,128)S(1)}, f32[64,128]{1,0:T(8,128)S(1)}, u32[]{:S(2)}, u32[]{:S(2)}) %collective-permute-start.24) | collective-permute-done | bytes 32800 | tf_op jit(solution)/shard_map/ppermute | solution.py:594
  85.1 2.7 %collective-permute-start.26 = (f32[4,24,128]{2,1,0:T(8,128)S(1)}, f32[4,24,128]{2,1,0:T(8,128)S(1)}, u32[]{:S(2)}, u32[]{:S(2)}) collective-permute-start(f32[4,24,128]{2,1,0:T(8,128)S(1)} %get-tuple-element.136), channel_id=1, source_target_pairs={{0,12},{4,0},{8,4},{12,8},{1,13},{5,1},{9,5},{13,9},{2,14},{6,2},{... | collective-permute-start | bytes 147464 | tf_op jit(solution)/shard_map/ppermute | solution.py:594
  87.9 1.4 %collective-permute-done.25 = f32[4,24,128]{2,1,0:T(8,128)S(1)} collective-permute-done((f32[4,24,128]{2,1,0:T(8,128)S(1)}, f32[4,24,128]{2,1,0:T(8,128)S(1)}, u32[]{:S(2)}, u32[]{:S(2)}) %collective-permute-start.25) | collective-permute-done | bytes 49184 | tf_op jit(solution)/shard_map/ppermute | solution.py:594
  89.3 1.8 %collective-permute-start.32 = (f32[4,112,128]{2,1,0:T(8,128)S(1)}, f32[4,112,128]{2,1,0:T(8,128)S(1)}, u32[]{:S(2)}, u32[]{:S(2)}) collective-permute-start(f32[4,112,128]{2,1,0:T(8,128)S(1)} %pad_maximum_fusion.1.refs_0_), channel_id=1, source_target_pairs={{0,64},{16,80},{32,96},{48,112},{64,0},{80,16},{96,32},{112,48},{1... | collective-permute-start | bytes 688136 | tf_op jit(solution)/shard_map/ppermute | solution.py:594
  92.5 3.5 %collective-permute-start.27 = (f32[4,112,128]{2,1,0:T(8,128)S(1)}, f32[4,112,128]{2,1,0:T(8,128)S(1)}, u32[]{:S(2)}, u32[]{:S(2)}) collective-permute-start(f32[4,112,128]{2,1,0:T(8,128)S(1)} %pad_maximum_fusion.1.refs_0_), channel_id=1, source_target_pairs={{0,16},{16,0},{32,48},{48,32},{64,80},{80,64},{96,112},{112,96},{1... | collective-permute-start | bytes 688136 | tf_op jit(solution)/shard_map/ppermute | solution.py:598
  96.0 5.4 %collective-permute-start.33 = (f32[4,112,128]{2,1,0:T(8,128)S(1)}, f32[4,112,128]{2,1,0:T(8,128)S(1)}, u32[]{:S(2)}, u32[]{:S(2)}) collective-permute-start(f32[4,112,128]{2,1,0:T(8,128)S(1)} %collective-permute-done.32.refs_6_), channel_id=1, source_target_pairs={{0,16},{16,0},{32,48},{48,32},{64,80},{80,64},{96,112},{112,96},{1... | collective-permute-start | bytes 688136 | tf_op jit(solution)/shard_map/ppermute | solution.py:598
  102.2 1.6 %collective-permute-start.29 = (f32[4,112,128]{2,1,0:T(8,128)S(1)}, f32[4,112,128]{2,1,0:T(8,128)S(1)}, u32[]{:S(2)}, u32[]{:S(2)}) collective-permute-start(f32[4,112,128]{2,1,0:T(8,128)S(1)} %collective-permute-done.28.refs_2_), channel_id=1, source_target_pairs={{0,16},{16,0},{32,48},{48,32},{64,80},{80,64},{96,112},{112,96},{1... | collective-permute-start | bytes 688136 | tf_op jit(solution)/shard_map/ppermute | solution.py:598
  104.9 7.3 %last.1 = f32[8,128,128]{2,1,0:T(8,128)} custom-call(s32[3]{0:T(128)S(1)} %pad_add_fusion.pos, f32[4,112,128]{2,1,0:T(8,128)S(1)} %pad_maximum_fusion.1.refs_0_, f32[4,112,128]{2,1,0:T(8,128)S(1)} %collective-permute-done.27.refs_1_, f32[4,112,128]{2,1,0:T(8,128)S(1)} %collective-permute-done.28.refs_2_, f32[4,112,128]{2,1,0:T(8,128)S(1)} %collective-permute-done.29.refs_3_, ...), custom_call_target="tpu_custom_call" | custom-call | tf_op jit(solution)/shard_map/last/pallas_call | solution.py:580
  (86 shorter events, 17.7 us)
Async XLA Ops:
  1.9 5.0 %collective-permute-start = (f32[128,128]{1,0:T(8,128)S(1)}, f32[128,128]{1,0:T(8,128)S(1)}, u32[]{:S(2)}, u32[]{:S(2)}) collective-permute-start(f32[128,128]{1,0:T(8,128)S(1)} %get-tuple-element.66), channel_id=1, source_target_pairs={{0,3},{1,0},{2,1},{3,2},{4,7},{5,4},{6,5},{7,6},{8,11},{9,8},{10,9... | collective-permute-start | bytes 196616 | tf_op jit(solution)/shard_map/ppermute | solution.py:594
  5.3 14.0 %collective-permute-start.1 = (f32[3,128,128]{2,1,0:T(8,128)S(1)}, f32[3,128,128]{2,1,0:T(8,128)S(1)}, u32[]{:S(2)}, u32[]{:S(2)}) collective-permute-start(f32[3,128,128]{2,1,0:T(8,128)S(1)} %slice_bitcast_fusion), channel_id=1, source_target_pairs={{0,112},{16,0},{32,16},{48,32},{64,48},{80,64},{96,80},{112,96},{1... | collective-permute-start | bytes 589832 | tf_op jit(solution)/shard_map/ppermute | solution.py:594
  6.9 6.8 %collective-permute-start.2 = (f32[32,128]{1,0:T(8,128)S(1)}, f32[32,128]{1,0:T(8,128)S(1)}, u32[]{:S(2)}, u32[]{:S(2)}) collective-permute-start(f32[32,128]{1,0:T(8,128)S(1)} %pad_maximum_fusion.14), channel_id=1, source_target_pairs={{0,12},{4,0},{8,4},{12,8},{1,13},{5,1},{9,5},{13,9},{2,14},{6,2},{... | collective-permute-start | bytes 49160 | tf_op jit(solution)/shard_map/ppermute | solution.py:594
  13.7 5.6 %collective-permute-start.3 = (f32[160,128]{1,0:T(8,128)S(1)}, f32[160,128]{1,0:T(8,128)S(1)}, u32[]{:S(2)}, u32[]{:S(2)}) collective-permute-start(f32[160,128]{1,0:T(8,128)S(1)} %pad_maximum_fusion.3), channel_id=1, source_target_pairs={{0,112},{16,0},{32,16},{48,32},{64,48},{80,64},{96,80},{112,96},{1... | collective-permute-start | bytes 245768 | tf_op jit(solution)/shard_map/ppermute | solution.py:594
  20.6 3.8 %collective-permute-start.7 = (f32[128,128]{1,0:T(8,128)S(1)}, f32[128,128]{1,0:T(8,128)S(1)}, u32[]{:S(2)}, u32[]{:S(2)}) collective-permute-start(f32[128,128]{1,0:T(8,128)S(1)} %get-tuple-element.80), channel_id=1, source_target_pairs={{0,3},{1,0},{2,1},{3,2},{4,7},{5,4},{6,5},{7,6},{8,11},{9,8},{10,9... | collective-permute-start | bytes 196616 | tf_op jit(solution)/shard_map/ppermute | solution.py:594
  23.1 4.3 %collective-permute-start.6 = (f32[128,128]{1,0:T(8,128)S(1)}, f32[128,128]{1,0:T(8,128)S(1)}, u32[]{:S(2)}, u32[]{:S(2)}) collective-permute-start(f32[128,128]{1,0:T(8,128)S(1)} %get-tuple-element.80), channel_id=1, source_target_pairs={{0,1},{1,2},{2,3},{3,0},{4,5},{5,6},{6,7},{7,4},{8,9},{9,10},{10,1... | collective-permute-start | bytes 196616 | tf_op jit(solution)/shard_map/ppermute | solution.py:594
  23.1 17.2 %collective-permute-start.4 = (f32[7,128,128]{2,1,0:T(8,128)S(1)}, f32[7,128,128]{2,1,0:T(8,128)S(1)}, u32[]{:S(2)}, u32[]{:S(2)}) collective-permute-start(f32[7,128,128]{2,1,0:T(8,128)S(1)} %get-tuple-element.77), channel_id=1, source_target_pairs={{0,16},{16,32},{32,48},{48,64},{64,80},{80,96},{96,112},{112,0},{1... | collective-permute-start | bytes 1376264 | tf_op jit(solution)/shard_map/ppermute | solution.py:594
  24.4 15.9 %collective-permute-start.5 = (f32[7,128,128]{2,1,0:T(8,128)S(1)}, f32[7,128,128]{2,1,0:T(8,128)S(1)}, u32[]{:S(2)}, u32[]{:S(2)}) collective-permute-start(f32[7,128,128]{2,1,0:T(8,128)S(1)} %get-tuple-element.78), channel_id=1, source_target_pairs={{0,112},{16,0},{32,16},{48,32},{64,48},{80,64},{96,80},{112,96},{1... | collective-permute-start | bytes 1376264 | tf_op jit(solution)/shard_map/ppermute | solution.py:594
  27.5 3.2 %collective-permute-start.9 = (f32[72,128]{1,0:T(8,128)S(1)}, f32[72,128]{1,0:T(8,128)S(1)}, u32[]{:S(2)}, u32[]{:S(2)}) collective-permute-start(f32[72,128]{1,0:T(8,128)S(1)} %pad_maximum_fusion.13), channel_id=1, source_target_pairs={{0,12},{4,0},{8,4},{12,8},{1,13},{5,1},{9,5},{13,9},{2,14},{6,2},{... | collective-permute-start | bytes 110600 | tf_op jit(solution)/shard_map/ppermute | solution.py:594
  29.5 4.0 %collective-permute-start.8 = (f32[72,128]{1,0:T(8,128)S(1)}, f32[72,128]{1,0:T(8,128)S(1)}, u32[]{:S(2)}, u32[]{:S(2)}) collective-permute-start(f32[72,128]{1,0:T(8,128)S(1)} %pad_maximum_fusion.12), channel_id=1, source_target_pairs={{0,4},{4,8},{8,12},{12,0},{1,5},{5,9},{9,13},{13,1},{2,6},{6,10},{... | collective-permute-start | bytes 110600 | tf_op jit(solution)/shard_map/ppermute | solution.py:594
  33.6 6.8 %collective-permute-start.11 = (f32[272,128]{1,0:T(8,128)S(1)}, f32[272,128]{1,0:T(8,128)S(1)}, u32[]{:S(2)}, u32[]{:S(2)}) collective-permute-start(f32[272,128]{1,0:T(8,128)S(1)} %pad_maximum_fusion.2.hc), channel_id=1, source_target_pairs={{0,112},{16,0},{32,16},{48,32},{64,48},{80,64},{96,80},{112,96},{1... | collective-permute-start | bytes 417800 | tf_op jit(solution)/shard_map/ppermute | solution.py:594
  36.1 4.2 %collective-permute-start.10 = (f32[272,128]{1,0:T(8,128)S(1)}, f32[272,128]{1,0:T(8,128)S(1)}, u32[]{:S(2)}, u32[]{:S(2)}) collective-permute-start(f32[272,128]{1,0:T(8,128)S(1)} %pad_maximum_fusion.2.hc), channel_id=1, source_target_pairs={{0,16},{16,32},{32,48},{48,64},{64,80},{80,96},{96,112},{112,0},{1... | collective-permute-start | bytes 417800 | tf_op jit(solution)/shard_map/ppermute | solution.py:594
  42.8 4.0 %collective-permute-start.13 = (f32[64,128]{1,0:T(8,128)S(1)}, f32[64,128]{1,0:T(8,128)S(1)}, u32[]{:S(2)}, u32[]{:S(2)}) collective-permute-start(f32[64,128]{1,0:T(8,128)S(1)} %get-tuple-element.94), channel_id=1, source_target_pairs={{0,1},{1,2},{2,3},{3,0},{4,5},{5,6},{6,7},{7,4},{8,9},{9,10},{10,1... | collective-permute-start | bytes 98312 | tf_op jit(solution)/shard_map/ppermute | solution.py:594
  42.9 4.2 %collective-permute-start.12 = (f32[64,128]{1,0:T(8,128)S(1)}, f32[64,128]{1,0:T(8,128)S(1)}, u32[]{:S(2)}, u32[]{:S(2)}) collective-permute-start(f32[64,128]{1,0:T(8,128)S(1)} %get-tuple-element.93), channel_id=1, source_target_pairs={{0,3},{1,0},{2,1},{3,2},{4,7},{5,4},{6,5},{7,6},{8,11},{9,8},{10,9... | collective-permute-start | bytes 98312 | tf_op jit(solution)/shard_map/ppermute | solution.py:594
  47.6 4.2 %collective-permute-start.14 = (f32[4,24,128]{2,1,0:T(8,128)S(1)}, f32[4,24,128]{2,1,0:T(8,128)S(1)}, u32[]{:S(2)}, u32[]{:S(2)}) collective-permute-start(f32[4,24,128]{2,1,0:T(8,128)S(1)} %get-tuple-element.137), channel_id=1, source_target_pairs={{0,4},{4,8},{8,12},{12,0},{1,5},{5,9},{9,13},{13,1},{2,6},{6,10},{... | collective-permute-start | bytes 147464 | tf_op jit(solution)/shard_map/ppermute | solution.py:594
  47.6 4.1 %collective-permute-start.15 = (f32[4,24,128]{2,1,0:T(8,128)S(1)}, f32[4,24,128]{2,1,0:T(8,128)S(1)}, u32[]{:S(2)}, u32[]{:S(2)}) collective-permute-start(f32[4,24,128]{2,1,0:T(8,128)S(1)} %get-tuple-element.138), channel_id=1, source_target_pairs={{0,12},{4,0},{8,4},{12,8},{1,13},{5,1},{9,5},{13,9},{2,14},{6,2},{... | collective-permute-start | bytes 147464 | tf_op jit(solution)/shard_map/ppermute | solution.py:594
  51.8 9.6 %collective-permute-start.21 = (f32[4,112,128]{2,1,0:T(8,128)S(1)}, f32[4,112,128]{2,1,0:T(8,128)S(1)}, u32[]{:S(2)}, u32[]{:S(2)}) collective-permute-start(f32[4,112,128]{2,1,0:T(8,128)S(1)} %pad_maximum_fusion.refs_0_), channel_id=1, source_target_pairs={{0,64},{16,80},{32,96},{48,112},{64,0},{80,16},{96,32},{112,48},{1... | collective-permute-start | bytes 688136 | tf_op jit(solution)/shard_map/ppermute | solution.py:594
  54.3 9.6 %collective-permute-start.19 = (f32[4,112,128]{2,1,0:T(8,128)S(1)}, f32[4,112,128]{2,1,0:T(8,128)S(1)}, u32[]{:S(2)}, u32[]{:S(2)}) collective-permute-start(f32[4,112,128]{2,1,0:T(8,128)S(1)} %pad_maximum_fusion.refs_0_), channel_id=1, source_target_pairs={{0,96},{16,112},{32,0},{48,16},{64,32},{80,48},{96,64},{112,80},{1... | collective-permute-start | bytes 688136 | tf_op jit(solution)/shard_map/ppermute | solution.py:594
  55.4 9.7 %collective-permute-start.17 = (f32[4,112,128]{2,1,0:T(8,128)S(1)}, f32[4,112,128]{2,1,0:T(8,128)S(1)}, u32[]{:S(2)}, u32[]{:S(2)}) collective-permute-start(f32[4,112,128]{2,1,0:T(8,128)S(1)} %pad_maximum_fusion.refs_0_), channel_id=1, source_target_pairs={{0,32},{16,48},{32,64},{48,80},{64,96},{80,112},{96,0},{112,16},{1... | collective-permute-start | bytes 688136 | tf_op jit(solution)/shard_map/ppermute | solution.py:594
  55.8 11.3 %collective-permute-start.16 = (f32[4,112,128]{2,1,0:T(8,128)S(1)}, f32[4,112,128]{2,1,0:T(8,128)S(1)}, u32[]{:S(2)}, u32[]{:S(2)}) collective-permute-start(f32[4,112,128]{2,1,0:T(8,128)S(1)} %pad_maximum_fusion.refs_0_), channel_id=1, source_target_pairs={{0,16},{16,0},{32,48},{48,32},{64,80},{80,64},{96,112},{112,96},{1... | collective-permute-start | bytes 688136 | tf_op jit(solution)/shard_map/ppermute | solution.py:598
  61.4 5.7 %collective-permute-start.22 = (f32[4,112,128]{2,1,0:T(8,128)S(1)}, f32[4,112,128]{2,1,0:T(8,128)S(1)}, u32[]{:S(2)}, u32[]{:S(2)}) collective-permute-start(f32[4,112,128]{2,1,0:T(8,128)S(1)} %collective-permute-done.21.refs_6_), channel_id=1, source_target_pairs={{0,16},{16,0},{32,48},{48,32},{64,80},{80,64},{96,112},{112,96},{1... | collective-permute-start | bytes 688136 | tf_op jit(solution)/shard_map/ppermute | solution.py:598
  64.0 3.1 %collective-permute-start.20 = (f32[4,112,128]{2,1,0:T(8,128)S(1)}, f32[4,112,128]{2,1,0:T(8,128)S(1)}, u32[]{:S(2)}, u32[]{:S(2)}) collective-permute-start(f32[4,112,128]{2,1,0:T(8,128)S(1)} %collective-permute-done.19.refs_4_), channel_id=1, source_target_pairs={{0,16},{16,0},{32,48},{48,32},{64,80},{80,64},{96,112},{112,96},{1... | collective-permute-start | bytes 688136 | tf_op jit(solution)/shard_map/ppermute | solution.py:598
  65.1 3.1 %collective-permute-start.18 = (f32[4,112,128]{2,1,0:T(8,128)S(1)}, f32[4,112,128]{2,1,0:T(8,128)S(1)}, u32[]{:S(2)}, u32[]{:S(2)}) collective-permute-start(f32[4,112,128]{2,1,0:T(8,128)S(1)} %collective-permute-done.17.refs_2_), channel_id=1, source_target_pairs={{0,16},{16,0},{32,48},{48,32},{64,80},{80,64},{96,112},{112,96},{1... | collective-permute-start | bytes 688136 | tf_op jit(solution)/shard_map/ppermute | solution.py:598
  80.3 4.0 %collective-permute-start.24 = (f32[64,128]{1,0:T(8,128)S(1)}, f32[64,128]{1,0:T(8,128)S(1)}, u32[]{:S(2)}, u32[]{:S(2)}) collective-permute-start(f32[64,128]{1,0:T(8,128)S(1)} %get-tuple-element.122), channel_id=1, source_target_pairs={{0,1},{1,2},{2,3},{3,0},{4,5},{5,6},{6,7},{7,4},{8,9},{9,10},{10,1... | collective-permute-start | bytes 98312 | tf_op jit(solution)/shard_map/ppermute | solution.py:594
  80.4 4.2 %collective-permute-start.23 = (f32[64,128]{1,0:T(8,128)S(1)}, f32[64,128]{1,0:T(8,128)S(1)}, u32[]{:S(2)}, u32[]{:S(2)}) collective-permute-start(f32[64,128]{1,0:T(8,128)S(1)} %get-tuple-element.121), channel_id=1, source_target_pairs={{0,3},{1,0},{2,1},{3,2},{4,7},{5,4},{6,5},{7,6},{8,11},{9,8},{10,9... | collective-permute-start | bytes 98312 | tf_op jit(solution)/shard_map/ppermute | solution.py:594
  85.0 4.2 %collective-permute-start.25 = (f32[4,24,128]{2,1,0:T(8,128)S(1)}, f32[4,24,128]{2,1,0:T(8,128)S(1)}, u32[]{:S(2)}, u32[]{:S(2)}) collective-permute-start(f32[4,24,128]{2,1,0:T(8,128)S(1)} %get-tuple-element.135), channel_id=1, source_target_pairs={{0,4},{4,8},{8,12},{12,0},{1,5},{5,9},{9,13},{13,1},{2,6},{6,10},{... | collective-permute-start | bytes 147464 | tf_op jit(solution)/shard_map/ppermute | solution.py:594
  85.1 4.1 %collective-permute-start.26 = (f32[4,24,128]{2,1,0:T(8,128)S(1)}, f32[4,24,128]{2,1,0:T(8,128)S(1)}, u32[]{:S(2)}, u32[]{:S(2)}) collective-permute-start(f32[4,24,128]{2,1,0:T(8,128)S(1)} %get-tuple-element.136), channel_id=1, source_target_pairs={{0,12},{4,0},{8,4},{12,8},{1,13},{5,1},{9,5},{13,9},{2,14},{6,2},{... | collective-permute-start | bytes 147464 | tf_op jit(solution)/shard_map/ppermute | solution.py:594
  89.3 6.7 %collective-permute-start.32 = (f32[4,112,128]{2,1,0:T(8,128)S(1)}, f32[4,112,128]{2,1,0:T(8,128)S(1)}, u32[]{:S(2)}, u32[]{:S(2)}) collective-permute-start(f32[4,112,128]{2,1,0:T(8,128)S(1)} %pad_maximum_fusion.1.refs_0_), channel_id=1, source_target_pairs={{0,64},{16,80},{32,96},{48,112},{64,0},{80,16},{96,32},{112,48},{1... | collective-permute-start | bytes 688136 | tf_op jit(solution)/shard_map/ppermute | solution.py:594
  91.0 10.4 %collective-permute-start.30 = (f32[4,112,128]{2,1,0:T(8,128)S(1)}, f32[4,112,128]{2,1,0:T(8,128)S(1)}, u32[]{:S(2)}, u32[]{:S(2)}) collective-permute-start(f32[4,112,128]{2,1,0:T(8,128)S(1)} %pad_maximum_fusion.1.refs_0_), channel_id=1, source_target_pairs={{0,96},{16,112},{32,0},{48,16},{64,32},{80,48},{96,64},{112,80},{1... | collective-permute-start | bytes 688136 | tf_op jit(solution)/shard_map/ppermute | solution.py:594
  92.0 10.2 %collective-permute-start.28 = (f32[4,112,128]{2,1,0:T(8,128)S(1)}, f32[4,112,128]{2,1,0:T(8,128)S(1)}, u32[]{:S(2)}, u32[]{:S(2)}) collective-permute-start(f32[4,112,128]{2,1,0:T(8,128)S(1)} %pad_maximum_fusion.1.refs_0_), channel_id=1, source_target_pairs={{0,32},{16,48},{32,64},{48,80},{64,96},{80,112},{96,0},{112,16},{1... | collective-permute-start | bytes 688136 | tf_op jit(solution)/shard_map/ppermute | solution.py:594
  92.5 11.3 %collective-permute-start.27 = (f32[4,112,128]{2,1,0:T(8,128)S(1)}, f32[4,112,128]{2,1,0:T(8,128)S(1)}, u32[]{:S(2)}, u32[]{:S(2)}) collective-permute-start(f32[4,112,128]{2,1,0:T(8,128)S(1)} %pad_maximum_fusion.1.refs_0_), channel_id=1, source_target_pairs={{0,16},{16,0},{32,48},{48,32},{64,80},{80,64},{96,112},{112,96},{1... | collective-permute-start | bytes 688136 | tf_op jit(solution)/shard_map/ppermute | solution.py:598
  96.0 7.8 %collective-permute-start.33 = (f32[4,112,128]{2,1,0:T(8,128)S(1)}, f32[4,112,128]{2,1,0:T(8,128)S(1)}, u32[]{:S(2)}, u32[]{:S(2)}) collective-permute-start(f32[4,112,128]{2,1,0:T(8,128)S(1)} %collective-permute-done.32.refs_6_), channel_id=1, source_target_pairs={{0,16},{16,0},{32,48},{48,32},{64,80},{80,64},{96,112},{112,96},{1... | collective-permute-start | bytes 688136 | tf_op jit(solution)/shard_map/ppermute | solution.py:598
  (5 other events, 20.8 us)

commit v8 on v7

--- a/solution.py
+++ b/solution.py
@@ -167,8 +167,9 @@
 
 
 def level0_sweep(pos, src, dst, fm, fs, wm, ws, t0, first, last, side):
-    lane = iota((144, 128), 1)
-    rows, up, dn = pl.ds(8, 144), pl.ds(7, 144), pl.ds(9, 144)
+    start, size = (8, 144) if side else (16, 128)
+    lane = iota((size, 128), 1)
+    rows, up, dn = pl.ds(start, size), pl.ds(start - 1, size), pl.ds(start + 1, size)
 
     def body(p, j):
         i = x_index(pos[0] * 8 + p - 8, 64)
@@ -213,8 +214,8 @@
     z_high[...] = edges[:, 128:]
 
 
-def level1_sweep(src, dst, f, w, t1, first, count):
-    mid, up, dn = pl.ds(8, 112), pl.ds(7, 112), pl.ds(9, 112)
+def level1_sweep(src, dst, f, w, t1, first, count, start=8, size=112):
+    mid, up, dn = pl.ds(start, size), pl.ds(start - 1, size), pl.ds(start + 1, size)
 
     def body(p, j):
         i = x_index(p - 5, 32)
@@ -247,7 +248,7 @@
         dst[p, mid] = KEEP * m + w[{1: 0, 8: 2}.get(p, 1), mid] * (f[p, mid] + S2 * tot)
 
 
-def coarse_levels(pos, blocks, tables, f1, va, vb, f2, a2, b2, tmp):
+def coarse_levels(pos, blocks, tables, f1, va, vb, f2, a2, b2, tmp, halo):
     w1, d1, w2, t1, dd, tdd, uu = tables
     gx = pos[0]
     zero = jnp.zeros((R1, 128), F32)
@@ -319,8 +320,8 @@
                     vb[5 + 2 * k + q, rows] = vb[5 + 2 * k + q, rows] + e
 
     planes(1, 8, 8, prolong)
-    level1_sweep(vb, va, f1, w1, t1, 4 * gx + 1, 12)
-    level1_sweep(va, vb, f1, w1, t1, 4 * gx + 2, 10)
+    level1_sweep(vb, va, f1, w1, t1, 4 * gx + 4 - halo, 6 + 2 * halo, 24, 80)
+    level1_sweep(va, vb, f1, w1, t1, 4 * gx + 5 - halo, 4 + 2 * halo, 24, 80)
 
 
 def level0_prolong(pos, e1, up0, old, new, first, last):
@@ -537,7 +538,7 @@
     up0, wm, ws, dm, t0, r0, tr0, zz, fm, fs, vm, vs = refs[15:27]
     om, os_, out, z_low, z_high, am, as_, bm, bs, f1, va, vb, f2, a2, b2, tmp = refs[27:]
     zero_pads((am, as_, bm, bs, om, os_), 2, 21)
-    coarse_levels(pos, blocks, tables, f1, va, vb, f2, a2, b2, tmp)
+    coarse_levels(pos, blocks, tables, f1, va, vb, f2, a2, b2, tmp, 3)
     level0_prolong(pos, vb, up0, (vm, vs), (am, as_), 2, 21)
     level0_sweep(pos, (am, as_), (bm, bs), fm, fs, wm, ws, t0, 3, 20, True)
     level0_sweep(pos, (bm, bs), (am, as_), fm, fs, wm, ws, t0, 4, 19, True)
@@ -551,7 +552,7 @@
     up0, wm, ws, t0, fm, fs, vm, vs, out = refs[15:24]
     am, as_, bm, bs, f1, va, vb, f2, a2, b2, tmp = refs[24:]
     zero_pads((am, as_, bm, bs), 6, 17)
-    coarse_levels(pos, blocks, tables, f1, va, vb, f2, a2, b2, tmp)
+    coarse_levels(pos, blocks, tables, f1, va, vb, f2, a2, b2, tmp, 1)
     level0_prolong(pos, vb, up0, (vm, vs), (am, as_), 6, 17)
     level0_sweep(pos, (am, as_), (bm, bs), fm, fs, wm, ws, t0, 7, 16, True)
     level0_sweep(pos, (bm, bs), (am, as_), fm, fs, wm, ws, t0, 8, 15, False)

time: 112 us -> 112 us (level)
  no operation moved by 1% of the time
where the time goes in v8:
time: 112 us
  starting transfers between devices  59.2 us (53%)
  Pallas kernels  33.2 us (30%)
  waiting for transfers between devices  15.9 us (14%)
  local copies, waits for them, and re-layouts  2.35 us (2%)
    ppermute x26, starting transfers between devices, shifted(): lax.ppermute(value, axis, [(i, (i + step) % size) for i in range(size)])  38.5 us
    pallas_call x11, Pallas kernels, call(): pl.pallas_call(kernel, out_shape=outs, in_specs=specs, out_specs=[VM] * l...  33.2 us
    ppermute x8, starting transfers between devices, swapped(): lax.ppermute(value, 'gx', [(i, i ^ 1) for i in range(lax.axis_size('gx'))])  20.7 us
    ppermute x26, waiting for transfers between devices, shifted(): lax.ppermute(value, axis, [(i, (i + step) % size) for i in range(size)])  13.7 us
  transfers between devices with their start and end apart: 34, of which 10 were waited for; matrix products, arithmetic and copies ran while one was open for 1% of the time, Pallas kernels for 9%

profile of v8, /device:TPU:1, one launch (start us, length us, event | category | flops | bytes accessed | tf_op | source)
XLA Modules:
  0.0 111.5 jit_solution(4961890411044087167)
XLA Ops:
  0.0 1.4 %copy-done.1 = f32[3,8,128,128]{3,2,1,0:T(8,128)S(1)} copy-done((f32[3,8,128,128]{3,2,1,0:T(8,128)S(1)}, f32[3,8,128,128]{3,2,1,0:T(8,128)}, u32[]{:S(2)}) %copy-start.1) | copy-done | bytes 1572888
  1.9 3.4 %collective-permute-start = (f32[128,128]{1,0:T(8,128)S(1)}, f32[128,128]{1,0:T(8,128)S(1)}, u32[]{:S(2)}, u32[]{:S(2)}) collective-permute-start(f32[128,128]{1,0:T(8,128)S(1)} %get-tuple-element.66), channel_id=1, source_target_pairs={{0,3},{1,0},{2,1},{3,2},{4,7},{5,4},{6,5},{7,6},{8,11},{9,8},{10,9... | collective-permute-start | bytes 196616 | tf_op jit(solution)/shard_map/ppermute | solution.py:595
  6.9 3.8 %collective-permute-start.2 = (f32[32,128]{1,0:T(8,128)S(1)}, f32[32,128]{1,0:T(8,128)S(1)}, u32[]{:S(2)}, u32[]{:S(2)}) collective-permute-start(f32[32,128]{1,0:T(8,128)S(1)} %pad_maximum_fusion.14), channel_id=1, source_target_pairs={{0,12},{4,0},{8,4},{12,8},{1,13},{5,1},{9,5},{13,9},{2,14},{6,2},{... | collective-permute-start | bytes 49160 | tf_op jit(solution)/shard_map/ppermute | solution.py:595
  10.8 2.9 %energy_first.1 = (f32[27,128,128]{2,1,0:T(8,128)S(1)}, f32[4,128,128]{2,1,0:T(8,128)S(1)}) custom-call(s32[3]{0:T(128)S(1)} %pad_add_fusion.pos, f32[27,128,128]{2,1,0:T(8,128)S(1)} %get-tuple-element.65.u0, f32[27,128,128]{2,1,0:T(8,128)S(1)} %get-tuple-element.68.bare, bf16[192,192]{1,0:T(8,128)(2,1)S(1)} %get-tuple-element.69.high, ...), custom_call_target="tpu_custom_call" | custom-call | tf_op jit(solution)/shard_map/energy_first/pallas_call | solution.py:581
  13.7 2.5 %collective-permute-start.3 = (f32[160,128]{1,0:T(8,128)S(1)}, f32[160,128]{1,0:T(8,128)S(1)}, u32[]{:S(2)}, u32[]{:S(2)}) collective-permute-start(f32[160,128]{1,0:T(8,128)S(1)} %pad_maximum_fusion.3), channel_id=1, source_target_pairs={{0,112},{16,0},{32,16},{48,32},{64,48},{80,64},{96,80},{112,96},{1... | collective-permute-start | bytes 245768 | tf_op jit(solution)/shard_map/ppermute | solution.py:595
  16.2 3.1 %energy_second.1.fb = f32[7,128,128]{2,1,0:T(8,128)S(1)} custom-call(s32[3]{0:T(128)S(1)} %pad_add_fusion.pos, f32[27,128,128]{2,1,0:T(8,128)S(1)} %get-tuple-element.65.u0, f32[27,128,128]{2,1,0:T(8,128)S(1)} %get-tuple-element.72.u1, bf16[192,192]{1,0:T(8,128)(2,1)S(1)} %get-tuple-element.69.high, bf16[192,192]{1,0:T(8,128)(2,1)S(1)} %get-tuple-element.70.low, ...), custom_call_target="tpu_custom_call" | custom-call | tf_op jit(solution)/shard_map/energy_second/pallas_call | solution.py:581
  19.3 1.3 %energy_last.1 = (f32[8,128,128]{2,1,0:T(8,128)S(1)}, f32[7,128,128]{2,1,0:T(8,128)S(1)}, f32[7,128,128]{2,1,0:T(8,128)S(1)}, f32[128,128]{1,0:T(8,128)S(1)}) custom-call(s32[3]{0:T(128)S(1)} %pad_add_fusion.pos, f32[27,128,128]{2,1,0:T(8,128)S(1)} %get-tuple-element.65.u0, f32[27,128,128]{2,1,0:T(8,128)S(1)} %get-tuple-element.72.u1, ...), custom_call_target="tpu_custom_call" | custom-call | tf_op jit(solution)/shard_map/energy_last/pallas_call | solution.py:581
  20.6 2.5 %collective-permute-start.7 = (f32[128,128]{1,0:T(8,128)S(1)}, f32[128,128]{1,0:T(8,128)S(1)}, u32[]{:S(2)}, u32[]{:S(2)}) collective-permute-start(f32[128,128]{1,0:T(8,128)S(1)} %get-tuple-element.80), channel_id=1, source_target_pairs={{0,3},{1,0},{2,1},{3,2},{4,7},{5,4},{6,5},{7,6},{8,11},{9,8},{10,9... | collective-permute-start | bytes 196616 | tf_op jit(solution)/shard_map/ppermute | solution.py:595
  23.1 1.3 %collective-permute-start.4 = (f32[7,128,128]{2,1,0:T(8,128)S(1)}, f32[7,128,128]{2,1,0:T(8,128)S(1)}, u32[]{:S(2)}, u32[]{:S(2)}) collective-permute-start(f32[7,128,128]{2,1,0:T(8,128)S(1)} %get-tuple-element.77), channel_id=1, source_target_pairs={{0,16},{16,32},{32,48},{48,64},{64,80},{80,96},{96,112},{112,0},{1... | collective-permute-start | bytes 1376264 | tf_op jit(solution)/shard_map/ppermute | solution.py:595
  24.4 3.0 %collective-permute-done.6 = f32[128,128]{1,0:T(8,128)S(1)} collective-permute-done((f32[128,128]{1,0:T(8,128)S(1)}, f32[128,128]{1,0:T(8,128)S(1)}, u32[]{:S(2)}, u32[]{:S(2)}) %collective-permute-start.6) | collective-permute-done | bytes 65568 | tf_op jit(solution)/shard_map/ppermute | solution.py:595
  27.5 2.0 %collective-permute-start.9 = (f32[72,128]{1,0:T(8,128)S(1)}, f32[72,128]{1,0:T(8,128)S(1)}, u32[]{:S(2)}, u32[]{:S(2)}) collective-permute-start(f32[72,128]{1,0:T(8,128)S(1)} %pad_maximum_fusion.13), channel_id=1, source_target_pairs={{0,12},{4,0},{8,4},{12,8},{1,13},{5,1},{9,5},{13,9},{2,14},{6,2},{... | collective-permute-start | bytes 110600 | tf_op jit(solution)/shard_map/ppermute | solution.py:595
  30.7 2.9 %collective-permute-done.8 = f32[72,128]{1,0:T(8,128)S(1)} collective-permute-done((f32[72,128]{1,0:T(8,128)S(1)}, f32[72,128]{1,0:T(8,128)S(1)}, u32[]{:S(2)}, u32[]{:S(2)}) %collective-permute-start.8) | collective-permute-done | bytes 36896 | tf_op jit(solution)/shard_map/ppermute | solution.py:595
  33.6 2.5 %collective-permute-start.11 = (f32[272,128]{1,0:T(8,128)S(1)}, f32[272,128]{1,0:T(8,128)S(1)}, u32[]{:S(2)}, u32[]{:S(2)}) collective-permute-start(f32[272,128]{1,0:T(8,128)S(1)} %pad_maximum_fusion.2.hc), channel_id=1, source_target_pairs={{0,112},{16,0},{32,16},{48,32},{64,48},{80,64},{96,80},{112,96},{1... | collective-permute-start | bytes 417800 | tf_op jit(solution)/shard_map/ppermute | solution.py:595
  40.4 2.4 %first.1 = (f32[24,160,128]{2,1,0:T(8,128)S(1)}, f32[24,160,128]{2,1,0:T(8,128)S(1)}, f32[24,160,128]{2,1,0:T(8,128)S(1)}, f32[24,160,128]{2,1,0:T(8,128)S(1)}, ...) custom-call(s32[3]{0:T(128)S(1)} %pad_add_fusion.pos, ...), custom_call_target="tpu_custom_call", output_to_operand_aliasing={{0}: (12, {}), {1}: (13, {}), {2}: (14, {}), {3}: (15, {})} | custom-call | tf_op jit(solution)/shard_map/first/pallas_call | solution.py:581
  42.9 2.7 %collective-permute-start.12 = (f32[64,128]{1,0:T(8,128)S(1)}, f32[64,128]{1,0:T(8,128)S(1)}, u32[]{:S(2)}, u32[]{:S(2)}) collective-permute-start(f32[64,128]{1,0:T(8,128)S(1)} %get-tuple-element.93), channel_id=1, source_target_pairs={{0,3},{1,0},{2,1},{3,2},{4,7},{5,4},{6,5},{7,6},{8,11},{9,8},{10,9... | collective-permute-start | bytes 98312 | tf_op jit(solution)/shard_map/ppermute | solution.py:595
  47.6 2.7 %collective-permute-start.15 = (f32[4,24,128]{2,1,0:T(8,128)S(1)}, f32[4,24,128]{2,1,0:T(8,128)S(1)}, u32[]{:S(2)}, u32[]{:S(2)}) collective-permute-start(f32[4,24,128]{2,1,0:T(8,128)S(1)} %get-tuple-element.138), channel_id=1, source_target_pairs={{0,12},{4,0},{8,4},{12,8},{1,13},{5,1},{9,5},{13,9},{2,14},{6,2},{... | collective-permute-start | bytes 147464 | tf_op jit(solution)/shard_map/ppermute | solution.py:595
  50.3 1.5 %collective-permute-done.14 = f32[4,24,128]{2,1,0:T(8,128)S(1)} collective-permute-done((f32[4,24,128]{2,1,0:T(8,128)S(1)}, f32[4,24,128]{2,1,0:T(8,128)S(1)}, u32[]{:S(2)}, u32[]{:S(2)}) %collective-permute-start.14) | collective-permute-done | bytes 49184 | tf_op jit(solution)/shard_map/ppermute | solution.py:595
  51.8 2.5 %collective-permute-start.21 = (f32[4,112,128]{2,1,0:T(8,128)S(1)}, f32[4,112,128]{2,1,0:T(8,128)S(1)}, u32[]{:S(2)}, u32[]{:S(2)}) collective-permute-start(f32[4,112,128]{2,1,0:T(8,128)S(1)} %pad_maximum_fusion.refs_0_), channel_id=1, source_target_pairs={{0,64},{16,80},{32,96},{48,112},{64,0},{80,16},{96,32},{112,48},{1... | collective-permute-start | bytes 688136 | tf_op jit(solution)/shard_map/ppermute | solution.py:595
  55.8 3.7 %collective-permute-start.16 = (f32[4,112,128]{2,1,0:T(8,128)S(1)}, f32[4,112,128]{2,1,0:T(8,128)S(1)}, u32[]{:S(2)}, u32[]{:S(2)}) collective-permute-start(f32[4,112,128]{2,1,0:T(8,128)S(1)} %pad_maximum_fusion.refs_0_), channel_id=1, source_target_pairs={{0,16},{16,0},{32,48},{48,32},{64,80},{80,64},{96,112},{112,96},{1... | collective-permute-start | bytes 688136 | tf_op jit(solution)/shard_map/ppermute | solution.py:599
  59.5 1.8 %outer.1 = (f32[24,160,128]{2,1,0:T(8,128)S(1)}, f32[24,160,128]{2,1,0:T(8,128)S(1)}, f32[24,160,128]{2,1,0:T(8,128)S(1)}, f32[24,160,128]{2,1,0:T(8,128)S(1)}, ...) custom-call(s32[3]{0:T(128)S(1)} %pad_add_fusion.pos, ...), custom_call_target="tpu_custom_call", output_to_operand_aliasing={{0}: (8, {}), {1}: (9, {}), {2}: (10, {}), {3}: (11, {}), {... | custom-call | tf_op jit(solution)/shard_map/outer/pallas_call | solution.py:581
  61.4 2.6 %collective-permute-start.22 = (f32[4,112,128]{2,1,0:T(8,128)S(1)}, f32[4,112,128]{2,1,0:T(8,128)S(1)}, u32[]{:S(2)}, u32[]{:S(2)}) collective-permute-start(f32[4,112,128]{2,1,0:T(8,128)S(1)} %collective-permute-done.21.refs_6_), channel_id=1, source_target_pairs={{0,16},{16,0},{32,48},{48,32},{64,80},{80,64},{96,112},{112,96},{1... | collective-permute-start | bytes 688136 | tf_op jit(solution)/shard_map/ppermute | solution.py:599
  65.1 2.0 %collective-permute-start.18 = (f32[4,112,128]{2,1,0:T(8,128)S(1)}, f32[4,112,128]{2,1,0:T(8,128)S(1)}, u32[]{:S(2)}, u32[]{:S(2)}) collective-permute-start(f32[4,112,128]{2,1,0:T(8,128)S(1)} %collective-permute-done.17.refs_2_), channel_id=1, source_target_pairs={{0,16},{16,0},{32,48},{48,32},{64,80},{80,64},{96,112},{112,96},{1... | collective-permute-start | bytes 688136 | tf_op jit(solution)/shard_map/ppermute | solution.py:599
  68.2 11.8 %middle.1 = (f32[24,160,128]{2,1,0:T(8,128)S(1)}, f32[24,160,128]{2,1,0:T(8,128)S(1)}, f32[4,64,128]{2,1,0:T(8,128)S(1)}, f32[64,128]{1,0:T(8,128)S(1)}, f32[64,128]{1,0:T(8,128)S(1)}) custom-call(s32[3]{0:T(128)S(1)} %pad_add_fusion.pos, f32[4,112,128]{2,1,0:T(8,128)S(1)} %pad_maximum_fusion.refs_0_, f32[4,112,128]{2,1,0:T(8,128)S(1)} %collective-permute-done.16.refs_1_, ...), custom_call_target="tpu_custom_call" | custom-call | tf_op jit(solution)/shard_map/middle/pallas_call | solution.py:581
  80.1 2.7 %collective-permute-start.23 = (f32[64,128]{1,0:T(8,128)S(1)}, f32[64,128]{1,0:T(8,128)S(1)}, u32[]{:S(2)}, u32[]{:S(2)}) collective-permute-start(f32[64,128]{1,0:T(8,128)S(1)} %get-tuple-element.121), channel_id=1, source_target_pairs={{0,3},{1,0},{2,1},{3,2},{4,7},{5,4},{6,5},{7,6},{8,11},{9,8},{10,9... | collective-permute-start | bytes 98312 | tf_op jit(solution)/shard_map/ppermute | solution.py:595
  82.8 1.3 %collective-permute-done.24 = f32[64,128]{1,0:T(8,128)S(1)} collective-permute-done((f32[64,128]{1,0:T(8,128)S(1)}, f32[64,128]{1,0:T(8,128)S(1)}, u32[]{:S(2)}, u32[]{:S(2)}) %collective-permute-start.24) | collective-permute-done | bytes 32800 | tf_op jit(solution)/shard_map/ppermute | solution.py:595
  84.9 2.7 %collective-permute-start.26 = (f32[4,24,128]{2,1,0:T(8,128)S(1)}, f32[4,24,128]{2,1,0:T(8,128)S(1)}, u32[]{:S(2)}, u32[]{:S(2)}) collective-permute-start(f32[4,24,128]{2,1,0:T(8,128)S(1)} %get-tuple-element.136), channel_id=1, source_target_pairs={{0,12},{4,0},{8,4},{12,8},{1,13},{5,1},{9,5},{13,9},{2,14},{6,2},{... | collective-permute-start | bytes 147464 | tf_op jit(solution)/shard_map/ppermute | solution.py:595
  87.6 1.4 %collective-permute-done.25 = f32[4,24,128]{2,1,0:T(8,128)S(1)} collective-permute-done((f32[4,24,128]{2,1,0:T(8,128)S(1)}, f32[4,24,128]{2,1,0:T(8,128)S(1)}, u32[]{:S(2)}, u32[]{:S(2)}) %collective-permute-start.25) | collective-permute-done | bytes 49184 | tf_op jit(solution)/shard_map/ppermute | solution.py:595
  89.0 1.8 %collective-permute-start.32 = (f32[4,112,128]{2,1,0:T(8,128)S(1)}, f32[4,112,128]{2,1,0:T(8,128)S(1)}, u32[]{:S(2)}, u32[]{:S(2)}) collective-permute-start(f32[4,112,128]{2,1,0:T(8,128)S(1)} %pad_maximum_fusion.1.refs_0_), channel_id=1, source_target_pairs={{0,64},{16,80},{32,96},{48,112},{64,0},{80,16},{96,32},{112,48},{1... | collective-permute-start | bytes 688136 | tf_op jit(solution)/shard_map/ppermute | solution.py:595
  92.3 3.5 %collective-permute-start.27 = (f32[4,112,128]{2,1,0:T(8,128)S(1)}, f32[4,112,128]{2,1,0:T(8,128)S(1)}, u32[]{:S(2)}, u32[]{:S(2)}) collective-permute-start(f32[4,112,128]{2,1,0:T(8,128)S(1)} %pad_maximum_fusion.1.refs_0_), channel_id=1, source_target_pairs={{0,16},{16,0},{32,48},{48,32},{64,80},{80,64},{96,112},{112,96},{1... | collective-permute-start | bytes 688136 | tf_op jit(solution)/shard_map/ppermute | solution.py:599
  95.8 5.4 %collective-permute-start.33 = (f32[4,112,128]{2,1,0:T(8,128)S(1)}, f32[4,112,128]{2,1,0:T(8,128)S(1)}, u32[]{:S(2)}, u32[]{:S(2)}) collective-permute-start(f32[4,112,128]{2,1,0:T(8,128)S(1)} %collective-permute-done.32.refs_6_), channel_id=1, source_target_pairs={{0,16},{16,0},{32,48},{48,32},{64,80},{80,64},{96,112},{112,96},{1... | collective-permute-start | bytes 688136 | tf_op jit(solution)/shard_map/ppermute | solution.py:599
  101.9 1.6 %collective-permute-start.29 = (f32[4,112,128]{2,1,0:T(8,128)S(1)}, f32[4,112,128]{2,1,0:T(8,128)S(1)}, u32[]{:S(2)}, u32[]{:S(2)}) collective-permute-start(f32[4,112,128]{2,1,0:T(8,128)S(1)} %collective-permute-done.28.refs_2_), channel_id=1, source_target_pairs={{0,16},{16,0},{32,48},{48,32},{64,80},{80,64},{96,112},{112,96},{1... | collective-permute-start | bytes 688136 | tf_op jit(solution)/shard_map/ppermute | solution.py:599
  104.7 6.8 %last.1 = f32[8,128,128]{2,1,0:T(8,128)} custom-call(s32[3]{0:T(128)S(1)} %pad_add_fusion.pos, f32[4,112,128]{2,1,0:T(8,128)S(1)} %pad_maximum_fusion.1.refs_0_, f32[4,112,128]{2,1,0:T(8,128)S(1)} %collective-permute-done.27.refs_1_, f32[4,112,128]{2,1,0:T(8,128)S(1)} %collective-permute-done.28.refs_2_, f32[4,112,128]{2,1,0:T(8,128)S(1)} %collective-permute-done.29.refs_3_, ...), custom_call_target="tpu_custom_call" | custom-call | tf_op jit(solution)/shard_map/last/pallas_call | solution.py:581
  (86 shorter events, 17.7 us)
Async XLA Ops:
  1.9 5.0 %collective-permute-start = (f32[128,128]{1,0:T(8,128)S(1)}, f32[128,128]{1,0:T(8,128)S(1)}, u32[]{:S(2)}, u32[]{:S(2)}) collective-permute-start(f32[128,128]{1,0:T(8,128)S(1)} %get-tuple-element.66), channel_id=1, source_target_pairs={{0,3},{1,0},{2,1},{3,2},{4,7},{5,4},{6,5},{7,6},{8,11},{9,8},{10,9... | collective-permute-start | bytes 196616 | tf_op jit(solution)/shard_map/ppermute | solution.py:595
  5.3 14.0 %collective-permute-start.1 = (f32[3,128,128]{2,1,0:T(8,128)S(1)}, f32[3,128,128]{2,1,0:T(8,128)S(1)}, u32[]{:S(2)}, u32[]{:S(2)}) collective-permute-start(f32[3,128,128]{2,1,0:T(8,128)S(1)} %slice_bitcast_fusion), channel_id=1, source_target_pairs={{0,112},{16,0},{32,16},{48,32},{64,48},{80,64},{96,80},{112,96},{1... | collective-permute-start | bytes 589832 | tf_op jit(solution)/shard_map/ppermute | solution.py:595
  6.9 6.8 %collective-permute-start.2 = (f32[32,128]{1,0:T(8,128)S(1)}, f32[32,128]{1,0:T(8,128)S(1)}, u32[]{:S(2)}, u32[]{:S(2)}) collective-permute-start(f32[32,128]{1,0:T(8,128)S(1)} %pad_maximum_fusion.14), channel_id=1, source_target_pairs={{0,12},{4,0},{8,4},{12,8},{1,13},{5,1},{9,5},{13,9},{2,14},{6,2},{... | collective-permute-start | bytes 49160 | tf_op jit(solution)/shard_map/ppermute | solution.py:595
  13.7 5.6 %collective-permute-start.3 = (f32[160,128]{1,0:T(8,128)S(1)}, f32[160,128]{1,0:T(8,128)S(1)}, u32[]{:S(2)}, u32[]{:S(2)}) collective-permute-start(f32[160,128]{1,0:T(8,128)S(1)} %pad_maximum_fusion.3), channel_id=1, source_target_pairs={{0,112},{16,0},{32,16},{48,32},{64,48},{80,64},{96,80},{112,96},{1... | collective-permute-start | bytes 245768 | tf_op jit(solution)/shard_map/ppermute | solution.py:595
  20.6 3.8 %collective-permute-start.7 = (f32[128,128]{1,0:T(8,128)S(1)}, f32[128,128]{1,0:T(8,128)S(1)}, u32[]{:S(2)}, u32[]{:S(2)}) collective-permute-start(f32[128,128]{1,0:T(8,128)S(1)} %get-tuple-element.80), channel_id=1, source_target_pairs={{0,3},{1,0},{2,1},{3,2},{4,7},{5,4},{6,5},{7,6},{8,11},{9,8},{10,9... | collective-permute-start | bytes 196616 | tf_op jit(solution)/shard_map/ppermute | solution.py:595
  23.1 4.3 %collective-permute-start.6 = (f32[128,128]{1,0:T(8,128)S(1)}, f32[128,128]{1,0:T(8,128)S(1)}, u32[]{:S(2)}, u32[]{:S(2)}) collective-permute-start(f32[128,128]{1,0:T(8,128)S(1)} %get-tuple-element.80), channel_id=1, source_target_pairs={{0,1},{1,2},{2,3},{3,0},{4,5},{5,6},{6,7},{7,4},{8,9},{9,10},{10,1... | collective-permute-start | bytes 196616 | tf_op jit(solution)/shard_map/ppermute | solution.py:595
  23.1 17.2 %collective-permute-start.4 = (f32[7,128,128]{2,1,0:T(8,128)S(1)}, f32[7,128,128]{2,1,0:T(8,128)S(1)}, u32[]{:S(2)}, u32[]{:S(2)}) collective-permute-start(f32[7,128,128]{2,1,0:T(8,128)S(1)} %get-tuple-element.77), channel_id=1, source_target_pairs={{0,16},{16,32},{32,48},{48,64},{64,80},{80,96},{96,112},{112,0},{1... | collective-permute-start | bytes 1376264 | tf_op jit(solution)/shard_map/ppermute | solution.py:595
  24.4 15.9 %collective-permute-start.5 = (f32[7,128,128]{2,1,0:T(8,128)S(1)}, f32[7,128,128]{2,1,0:T(8,128)S(1)}, u32[]{:S(2)}, u32[]{:S(2)}) collective-permute-start(f32[7,128,128]{2,1,0:T(8,128)S(1)} %get-tuple-element.78), channel_id=1, source_target_pairs={{0,112},{16,0},{32,16},{48,32},{64,48},{80,64},{96,80},{112,96},{1... | collective-permute-start | bytes 1376264 | tf_op jit(solution)/shard_map/ppermute | solution.py:595
  27.5 3.2 %collective-permute-start.9 = (f32[72,128]{1,0:T(8,128)S(1)}, f32[72,128]{1,0:T(8,128)S(1)}, u32[]{:S(2)}, u32[]{:S(2)}) collective-permute-start(f32[72,128]{1,0:T(8,128)S(1)} %pad_maximum_fusion.13), channel_id=1, source_target_pairs={{0,12},{4,0},{8,4},{12,8},{1,13},{5,1},{9,5},{13,9},{2,14},{6,2},{... | collective-permute-start | bytes 110600 | tf_op jit(solution)/shard_map/ppermute | solution.py:595
  29.5 4.0 %collective-permute-start.8 = (f32[72,128]{1,0:T(8,128)S(1)}, f32[72,128]{1,0:T(8,128)S(1)}, u32[]{:S(2)}, u32[]{:S(2)}) collective-permute-start(f32[72,128]{1,0:T(8,128)S(1)} %pad_maximum_fusion.12), channel_id=1, source_target_pairs={{0,4},{4,8},{8,12},{12,0},{1,5},{5,9},{9,13},{13,1},{2,6},{6,10},{... | collective-permute-start | bytes 110600 | tf_op jit(solution)/shard_map/ppermute | solution.py:595
  33.6 6.8 %collective-permute-start.11 = (f32[272,128]{1,0:T(8,128)S(1)}, f32[272,128]{1,0:T(8,128)S(1)}, u32[]{:S(2)}, u32[]{:S(2)}) collective-permute-start(f32[272,128]{1,0:T(8,128)S(1)} %pad_maximum_fusion.2.hc), channel_id=1, source_target_pairs={{0,112},{16,0},{32,16},{48,32},{64,48},{80,64},{96,80},{112,96},{1... | collective-permute-start | bytes 417800 | tf_op jit(solution)/shard_map/ppermute | solution.py:595
  36.1 4.2 %collective-permute-start.10 = (f32[272,128]{1,0:T(8,128)S(1)}, f32[272,128]{1,0:T(8,128)S(1)}, u32[]{:S(2)}, u32[]{:S(2)}) collective-permute-start(f32[272,128]{1,0:T(8,128)S(1)} %pad_maximum_fusion.2.hc), channel_id=1, source_target_pairs={{0,16},{16,32},{32,48},{48,64},{64,80},{80,96},{96,112},{112,0},{1... | collective-permute-start | bytes 417800 | tf_op jit(solution)/shard_map/ppermute | solution.py:595
  42.8 4.0 %collective-permute-start.13 = (f32[64,128]{1,0:T(8,128)S(1)}, f32[64,128]{1,0:T(8,128)S(1)}, u32[]{:S(2)}, u32[]{:S(2)}) collective-permute-start(f32[64,128]{1,0:T(8,128)S(1)} %get-tuple-element.94), channel_id=1, source_target_pairs={{0,1},{1,2},{2,3},{3,0},{4,5},{5,6},{6,7},{7,4},{8,9},{9,10},{10,1... | collective-permute-start | bytes 98312 | tf_op jit(solution)/shard_map/ppermute | solution.py:595
  42.9 4.2 %collective-permute-start.12 = (f32[64,128]{1,0:T(8,128)S(1)}, f32[64,128]{1,0:T(8,128)S(1)}, u32[]{:S(2)}, u32[]{:S(2)}) collective-permute-start(f32[64,128]{1,0:T(8,128)S(1)} %get-tuple-element.93), channel_id=1, source_target_pairs={{0,3},{1,0},{2,1},{3,2},{4,7},{5,4},{6,5},{7,6},{8,11},{9,8},{10,9... | collective-permute-start | bytes 98312 | tf_op jit(solution)/shard_map/ppermute | solution.py:595
  47.6 4.2 %collective-permute-start.14 = (f32[4,24,128]{2,1,0:T(8,128)S(1)}, f32[4,24,128]{2,1,0:T(8,128)S(1)}, u32[]{:S(2)}, u32[]{:S(2)}) collective-permute-start(f32[4,24,128]{2,1,0:T(8,128)S(1)} %get-tuple-element.137), channel_id=1, source_target_pairs={{0,4},{4,8},{8,12},{12,0},{1,5},{5,9},{9,13},{13,1},{2,6},{6,10},{... | collective-permute-start | bytes 147464 | tf_op jit(solution)/shard_map/ppermute | solution.py:595
  47.6 4.1 %collective-permute-start.15 = (f32[4,24,128]{2,1,0:T(8,128)S(1)}, f32[4,24,128]{2,1,0:T(8,128)S(1)}, u32[]{:S(2)}, u32[]{:S(2)}) collective-permute-start(f32[4,24,128]{2,1,0:T(8,128)S(1)} %get-tuple-element.138), channel_id=1, source_target_pairs={{0,12},{4,0},{8,4},{12,8},{1,13},{5,1},{9,5},{13,9},{2,14},{6,2},{... | collective-permute-start | bytes 147464 | tf_op jit(solution)/shard_map/ppermute | solution.py:595
  51.8 9.6 %collective-permute-start.21 = (f32[4,112,128]{2,1,0:T(8,128)S(1)}, f32[4,112,128]{2,1,0:T(8,128)S(1)}, u32[]{:S(2)}, u32[]{:S(2)}) collective-permute-start(f32[4,112,128]{2,1,0:T(8,128)S(1)} %pad_maximum_fusion.refs_0_), channel_id=1, source_target_pairs={{0,64},{16,80},{32,96},{48,112},{64,0},{80,16},{96,32},{112,48},{1... | collective-permute-start | bytes 688136 | tf_op jit(solution)/shard_map/ppermute | solution.py:595
  54.3 9.6 %collective-permute-start.19 = (f32[4,112,128]{2,1,0:T(8,128)S(1)}, f32[4,112,128]{2,1,0:T(8,128)S(1)}, u32[]{:S(2)}, u32[]{:S(2)}) collective-permute-start(f32[4,112,128]{2,1,0:T(8,128)S(1)} %pad_maximum_fusion.refs_0_), channel_id=1, source_target_pairs={{0,96},{16,112},{32,0},{48,16},{64,32},{80,48},{96,64},{112,80},{1... | collective-permute-start | bytes 688136 | tf_op jit(solution)/shard_map/ppermute | solution.py:595
  55.4 9.7 %collective-permute-start.17 = (f32[4,112,128]{2,1,0:T(8,128)S(1)}, f32[4,112,128]{2,1,0:T(8,128)S(1)}, u32[]{:S(2)}, u32[]{:S(2)}) collective-permute-start(f32[4,112,128]{2,1,0:T(8,128)S(1)} %pad_maximum_fusion.refs_0_), channel_id=1, source_target_pairs={{0,32},{16,48},{32,64},{48,80},{64,96},{80,112},{96,0},{112,16},{1... | collective-permute-start | bytes 688136 | tf_op jit(solution)/shard_map/ppermute | solution.py:595
  55.8 11.3 %collective-permute-start.16 = (f32[4,112,128]{2,1,0:T(8,128)S(1)}, f32[4,112,128]{2,1,0:T(8,128)S(1)}, u32[]{:S(2)}, u32[]{:S(2)}) collective-permute-start(f32[4,112,128]{2,1,0:T(8,128)S(1)} %pad_maximum_fusion.refs_0_), channel_id=1, source_target_pairs={{0,16},{16,0},{32,48},{48,32},{64,80},{80,64},{96,112},{112,96},{1... | collective-permute-start | bytes 688136 | tf_op jit(solution)/shard_map/ppermute | solution.py:599
  61.4 5.7 %collective-permute-start.22 = (f32[4,112,128]{2,1,0:T(8,128)S(1)}, f32[4,112,128]{2,1,0:T(8,128)S(1)}, u32[]{:S(2)}, u32[]{:S(2)}) collective-permute-start(f32[4,112,128]{2,1,0:T(8,128)S(1)} %collective-permute-done.21.refs_6_), channel_id=1, source_target_pairs={{0,16},{16,0},{32,48},{48,32},{64,80},{80,64},{96,112},{112,96},{1... | collective-permute-start | bytes 688136 | tf_op jit(solution)/shard_map/ppermute | solution.py:599
  64.0 3.1 %collective-permute-start.20 = (f32[4,112,128]{2,1,0:T(8,128)S(1)}, f32[4,112,128]{2,1,0:T(8,128)S(1)}, u32[]{:S(2)}, u32[]{:S(2)}) collective-permute-start(f32[4,112,128]{2,1,0:T(8,128)S(1)} %collective-permute-done.19.refs_4_), channel_id=1, source_target_pairs={{0,16},{16,0},{32,48},{48,32},{64,80},{80,64},{96,112},{112,96},{1... | collective-permute-start | bytes 688136 | tf_op jit(solution)/shard_map/ppermute | solution.py:599
  65.1 3.1 %collective-permute-start.18 = (f32[4,112,128]{2,1,0:T(8,128)S(1)}, f32[4,112,128]{2,1,0:T(8,128)S(1)}, u32[]{:S(2)}, u32[]{:S(2)}) collective-permute-start(f32[4,112,128]{2,1,0:T(8,128)S(1)} %collective-permute-done.17.refs_2_), channel_id=1, source_target_pairs={{0,16},{16,0},{32,48},{48,32},{64,80},{80,64},{96,112},{112,96},{1... | collective-permute-start | bytes 688136 | tf_op jit(solution)/shard_map/ppermute | solution.py:599
  80.1 4.0 %collective-permute-start.24 = (f32[64,128]{1,0:T(8,128)S(1)}, f32[64,128]{1,0:T(8,128)S(1)}, u32[]{:S(2)}, u32[]{:S(2)}) collective-permute-start(f32[64,128]{1,0:T(8,128)S(1)} %get-tuple-element.122), channel_id=1, source_target_pairs={{0,1},{1,2},{2,3},{3,0},{4,5},{5,6},{6,7},{7,4},{8,9},{9,10},{10,1... | collective-permute-start | bytes 98312 | tf_op jit(solution)/shard_map/ppermute | solution.py:595
  80.1 4.2 %collective-permute-start.23 = (f32[64,128]{1,0:T(8,128)S(1)}, f32[64,128]{1,0:T(8,128)S(1)}, u32[]{:S(2)}, u32[]{:S(2)}) collective-permute-start(f32[64,128]{1,0:T(8,128)S(1)} %get-tuple-element.121), channel_id=1, source_target_pairs={{0,3},{1,0},{2,1},{3,2},{4,7},{5,4},{6,5},{7,6},{8,11},{9,8},{10,9... | collective-permute-start | bytes 98312 | tf_op jit(solution)/shard_map/ppermute | solution.py:595
  84.8 4.2 %collective-permute-start.25 = (f32[4,24,128]{2,1,0:T(8,128)S(1)}, f32[4,24,128]{2,1,0:T(8,128)S(1)}, u32[]{:S(2)}, u32[]{:S(2)}) collective-permute-start(f32[4,24,128]{2,1,0:T(8,128)S(1)} %get-tuple-element.135), channel_id=1, source_target_pairs={{0,4},{4,8},{8,12},{12,0},{1,5},{5,9},{9,13},{13,1},{2,6},{6,10},{... | collective-permute-start | bytes 147464 | tf_op jit(solution)/shard_map/ppermute | solution.py:595
  84.9 4.1 %collective-permute-start.26 = (f32[4,24,128]{2,1,0:T(8,128)S(1)}, f32[4,24,128]{2,1,0:T(8,128)S(1)}, u32[]{:S(2)}, u32[]{:S(2)}) collective-permute-start(f32[4,24,128]{2,1,0:T(8,128)S(1)} %get-tuple-element.136), channel_id=1, source_target_pairs={{0,12},{4,0},{8,4},{12,8},{1,13},{5,1},{9,5},{13,9},{2,14},{6,2},{... | collective-permute-start | bytes 147464 | tf_op jit(solution)/shard_map/ppermute | solution.py:595
  89.0 6.7 %collective-permute-start.32 = (f32[4,112,128]{2,1,0:T(8,128)S(1)}, f32[4,112,128]{2,1,0:T(8,128)S(1)}, u32[]{:S(2)}, u32[]{:S(2)}) collective-permute-start(f32[4,112,128]{2,1,0:T(8,128)S(1)} %pad_maximum_fusion.1.refs_0_), channel_id=1, source_target_pairs={{0,64},{16,80},{32,96},{48,112},{64,0},{80,16},{96,32},{112,48},{1... | collective-permute-start | bytes 688136 | tf_op jit(solution)/shard_map/ppermute | solution.py:595
  90.8 10.4 %collective-permute-start.30 = (f32[4,112,128]{2,1,0:T(8,128)S(1)}, f32[4,112,128]{2,1,0:T(8,128)S(1)}, u32[]{:S(2)}, u32[]{:S(2)}) collective-permute-start(f32[4,112,128]{2,1,0:T(8,128)S(1)} %pad_maximum_fusion.1.refs_0_), channel_id=1, source_target_pairs={{0,96},{16,112},{32,0},{48,16},{64,32},{80,48},{96,64},{112,80},{1... | collective-permute-start | bytes 688136 | tf_op jit(solution)/shard_map/ppermute | solution.py:595
  91.8 10.2 %collective-permute-start.28 = (f32[4,112,128]{2,1,0:T(8,128)S(1)}, f32[4,112,128]{2,1,0:T(8,128)S(1)}, u32[]{:S(2)}, u32[]{:S(2)}) collective-permute-start(f32[4,112,128]{2,1,0:T(8,128)S(1)} %pad_maximum_fusion.1.refs_0_), channel_id=1, source_target_pairs={{0,32},{16,48},{32,64},{48,80},{64,96},{80,112},{96,0},{112,16},{1... | collective-permute-start | bytes 688136 | tf_op jit(solution)/shard_map/ppermute | solution.py:595
  92.3 11.3 %collective-permute-start.27 = (f32[4,112,128]{2,1,0:T(8,128)S(1)}, f32[4,112,128]{2,1,0:T(8,128)S(1)}, u32[]{:S(2)}, u32[]{:S(2)}) collective-permute-start(f32[4,112,128]{2,1,0:T(8,128)S(1)} %pad_maximum_fusion.1.refs_0_), channel_id=1, source_target_pairs={{0,16},{16,0},{32,48},{48,32},{64,80},{80,64},{96,112},{112,96},{1... | collective-permute-start | bytes 688136 | tf_op jit(solution)/shard_map/ppermute | solution.py:599
  95.8 7.8 %collective-permute-start.33 = (f32[4,112,128]{2,1,0:T(8,128)S(1)}, f32[4,112,128]{2,1,0:T(8,128)S(1)}, u32[]{:S(2)}, u32[]{:S(2)}) collective-permute-start(f32[4,112,128]{2,1,0:T(8,128)S(1)} %collective-permute-done.32.refs_6_), channel_id=1, source_target_pairs={{0,16},{16,0},{32,48},{48,32},{64,80},{80,64},{96,112},{112,96},{1... | collective-permute-start | bytes 688136 | tf_op jit(solution)/shard_map/ppermute | solution.py:599
  (5 other events, 20.8 us)

commit v9 on v8

--- a/solution.py
+++ b/solution.py
@@ -231,9 +231,9 @@
     planes(first, count, 16, body)
 
 
-def level2_sweep(src, dst, f, w):
-    lane = iota((56, 128), 1)
-    mid, up, dn = pl.ds(8, 56), pl.ds(7, 56), pl.ds(9, 56)
+def level2_sweep(src, dst, f, w, start, size):
+    lane = iota((size, 128), 1)
+    mid, up, dn = pl.ds(start, size), pl.ds(start - 1, size), pl.ds(start + 1, size)
     for p in range(1, 9):
         m = src[p, mid]
         if p == 1:
@@ -306,17 +306,17 @@
     planes(1, 8, 8, restrict)
 
     src2, dst2 = a2, b2
-    for _ in range(7):
-        level2_sweep(src2, dst2, f2, w2)
+    for n in range(7):
+        level2_sweep(src2, dst2, f2, w2, *((8, 56) if n < 5 else (16, 40)))
         src2, dst2 = dst2, src2
 
     def prolong(p, j):
-        both = select(src2[p, pl.ds(8, 56)], uu[...])
+        both = select(src2[p, pl.ds(16, 40)], uu[...])
         for n, k in ((0, p - 1), (1, p + 7)):
             e = both[:, 128 * n:128 * n + 128]
             for q in (0, 1):
                 for h in (0, 1):
-                    rows = pl.ds(8 + h, 56, stride=2)
+                    rows = pl.ds(24 + h, 40, stride=2)
                     vb[5 + 2 * k + q, rows] = vb[5 + 2 * k + q, rows] + e
 
     planes(1, 8, 8, prolong)

time: 112 us -> 112 us (level)
  no operation moved by 1% of the time
where the time goes in v9:
time: 112 us; the launch traced here: 111 us
  starting transfers between devices  59.2 us (53%)
  Pallas kernels  33.1 us (30%)
  waiting for transfers between devices  15.9 us (14%)
  local copies, waits for them, and re-layouts  2.35 us (2%)
    ppermute x26, starting transfers between devices, shifted(): lax.ppermute(value, axis, [(i, (i + step) % size) for i in range(size)])  38.5 us
    pallas_call x11, Pallas kernels, call(): pl.pallas_call(kernel, out_shape=outs, in_specs=specs, out_specs=[VM] * l...  33.1 us
    ppermute x8, starting transfers between devices, swapped(): lax.ppermute(value, 'gx', [(i, i ^ 1) for i in range(lax.axis_size('gx'))])  20.7 us
    ppermute x26, waiting for transfers between devices, shifted(): lax.ppermute(value, axis, [(i, (i + step) % size) for i in range(size)])  13.7 us
  transfers between devices with their start and end apart: 34, of which 10 were waited for; matrix products, arithmetic and copies ran while one was open for 1% of the time, Pallas kernels for 9%

profile of v9, /device:TPU:1, one launch (start us, length us, event | category | flops | bytes accessed | tf_op | source)
XLA Modules:
  0.0 111.4 jit_solution(1228619683838400216)
XLA Ops:
  0.0 1.4 %copy-done.1 = f32[3,8,128,128]{3,2,1,0:T(8,128)S(1)} copy-done((f32[3,8,128,128]{3,2,1,0:T(8,128)S(1)}, f32[3,8,128,128]{3,2,1,0:T(8,128)}, u32[]{:S(2)}) %copy-start.1) | copy-done | bytes 1572888
  1.9 3.4 %collective-permute-start = (f32[128,128]{1,0:T(8,128)S(1)}, f32[128,128]{1,0:T(8,128)S(1)}, u32[]{:S(2)}, u32[]{:S(2)}) collective-permute-start(f32[128,128]{1,0:T(8,128)S(1)} %get-tuple-element.66), channel_id=1, source_target_pairs={{0,3},{1,0},{2,1},{3,2},{4,7},{5,4},{6,5},{7,6},{8,11},{9,8},{10,9... | collective-permute-start | bytes 196616 | tf_op jit(solution)/shard_map/ppermute | solution.py:595
  6.9 3.8 %collective-permute-start.2 = (f32[32,128]{1,0:T(8,128)S(1)}, f32[32,128]{1,0:T(8,128)S(1)}, u32[]{:S(2)}, u32[]{:S(2)}) collective-permute-start(f32[32,128]{1,0:T(8,128)S(1)} %pad_maximum_fusion.14), channel_id=1, source_target_pairs={{0,12},{4,0},{8,4},{12,8},{1,13},{5,1},{9,5},{13,9},{2,14},{6,2},{... | collective-permute-start | bytes 49160 | tf_op jit(solution)/shard_map/ppermute | solution.py:595
  10.8 2.9 %energy_first.1 = (f32[27,128,128]{2,1,0:T(8,128)S(1)}, f32[4,128,128]{2,1,0:T(8,128)S(1)}) custom-call(s32[3]{0:T(128)S(1)} %pad_add_fusion.pos, f32[27,128,128]{2,1,0:T(8,128)S(1)} %get-tuple-element.65.u0, f32[27,128,128]{2,1,0:T(8,128)S(1)} %get-tuple-element.68.bare, bf16[192,192]{1,0:T(8,128)(2,1)S(1)} %get-tuple-element.69.high, ...), custom_call_target="tpu_custom_call" | custom-call | tf_op jit(solution)/shard_map/energy_first/pallas_call | solution.py:581
  13.7 2.5 %collective-permute-start.3 = (f32[160,128]{1,0:T(8,128)S(1)}, f32[160,128]{1,0:T(8,128)S(1)}, u32[]{:S(2)}, u32[]{:S(2)}) collective-permute-start(f32[160,128]{1,0:T(8,128)S(1)} %pad_maximum_fusion.3), channel_id=1, source_target_pairs={{0,112},{16,0},{32,16},{48,32},{64,48},{80,64},{96,80},{112,96},{1... | collective-permute-start | bytes 245768 | tf_op jit(solution)/shard_map/ppermute | solution.py:595
  16.2 3.1 %energy_second.1.fb = f32[7,128,128]{2,1,0:T(8,128)S(1)} custom-call(s32[3]{0:T(128)S(1)} %pad_add_fusion.pos, f32[27,128,128]{2,1,0:T(8,128)S(1)} %get-tuple-element.65.u0, f32[27,128,128]{2,1,0:T(8,128)S(1)} %get-tuple-element.72.u1, bf16[192,192]{1,0:T(8,128)(2,1)S(1)} %get-tuple-element.69.high, bf16[192,192]{1,0:T(8,128)(2,1)S(1)} %get-tuple-element.70.low, ...), custom_call_target="tpu_custom_call" | custom-call | tf_op jit(solution)/shard_map/energy_second/pallas_call | solution.py:581
  19.3 1.3 %energy_last.1 = (f32[8,128,128]{2,1,0:T(8,128)S(1)}, f32[7,128,128]{2,1,0:T(8,128)S(1)}, f32[7,128,128]{2,1,0:T(8,128)S(1)}, f32[128,128]{1,0:T(8,128)S(1)}) custom-call(s32[3]{0:T(128)S(1)} %pad_add_fusion.pos, f32[27,128,128]{2,1,0:T(8,128)S(1)} %get-tuple-element.65.u0, f32[27,128,128]{2,1,0:T(8,128)S(1)} %get-tuple-element.72.u1, ...), custom_call_target="tpu_custom_call" | custom-call | tf_op jit(solution)/shard_map/energy_last/pallas_call | solution.py:581
  20.6 2.5 %collective-permute-start.7 = (f32[128,128]{1,0:T(8,128)S(1)}, f32[128,128]{1,0:T(8,128)S(1)}, u32[]{:S(2)}, u32[]{:S(2)}) collective-permute-start(f32[128,128]{1,0:T(8,128)S(1)} %get-tuple-element.80), channel_id=1, source_target_pairs={{0,3},{1,0},{2,1},{3,2},{4,7},{5,4},{6,5},{7,6},{8,11},{9,8},{10,9... | collective-permute-start | bytes 196616 | tf_op jit(solution)/shard_map/ppermute | solution.py:595
  23.1 1.3 %collective-permute-start.4 = (f32[7,128,128]{2,1,0:T(8,128)S(1)}, f32[7,128,128]{2,1,0:T(8,128)S(1)}, u32[]{:S(2)}, u32[]{:S(2)}) collective-permute-start(f32[7,128,128]{2,1,0:T(8,128)S(1)} %get-tuple-element.77), channel_id=1, source_target_pairs={{0,16},{16,32},{32,48},{48,64},{64,80},{80,96},{96,112},{112,0},{1... | collective-permute-start | bytes 1376264 | tf_op jit(solution)/shard_map/ppermute | solution.py:595
  24.4 3.0 %collective-permute-done.6 = f32[128,128]{1,0:T(8,128)S(1)} collective-permute-done((f32[128,128]{1,0:T(8,128)S(1)}, f32[128,128]{1,0:T(8,128)S(1)}, u32[]{:S(2)}, u32[]{:S(2)}) %collective-permute-start.6) | collective-permute-done | bytes 65568 | tf_op jit(solution)/shard_map/ppermute | solution.py:595
  27.5 2.0 %collective-permute-start.9 = (f32[72,128]{1,0:T(8,128)S(1)}, f32[72,128]{1,0:T(8,128)S(1)}, u32[]{:S(2)}, u32[]{:S(2)}) collective-permute-start(f32[72,128]{1,0:T(8,128)S(1)} %pad_maximum_fusion.13), channel_id=1, source_target_pairs={{0,12},{4,0},{8,4},{12,8},{1,13},{5,1},{9,5},{13,9},{2,14},{6,2},{... | collective-permute-start | bytes 110600 | tf_op jit(solution)/shard_map/ppermute | solution.py:595
  30.7 2.9 %collective-permute-done.8 = f32[72,128]{1,0:T(8,128)S(1)} collective-permute-done((f32[72,128]{1,0:T(8,128)S(1)}, f32[72,128]{1,0:T(8,128)S(1)}, u32[]{:S(2)}, u32[]{:S(2)}) %collective-permute-start.8) | collective-permute-done | bytes 36896 | tf_op jit(solution)/shard_map/ppermute | solution.py:595
  33.6 2.5 %collective-permute-start.11 = (f32[272,128]{1,0:T(8,128)S(1)}, f32[272,128]{1,0:T(8,128)S(1)}, u32[]{:S(2)}, u32[]{:S(2)}) collective-permute-start(f32[272,128]{1,0:T(8,128)S(1)} %pad_maximum_fusion.2.hc), channel_id=1, source_target_pairs={{0,112},{16,0},{32,16},{48,32},{64,48},{80,64},{96,80},{112,96},{1... | collective-permute-start | bytes 417800 | tf_op jit(solution)/shard_map/ppermute | solution.py:595
  40.4 2.4 %first.1 = (f32[24,160,128]{2,1,0:T(8,128)S(1)}, f32[24,160,128]{2,1,0:T(8,128)S(1)}, f32[24,160,128]{2,1,0:T(8,128)S(1)}, f32[24,160,128]{2,1,0:T(8,128)S(1)}, ...) custom-call(s32[3]{0:T(128)S(1)} %pad_add_fusion.pos, ...), custom_call_target="tpu_custom_call", output_to_operand_aliasing={{0}: (12, {}), {1}: (13, {}), {2}: (14, {}), {3}: (15, {})} | custom-call | tf_op jit(solution)/shard_map/first/pallas_call | solution.py:581
  42.9 2.7 %collective-permute-start.12 = (f32[64,128]{1,0:T(8,128)S(1)}, f32[64,128]{1,0:T(8,128)S(1)}, u32[]{:S(2)}, u32[]{:S(2)}) collective-permute-start(f32[64,128]{1,0:T(8,128)S(1)} %get-tuple-element.93), channel_id=1, source_target_pairs={{0,3},{1,0},{2,1},{3,2},{4,7},{5,4},{6,5},{7,6},{8,11},{9,8},{10,9... | collective-permute-start | bytes 98312 | tf_op jit(solution)/shard_map/ppermute | solution.py:595
  47.6 2.7 %collective-permute-start.15 = (f32[4,24,128]{2,1,0:T(8,128)S(1)}, f32[4,24,128]{2,1,0:T(8,128)S(1)}, u32[]{:S(2)}, u32[]{:S(2)}) collective-permute-start(f32[4,24,128]{2,1,0:T(8,128)S(1)} %get-tuple-element.138), channel_id=1, source_target_pairs={{0,12},{4,0},{8,4},{12,8},{1,13},{5,1},{9,5},{13,9},{2,14},{6,2},{... | collective-permute-start | bytes 147464 | tf_op jit(solution)/shard_map/ppermute | solution.py:595
  50.3 1.5 %collective-permute-done.14 = f32[4,24,128]{2,1,0:T(8,128)S(1)} collective-permute-done((f32[4,24,128]{2,1,0:T(8,128)S(1)}, f32[4,24,128]{2,1,0:T(8,128)S(1)}, u32[]{:S(2)}, u32[]{:S(2)}) %collective-permute-start.14) | collective-permute-done | bytes 49184 | tf_op jit(solution)/shard_map/ppermute | solution.py:595
  51.8 2.5 %collective-permute-start.21 = (f32[4,112,128]{2,1,0:T(8,128)S(1)}, f32[4,112,128]{2,1,0:T(8,128)S(1)}, u32[]{:S(2)}, u32[]{:S(2)}) collective-permute-start(f32[4,112,128]{2,1,0:T(8,128)S(1)} %pad_maximum_fusion.refs_0_), channel_id=1, source_target_pairs={{0,64},{16,80},{32,96},{48,112},{64,0},{80,16},{96,32},{112,48},{1... | collective-permute-start | bytes 688136 | tf_op jit(solution)/shard_map/ppermute | solution.py:595
  55.8 3.7 %collective-permute-start.16 = (f32[4,112,128]{2,1,0:T(8,128)S(1)}, f32[4,112,128]{2,1,0:T(8,128)S(1)}, u32[]{:S(2)}, u32[]{:S(2)}) collective-permute-start(f32[4,112,128]{2,1,0:T(8,128)S(1)} %pad_maximum_fusion.refs_0_), channel_id=1, source_target_pairs={{0,16},{16,0},{32,48},{48,32},{64,80},{80,64},{96,112},{112,96},{1... | collective-permute-start | bytes 688136 | tf_op jit(solution)/shard_map/ppermute | solution.py:599
  59.5 1.8 %outer.1 = (f32[24,160,128]{2,1,0:T(8,128)S(1)}, f32[24,160,128]{2,1,0:T(8,128)S(1)}, f32[24,160,128]{2,1,0:T(8,128)S(1)}, f32[24,160,128]{2,1,0:T(8,128)S(1)}, ...) custom-call(s32[3]{0:T(128)S(1)} %pad_add_fusion.pos, ...), custom_call_target="tpu_custom_call", output_to_operand_aliasing={{0}: (8, {}), {1}: (9, {}), {2}: (10, {}), {3}: (11, {}), {... | custom-call | tf_op jit(solution)/shard_map/outer/pallas_call | solution.py:581
  61.4 2.6 %collective-permute-start.22 = (f32[4,112,128]{2,1,0:T(8,128)S(1)}, f32[4,112,128]{2,1,0:T(8,128)S(1)}, u32[]{:S(2)}, u32[]{:S(2)}) collective-permute-start(f32[4,112,128]{2,1,0:T(8,128)S(1)} %collective-permute-done.21.refs_6_), channel_id=1, source_target_pairs={{0,16},{16,0},{32,48},{48,32},{64,80},{80,64},{96,112},{112,96},{1... | collective-permute-start | bytes 688136 | tf_op jit(solution)/shard_map/ppermute | solution.py:599
  65.1 2.0 %collective-permute-start.18 = (f32[4,112,128]{2,1,0:T(8,128)S(1)}, f32[4,112,128]{2,1,0:T(8,128)S(1)}, u32[]{:S(2)}, u32[]{:S(2)}) collective-permute-start(f32[4,112,128]{2,1,0:T(8,128)S(1)} %collective-permute-done.17.refs_2_), channel_id=1, source_target_pairs={{0,16},{16,0},{32,48},{48,32},{64,80},{80,64},{96,112},{112,96},{1... | collective-permute-start | bytes 688136 | tf_op jit(solution)/shard_map/ppermute | solution.py:599
  68.2 11.8 %middle.1 = (f32[24,160,128]{2,1,0:T(8,128)S(1)}, f32[24,160,128]{2,1,0:T(8,128)S(1)}, f32[4,64,128]{2,1,0:T(8,128)S(1)}, f32[64,128]{1,0:T(8,128)S(1)}, f32[64,128]{1,0:T(8,128)S(1)}) custom-call(s32[3]{0:T(128)S(1)} %pad_add_fusion.pos, f32[4,112,128]{2,1,0:T(8,128)S(1)} %pad_maximum_fusion.refs_0_, f32[4,112,128]{2,1,0:T(8,128)S(1)} %collective-permute-done.16.refs_1_, ...), custom_call_target="tpu_custom_call" | custom-call | tf_op jit(solution)/shard_map/middle/pallas_call | solution.py:581
  80.1 2.7 %collective-permute-start.23 = (f32[64,128]{1,0:T(8,128)S(1)}, f32[64,128]{1,0:T(8,128)S(1)}, u32[]{:S(2)}, u32[]{:S(2)}) collective-permute-start(f32[64,128]{1,0:T(8,128)S(1)} %get-tuple-element.121), channel_id=1, source_target_pairs={{0,3},{1,0},{2,1},{3,2},{4,7},{5,4},{6,5},{7,6},{8,11},{9,8},{10,9... | collective-permute-start | bytes 98312 | tf_op jit(solution)/shard_map/ppermute | solution.py:595
  82.8 1.3 %collective-permute-done.24 = f32[64,128]{1,0:T(8,128)S(1)} collective-permute-done((f32[64,128]{1,0:T(8,128)S(1)}, f32[64,128]{1,0:T(8,128)S(1)}, u32[]{:S(2)}, u32[]{:S(2)}) %collective-permute-start.24) | collective-permute-done | bytes 32800 | tf_op jit(solution)/shard_map/ppermute | solution.py:595
  84.8 2.7 %collective-permute-start.26 = (f32[4,24,128]{2,1,0:T(8,128)S(1)}, f32[4,24,128]{2,1,0:T(8,128)S(1)}, u32[]{:S(2)}, u32[]{:S(2)}) collective-permute-start(f32[4,24,128]{2,1,0:T(8,128)S(1)} %get-tuple-element.136), channel_id=1, source_target_pairs={{0,12},{4,0},{8,4},{12,8},{1,13},{5,1},{9,5},{13,9},{2,14},{6,2},{... | collective-permute-start | bytes 147464 | tf_op jit(solution)/shard_map/ppermute | solution.py:595
  87.6 1.4 %collective-permute-done.25 = f32[4,24,128]{2,1,0:T(8,128)S(1)} collective-permute-done((f32[4,24,128]{2,1,0:T(8,128)S(1)}, f32[4,24,128]{2,1,0:T(8,128)S(1)}, u32[]{:S(2)}, u32[]{:S(2)}) %collective-permute-start.25) | collective-permute-done | bytes 49184 | tf_op jit(solution)/shard_map/ppermute | solution.py:595
  89.0 1.8 %collective-permute-start.32 = (f32[4,112,128]{2,1,0:T(8,128)S(1)}, f32[4,112,128]{2,1,0:T(8,128)S(1)}, u32[]{:S(2)}, u32[]{:S(2)}) collective-permute-start(f32[4,112,128]{2,1,0:T(8,128)S(1)} %pad_maximum_fusion.1.refs_0_), channel_id=1, source_target_pairs={{0,64},{16,80},{32,96},{48,112},{64,0},{80,16},{96,32},{112,48},{1... | collective-permute-start | bytes 688136 | tf_op jit(solution)/shard_map/ppermute | solution.py:595
  92.2 3.5 %collective-permute-start.27 = (f32[4,112,128]{2,1,0:T(8,128)S(1)}, f32[4,112,128]{2,1,0:T(8,128)S(1)}, u32[]{:S(2)}, u32[]{:S(2)}) collective-permute-start(f32[4,112,128]{2,1,0:T(8,128)S(1)} %pad_maximum_fusion.1.refs_0_), channel_id=1, source_target_pairs={{0,16},{16,0},{32,48},{48,32},{64,80},{80,64},{96,112},{112,96},{1... | collective-permute-start | bytes 688136 | tf_op jit(solution)/shard_map/ppermute | solution.py:599
  95.8 5.4 %collective-permute-start.33 = (f32[4,112,128]{2,1,0:T(8,128)S(1)}, f32[4,112,128]{2,1,0:T(8,128)S(1)}, u32[]{:S(2)}, u32[]{:S(2)}) collective-permute-start(f32[4,112,128]{2,1,0:T(8,128)S(1)} %collective-permute-done.32.refs_6_), channel_id=1, source_target_pairs={{0,16},{16,0},{32,48},{48,32},{64,80},{80,64},{96,112},{112,96},{1... | collective-permute-start | bytes 688136 | tf_op jit(solution)/shard_map/ppermute | solution.py:599
  101.9 1.6 %collective-permute-start.29 = (f32[4,112,128]{2,1,0:T(8,128)S(1)}, f32[4,112,128]{2,1,0:T(8,128)S(1)}, u32[]{:S(2)}, u32[]{:S(2)}) collective-permute-start(f32[4,112,128]{2,1,0:T(8,128)S(1)} %collective-permute-done.28.refs_2_), channel_id=1, source_target_pairs={{0,16},{16,0},{32,48},{48,32},{64,80},{80,64},{96,112},{112,96},{1... | collective-permute-start | bytes 688136 | tf_op jit(solution)/shard_map/ppermute | solution.py:599
  104.7 6.8 %last.1 = f32[8,128,128]{2,1,0:T(8,128)} custom-call(s32[3]{0:T(128)S(1)} %pad_add_fusion.pos, f32[4,112,128]{2,1,0:T(8,128)S(1)} %pad_maximum_fusion.1.refs_0_, f32[4,112,128]{2,1,0:T(8,128)S(1)} %collective-permute-done.27.refs_1_, f32[4,112,128]{2,1,0:T(8,128)S(1)} %collective-permute-done.28.refs_2_, f32[4,112,128]{2,1,0:T(8,128)S(1)} %collective-permute-done.29.refs_3_, ...), custom_call_target="tpu_custom_call" | custom-call | tf_op jit(solution)/shard_map/last/pallas_call | solution.py:581
  (86 shorter events, 17.7 us)
Async XLA Ops:
  1.9 5.0 %collective-permute-start = (f32[128,128]{1,0:T(8,128)S(1)}, f32[128,128]{1,0:T(8,128)S(1)}, u32[]{:S(2)}, u32[]{:S(2)}) collective-permute-start(f32[128,128]{1,0:T(8,128)S(1)} %get-tuple-element.66), channel_id=1, source_target_pairs={{0,3},{1,0},{2,1},{3,2},{4,7},{5,4},{6,5},{7,6},{8,11},{9,8},{10,9... | collective-permute-start | bytes 196616 | tf_op jit(solution)/shard_map/ppermute | solution.py:595
  5.3 14.0 %collective-permute-start.1 = (f32[3,128,128]{2,1,0:T(8,128)S(1)}, f32[3,128,128]{2,1,0:T(8,128)S(1)}, u32[]{:S(2)}, u32[]{:S(2)}) collective-permute-start(f32[3,128,128]{2,1,0:T(8,128)S(1)} %slice_bitcast_fusion), channel_id=1, source_target_pairs={{0,112},{16,0},{32,16},{48,32},{64,48},{80,64},{96,80},{112,96},{1... | collective-permute-start | bytes 589832 | tf_op jit(solution)/shard_map/ppermute | solution.py:595
  6.9 6.8 %collective-permute-start.2 = (f32[32,128]{1,0:T(8,128)S(1)}, f32[32,128]{1,0:T(8,128)S(1)}, u32[]{:S(2)}, u32[]{:S(2)}) collective-permute-start(f32[32,128]{1,0:T(8,128)S(1)} %pad_maximum_fusion.14), channel_id=1, source_target_pairs={{0,12},{4,0},{8,4},{12,8},{1,13},{5,1},{9,5},{13,9},{2,14},{6,2},{... | collective-permute-start | bytes 49160 | tf_op jit(solution)/shard_map/ppermute | solution.py:595
  13.7 5.6 %collective-permute-start.3 = (f32[160,128]{1,0:T(8,128)S(1)}, f32[160,128]{1,0:T(8,128)S(1)}, u32[]{:S(2)}, u32[]{:S(2)}) collective-permute-start(f32[160,128]{1,0:T(8,128)S(1)} %pad_maximum_fusion.3), channel_id=1, source_target_pairs={{0,112},{16,0},{32,16},{48,32},{64,48},{80,64},{96,80},{112,96},{1... | collective-permute-start | bytes 245768 | tf_op jit(solution)/shard_map/ppermute | solution.py:595
  20.6 3.8 %collective-permute-start.7 = (f32[128,128]{1,0:T(8,128)S(1)}, f32[128,128]{1,0:T(8,128)S(1)}, u32[]{:S(2)}, u32[]{:S(2)}) collective-permute-start(f32[128,128]{1,0:T(8,128)S(1)} %get-tuple-element.80), channel_id=1, source_target_pairs={{0,3},{1,0},{2,1},{3,2},{4,7},{5,4},{6,5},{7,6},{8,11},{9,8},{10,9... | collective-permute-start | bytes 196616 | tf_op jit(solution)/shard_map/ppermute | solution.py:595
  23.1 4.3 %collective-permute-start.6 = (f32[128,128]{1,0:T(8,128)S(1)}, f32[128,128]{1,0:T(8,128)S(1)}, u32[]{:S(2)}, u32[]{:S(2)}) collective-permute-start(f32[128,128]{1,0:T(8,128)S(1)} %get-tuple-element.80), channel_id=1, source_target_pairs={{0,1},{1,2},{2,3},{3,0},{4,5},{5,6},{6,7},{7,4},{8,9},{9,10},{10,1... | collective-permute-start | bytes 196616 | tf_op jit(solution)/shard_map/ppermute | solution.py:595
  23.1 17.2 %collective-permute-start.4 = (f32[7,128,128]{2,1,0:T(8,128)S(1)}, f32[7,128,128]{2,1,0:T(8,128)S(1)}, u32[]{:S(2)}, u32[]{:S(2)}) collective-permute-start(f32[7,128,128]{2,1,0:T(8,128)S(1)} %get-tuple-element.77), channel_id=1, source_target_pairs={{0,16},{16,32},{32,48},{48,64},{64,80},{80,96},{96,112},{112,0},{1... | collective-permute-start | bytes 1376264 | tf_op jit(solution)/shard_map/ppermute | solution.py:595
  24.4 15.9 %collective-permute-start.5 = (f32[7,128,128]{2,1,0:T(8,128)S(1)}, f32[7,128,128]{2,1,0:T(8,128)S(1)}, u32[]{:S(2)}, u32[]{:S(2)}) collective-permute-start(f32[7,128,128]{2,1,0:T(8,128)S(1)} %get-tuple-element.78), channel_id=1, source_target_pairs={{0,112},{16,0},{32,16},{48,32},{64,48},{80,64},{96,80},{112,96},{1... | collective-permute-start | bytes 1376264 | tf_op jit(solution)/shard_map/ppermute | solution.py:595
  27.5 3.2 %collective-permute-start.9 = (f32[72,128]{1,0:T(8,128)S(1)}, f32[72,128]{1,0:T(8,128)S(1)}, u32[]{:S(2)}, u32[]{:S(2)}) collective-permute-start(f32[72,128]{1,0:T(8,128)S(1)} %pad_maximum_fusion.13), channel_id=1, source_target_pairs={{0,12},{4,0},{8,4},{12,8},{1,13},{5,1},{9,5},{13,9},{2,14},{6,2},{... | collective-permute-start | bytes 110600 | tf_op jit(solution)/shard_map/ppermute | solution.py:595
  29.5 4.0 %collective-permute-start.8 = (f32[72,128]{1,0:T(8,128)S(1)}, f32[72,128]{1,0:T(8,128)S(1)}, u32[]{:S(2)}, u32[]{:S(2)}) collective-permute-start(f32[72,128]{1,0:T(8,128)S(1)} %pad_maximum_fusion.12), channel_id=1, source_target_pairs={{0,4},{4,8},{8,12},{12,0},{1,5},{5,9},{9,13},{13,1},{2,6},{6,10},{... | collective-permute-start | bytes 110600 | tf_op jit(solution)/shard_map/ppermute | solution.py:595
  33.6 6.8 %collective-permute-start.11 = (f32[272,128]{1,0:T(8,128)S(1)}, f32[272,128]{1,0:T(8,128)S(1)}, u32[]{:S(2)}, u32[]{:S(2)}) collective-permute-start(f32[272,128]{1,0:T(8,128)S(1)} %pad_maximum_fusion.2.hc), channel_id=1, source_target_pairs={{0,112},{16,0},{32,16},{48,32},{64,48},{80,64},{96,80},{112,96},{1... | collective-permute-start | bytes 417800 | tf_op jit(solution)/shard_map/ppermute | solution.py:595
  36.1 4.2 %collective-permute-start.10 = (f32[272,128]{1,0:T(8,128)S(1)}, f32[272,128]{1,0:T(8,128)S(1)}, u32[]{:S(2)}, u32[]{:S(2)}) collective-permute-start(f32[272,128]{1,0:T(8,128)S(1)} %pad_maximum_fusion.2.hc), channel_id=1, source_target_pairs={{0,16},{16,32},{32,48},{48,64},{64,80},{80,96},{96,112},{112,0},{1... | collective-permute-start | bytes 417800 | tf_op jit(solution)/shard_map/ppermute | solution.py:595
  42.8 4.0 %collective-permute-start.13 = (f32[64,128]{1,0:T(8,128)S(1)}, f32[64,128]{1,0:T(8,128)S(1)}, u32[]{:S(2)}, u32[]{:S(2)}) collective-permute-start(f32[64,128]{1,0:T(8,128)S(1)} %get-tuple-element.94), channel_id=1, source_target_pairs={{0,1},{1,2},{2,3},{3,0},{4,5},{5,6},{6,7},{7,4},{8,9},{9,10},{10,1... | collective-permute-start | bytes 98312 | tf_op jit(solution)/shard_map/ppermute | solution.py:595
  42.9 4.2 %collective-permute-start.12 = (f32[64,128]{1,0:T(8,128)S(1)}, f32[64,128]{1,0:T(8,128)S(1)}, u32[]{:S(2)}, u32[]{:S(2)}) collective-permute-start(f32[64,128]{1,0:T(8,128)S(1)} %get-tuple-element.93), channel_id=1, source_target_pairs={{0,3},{1,0},{2,1},{3,2},{4,7},{5,4},{6,5},{7,6},{8,11},{9,8},{10,9... | collective-permute-start | bytes 98312 | tf_op jit(solution)/shard_map/ppermute | solution.py:595
  47.6 4.2 %collective-permute-start.14 = (f32[4,24,128]{2,1,0:T(8,128)S(1)}, f32[4,24,128]{2,1,0:T(8,128)S(1)}, u32[]{:S(2)}, u32[]{:S(2)}) collective-permute-start(f32[4,24,128]{2,1,0:T(8,128)S(1)} %get-tuple-element.137), channel_id=1, source_target_pairs={{0,4},{4,8},{8,12},{12,0},{1,5},{5,9},{9,13},{13,1},{2,6},{6,10},{... | collective-permute-start | bytes 147464 | tf_op jit(solution)/shard_map/ppermute | solution.py:595
  47.6 4.1 %collective-permute-start.15 = (f32[4,24,128]{2,1,0:T(8,128)S(1)}, f32[4,24,128]{2,1,0:T(8,128)S(1)}, u32[]{:S(2)}, u32[]{:S(2)}) collective-permute-start(f32[4,24,128]{2,1,0:T(8,128)S(1)} %get-tuple-element.138), channel_id=1, source_target_pairs={{0,12},{4,0},{8,4},{12,8},{1,13},{5,1},{9,5},{13,9},{2,14},{6,2},{... | collective-permute-start | bytes 147464 | tf_op jit(solution)/shard_map/ppermute | solution.py:595
  51.8 9.6 %collective-permute-start.21 = (f32[4,112,128]{2,1,0:T(8,128)S(1)}, f32[4,112,128]{2,1,0:T(8,128)S(1)}, u32[]{:S(2)}, u32[]{:S(2)}) collective-permute-start(f32[4,112,128]{2,1,0:T(8,128)S(1)} %pad_maximum_fusion.refs_0_), channel_id=1, source_target_pairs={{0,64},{16,80},{32,96},{48,112},{64,0},{80,16},{96,32},{112,48},{1... | collective-permute-start | bytes 688136 | tf_op jit(solution)/shard_map/ppermute | solution.py:595
  54.3 9.6 %collective-permute-start.19 = (f32[4,112,128]{2,1,0:T(8,128)S(1)}, f32[4,112,128]{2,1,0:T(8,128)S(1)}, u32[]{:S(2)}, u32[]{:S(2)}) collective-permute-start(f32[4,112,128]{2,1,0:T(8,128)S(1)} %pad_maximum_fusion.refs_0_), channel_id=1, source_target_pairs={{0,96},{16,112},{32,0},{48,16},{64,32},{80,48},{96,64},{112,80},{1... | collective-permute-start | bytes 688136 | tf_op jit(solution)/shard_map/ppermute | solution.py:595
  55.4 9.7 %collective-permute-start.17 = (f32[4,112,128]{2,1,0:T(8,128)S(1)}, f32[4,112,128]{2,1,0:T(8,128)S(1)}, u32[]{:S(2)}, u32[]{:S(2)}) collective-permute-start(f32[4,112,128]{2,1,0:T(8,128)S(1)} %pad_maximum_fusion.refs_0_), channel_id=1, source_target_pairs={{0,32},{16,48},{32,64},{48,80},{64,96},{80,112},{96,0},{112,16},{1... | collective-permute-start | bytes 688136 | tf_op jit(solution)/shard_map/ppermute | solution.py:595
  55.8 11.3 %collective-permute-start.16 = (f32[4,112,128]{2,1,0:T(8,128)S(1)}, f32[4,112,128]{2,1,0:T(8,128)S(1)}, u32[]{:S(2)}, u32[]{:S(2)}) collective-permute-start(f32[4,112,128]{2,1,0:T(8,128)S(1)} %pad_maximum_fusion.refs_0_), channel_id=1, source_target_pairs={{0,16},{16,0},{32,48},{48,32},{64,80},{80,64},{96,112},{112,96},{1... | collective-permute-start | bytes 688136 | tf_op jit(solution)/shard_map/ppermute | solution.py:599
  61.4 5.7 %collective-permute-start.22 = (f32[4,112,128]{2,1,0:T(8,128)S(1)}, f32[4,112,128]{2,1,0:T(8,128)S(1)}, u32[]{:S(2)}, u32[]{:S(2)}) collective-permute-start(f32[4,112,128]{2,1,0:T(8,128)S(1)} %collective-permute-done.21.refs_6_), channel_id=1, source_target_pairs={{0,16},{16,0},{32,48},{48,32},{64,80},{80,64},{96,112},{112,96},{1... | collective-permute-start | bytes 688136 | tf_op jit(solution)/shard_map/ppermute | solution.py:599
  64.0 3.1 %collective-permute-start.20 = (f32[4,112,128]{2,1,0:T(8,128)S(1)}, f32[4,112,128]{2,1,0:T(8,128)S(1)}, u32[]{:S(2)}, u32[]{:S(2)}) collective-permute-start(f32[4,112,128]{2,1,0:T(8,128)S(1)} %collective-permute-done.19.refs_4_), channel_id=1, source_target_pairs={{0,16},{16,0},{32,48},{48,32},{64,80},{80,64},{96,112},{112,96},{1... | collective-permute-start | bytes 688136 | tf_op jit(solution)/shard_map/ppermute | solution.py:599
  65.1 3.1 %collective-permute-start.18 = (f32[4,112,128]{2,1,0:T(8,128)S(1)}, f32[4,112,128]{2,1,0:T(8,128)S(1)}, u32[]{:S(2)}, u32[]{:S(2)}) collective-permute-start(f32[4,112,128]{2,1,0:T(8,128)S(1)} %collective-permute-done.17.refs_2_), channel_id=1, source_target_pairs={{0,16},{16,0},{32,48},{48,32},{64,80},{80,64},{96,112},{112,96},{1... | collective-permute-start | bytes 688136 | tf_op jit(solution)/shard_map/ppermute | solution.py:599
  80.0 4.0 %collective-permute-start.24 = (f32[64,128]{1,0:T(8,128)S(1)}, f32[64,128]{1,0:T(8,128)S(1)}, u32[]{:S(2)}, u32[]{:S(2)}) collective-permute-start(f32[64,128]{1,0:T(8,128)S(1)} %get-tuple-element.122), channel_id=1, source_target_pairs={{0,1},{1,2},{2,3},{3,0},{4,5},{5,6},{6,7},{7,4},{8,9},{9,10},{10,1... | collective-permute-start | bytes 98312 | tf_op jit(solution)/shard_map/ppermute | solution.py:595
  80.1 4.2 %collective-permute-start.23 = (f32[64,128]{1,0:T(8,128)S(1)}, f32[64,128]{1,0:T(8,128)S(1)}, u32[]{:S(2)}, u32[]{:S(2)}) collective-permute-start(f32[64,128]{1,0:T(8,128)S(1)} %get-tuple-element.121), channel_id=1, source_target_pairs={{0,3},{1,0},{2,1},{3,2},{4,7},{5,4},{6,5},{7,6},{8,11},{9,8},{10,9... | collective-permute-start | bytes 98312 | tf_op jit(solution)/shard_map/ppermute | solution.py:595
  84.8 4.2 %collective-permute-start.25 = (f32[4,24,128]{2,1,0:T(8,128)S(1)}, f32[4,24,128]{2,1,0:T(8,128)S(1)}, u32[]{:S(2)}, u32[]{:S(2)}) collective-permute-start(f32[4,24,128]{2,1,0:T(8,128)S(1)} %get-tuple-element.135), channel_id=1, source_target_pairs={{0,4},{4,8},{8,12},{12,0},{1,5},{5,9},{9,13},{13,1},{2,6},{6,10},{... | collective-permute-start | bytes 147464 | tf_op jit(solution)/shard_map/ppermute | solution.py:595
  84.8 4.1 %collective-permute-start.26 = (f32[4,24,128]{2,1,0:T(8,128)S(1)}, f32[4,24,128]{2,1,0:T(8,128)S(1)}, u32[]{:S(2)}, u32[]{:S(2)}) collective-permute-start(f32[4,24,128]{2,1,0:T(8,128)S(1)} %get-tuple-element.136), channel_id=1, source_target_pairs={{0,12},{4,0},{8,4},{12,8},{1,13},{5,1},{9,5},{13,9},{2,14},{6,2},{... | collective-permute-start | bytes 147464 | tf_op jit(solution)/shard_map/ppermute | solution.py:595
  89.0 6.7 %collective-permute-start.32 = (f32[4,112,128]{2,1,0:T(8,128)S(1)}, f32[4,112,128]{2,1,0:T(8,128)S(1)}, u32[]{:S(2)}, u32[]{:S(2)}) collective-permute-start(f32[4,112,128]{2,1,0:T(8,128)S(1)} %pad_maximum_fusion.1.refs_0_), channel_id=1, source_target_pairs={{0,64},{16,80},{32,96},{48,112},{64,0},{80,16},{96,32},{112,48},{1... | collective-permute-start | bytes 688136 | tf_op jit(solution)/shard_map/ppermute | solution.py:595
  90.8 10.4 %collective-permute-start.30 = (f32[4,112,128]{2,1,0:T(8,128)S(1)}, f32[4,112,128]{2,1,0:T(8,128)S(1)}, u32[]{:S(2)}, u32[]{:S(2)}) collective-permute-start(f32[4,112,128]{2,1,0:T(8,128)S(1)} %pad_maximum_fusion.1.refs_0_), channel_id=1, source_target_pairs={{0,96},{16,112},{32,0},{48,16},{64,32},{80,48},{96,64},{112,80},{1... | collective-permute-start | bytes 688136 | tf_op jit(solution)/shard_map/ppermute | solution.py:595
  91.8 10.2 %collective-permute-start.28 = (f32[4,112,128]{2,1,0:T(8,128)S(1)}, f32[4,112,128]{2,1,0:T(8,128)S(1)}, u32[]{:S(2)}, u32[]{:S(2)}) collective-permute-start(f32[4,112,128]{2,1,0:T(8,128)S(1)} %pad_maximum_fusion.1.refs_0_), channel_id=1, source_target_pairs={{0,32},{16,48},{32,64},{48,80},{64,96},{80,112},{96,0},{112,16},{1... | collective-permute-start | bytes 688136 | tf_op jit(solution)/shard_map/ppermute | solution.py:595
  92.2 11.3 %collective-permute-start.27 = (f32[4,112,128]{2,1,0:T(8,128)S(1)}, f32[4,112,128]{2,1,0:T(8,128)S(1)}, u32[]{:S(2)}, u32[]{:S(2)}) collective-permute-start(f32[4,112,128]{2,1,0:T(8,128)S(1)} %pad_maximum_fusion.1.refs_0_), channel_id=1, source_target_pairs={{0,16},{16,0},{32,48},{48,32},{64,80},{80,64},{96,112},{112,96},{1... | collective-permute-start | bytes 688136 | tf_op jit(solution)/shard_map/ppermute | solution.py:599
  95.8 7.8 %collective-permute-start.33 = (f32[4,112,128]{2,1,0:T(8,128)S(1)}, f32[4,112,128]{2,1,0:T(8,128)S(1)}, u32[]{:S(2)}, u32[]{:S(2)}) collective-permute-start(f32[4,112,128]{2,1,0:T(8,128)S(1)} %collective-permute-done.32.refs_6_), channel_id=1, source_target_pairs={{0,16},{16,0},{32,48},{48,32},{64,80},{80,64},{96,112},{112,96},{1... | collective-permute-start | bytes 688136 | tf_op jit(solution)/shard_map/ppermute | solution.py:599
  (5 other events, 20.8 us)
